TPU v7x, 32 devices: a whole 2x2x4 slice. The times are simulated.
32 devices in a mesh: tok: 16 (over z, y, x), row: 2 (over core).
Axes of the slice: x: 2, y: 2, z: 4, core: 2. Of those that a mesh axis runs over, the one named last changes fastest.
Arguments:
- tokens: bfloat16 [8, 4096, 768], P('row', 'tok'), may hold values from -6 to 6
- out_grad: bfloat16 [8, 4096, 768], P('row', 'tok'), may hold values from -6 to 6
- doc_lengths: int32 [8, 4, 8], P('row'), may hold values from 1 to 512, 1024 in all within a row
- first_gain: float32 [768], replicated, may hold values from 0.1 to 1.9
- first_bias: float32 [768], replicated, may hold values from -3 to 3
- qkv_weight: bfloat16 [768, 2304], P('tok', 'row'), may hold values from -0.21875 to 0.21875
- query_bias: float32 [768], replicated, may hold values from -3 to 3
- value_bias: float32 [768], replicated, may hold values from -3 to 3
- proj_weight: bfloat16 [768, 768], P('tok', 'row'), may hold values from -3.5 to 3.5
- proj_bias: float32 [768], replicated, may hold values from -4 to 4
- second_gain: float32 [768], replicated, may hold values from 0.1 to 1.9
- second_bias: float32 [768], replicated, may hold values from -3 to 3
- up_weight: bfloat16 [768, 3072], P('tok', 'row'), may hold values from -0.21875 to 0.21875
- up_bias: float32 [3072], replicated, may hold values from -3 to 3
- down_weight: bfloat16 [3072, 768], P('tok', 'row'), may hold values from -0.875 to 0.875
- down_bias: float32 [768], replicated, may hold values from -4 to 4
Outputs:
- output: bfloat16 [8, 4096, 768], P('row', 'tok')
- tokens_grad: bfloat16 [8, 4096, 768], P('row', 'tok')
- qkv_weight_grad: float32 [768, 2304], P('tok', 'row')
- proj_weight_grad: float32 [768, 768], P('tok', 'row')
- up_weight_grad: float32 [768, 3072], P('tok', 'row')
- down_weight_grad: float32 [3072, 768], P('tok', 'row')
- first_gain_grad: float32 [768], replicated
- first_bias_grad: float32 [768], replicated
- query_bias_grad: float32 [768], replicated
- value_bias_grad: float32 [768], replicated
- proj_bias_grad: float32 [768], replicated
- second_gain_grad: float32 [768], replicated
- second_bias_grad: float32 [768], replicated
- up_bias_grad: float32 [3072], replicated
- down_bias_grad: float32 [768], replicated
Inputs may be any that keep to these rules, and one draw needn't show every extreme that they name: `doc_lengths`: each packed row holds 8 documents whose lengths, in order, sum to 1024; some document has exactly 512 tokens.
All inputs are finite; a program needn't handle non-finite values.
Results may differ from a plain program's by a relative error of at most 0.018.
Values may be sent and summed in bfloat16 or wider, within the bound.
No kernel may reach another device: no remote copies, remote signals or barrier semaphores. Data moves between devices by JAX's collectives and lax.ppermute only.
A program may use at most 192 MiB of HBM per device.

v0:
```python
import math

import jax
import jax.numpy as jnp
from jax import lax
from jax.sharding import PartitionSpec as P

H = 12
HD = 64
DEPTH = 48


EPSILON = 1e-05
MASKED = -1000000000.0
TANH_ROOT = 0.7978845608028654
TANH_CUBIC = 0.044715


def from_partner(block, axis, apart):
    count = lax.axis_size(axis)
    route = []
    for low in range(count):
        high = low | 1 << apart
        if high != low and high < count:
            route += [(low, high), (high, low)]
    return lax.ppermute(block, axis, route)


def norm_parts(values):
    centre = values - jnp.mean(values, axis=-1, keepdims=True)
    inverse = lax.rsqrt(jnp.mean(centre * centre, axis=-1, keepdims=True) + EPSILON)
    return (centre * inverse, inverse)


def norm_back(grad_norm, normed, inverse, gain_vec):
    spread = grad_norm * gain_vec
    return inverse * (
        spread
        - jnp.mean(spread, axis=-1, keepdims=True)
        - normed * jnp.mean(spread * normed, axis=-1, keepdims=True)
    )


def gelu_value(pre_act):
    return (
        0.5
        * pre_act
        * (1.0 + jnp.tanh(TANH_ROOT * (pre_act + TANH_CUBIC * pre_act * pre_act * pre_act)))
    )


def gelu_slope(pre_act):
    tanh_part = jnp.tanh(TANH_ROOT * (pre_act + TANH_CUBIC * pre_act * pre_act * pre_act))
    return 0.5 * (1.0 + tanh_part) + 0.5 * pre_act * (1.0 - tanh_part * tanh_part) * TANH_ROOT * (
        1.0 + 3.0 * TANH_CUBIC * pre_act * pre_act
    )


def slot_picker(quad_place):
    order = jnp.bitwise_xor(jnp.arange(4, dtype=jnp.int32), quad_place)
    return (order[:, None] == jnp.arange(4, dtype=jnp.int32)[None, :]).astype(jnp.bfloat16)


def quad_exchange(slots, sender):
    full_shape = slots.shape
    halves = slots.reshape((2, 2) + full_shape[1:])
    arrived = sender(halves[:, 1], 0)
    halves = jnp.stack([halves[:, 0], arrived], axis=1)
    arrived = sender(halves[1], 1)
    halves = jnp.stack([halves[0], arrived], axis=0)
    return halves.reshape(full_shape)


def to_items(slots, heads_here):
    row_count = slots.shape[1]
    piece_len = slots.shape[2]
    split = slots.reshape(4, row_count, piece_len, heads_here, HD)
    return split.transpose(1, 3, 0, 2, 4).reshape(row_count * heads_here, 4 * piece_len, HD)


def from_items(items, row_count, heads_here):
    row_len = items.shape[1]
    split = items.reshape(row_count, heads_here, 4, row_len // 4, HD)
    return split.transpose(2, 0, 3, 1, 4).reshape(4, row_count, row_len // 4, heads_here * HD)


def allowed_keys(segment_row, positions):
    return (segment_row[:, None] == segment_row[None, :]) & (
        positions[None, :] <= positions[:, None]
    )


def attend(queries, keys_in, values_in, segment_row, positions, score_scale):
    scores = (
        jnp.einsum("qd,kd->qk", queries, keys_in, preferred_element_type=jnp.float32) * score_scale
    )
    scores = jnp.where(allowed_keys(segment_row, positions), scores, MASKED)
    row_max = jnp.max(scores, axis=-1, keepdims=True)
    shifted = jnp.exp(scores - row_max)
    row_total = jnp.sum(shifted, axis=-1, keepdims=True)
    weights = (shifted / row_total).astype(jnp.bfloat16)
    result = jnp.dot(weights, values_in, preferred_element_type=jnp.float32).astype(jnp.bfloat16)
    return (result, (row_max + jnp.log(row_total))[:, 0])


def attend_back(
    queries, keys_in, values_in, grad_result, segment_row, log_total, positions, score_scale
):
    scores = (
        jnp.einsum("qd,kd->qk", queries, keys_in, preferred_element_type=jnp.float32) * score_scale
    )
    weights = jnp.where(
        allowed_keys(segment_row, positions), jnp.exp(scores - log_total[:, None]), 0.0
    )
    grad_values = jnp.einsum(
        "qk,qd->kd", weights.astype(jnp.bfloat16), grad_result, preferred_element_type=jnp.float32
    )
    grad_weights = jnp.einsum(
        "qd,kd->qk", grad_result, values_in, preferred_element_type=jnp.float32
    )
    inner = jnp.sum(weights * grad_weights, axis=-1, keepdims=True)
    grad_scores = (weights * (grad_weights - inner)).astype(jnp.bfloat16)
    grad_queries = jnp.dot(grad_scores, keys_in, preferred_element_type=jnp.float32) * score_scale
    grad_keys = (
        jnp.einsum("qk,qd->kd", grad_scores, queries, preferred_element_type=jnp.float32)
        * score_scale
    )
    return (
        grad_queries.astype(jnp.bfloat16),
        grad_keys.astype(jnp.bfloat16),
        grad_values.astype(jnp.bfloat16),
    )


def per_device(
    tokens,
    out_grad,
    doc_lengths,
    first_gain,
    first_bias,
    qkv_weight,
    query_bias,
    value_bias,
    proj_weight,
    proj_bias,
    second_gain,
    second_bias,
    up_weight,
    up_bias,
    down_weight,
    down_bias,
):
    row_count, piece_len, model_width = tokens.shape
    token_count = row_count * piece_len
    heads_here = H // 4
    head_cols = heads_here * HD
    row_len = 4 * piece_len
    branch_scale = 1.0 / math.sqrt(DEPTH)
    score_scale = 1.0 / math.sqrt(HD)
    tok_index = lax.axis_index("tok")
    quad_place = tok_index % 4
    picker = slot_picker(quad_place)

    def attn_weights():
        by_rows = (
            lax.all_gather(qkv_weight, "tok", axis=0, tiled=True),
            lax.all_gather(proj_weight, "tok", axis=0, tiled=True),
        )
        return (
            lax.all_gather(by_rows[0], "row", axis=1, tiled=True),
            lax.all_gather(by_rows[1], "row", axis=1, tiled=True),
        )

    def mlp_weights():
        by_rows = (
            lax.all_gather(up_weight, "tok", axis=0, tiled=True),
            lax.all_gather(down_weight, "tok", axis=0, tiled=True),
        )
        return (
            lax.all_gather(by_rows[0], "row", axis=1, tiled=True),
            lax.all_gather(by_rows[1], "row", axis=1, tiled=True),
        )

    def send_heads(halfway, which_bit):
        return from_partner(halfway, "tok", which_bit)

    def send_results(halfway, which_bit):
        return from_partner(halfway, "tok", which_bit)

    def send_result_grads(halfway, which_bit):
        return from_partner(halfway, "tok", which_bit)

    def send_input_grads(halfway, which_bit):
        return from_partner(halfway, "tok", which_bit)

    my_lengths = lax.dynamic_slice_in_dim(doc_lengths, tok_index // 4, 1, 1)[:, 0, :]
    doc_ends = jnp.cumsum(my_lengths, axis=-1)
    offsets = jnp.arange(row_len, dtype=jnp.int32)
    positions = jnp.bitwise_xor(offsets // piece_len, quad_place) * piece_len + offsets % piece_len
    segment = jnp.sum((doc_ends[:, None, :] <= positions[None, :, None]).astype(jnp.int32), axis=-1)
    segment_items = jnp.repeat(segment, heads_here, axis=0)
    inputs = tokens.reshape(token_count, model_width).astype(jnp.float32)
    normed_one, inverse_one = norm_parts(inputs)
    act_one = (normed_one * first_gain + first_bias).astype(jnp.bfloat16)
    full_qkv, full_proj = attn_weights()
    qkv_bias = jnp.concatenate([query_bias, jnp.zeros_like(query_bias), value_bias])
    qkv = (jnp.dot(act_one, full_qkv, preferred_element_type=jnp.float32) + qkv_bias).astype(
        jnp.bfloat16
    )
    qkv_slots = jnp.einsum(
        "sh,rcthk->srctk",
        picker,
        qkv.reshape(row_count, piece_len, 3, 4, head_cols),
        preferred_element_type=jnp.float32,
    ).astype(jnp.bfloat16)
    qkv_slots = quad_exchange(qkv_slots, send_heads)
    query_items = to_items(qkv_slots[:, :, :, 0], heads_here)
    key_items = to_items(qkv_slots[:, :, :, 1], heads_here)
    value_items = to_items(qkv_slots[:, :, :, 2], heads_here)

    def attend_single(single):
        return attend(single[0], single[1], single[2], single[3], positions, score_scale)

    result_items, log_totals = lax.map(
        attend_single, (query_items, key_items, value_items, segment_items)
    )
    result_slots = quad_exchange(from_items(result_items, row_count, heads_here), send_results)
    attended = (
        jnp.einsum("hs,srck->rchk", picker, result_slots, preferred_element_type=jnp.float32)
        .astype(jnp.bfloat16)
        .reshape(token_count, model_width)
    )
    mixed = jnp.dot(attended, full_proj, preferred_element_type=jnp.float32) + proj_bias
    middle = inputs + branch_scale * mixed
    normed_two, inverse_two = norm_parts(middle)
    act_two = (normed_two * second_gain + second_bias).astype(jnp.bfloat16)
    full_up, full_down = mlp_weights()
    pre_act = jnp.dot(act_two, full_up, preferred_element_type=jnp.float32) + up_bias
    hidden = gelu_value(pre_act).astype(jnp.bfloat16)
    branch_out = jnp.dot(hidden, full_down, preferred_element_type=jnp.float32) + down_bias
    output = (
        (middle + branch_scale * branch_out)
        .astype(jnp.bfloat16)
        .reshape(row_count, piece_len, model_width)
    )
    full_up, full_down = mlp_weights()
    cotangent = out_grad.reshape(token_count, model_width).astype(jnp.float32)
    grad_branch = (branch_scale * cotangent).astype(jnp.bfloat16)
    down_grad = jnp.einsum("nf,nd->fd", hidden, grad_branch, preferred_element_type=jnp.float32)
    down_bias_grad = jnp.sum(grad_branch.astype(jnp.float32), axis=0)
    grad_hidden = jnp.einsum(
        "nd,fd->nf", grad_branch, full_down, preferred_element_type=jnp.float32
    )
    grad_pre = (grad_hidden * gelu_slope(pre_act)).astype(jnp.bfloat16)
    up_grad = jnp.einsum("nk,nf->kf", act_two, grad_pre, preferred_element_type=jnp.float32)
    up_bias_grad = jnp.sum(grad_pre.astype(jnp.float32), axis=0)
    grad_act_two = jnp.einsum("nf,kf->nk", grad_pre, full_up, preferred_element_type=jnp.float32)
    second_gain_grad = jnp.sum(grad_act_two * normed_two, axis=0)
    second_bias_grad = jnp.sum(grad_act_two, axis=0)
    grad_middle = cotangent + norm_back(grad_act_two, normed_two, inverse_two, second_gain)
    grad_mixed = (branch_scale * grad_middle).astype(jnp.bfloat16)
    full_qkv, full_proj = attn_weights()
    proj_grad = jnp.einsum("nk,nd->kd", attended, grad_mixed, preferred_element_type=jnp.float32)
    proj_bias_grad = jnp.sum(grad_mixed.astype(jnp.float32), axis=0)
    grad_attended = jnp.einsum(
        "nd,kd->nk", grad_mixed, full_proj, preferred_element_type=jnp.float32
    ).astype(jnp.bfloat16)
    grad_slots = jnp.einsum(
        "sh,rchk->srck",
        picker,
        grad_attended.reshape(row_count, piece_len, 4, head_cols),
        preferred_element_type=jnp.float32,
    ).astype(jnp.bfloat16)
    grad_slots = quad_exchange(grad_slots, send_result_grads)
    grad_result_items = to_items(grad_slots, heads_here)

    def attend_single_back(single):
        return attend_back(
            single[0], single[1], single[2], single[3], single[4], single[5], positions, score_scale
        )

    grad_q, grad_k, grad_v = lax.map(
        attend_single_back,
        (query_items, key_items, value_items, grad_result_items, segment_items, log_totals),
    )
    input_slots = jnp.stack(
        [
            from_items(grad_q, row_count, heads_here),
            from_items(grad_k, row_count, heads_here),
            from_items(grad_v, row_count, heads_here),
        ],
        axis=3,
    )
    input_slots = quad_exchange(input_slots, send_input_grads)
    grad_qkv = (
        jnp.einsum("hs,srctk->rcthk", picker, input_slots, preferred_element_type=jnp.float32)
        .astype(jnp.bfloat16)
        .reshape(token_count, 3 * model_width)
    )
    qkv_grad = jnp.einsum("nk,nf->kf", act_one, grad_qkv, preferred_element_type=jnp.float32)
    qkv_bias_grad = jnp.sum(grad_qkv.astype(jnp.float32), axis=0)
    query_bias_grad = qkv_bias_grad[:model_width]
    value_bias_grad = qkv_bias_grad[2 * model_width :]
    grad_act_one = jnp.einsum("nf,kf->nk", grad_qkv, full_qkv, preferred_element_type=jnp.float32)
    first_gain_grad = jnp.sum(grad_act_one * normed_one, axis=0)
    first_bias_grad = jnp.sum(grad_act_one, axis=0)
    tokens_grad = (
        (grad_middle + norm_back(grad_act_one, normed_one, inverse_one, first_gain))
        .astype(jnp.bfloat16)
        .reshape(row_count, piece_len, model_width)
    )
    section_one = (
        lax.psum_scatter(
            qkv_grad.astype(jnp.bfloat16), "row", scatter_dimension=1, tiled=True
        ).astype(jnp.float32),
        lax.psum_scatter(
            proj_grad.astype(jnp.bfloat16), "row", scatter_dimension=1, tiled=True
        ).astype(jnp.float32),
        lax.psum_scatter(
            up_grad.astype(jnp.bfloat16), "row", scatter_dimension=1, tiled=True
        ).astype(jnp.float32),
        lax.psum_scatter(
            down_grad.astype(jnp.bfloat16), "row", scatter_dimension=1, tiled=True
        ).astype(jnp.float32),
    )
    weight_grads = (
        lax.psum_scatter(
            section_one[0].astype(jnp.bfloat16), "tok", scatter_dimension=0, tiled=True
        ).astype(jnp.float32),
        lax.psum_scatter(
            section_one[1].astype(jnp.bfloat16), "tok", scatter_dimension=0, tiled=True
        ).astype(jnp.float32),
        lax.psum_scatter(
            section_one[2].astype(jnp.bfloat16), "tok", scatter_dimension=0, tiled=True
        ).astype(jnp.float32),
        lax.psum_scatter(
            section_one[3].astype(jnp.bfloat16), "tok", scatter_dimension=0, tiled=True
        ).astype(jnp.float32),
    )
    vectors = lax.psum(
        (
            first_gain_grad,
            first_bias_grad,
            query_bias_grad,
            value_bias_grad,
            proj_bias_grad,
            second_gain_grad,
            second_bias_grad,
            up_bias_grad,
            down_bias_grad,
        ),
        ("tok", "row"),
    )
    return (
        output,
        tokens_grad,
        weight_grads[0],
        weight_grads[1],
        weight_grads[2],
        weight_grads[3],
        vectors[0],
        vectors[1],
        vectors[2],
        vectors[3],
        vectors[4],
        vectors[5],
        vectors[6],
        vectors[7],
        vectors[8],
    )


def solution(mesh):
    in_specs = (
        P("row", "tok", None),
        P("row", "tok", None),
        P("row", None, None),
        P(),
        P(),
        P("tok", "row"),
        P(),
        P(),
        P("tok", "row"),
        P(),
        P(),
        P(),
        P("tok", "row"),
        P(),
        P("tok", "row"),
        P(),
    )
    out_specs = (
        P("row", "tok", None),
        P("row", "tok", None),
        P("tok", "row"),
        P("tok", "row"),
        P("tok", "row"),
        P("tok", "row"),
        P(),
        P(),
        P(),
        P(),
        P(),
        P(),
        P(),
        P(),
        P(),
    )
    return jax.shard_map(
        per_device, mesh=mesh, in_specs=in_specs, out_specs=out_specs, check_vma=False
    )
```

profile of v0, /device:TPU:0, one launch (start us, length us, event | category | flops | bytes accessed | tf_op | source)
XLA Modules:
  0.0 1364.1 jit_solution(8008923260589269110)
XLA Ops:
  8.0 64.5 %all-gather.8.cloned.1.call-done = bf16[768,1152]{1,0:T(8,128)(2,1)} async-done(((bf16[48,1152]{1,0:T(8,128)(2,1)}), bf16[768,1152]{1,0:T(8,128)(2,1)}) %all-gather.8.cloned.1.call-update) | async-done | bytes 1769488 | tf_op jit(solution)/shard_map/all_gather | solution.py:166
  73.9 45.4 %all_gather.34 = bf16[768,384]{1,0:T(8,128)(2,1)} all-gather(bf16[48,384]{1,0:T(8,128)(2,1)} %param.28), channel_id=1, replica_groups=mesh['tok'=16,'row'=2] {'tok'}, dimensions={0}, use_global_device_ids=true | all-gather | bytes 626688 | tf_op jit(solution)/shard_map/all_gather | solution.py:167
  122.2 7.5 add_convert_fusion
  129.7 12.8 reshape.281
  142.5 13.1 copy.186
  155.6 7.1 convolution_convert_fusion.3
  162.7 10.5 reshape.259
  173.2 10.6 fusion.141
  185.9 2.9 copy.242
  188.8 54.4 %collective-permute-done = bf16[2,4,256,3,192]{2,4,3,1,0:T(8,128)(2,1)} collective-permute-done((bf16[2,4,256,3,192]{2,4,3,1,0:T(8,128)(2,1)}, bf16[2,4,256,3,192]{2,4,3,1,0:T(8,128)(2,1)}, u32[]{:S(2)}, u32[]{:S(2)}) %collective-permute-start) | collective-permute-done | bytes 2359328 | tf_op jit(solution)/shard_map/ppermute | solution.py:26
  243.2 3.8 fusion.104
  247.5 47.3 %collective-permute-done.1 = bf16[2,4,256,3,192]{2,4,3,1,0:T(8,128)(2,1)} collective-permute-done((bf16[2,4,256,3,192]{2,4,3,1,0:T(8,128)(2,1)}, bf16[2,4,256,3,192]{2,4,3,1,0:T(8,128)(2,1)}, u32[]{:S(2)}, u32[]{:S(2)}) %collective-permute-start.1) | collective-permute-done | bytes 2359328 | tf_op jit(solution)/shard_map/ppermute | solution.py:26
  294.8 2.8 pad_maximum_fusion
  300.2 4.5 copy.236
  304.7 4.2 copy.237
  311.7 59.3 %while.28 = (s32[]{:T(128)}, bf16[12,1024,64]{1,2,0:T(8,128)(2,1)S(1)}, f32[12,1024]{1,0:T(8,128)S(1)}, s32[12,1024]{1,0:T(8,128)S(1)}, bf16[12,1024,64]{2,1,0:T...) while((s32[]{:T(128)}, ...), condition=%wide.region_7.8_spmd.clone, body=%wide.region_4.7_spmd.clone.sunk | while | flops 280049664 | bytes 13572217 | solution.py:224
  375.9 12.4 collective-permute-done.2
  390.5 10.1 collective-permute-done.3
  404.8 3.5 fusion.145
  410.5 11.3 fusion.137
  421.9 14.9 %convert_reduce_fusion = (f32[3072]{0:T(1024)}, bf16[1024,3072]{1,0:T(8,128)(2,1)S(1)}) fusion(f32[1024,3072]{1,0:T(8,128)} %fusion.137, f32[3072]{0:T(1024)S(1)} %copy-done.35, bf16[1024,768]{1,0:T(8,128)(2,1)S(1)} %copy-done.12, bf16[3072,768]{1,0:T(8,128)(2,1)} %all-gather.20.cloned.1.call-done), kind=kOutput, calls=%fused_computation.95 | convolution fusion | flops 4901041152 | bytes 25190400 | tf_op jit(solution)/shard_map/nd,fd->nf/dot_general | solution.py:251
  436.8 6.2 multiply_reduce_fusion.1
  449.8 10.4 convolution_convert_fusion.1
  460.4 3.7 convolution_convert_fusion.6
  464.1 2.8 reshape.282
  466.9 5.5 copy.200
  474.6 3.6 reshape.269
  482.1 10.6 collective-permute-done.4
  494.3 12.2 convolution_convert_fusion
  506.5 6.7 copy.233
  519.5 143.6 %while.29 = (s32[]{:T(128)}, bf16[12,1024,64]{1,2,0:T(8,128)(2,1)}, bf16[12,1024,64]{1,2,0:T(8,128)(2,1)}, bf16[12,1024,64]{1,2,0:T(8,128)(2,1)S(1)}, s32[12,102...) while((s32[]{:T(128)}, bf16[12,1024,64]{1,2,0:T(8,128)(2,1)}, ...), condition=%wide.region_14.15_spmd.clone, body=%wide.region_12.14_spmd.clone.sunk | while | flops 684013568 | bytes 33739912 | solution.py:282
  521.5 2.9 multiply_reduce_fusion.7
  533.5 2.8 multiply_reduce_fusion.7
  545.4 2.8 multiply_reduce_fusion.7
  557.4 2.8 multiply_reduce_fusion.7
  569.3 2.8 multiply_reduce_fusion.7
  581.3 2.8 multiply_reduce_fusion.7
  593.2 2.8 multiply_reduce_fusion.7
  605.2 2.8 multiply_reduce_fusion.7
  617.1 2.8 multiply_reduce_fusion.7
  629.1 2.8 multiply_reduce_fusion.7
  641.0 2.8 multiply_reduce_fusion.7
  653.0 2.8 multiply_reduce_fusion.7
  665.5 2.8 copy.211
  668.4 4.0 reshape.271
  672.4 2.9 copy.209
  682.6 42.5 %collective-permute-done.6 = bf16[2,4,256,3,192]{2,4,1,0,3:T(8,128)(2,1)S(1)} collective-permute-done((bf16[2,4,256,3,192]{2,4,1,0,3:T(8,128)(2,1)S(1)}, bf16[2,4,256,3,192]{2,4,1,0,3:T(8,128)(2,1)S(1)}, u32[]{:S(2)}, u32[]{:S(2)}) %collective-permute-start.6) | collective-permute-done | bytes 2359328 | tf_op jit(solution)/shard_map/ppermute | solution.py:26
  728.4 40.6 %collective-permute-done.7 = bf16[2,4,256,3,192]{2,4,1,0,3:T(8,128)(2,1)S(1)} collective-permute-done((bf16[2,4,256,3,192]{2,4,1,0,3:T(8,128)(2,1)S(1)}, bf16[2,4,256,3,192]{2,4,1,0,3:T(8,128)(2,1)S(1)}, u32[]{:S(2)}, u32[]{:S(2)}) %collective-permute-start.7) | collective-permute-done | bytes 2359328 | tf_op jit(solution)/shard_map/ppermute | solution.py:26
  771.6 9.4 copy.215
  780.9 11.6 reshape.274
  792.6 8.0 convert_reduce_fusion.1
  800.6 6.0 copy.216
  810.3 5.4 convolution_convert_fusion.2
  815.7 5.8 copy.229
  824.8 4.5 copy.234
  830.5 3.9 copy.230
  834.4 13.5 add_convert_fusion.1
  847.9 111.0 %reduce-scatter.17.cloned.1.call-done = bf16[48,384]{1,0:T(8,128)(2,1)} async-done(((bf16[768,384]{1,0:T(8,128)(2,1)}), bf16[48,384]{1,0:T(8,128)(2,1)}) %reduce-scatter.17.cloned.1.call-update) | async-done | bytes 36880 | tf_op jit(solution)/shard_map/reduce_scatter | solution.py:330
  960.7 9.7 fusion.101
  970.3 41.7 %all-reduce = (f32[768]{0:T(1024)}, f32[768]{0:T(1024)}, f32[768]{0:T(1024)}, f32[768]{0:T(1024)}, f32[768]{0:T(1024)}, /*index=5*/f32[768]{0:T(1024)}, f32[768]{0:T(1024)}, f32[3072]{0:T(1024)}, f32[768]{0:T(1024)}) all-reduce(f32[768]{0:T(1024)S(1)} %get-tuple-element.263, ...), channel_id=1, replica_groups=mesh['tok'=16,'row'=2] {'tok','row'}, use_global_device_ids=true, to_apply=%region_26.27 | all-reduce | flops 9216 | bytes 73728 | tf_op jit(solution)/shard_map/psum | solution.py:340
  1012.1 4.4 fusion.100
  1016.5 75.7 %reduce-scatter.21.cloned.1.call-done = bf16[48,1536]{1,0:T(8,128)(2,1)} async-done(((bf16[768,1536]{1,0:T(8,128)(2,1)}), bf16[48,1536]{1,0:T(8,128)(2,1)}) %reduce-scatter.21.cloned.1.call-update) | async-done | bytes 147472 | tf_op jit(solution)/shard_map/reduce_scatter | solution.py:333
  1093.8 130.6 %reduce-scatter.23.cloned.1.call-done = bf16[192,384]{1,0:T(8,128)(2,1)} async-done(((bf16[3072,384]{1,0:T(8,128)(2,1)}), bf16[192,384]{1,0:T(8,128)(2,1)}) %reduce-scatter.23.cloned.1.call-update) | async-done | bytes 147472 | tf_op jit(solution)/shard_map/reduce_scatter | solution.py:336
  1226.0 129.5 %reduce-scatter.15.cloned.1.call-done = bf16[48,1152]{1,0:T(8,128)(2,1)} async-done(((bf16[768,1152]{1,0:T(8,128)(2,1)}), bf16[48,1152]{1,0:T(8,128)(2,1)}) %reduce-scatter.15.cloned.1.call-update) | async-done | bytes 110608 | tf_op jit(solution)/shard_map/reduce_scatter | solution.py:327
  (380 shorter events, 245.5 us)
Async XLA Ops:
  7.2 239.8 %copy-start = (s32[4,4,8]{2,1,0:T(4,128)S(1)}, s32[4,4,8]{2,1,0:T(4,128)}, u32[]{:S(2)}) copy-start(s32[4,4,8]{2,1,0:T(4,128)} %param.22) | copy-start | bytes 1540
  7.2 112.2 %copy-start.2 = (bf16[4,256,768]{2,1,0:T(8,128)(2,1)S(1)}, bf16[4,256,768]{2,1,0:T(8,128)(2,1)}, u32[]{:S(2)}) copy-start(bf16[4,256,768]{2,1,0:T(8,128)(2,1)} %param.20) | copy-start | bytes 4718596
  7.2 65.3 %all-gather.8.cloned.1.call-start = ((), (), s32[]{:S(2)}) async-start(), calls=%async_computation.8 | async-start | bytes 1880064 | tf_op jit(solution)/shard_map/all_gather | solution.py:166
  7.9 114.2 %all-gather.10.cloned.1.call-start = ((), (), s32[]{:S(2)}) async-start(), calls=%async_computation.9 | async-start | bytes 5308416 | tf_op jit(solution)/shard_map/all_gather | solution.py:170
  72.5 48.4 %copy-start.30 = (f32[768]{0:T(1024)S(1)}, f32[768]{0:T(1024)}, u32[]{:S(2)}) copy-start(f32[768]{0:T(1024)} %param.27) | copy-start | bytes 9220
  72.5 48.4 %copy-start.31 = (f32[768]{0:T(1024)S(1)}, f32[768]{0:T(1024)}, u32[]{:S(2)}) copy-start(f32[768]{0:T(1024)} %param.26) | copy-start | bytes 9220
  72.5 49.0 %copy-start.16 = (f32[768]{0:T(1024)S(1)}, f32[768]{0:T(1024)}, u32[]{:S(2)}) copy-start(f32[768]{0:T(1024)} %param.23) | copy-start | bytes 9220
  72.5 49.0 %copy-start.24 = (f32[768]{0:T(1024)S(1)}, f32[768]{0:T(1024)}, u32[]{:S(2)}) copy-start(f32[768]{0:T(1024)} %param.24) | copy-start | bytes 9220
  72.5 113.3 %all-gather.14.cloned.1.call-start = ((), (), s32[]{:S(2)}) async-start(), calls=%async_computation.11 | async-start | bytes 2506752 | tf_op jit(solution)/shard_map/all_gather | solution.py:176
  73.3 174.1 %all-gather.18.cloned.1.call-start = ((), (), s32[]{:S(2)}) async-start(), calls=%async_computation.13 | async-start | bytes 2506752 | tf_op jit(solution)/shard_map/all_gather | solution.py:177
  73.8 330.9 %all-gather.12.cloned.1.call-start = ((), (), s32[]{:S(2)}) async-start(), calls=%async_computation.10 | async-start | bytes 1769472 | tf_op jit(solution)/shard_map/all_gather | solution.py:171
  119.3 291.2 %all-gather.16.cloned.1.call-start = ((), (), s32[]{:S(2)}) async-start(), calls=%async_computation.12 | async-start | bytes 7077888 | tf_op jit(solution)/shard_map/all_gather | solution.py:180
  119.7 1.3 copy-start.18
  119.7 1.3 copy-start.20
  120.9 0.6 copy-start.22
  185.8 57.4 %collective-permute-start = (bf16[2,4,256,3,192]{2,4,3,1,0:T(8,128)(2,1)}, bf16[2,4,256,3,192]{2,4,3,1,0:T(8,128)(2,1)}, u32[]{:S(2)}, u32[]{:S(2)}) collective-permute-start(bf16[2,4,256,3,192]{2,4,3,1,0:T(8,128)(2,1)} %bitcast.225), channel_id=1, source_target_pairs={{0,2},{2,0},{4,6},{6,4},{8,10},{10,8},{12,14},{14,12},{16,18},{18,... | collective-permute-start | bytes 7077896 | tf_op jit(solution)/shard_map/ppermute | solution.py:26
  185.8 236.0 %all-gather.20.cloned.1.call-start = ((), (), s32[]{:S(2)}) async-start(), calls=%async_computation.14 | async-start | bytes 7077888 | tf_op jit(solution)/shard_map/all_gather | solution.py:181
  247.0 47.8 %collective-permute-start.1 = (bf16[2,4,256,3,192]{2,4,3,1,0:T(8,128)(2,1)}, bf16[2,4,256,3,192]{2,4,3,1,0:T(8,128)(2,1)}, u32[]{:S(2)}, u32[]{:S(2)}) collective-permute-start(bf16[2,4,256,3,192]{2,4,3,1,0:T(8,128)(2,1)} %get-tuple-element.330), channel_id=1, source_target_pairs={{0,4},{4,0},{2,6},{6,2},{8,12},{12,8},{10,14},{14,10},{16,20},{20,... | collective-permute-start | bytes 7077896 | tf_op jit(solution)/shard_map/ppermute | solution.py:26
  247.4 574.4 %reduce-scatter.27.cloned.1.call-start = ((), (), s32[]{:S(2)}) async-start(), calls=%async_computation.21 | async-start | bytes 1769472
  375.1 13.8 %copy-start.4 = (bf16[4,256,768]{2,1,0:T(8,128)(2,1)S(1)}, bf16[4,256,768]{2,1,0:T(8,128)(2,1)}, u32[]{:S(2)}) copy-start(bf16[4,256,768]{2,1,0:T(8,128)(2,1)} %param.21) | copy-start | bytes 4718596
  375.3 13.0 collective-permute-start.2
  388.4 12.1 collective-permute-start.3
  402.0 2.7 copy-start.36
  408.2 1.7 copy-start.5
  408.2 2.3 copy-start.29
  408.3 2.3 copy-start.37
  410.4 11.4 copy-start.12
  410.5 11.4 copy-start.35
  421.9 14.9 %copy-start.6 = (f32[1024,768]{1,0:T(8,128)S(1)}, f32[1024,768]{1,0:T(8,128)}, u32[]{:S(2)}) copy-start(f32[1024,768]{1,0:T(8,128)} %copy-done.5) | copy-start | bytes 9437188
  421.9 14.9 %copy-start.34 = (bf16[768,3072]{1,0:T(8,128)(2,1)S(1)}, bf16[768,3072]{1,0:T(8,128)(2,1)}, u32[]{:S(2)}) copy-start(bf16[768,3072]{1,0:T(8,128)(2,1)} %all-gather.16.cloned.1.call-done) | copy-start | bytes 14155780
  436.8 6.2 copy-start.39
  443.0 3.8 copy-start.14
  445.1 1.7 copy-start.7
  449.7 374.3 %reduce-scatter.19.cloned.1.call-start = ((), (), s32[]{:S(2)}) async-start(), calls=%async_computation.17 | async-start | bytes 7077888 | tf_op jit(solution)/shard_map/reduce_scatter | solution.py:319
  460.2 364.6 %reduce-scatter.29.cloned.1.call-start = ((), (), s32[]{:S(2)}) async-start(), calls=%async_computation.22 | async-start | bytes 7077888
  480.6 13.7 %copy-start.13 = (bf16[1024,768]{1,0:T(8,128)(2,1)S(1)}, bf16[1024,768]{1,0:T(8,128)(2,1)}, u32[]{:S(2)}) copy-start(bf16[1024,768]{1,0:T(8,128)(2,1)} %fusion.82) | copy-start | bytes 4718596
  480.6 12.1 collective-permute-start.4
  493.7 19.9 %collective-permute-start.5 = (bf16[2,4,256,192]{2,3,1,0:T(8,128)(2,1)}, bf16[2,4,256,192]{2,3,1,0:T(8,128)(2,1)S(1)}, u32[]{:S(2)}, u32[]{:S(2)}) collective-permute-start(bf16[2,4,256,192]{2,3,1,0:T(8,128)(2,1)} %get-tuple-element.334), channel_id=1, source_target_pairs={{0,4},{4,0},{2,6},{6,2},{8,12},{12,8},{10,14},{14,10},{16,20},{20,... | collective-permute-start | bytes 2359304 | tf_op jit(solution)/shard_map/ppermute | solution.py:26
  513.1 317.4 %reduce-scatter.25.cloned.1.call-start = ((), (), s32[]{:S(2)}) async-start(), calls=%async_computation.20 | async-start | bytes 5308416
  668.4 6.9 copy-start.8
  677.6 1.9 copy-start.9
  677.6 2.4 copy-start.10
  680.8 44.2 %collective-permute-start.6 = (bf16[2,4,256,3,192]{2,4,1,0,3:T(8,128)(2,1)S(1)}, bf16[2,4,256,3,192]{2,4,1,0,3:T(8,128)(2,1)S(1)}, u32[]{:S(2)}, u32[]{:S(2)}) collective-permute-start(bf16[2,4,256,3,192]{2,4,1,0,3:T(8,128)(2,1)S(1)} %get-tuple-element.325), channel_id=1, source_target_pairs={{0,2},{2,0},{4,6},{6,4},{8,10},{10,8},{12,14},{14,12},{16,18},{18,... | collective-permute-start | bytes 7077896 | tf_op jit(solution)/shard_map/ppermute | solution.py:26
  725.1 1.6 copy-start.3
  725.1 1.6 copy-start.17
  725.1 1.6 copy-start.19
  725.1 1.6 copy-start.25
  725.1 1.6 copy-start.26
  725.7 43.3 %collective-permute-start.7 = (bf16[2,4,256,3,192]{2,4,1,0,3:T(8,128)(2,1)S(1)}, bf16[2,4,256,3,192]{2,4,1,0,3:T(8,128)(2,1)S(1)}, u32[]{:S(2)}, u32[]{:S(2)}) collective-permute-start(bf16[2,4,256,3,192]{2,4,1,0,3:T(8,128)(2,1)S(1)} %get-tuple-element.323), channel_id=1, source_target_pairs={{0,4},{4,0},{2,6},{6,2},{8,12},{12,8},{10,14},{14,10},{16,20},{20,... | collective-permute-start | bytes 7077896 | tf_op jit(solution)/shard_map/ppermute | solution.py:26
  806.6 3.7 copy-start.15
  808.1 2.2 copy-start.11
  821.5 137.4 %reduce-scatter.17.cloned.1.call-start = ((), (), s32[]{:S(2)}) async-start(), calls=%async_computation.16 | async-start | bytes 626688 | tf_op jit(solution)/shard_map/reduce_scatter | solution.py:330
  824.0 268.2 %reduce-scatter.21.cloned.1.call-start = ((), (), s32[]{:S(2)}) async-start(), calls=%async_computation.18 | async-start | bytes 2506752 | tf_op jit(solution)/shard_map/reduce_scatter | solution.py:333
  824.7 399.7 %reduce-scatter.23.cloned.1.call-start = ((), (), s32[]{:S(2)}) async-start(), calls=%async_computation.19 | async-start | bytes 2506752 | tf_op jit(solution)/shard_map/reduce_scatter | solution.py:336
  829.3 5.0 copy-start.38
  829.4 526.2 %reduce-scatter.15.cloned.1.call-start = ((), (), s32[]{:S(2)}) async-start(), calls=%async_computation.15 | async-start | bytes 1880064 | tf_op jit(solution)/shard_map/reduce_scatter | solution.py:327
  834.4 126.2 %copy-start.21 = (f32[1,2,4,128]{3,1,2,0:T(2,128)S(1)}, f32[1,2,4,128]{3,1,2,0:T(2,128)}, u32[]{:S(2)}) copy-start(f32[1,2,4,128]{3,1,2,0:T(2,128)} %copy-done.20) | copy-start | bytes 12292
  834.4 126.2 %copy-start.23 = (f32[1,2,4,128]{3,1,2,0:T(2,128)S(1)}, f32[1,2,4,128]{3,1,2,0:T(2,128)}, u32[]{:S(2)}) copy-start(f32[1,2,4,128]{3,1,2,0:T(2,128)} %copy-done.22) | copy-start | bytes 12292
  960.6 9.7 copy-start.27
  960.6 9.7 copy-start.28
  960.6 9.7 copy-start.32
  960.7 9.7 copy-start.33
  1012.1 345.1 %copy-start.1 = (s32[4,4,8]{2,1,0:T(4,128)S(1)}, s32[4,4,8]{2,1,0:T(4,128)}, u32[]{:S(2)}) copy-start(s32[4,4,8]{2,1,0:T(4,128)} %param.22) | copy-start | bytes 1540
Sparse Core Ops, SparseCore 0:
  10.8 61.6 all-gather.7
  74.0 11.4 all-gather.9
  88.3 64.0 all-gather.13
  155.1 71.9 all-gather.17
  228.4 8.0 all-gather.11
  237.9 15.5 all-gather.15
  255.1 15.4 all-gather.19
  449.8 6.0 reduce-scatter.26
  460.3 11.8 reduce-scatter.18
  513.2 10.4 reduce-scatter.28
  821.6 8.8 reduce-scatter.24
  835.6 123.2 reduce-scatter.16
  964.5 127.5 reduce-scatter.20
  1096.9 127.4 reduce-scatter.22
  1229.8 125.6 reduce-scatter.14
where the time goes:
time: 1380 us; the launch traced here: 1360 us
  waiting for transfers between devices  733 us (53%)
  matrix products  298 us (22%)
  local copies, waits for them, and re-layouts  171 us (12%)
  blocking collectives  87.1 us (6%)
  other arithmetic  51.9 us (4%)
  between operations  15.1 us (1%)
    ppermute x8, waiting for transfers between devices, from_partner(): return lax.ppermute(block, axis, route)  218 us
    reduce_scatter x1, waiting for transfers between devices, per_device(): lax.psum_scatter(section_one[3].astype(jnp.bfloat16), 'tok', scatter_dime...  131 us
    reduce_scatter x1, waiting for transfers between devices, per_device(): lax.psum_scatter(section_one[0].astype(jnp.bfloat16), 'tok', scatter_dime...  130 us
    reduce_scatter x1, waiting for transfers between devices, per_device(): lax.psum_scatter(section_one[1].astype(jnp.bfloat16), 'tok', scatter_dime...  111 us
    reduce_scatter x1, waiting for transfers between devices, per_device(): lax.psum_scatter(section_one[2].astype(jnp.bfloat16), 'tok', scatter_dime...  75.7 us
    all_gather x1, waiting for transfers between devices, attn_weights(): lax.all_gather(qkv_weight, 'tok', axis=0, tiled=True)  64.5 us
    unnamed x98, local copies, waits for them, and re-layouts  53.4 us
    all_gather x1, blocking collectives, attn_weights(): lax.all_gather(proj_weight, 'tok', axis=0, tiled=True)  45.4 us
  transfers between devices with their start and end apart: 23, of which 13 were waited for; matrix products, arithmetic and copies ran while one was open for 36% of the time, Pallas kernels for 0%

commit v1 on v0

v1 whole, which is shorter than its diff:
```python
import math

import jax
import jax.numpy as jnp
from jax import lax
from jax.experimental import pallas as pl
from jax.experimental.pallas import tpu as pltpu
from jax.sharding import PartitionSpec as P

D = 768
H = 12
HD = 64
FF = 3072
DEPTH = 48
DOCS = 8
BLK = 256
QUAD = 4

EPSILON = 1e-05
TANH_ROOT = 0.7978845608028654
TANH_CUBIC = 0.044715
BETA = 1.0 / math.sqrt(DEPTH)
SCALE = 1.0 / math.sqrt(HD)
F32 = jnp.float32
BF16 = jnp.bfloat16
VMEM_LIMIT = 56 * 2**20

NT = (((1,), (1,)), ((), ()))
NN = (((1,), (0,)), ((), ()))
TN = (((0,), (0,)), ((), ()))


def mm(a, b, dims=NN):
    return lax.dot_general(a, b, dims, preferred_element_type=F32)


def params():
    return pltpu.CompilerParams(vmem_limit_bytes=VMEM_LIMIT)


def cost(flops, nbytes, trans=0):
    return pl.CostEstimate(flops=int(flops), bytes_accessed=int(nbytes), transcendentals=int(trans))


def norm_parts(x):
    centre = x - jnp.mean(x, axis=-1, keepdims=True)
    inverse = lax.rsqrt(jnp.mean(centre * centre, axis=-1, keepdims=True) + EPSILON)
    return centre * inverse, inverse


def norm_back(grad, normed, inverse, gain):
    spread = grad * gain
    return inverse * (
        spread
        - jnp.mean(spread, axis=-1, keepdims=True)
        - normed * jnp.mean(spread * normed, axis=-1, keepdims=True)
    )


def halves_copies(w_hbm, w_vmem, sem):
    width = w_hbm.shape[2]
    return [
        pltpu.make_async_copy(w_hbm.at[h], w_vmem.at[:, pl.ds(h * width, width)], sem.at[h])
        for h in range(2)
    ]


def qkv_kernel(x_ref, g_ref, b_ref, qb_ref, w_hbm, act_ref, qkv_ref, w_vmem, sem):
    first = pl.program_id(0) == 0

    @pl.when(first)
    def _():
        for c in halves_copies(w_hbm, w_vmem, sem):
            c.start()

    normed, _ = norm_parts(x_ref[...].astype(F32))
    act = (normed * g_ref[...] + b_ref[...]).astype(BF16)
    act_ref[...] = act

    @pl.when(first)
    def _():
        for c in halves_copies(w_hbm, w_vmem, sem):
            c.wait()

    qkv_ref[...] = (mm(act, w_vmem[...]) + qb_ref[...]).astype(BF16)


def norm_qkv(x, gain, bias, qkv_bias, w):
    n = x.shape[0]
    tile = BLK
    const = lambda i: (0, 0)
    return pl.pallas_call(
        qkv_kernel,
        grid=(n // tile,),
        in_specs=[
            pl.BlockSpec((tile, D), lambda i: (i, 0)),
            pl.BlockSpec((1, D), const),
            pl.BlockSpec((1, D), const),
            pl.BlockSpec((1, 3 * D), const),
            pl.BlockSpec(memory_space=pl.ANY),
        ],
        out_specs=[
            pl.BlockSpec((tile, D), lambda i: (i, 0)),
            pl.BlockSpec((tile, 3 * D), lambda i: (i, 0)),
        ],
        out_shape=[
            jax.ShapeDtypeStruct((n, D), BF16),
            jax.ShapeDtypeStruct((n, 3 * D), BF16),
        ],
        scratch_shapes=[pltpu.VMEM((D, 3 * D), BF16), pltpu.SemaphoreType.DMA((2,))],
        compiler_params=params(),
        cost_estimate=cost(2 * n * D * 3 * D, 2 * (n * 5 * D + 3 * D * D)),
        name="norm_qkv",
    )(x, gain, bias, qkv_bias, w)


def first_of_doc(lens_ref, positions):
    start = jnp.zeros_like(positions)
    end = 0
    for d in range(DOCS):
        end = end + lens_ref[0, d]
        start = jnp.where(positions >= end, end, start)
    return start


def lane_half(h):
    lane = lax.broadcasted_iota(jnp.int32, (1, 128), 1)
    return (lane >= h * HD) & (lane < (h + 1) * HD)


def attn_kernel(lens_ref, q_ref, k_ref, v_ref, o_ref, l_ref, start_ref):
    pair = pl.program_id(0)
    n = q_ref.shape[0]
    nb = n // BLK

    @pl.when(pair == 0)
    def _():
        start_ref[...] = first_of_doc(lens_ref, lax.broadcasted_iota(jnp.int32, (n, 1), 0))
        l_ref[...] = jnp.zeros_like(l_ref)

    lane = lax.broadcasted_iota(jnp.int32, (1, 128), 1)
    for i in range(nb):
        lo = max(0, i - 2)
        rows = pl.ds(i * BLK, BLK)
        keys = pl.ds(lo * BLK, (i + 1 - lo) * BLK)
        width = (i + 1 - lo) * BLK
        q = q_ref[rows, :] * jnp.asarray(SCALE, BF16)
        k = k_ref[keys, :]
        v = v_ref[keys, :]
        kpos = lax.broadcasted_iota(jnp.int32, (1, width), 1) + lo * BLK
        qpos = lax.broadcasted_iota(jnp.int32, (BLK, 1), 0) + i * BLK
        allowed = (kpos >= start_ref[rows, :]) & (kpos <= qpos)
        outs = []
        stats = l_ref[rows, :]
        for h in range(2):
            qh = jnp.where(lane_half(h), q, jnp.zeros_like(q))
            s = jnp.where(allowed, mm(qh, k, NT), -1e9)
            m = jnp.max(s, axis=-1, keepdims=True)
            p = jnp.exp(s - m)
            total = jnp.sum(p, axis=-1, keepdims=True)
            outs.append(mm(p.astype(BF16), v) / total)
            stats = jnp.where(lane == 2 * pair + h, m + jnp.log(total), stats)
        l_ref[rows, :] = stats
        o_ref[rows, :] = jnp.where(lane_half(0), outs[0], outs[1]).astype(BF16)


def attention(lens, qkv):
    n = qkv.shape[0]
    pairs = H // 2
    spec = lambda w: pl.BlockSpec((n, 128), lambda p: (0, w * pairs + p))
    return pl.pallas_call(
        attn_kernel,
        grid=(pairs,),
        in_specs=[pl.BlockSpec(memory_space=pltpu.SMEM), spec(0), spec(1), spec(2)],
        out_specs=[
            pl.BlockSpec((n, 128), lambda p: (0, p)),
            pl.BlockSpec((n, 128), lambda p: (0, 0)),
        ],
        out_shape=[jax.ShapeDtypeStruct((n, D), BF16), jax.ShapeDtypeStruct((n, 128), F32)],
        scratch_shapes=[pltpu.VMEM((n, 1), jnp.int32)],
        compiler_params=params(),
        cost_estimate=cost(2 * 2 * H * n * n * HD * 0.6, 2 * n * 4 * D, H * n * n * 0.6),
        name="attention",
    )(lens, qkv, qkv, qkv)


def attn_back_kernel(
    lens_ref, q_ref, k_ref, v_ref, o_ref, do_ref, l_ref, dq_ref, dk_ref, dv_ref,
    start_ref, lt_ref, dk_acc, dv_acc,
):
    pair = pl.program_id(0)
    n = q_ref.shape[0]
    nb = n // BLK

    @pl.when(pair == 0)
    def _():
        start_ref[...] = first_of_doc(lens_ref, lax.broadcasted_iota(jnp.int32, (8, n), 1))
        lt_ref[...] = l_ref[...].T

    prod = (o_ref[...].astype(F32) * do_ref[...].astype(F32)).T
    for h in range(2):
        half = lane_half(h)
        delta = jnp.sum(prod[h * HD : (h + 1) * HD, :], axis=0, keepdims=True)
        logs = lt_ref[pl.ds(2 * pair + h, 1), :]
        for i in range(nb):
            rows = pl.ds(i * BLK, BLK)
            q = q_ref[rows, :] * jnp.asarray(SCALE, BF16)
            q = jnp.where(half, q, jnp.zeros_like(q))
            do = do_ref[rows, :]
            do = jnp.where(half, do, jnp.zeros_like(do))
            logs_i = logs[:, i * BLK : (i + 1) * BLK]
            delta_i = delta[:, i * BLK : (i + 1) * BLK]
            start_i = start_ref[0:1, i * BLK : (i + 1) * BLK]
            qpos = lax.broadcasted_iota(jnp.int32, (1, BLK), 1) + i * BLK
            dq = jnp.zeros((BLK, 128), F32)
            for j in range(max(0, i - 2), i + 1):
                keys = pl.ds(j * BLK, BLK)
                k = k_ref[keys, :]
                v = v_ref[keys, :]
                kpos = lax.broadcasted_iota(jnp.int32, (BLK, 1), 0) + j * BLK
                allowed = kpos >= start_i
                if i == j:
                    allowed = allowed & (kpos <= qpos)
                p = jnp.where(allowed, jnp.exp(mm(k, q, NT) - logs_i), 0.0)
                dp = mm(v, do, NT)
                ds = (p * (dp - delta_i)).astype(BF16)
                dv = mm(p.astype(BF16), do)
                dk = mm(ds, q)
                if h == 0 and i == j:
                    dv_acc[keys, :] = dv
                    dk_acc[keys, :] = dk
                else:
                    dv_acc[keys, :] += dv
                    dk_acc[keys, :] += dk
                kh = jnp.where(half, k, jnp.zeros_like(k))
                dq = dq + mm(ds, kh, TN)
            dq = (dq * SCALE).astype(BF16)
            if h == 0:
                dq_ref[rows, :] = dq
            else:
                dq_ref[rows, :] = jnp.where(half, dq, dq_ref[rows, :])
    dk_ref[...] = dk_acc[...].astype(BF16)
    dv_ref[...] = dv_acc[...].astype(BF16)


def attention_back(lens, qkv, attended, dout, stats):
    n = qkv.shape[0]
    pairs = H // 2
    spec = lambda w: pl.BlockSpec((n, 128), lambda p: (0, w * pairs + p))
    one = pl.BlockSpec((n, 128), lambda p: (0, p))
    return pl.pallas_call(
        attn_back_kernel,
        grid=(pairs,),
        in_specs=[
            pl.BlockSpec(memory_space=pltpu.SMEM), spec(0), spec(1), spec(2), one, one,
            pl.BlockSpec((n, 128), lambda p: (0, 0)),
        ],
        out_specs=[one, one, one],
        out_shape=[jax.ShapeDtypeStruct((n, D), BF16)] * 3,
        scratch_shapes=[
            pltpu.VMEM((8, n), jnp.int32),
            pltpu.VMEM((128, n), F32),
            pltpu.VMEM((n, 128), F32),
            pltpu.VMEM((n, 128), F32),
        ],
        compiler_params=params(),
        cost_estimate=cost(5 * 2 * H * n * n * HD * 0.6, 2 * n * 8 * D, H * n * n * 0.6),
        name="attention_back",
    )(lens, qkv, qkv, qkv, attended, dout, stats)


def mlp_kernel(
    x_ref, c_ref, att_ref, pb_ref, g_ref, b_ref, ub_ref, db_ref, wp_hbm, wu_hbm, wd_hbm,
    out_ref, hid_ref, du_ref, act_ref, dz_ref, dm_ref, dy_ref, do_ref, vec_ref, uvec_ref,
    wp, wu, wd, sem,
):
    step = pl.program_id(0)
    copies = [
        halves_copies(wp_hbm, wp, sem.at[0]),
        halves_copies(wu_hbm, wu, sem.at[1]),
        halves_copies(wd_hbm, wd, sem.at[2]),
    ]

    @pl.when(step == 0)
    def _():
        for pair in copies:
            for c in pair:
                c.start()
        vec_ref[...] = jnp.zeros_like(vec_ref)
        uvec_ref[...] = jnp.zeros_like(uvec_ref)
        for c in copies[0]:
            c.wait()

    middle = x_ref[...].astype(F32) + BETA * (mm(att_ref[...], wp[...]) + pb_ref[...])
    normed, inverse = norm_parts(middle)
    act = (normed * g_ref[...] + b_ref[...]).astype(BF16)
    act_ref[...] = act
    grad_out = c_ref[...].astype(F32)
    dz = (BETA * grad_out).astype(BF16)
    dz_ref[...] = dz

    @pl.when(step == 0)
    def _():
        for c in copies[1] + copies[2]:
            c.wait()

    chunk = 768
    branch = jnp.zeros(middle.shape, F32)
    da = jnp.zeros(middle.shape, F32)
    for f in range(FF // chunk):
        cols = pl.ds(f * chunk, chunk)
        u = mm(act, wu[:, cols]) + ub_ref[:, cols]
        u2 = u * u
        half_t = 0.5 * jnp.tanh(u * (TANH_ROOT + (TANH_ROOT * TANH_CUBIC) * u2))
        gate = 0.5 + half_t
        hidden = (u * gate).astype(BF16)
        hid_ref[:, cols] = hidden
        branch = branch + mm(hidden, wd[cols, :])
        slope = gate + u * (0.5 - 2.0 * half_t * half_t) * (
            TANH_ROOT + (3.0 * TANH_ROOT * TANH_CUBIC) * u2
        )
        du = (mm(dz, wd[cols, :], NT) * slope).astype(BF16)
        du_ref[:, cols] = du
        uvec_ref[0:1, cols] += jnp.sum(du.astype(F32), axis=0, keepdims=True)
        da = da + mm(du, wu[:, cols], NT)
    out_ref[...] = (middle + BETA * (branch + db_ref[...])).astype(BF16)
    dm = grad_out + norm_back(da, normed, inverse, g_ref[...])
    dm_ref[...] = dm
    dy = (BETA * dm).astype(BF16)
    dy_ref[...] = dy
    do_ref[...] = mm(dy, wp[...], NT).astype(BF16)
    vec_ref[0:1, :] += jnp.sum(da * normed, axis=0, keepdims=True)
    vec_ref[1:2, :] += jnp.sum(da, axis=0, keepdims=True)
    vec_ref[2:3, :] += jnp.sum(dy.astype(F32), axis=0, keepdims=True)
    vec_ref[3:4, :] += jnp.sum(dz.astype(F32), axis=0, keepdims=True)


def mlp(x, c, att, pb, gain, bias, ub, db, wp, wu, wd):
    n = x.shape[0]
    tile = BLK
    const = lambda i: (0, 0)
    row = lambda w: pl.BlockSpec((tile, w), lambda i: (i, 0))
    vec = lambda w: pl.BlockSpec((1, w), const)
    hbm = pl.BlockSpec(memory_space=pl.ANY)
    sds = jax.ShapeDtypeStruct
    return pl.pallas_call(
        mlp_kernel,
        grid=(n // tile,),
        in_specs=[row(D), row(D), row(D), vec(D), vec(D), vec(D), vec(FF), vec(D), hbm, hbm, hbm],
        out_specs=[
            row(D), row(FF), row(FF), row(D), row(D), row(D), row(D), row(D),
            pl.BlockSpec((8, D), const), pl.BlockSpec((8, FF), const),
        ],
        out_shape=[
            sds((n, D), BF16), sds((n, FF), BF16), sds((n, FF), BF16), sds((n, D), BF16),
            sds((n, D), BF16), sds((n, D), F32), sds((n, D), BF16), sds((n, D), BF16),
            sds((8, D), F32), sds((8, FF), F32),
        ],
        scratch_shapes=[
            pltpu.VMEM((D, D), BF16),
            pltpu.VMEM((D, FF), BF16),
            pltpu.VMEM((FF, D), BF16),
            pltpu.SemaphoreType.DMA((3, 2)),
        ],
        compiler_params=params(),
        cost_estimate=cost(2 * n * (4 * D * FF + 2 * D * D), 2 * n * (10 * D + 2 * FF), n * FF),
        name="mlp",
    )(x, c, att, pb, gain, bias, ub, db, wp, wu, wd)


def outer_kernel(a_ref, b_ref, o_ref):
    r = mm(a_ref[...], b_ref[...], TN)
    if o_ref.shape[0] == 1:
        o_ref[0] = r.astype(BF16)
    else:
        width = o_ref.shape[2]
        o_ref[0] = r[:, :width].astype(BF16)
        o_ref[1] = r[:, width:].astype(BF16)


def outer_rows(a, b):
    n, left = a.shape
    right = b.shape[1]
    tile = 768
    return pl.pallas_call(
        outer_kernel,
        grid=(left // tile,),
        in_specs=[
            pl.BlockSpec((n, tile), lambda i: (0, i)),
            pl.BlockSpec((n, right), lambda i: (0, 0)),
        ],
        out_specs=pl.BlockSpec((2, tile, right // 2), lambda i: (0, i, 0)),
        out_shape=jax.ShapeDtypeStruct((2, left, right // 2), BF16),
        compiler_params=params(),
        cost_estimate=cost(2 * n * left * right, 2 * (n * (left + right) + left * right)),
        name="outer_rows",
    )(a, b)


def outer_cols(a, b, tile):
    n, left = a.shape
    right = b.shape[1]
    per = right // 2 // tile
    return pl.pallas_call(
        outer_kernel,
        grid=(right // tile,),
        in_specs=[
            pl.BlockSpec((n, left), lambda i: (0, 0)),
            pl.BlockSpec((n, tile), lambda i: (0, i)),
        ],
        out_specs=pl.BlockSpec((1, left, tile), lambda i: (i // per, 0, i % per)),
        out_shape=jax.ShapeDtypeStruct((2, left, right // 2), BF16),
        compiler_params=params(),
        cost_estimate=cost(2 * n * left * right, 2 * (n * (left + right) + left * right)),
        name="outer_cols",
    )(a, b)


def qkv_outer_kernel(a_ref, q_ref, k_ref, v_ref, o_ref, s_ref):
    for w, ref in enumerate((q_ref, k_ref, v_ref)):
        g = ref[...]
        r = mm(a_ref[...], g, TN).astype(BF16)
        if w == 0:
            o_ref[0, :, 0:D] = r
        elif w == 1:
            o_ref[0, :, D:] = r[:, : D // 2]
            o_ref[1, :, 0 : D // 2] = r[:, D // 2 :]
        else:
            o_ref[1, :, D // 2 :] = r
        s_ref[w : w + 1, :] = jnp.sum(g.astype(F32), axis=0, keepdims=True)


def qkv_outer(act, dq, dk, dv):
    n = act.shape[0]
    return pl.pallas_call(
        qkv_outer_kernel,
        out_shape=[
            jax.ShapeDtypeStruct((2, D, 3 * D // 2), BF16),
            jax.ShapeDtypeStruct((8, D), F32),
        ],
        compiler_params=params(),
        cost_estimate=cost(2 * n * D * 3 * D, 2 * (n * 4 * D + 3 * D * D)),
        name="qkv_outer",
    )(act, dq, dk, dv)


def input_grad_kernel(x_ref, dm_ref, g_ref, dq_ref, dk_ref, dv_ref, w_hbm, o_ref, vec_ref, w, sem):
    first = pl.program_id(0) == 0

    @pl.when(first)
    def _():
        for c in halves_copies(w_hbm, w, sem):
            c.start()
        vec_ref[...] = jnp.zeros_like(vec_ref)
        for c in halves_copies(w_hbm, w, sem):
            c.wait()

    da = mm(dq_ref[...], w[:, 0:D], NT)
    da = da + mm(dk_ref[...], w[:, D : 2 * D], NT)
    da = da + mm(dv_ref[...], w[:, 2 * D : 3 * D], NT)
    normed, inverse = norm_parts(x_ref[...].astype(F32))
    o_ref[...] = (dm_ref[...] + norm_back(da, normed, inverse, g_ref[...])).astype(BF16)
    vec_ref[0:1, :] += jnp.sum(da * normed, axis=0, keepdims=True)
    vec_ref[1:2, :] += jnp.sum(da, axis=0, keepdims=True)


def input_grad(x, dm, gain, dq, dk, dv, w):
    n = x.shape[0]
    tile = BLK
    const = lambda i: (0, 0)
    row = pl.BlockSpec((tile, D), lambda i: (i, 0))
    return pl.pallas_call(
        input_grad_kernel,
        grid=(n // tile,),
        in_specs=[row, row, pl.BlockSpec((1, D), const), row, row, row, pl.BlockSpec(memory_space=pl.ANY)],
        out_specs=[row, pl.BlockSpec((8, D), const)],
        out_shape=[jax.ShapeDtypeStruct((n, D), BF16), jax.ShapeDtypeStruct((8, D), F32)],
        scratch_shapes=[pltpu.VMEM((D, 3 * D), BF16), pltpu.SemaphoreType.DMA((2,))],
        compiler_params=params(),
        cost_estimate=cost(2 * n * D * 3 * D, 2 * (n * 7 * D + 3 * D * D)),
        name="input_grad",
    )(x, dm, gain, dq, dk, dv, w)


def quad_swap(pieces):
    count = lax.axis_size("tok")
    groups = [list(range(g, g + QUAD)) for g in range(0, count, QUAD)]
    return lax.all_to_all(pieces, "tok", 0, 0, axis_index_groups=groups, tiled=True)


def gather(shard):
    rows, cols = shard.shape
    over_row = lax.axis_size("row")
    whole = lax.all_gather(shard, ("row", "tok"), axis=0, tiled=True)
    height = rows * lax.axis_size("tok")
    whole = whole.reshape(over_row, height, cols)
    if over_row == 2:
        return whole
    return (
        whole.reshape(2, over_row // 2, height, cols)
        .transpose(0, 2, 1, 3)
        .reshape(2, height, over_row // 2 * cols)
    )


def scatter(halves):
    over_row = lax.axis_size("row")
    _, height, width = halves.shape
    if over_row != 2:
        cols = 2 * width // over_row
        halves = halves.reshape(2, height, over_row // 2, cols).transpose(0, 2, 1, 3)
        width = cols
    flat = halves.reshape(over_row * height, width)
    return lax.psum_scatter(flat, ("row", "tok"), scatter_dimension=0, tiled=True).astype(F32)


def per_device(
    tokens,
    out_grad,
    doc_lengths,
    first_gain,
    first_bias,
    qkv_weight,
    query_bias,
    value_bias,
    proj_weight,
    proj_bias,
    second_gain,
    second_bias,
    up_weight,
    up_bias,
    down_weight,
    down_bias,
):
    row_count, piece_len, width = tokens.shape
    n = row_count * piece_len
    tok_index = lax.axis_index("tok")
    lens = lax.dynamic_slice(
        doc_lengths,
        (tok_index % QUAD, tok_index // QUAD, 0),
        (1, 1, doc_lengths.shape[2]),
    )[0]

    x = quad_swap(tokens).reshape(n, width)
    c = quad_swap(out_grad).reshape(n, width)
    qkv_full = gather(qkv_weight)
    proj_full = gather(proj_weight)
    up_full = gather(up_weight)
    down_full = gather(down_weight)

    qkv_bias = jnp.concatenate([query_bias, jnp.zeros_like(query_bias), value_bias])[None]
    act1, qkv = norm_qkv(x, first_gain[None], first_bias[None], qkv_bias, qkv_full)
    attended, stats = attention(lens, qkv)
    out, hidden, du, act2, dz, dm, dy, dout, vecs, uvec = mlp(
        x, c, attended, proj_bias[None], second_gain[None], second_bias[None],
        up_bias[None], down_bias[None], proj_full, up_full, down_full,
    )
    output = quad_swap(out.reshape(row_count, piece_len, width))
    down_grad = scatter(outer_rows(hidden, dz))
    up_grad = scatter(outer_cols(act2, du, 768))
    proj_grad = scatter(outer_rows(attended, dy))
    dq, dk, dv = attention_back(lens, qkv, attended, dout, stats)
    qkv_outer_grad, qkv_vec = qkv_outer(act1, dq, dk, dv)
    qkv_grad = scatter(qkv_outer_grad)
    dx, vecs1 = input_grad(x, dm, first_gain[None], dq, dk, dv, qkv_full)
    tokens_grad = quad_swap(dx.reshape(row_count, piece_len, width))

    packed = jnp.concatenate(
        [
            vecs1[0], vecs1[1], qkv_vec[0], qkv_vec[2], vecs[2], vecs[0], vecs[1],
            vecs[3], uvec[0],
        ]
    ).reshape(-1, 128)
    total = lax.psum(packed, ("tok", "row")).reshape(-1)
    v = [total[i * D : (i + 1) * D] for i in range(8)]
    return (
        output, tokens_grad, qkv_grad, proj_grad, up_grad, down_grad,
        v[0], v[1], v[2], v[3], v[4], v[5], v[6], total[8 * D :], v[7],
    )


def solution(mesh):
    rows = P("row", "tok", None)
    weight = P("tok", "row")
    in_specs = (
        rows, rows, P("row", None, None), P(), P(), weight, P(), P(), weight, P(), P(), P(),
        weight, P(), weight, P(),
    )
    out_specs = (rows, rows, weight, weight, weight, weight) + (P(),) * 9
    return jax.shard_map(
        per_device, mesh=mesh, in_specs=in_specs, out_specs=out_specs, check_vma=False
    )
```

time: 1380 us -> 742 us (0.54); the launches traced: 1360 us -> 741 us
  matrix products: 298 us -> 0 us
  waiting for transfers between devices: 733 us -> 477 us
  local copies, waits for them, and re-layouts: 171 us -> 10.8 us
  Pallas kernels: 0 us -> 144 us
  other arithmetic: 51.9 us -> 6.3 us
    dot_general x100 -> x0, matrix products: 298 us -> none  [the longest x12 34 us: attend_back(): jnp.einsum('qd,kd->qk', queries, keys_in, preferred_element_type=jnp.floa...]
    ppermute x8 -> x0, waiting for transfers between devices: 218 us -> none  [from_partner(): return lax.ppermute(block, axis, route)]
    reduce_scatter x5 -> x4, waiting for transfers between devices: 447 us -> 269 us  [scatter(): lax.psum_scatter(flat, ('row', 'tok'), scatter_dimension=0, tiled=True)]
    pallas_call x0 -> x9, Pallas kernels: none -> 144 us  [the longest x1 35.6 us: mlp(): pl.pallas_call(mlp_kernel, grid=(n // tile,), in_specs=[row(D), row(D), r...]
    all_gather x7 -> x4, waiting for transfers between devices: 64.6 us -> 186 us  [gather(): whole = lax.all_gather(shard, ('row', 'tok'), axis=0, tiled=True)]
    reshape x12 -> x0, local copies, waits for them, and re-layouts: 71.1 us -> none  [the longest x2 25.9 us: per_device(): qkv.reshape(row_count, piece_len, 3, 4, head_cols)]
    unnamed x98 -> x34, local copies, waits for them, and re-layouts: 53.4 us -> 2.39 us
    all_gather x1 -> x0, blocking collectives: 45.4 us -> none  [attn_weights(): lax.all_gather(proj_weight, 'tok', axis=0, tiled=True)]
  transfers between devices with their start and end apart: 23 -> 11, of which waited for: 13 -> 8; matrix products, arithmetic and copies ran while one was open for 36% -> 2% of each run, Pallas kernels for 0% -> 14%
where the time goes in v1:
time: 742 us; the launch traced here: 741 us
  waiting for transfers between devices  477 us (64%)
  Pallas kernels  144 us (19%)
  blocking collectives  77.6 us (10%)
  between operations  14.4 us (2%)
  starting transfers between devices  11.3 us (2%)
  local copies, waits for them, and re-layouts  10.8 us (1%)
    reduce_scatter x4, waiting for transfers between devices, scatter(): lax.psum_scatter(flat, ('row', 'tok'), scatter_dimension=0, tiled=True)  269 us
    all_gather x4, waiting for transfers between devices, gather(): whole = lax.all_gather(shard, ('row', 'tok'), axis=0, tiled=True)  186 us
    psum x1, blocking collectives, per_device(): total = lax.psum(packed, ('tok', 'row')).reshape(-1)  51.1 us
    pallas_call x1, Pallas kernels, mlp(): pl.pallas_call(mlp_kernel, grid=(n // tile,), in_specs=[row(D), row(D), r...  35.6 us
    pallas_call x1, Pallas kernels, attention_back(): pl.pallas_call(attn_back_kernel, grid=(pairs,), in_specs=[pl.BlockSpec(me...  33.9 us
    all_to_all x1, blocking collectives, quad_swap(): lax.all_to_all(pieces, 'tok', 0, 0, axis_index_groups=groups, tiled=True)  26.5 us
    pallas_call x1, Pallas kernels, attention(): pl.pallas_call(attn_kernel, grid=(pairs,), in_specs=[pl.BlockSpec(memory_...  22.8 us
    all_to_all x3, waiting for transfers between devices, quad_swap(): lax.all_to_all(pieces, 'tok', 0, 0, axis_index_groups=groups, tiled=True)  18.5 us
  transfers between devices with their start and end apart: 11, of which 8 were waited for; matrix products, arithmetic and copies ran while one was open for 2% of the time, Pallas kernels for 14%

profile of v1, /device:TPU:0, one launch (start us, length us, event | category | flops | bytes accessed | tf_op | source)
XLA Modules:
  0.0 741.3 jit_solution(13346830956739202743)
XLA Ops:
  7.2 0.0 copy-start
  7.2 0.0 all-gather.5.cloned.1.call-start
  7.2 0.7 all-gather.5.cloned.1.call-update
  7.9 0.0 all-gather.7.cloned.1.call-start
  8.0 0.7 all-gather.7.cloned.1.call-update
  8.7 0.0 all-gather.9.cloned.1.call-start
  8.7 0.7 all-gather.9.cloned.1.call-update
  9.4 0.0 all-gather.11.cloned.1.call-start
  9.5 0.5 all-gather.11.cloned.1.call-update
  10.0 26.5 %all_to_all.20 = bf16[4,256,768]{2,1,0:T(8,128)(2,1)} all-to-all(bf16[4,256,768]{2,1,0:T(8,128)(2,1)} %param.16), channel_id=1, replica_groups={{0,2,4,6},{8,10,12,14},{16,18,20,22},{24,26,28,30},{1,3,5,7},{9,11,13,1..., dimensions={0} | all-to-all | bytes 3145728 | tf_op jit(solution)/shard_map/all_to_all | solution.py:488
  36.5 0.0 copy-start.6
  36.5 0.0 copy-start.7
  36.5 0.0 copy-start.8
  36.6 0.0 copy-start.9
  36.6 3.7 all-to-all-start.1
  40.3 0.0 reduce-scatter.7.cloned.1.call-start
  40.4 0.6 broadcast_in_dim.28.g_ref
  41.0 0.6 broadcast_in_dim.31.qb_ref
  41.6 0.6 broadcast_in_dim.29.b_ref
  42.2 0.6 broadcast_in_dim.32.pb_ref
  42.8 0.6 broadcast_in_dim.33.g_ref
  43.3 0.6 broadcast_in_dim.34.b_ref
  43.9 0.6 broadcast_in_dim.36.db_ref
  44.5 0.5 dynamic-slice_bitcast_fusion.lens_ref
  45.0 32.2 %all-gather.5.cloned.1.call-done = bf16[1536,1152]{1,0:T(8,128)(2,1)} async-done(((bf16[48,1152]{1,0:T(8,128)(2,1)}), bf16[1536,1152]{1,0:T(8,128)(2,1)}) %all-gather.5.cloned.1.call-update) | async-done | bytes 3538960 | tf_op jit(solution)/shard_map/all_gather | solution.py:494
  77.2 9.5 %norm_qkv.1 = (bf16[1024,768]{1,0:T(8,128)(2,1)}, bf16[1024,2304]{1,0:T(8,128)(2,1)}) custom-call(bf16[1024,768]{1,0:T(8,128)(2,1)} %bitcast.38, f32[1,768]{1,0:T(1,128)} %broadcast_in_dim.28.g_ref, f32[1,768]{1,0:T(1,128)} %broadcast_in_dim.29.b_ref, f32[1,2304]{1,0:T(1,128)} %broadcast_in_dim.31.qb_ref, bf16[2,768,1152]{2,1,0:T(8,128)(2,1)} %bitcast.49), custom_call_target="tpu_custom_call" | custom-call | flops 3623878656 | bytes 11403264 | tf_op jit(solution)/shard_map/norm_qkv/pallas_call | solution.py:92
  86.7 22.8 %attention.1 = (bf16[1024,768]{1,0:T(8,128)(2,1)}, f32[1024,128]{1,0:T(8,128)}) custom-call(s32[1,8]{1,0:T(1,128)} %dynamic-slice_bitcast_fusion.lens_ref, bf16[1024,2304]{1,0:T(8,128)(2,1)} %get-tuple-element.36.q_ref.k_ref.v_ref, bf16[1024,2304]{1,0:T(8,128)(2,1)} %get-tuple-element.36.q_ref.k_ref.v_ref, bf16[1024,2304]{1,0:T(8,128)(2,1)} %get-tuple-element.36.q_ref.k_ref.v_ref), custom_call_target="tpu_custom_call" | custom-call | flops 1932735232 | bytes 6291456 | tf_op jit(solution)/shard_map/attention/pallas_call | solution.py:171
  109.6 0.0 copy-start.2
  109.6 23.1 %all-gather.7.cloned.1.call-done = bf16[1536,384]{1,0:T(8,128)(2,1)} async-done(((bf16[48,384]{1,0:T(8,128)(2,1)}), bf16[1536,384]{1,0:T(8,128)(2,1)}) %all-gather.7.cloned.1.call-update) | async-done | bytes 1179664 | tf_op jit(solution)/shard_map/all_gather | solution.py:494
  132.7 65.4 %all-gather.9.cloned.1.call-done = bf16[1536,1536]{1,0:T(8,128)(2,1)} async-done(((bf16[48,1536]{1,0:T(8,128)(2,1)}), bf16[1536,1536]{1,0:T(8,128)(2,1)}) %all-gather.9.cloned.1.call-update) | async-done | bytes 4718608 | tf_op jit(solution)/shard_map/all_gather | solution.py:494
  198.1 65.1 %all-gather.11.cloned.1.call-done = bf16[6144,384]{1,0:T(8,128)(2,1)} async-done(((bf16[192,384]{1,0:T(8,128)(2,1)}), bf16[6144,384]{1,0:T(8,128)(2,1)}) %all-gather.11.cloned.1.call-update) | async-done | bytes 4718608 | tf_op jit(solution)/shard_map/all_gather | solution.py:494
  263.3 35.6 %mlp.1 = (bf16[1024,768]{1,0:T(8,128)(2,1)}, bf16[1024,3072]{1,0:T(8,128)(2,1)}, bf16[1024,3072]{1,0:T(8,128)(2,1)}, bf16[1024,768]{1,0:T(8,128)(2,1)}, bf16[102...) custom-call(bf16[1024,768]{1,0:T(8,128)(2,1)} %bitcast.39, ...), custom_call_target="tpu_custom_call" | custom-call | flops 21743271936 | bytes 28311552 | tf_op jit(solution)/shard_map/mlp/pallas_call | solution.py:346
  298.9 4.4 outer_rows.2
  303.2 0.0 reduce-scatter.7.cloned.1.call-update
  303.2 0.0 reduce-scatter.5.cloned.1.call-start
  303.3 33.9 %attention_back.1 = (bf16[1024,768]{1,0:T(8,128)(2,1)}, bf16[1024,768]{1,0:T(8,128)(2,1)}, bf16[1024,768]{1,0:T(8,128)(2,1)}) custom-call(s32[1,8]{1,0:T(1,128)} %dynamic-slice_bitcast_fusion.lens_ref, bf16[1024,2304]{1,0:T(8,128)(2,1)} %get-tuple-element.36.q_ref.k_ref.v_ref, bf16[1024,2304]{1,0:T(8,128)(2,1)} %get-tuple-element.36.q_ref.k_ref.v_ref, ...), custom_call_target="tpu_custom_call" | custom-call | flops 4831838208 | bytes 12582912 | tf_op jit(solution)/shard_map/attention_back/pallas_call | solution.py:251
  337.2 8.5 %qkv_outer.1 = (bf16[2,768,1152]{2,1,0:T(8,128)(2,1)}, f32[8,768]{1,0:T(8,128)}) custom-call(bf16[1024,768]{1,0:T(8,128)(2,1)} %get-tuple-element.46.a_ref, bf16[1024,768]{1,0:T(8,128)(2,1)} %get-tuple-element.42.dq_ref.q_ref, bf16[1024,768]{1,0:T(8,128)(2,1)} %get-tuple-element.43.dk_ref.k_ref, bf16[1024,768]{1,0:T(8,128)(2,1)} %get-tuple-element.44.dv_ref.v_ref), custom_call_target="tpu_custom_call" | custom-call | flops 3623878656 | bytes 9830400 | tf_op jit(solution)/shard_map/qkv_outer/pallas_call | solution.py:435
  345.6 0.0 reduce-scatter.5.cloned.1.call-update
  345.7 0.0 reduce-scatter.11.cloned.1.call-start
  345.7 9.2 %outer_rows.3 = bf16[2,3072,384]{2,1,0:T(8,128)(2,1)} custom-call(bf16[1024,3072]{1,0:T(8,128)(2,1)} %get-tuple-element.51.a_ref, bf16[1024,768]{1,0:T(8,128)(2,1)} %get-tuple-element.52.b_ref), custom_call_target="tpu_custom_call" | custom-call | flops 4831838208 | bytes 12582912 | tf_op jit(solution)/shard_map/outer_rows/pallas_call | solution.py:385
  354.9 0.0 reduce-scatter.11.cloned.1.call-update
  354.9 0.0 reduce-scatter.9.cloned.1.call-start
  355.0 9.6 %outer_cols.1 = bf16[2,768,1536]{2,1,0:T(8,128)(2,1)} custom-call(bf16[1024,768]{1,0:T(8,128)(2,1)} %get-tuple-element.49.a_ref, bf16[1024,3072]{1,0:T(8,128)(2,1)} %get-tuple-element.50.b_ref), custom_call_target="tpu_custom_call" | custom-call | flops 4831838208 | bytes 12582912 | tf_op jit(solution)/shard_map/outer_cols/pallas_call | solution.py:404
  364.6 0.0 reduce-scatter.9.cloned.1.call-update
  364.6 10.8 %input_grad.1 = (bf16[1024,768]{1,0:T(8,128)(2,1)}, f32[8,768]{1,0:T(8,128)}) custom-call(bf16[1024,768]{1,0:T(8,128)(2,1)} %bitcast.40, f32[1024,768]{1,0:T(8,128)} %get-tuple-element.39.dm_ref, f32[1,768]{1,0:T(1,128)} %broadcast_in_dim.28.g_ref, bf16[1024,768]{1,0:T(8,128)(2,1)} %get-tuple-element.42.dq_ref.q_ref, ...), custom_call_target="tpu_custom_call" | custom-call | flops 3623878656 | bytes 14548992 | tf_op jit(solution)/shard_map/input_grad/pallas_call | solution.py:472
  375.5 3.6 all-to-all-start.3
  379.1 0.8 slice_reduce_fusion.6
  379.9 0.8 slice_reduce_fusion.4
  380.8 18.5 %all-to-all-done.3 = bf16[4,256,768]{2,1,0:T(8,128)(2,1)S(1)} async-done(((bf16[4,256,768]{2,1,0:T(8,128)(2,1)}), bf16[4,256,768]{2,1,0:T(8,128)(2,1)S(1)}, u32[]{:S(2)}, u32[]{:S(2)}) %all-to-all-start.3) | async-done | bytes 1572896 | tf_op jit(solution)/shard_map/all_to_all | solution.py:488
  399.3 3.7 all-to-all-start.2
  403.0 0.9 slice.89
  404.0 51.1 %psum.7 = f32[72,128]{1,0:T(8,128)S(1)} all-reduce(f32[72,128]{1,0:T(8,128)S(1)} %bitcast.46), channel_id=1, replica_groups=mesh['tok'=16,'row'=2] {'tok','row'}, use_global_device_ids=true, to_apply=%region_4.5 | all-reduce | flops 9216 | bytes 73728 | tf_op jit(solution)/shard_map/psum | solution.py:574
  455.1 0.6 slice_bitcast_fusion
  455.7 0.6 slice_bitcast_fusion.1
  456.3 0.0 reduce-scatter.7.cloned.1.call-done
  456.4 1.4 convert_element_type.13
  457.8 48.7 %reduce-scatter.5.cloned.1.call-done = bf16[48,1152]{1,0:T(8,128)(2,1)} async-done(((bf16[1536,1152]{1,0:T(8,128)(2,1)}), bf16[48,1152]{1,0:T(8,128)(2,1)}) %reduce-scatter.5.cloned.1.call-update) | async-done | bytes 110608 | tf_op jit(solution)/shard_map/reduce_scatter | solution.py:514
  506.5 1.6 convert_element_type.12
  508.1 109.9 %reduce-scatter.11.cloned.1.call-done = bf16[192,384]{1,0:T(8,128)(2,1)} async-done(((bf16[6144,384]{1,0:T(8,128)(2,1)}), bf16[192,384]{1,0:T(8,128)(2,1)}) %reduce-scatter.11.cloned.1.call-update) | async-done | bytes 147472 | tf_op jit(solution)/shard_map/reduce_scatter | solution.py:514
  618.0 1.6 convert_element_type.15
  619.6 110.9 %reduce-scatter.9.cloned.1.call-done = bf16[48,1536]{1,0:T(8,128)(2,1)} async-done(((bf16[1536,1536]{1,0:T(8,128)(2,1)}), bf16[48,1536]{1,0:T(8,128)(2,1)}) %reduce-scatter.9.cloned.1.call-update) | async-done | bytes 147472 | tf_op jit(solution)/shard_map/reduce_scatter | solution.py:514
  730.5 1.6 convert_element_type.14
  732.1 1.1 copy.42
  733.3 1.1 copy.43
  (33 shorter events, 0.1 us)
Async XLA Ops:
  7.2 37.3 %copy-start = (s32[4,4,8]{2,1,0:T(4,128)S(1)}, s32[4,4,8]{2,1,0:T(4,128)}, u32[]{:S(2)}) copy-start(s32[4,4,8]{2,1,0:T(4,128)} %param.18) | copy-start | bytes 1540
  7.2 70.0 %all-gather.5.cloned.1.call-start = ((), (), s32[]{:S(2)}) async-start(), calls=%async_computation.8 | async-start | bytes 3649536 | tf_op jit(solution)/shard_map/all_gather | solution.py:494
  7.9 124.8 %all-gather.7.cloned.1.call-start = ((), (), s32[]{:S(2)}) async-start(), calls=%async_computation.9 | async-start | bytes 1216512 | tf_op jit(solution)/shard_map/all_gather | solution.py:494
  8.7 189.4 %all-gather.9.cloned.1.call-start = ((), (), s32[]{:S(2)}) async-start(), calls=%async_computation.10 | async-start | bytes 4866048 | tf_op jit(solution)/shard_map/all_gather | solution.py:494
  9.4 253.9 %all-gather.11.cloned.1.call-start = ((), (), s32[]{:S(2)}) async-start(), calls=%async_computation.11 | async-start | bytes 4866048 | tf_op jit(solution)/shard_map/all_gather | solution.py:494
  36.5 3.9 copy-start.4
  36.5 4.4 copy-start.10
  36.5 4.4 copy-start.11
  36.5 5.1 copy-start.5
  36.5 5.6 copy-start.6
  36.5 6.2 copy-start.7
  36.5 6.8 copy-start.8
  36.6 7.4 copy-start.9
  36.6 73.0 %all-to-all-start.1 = ((bf16[4,256,768]{2,1,0:T(8,128)(2,1)}), bf16[4,256,768]{2,1,0:T(8,128)(2,1)S(1)}, u32[]{:S(2)}, u32[]{:S(2)}) async-start(bf16[4,256,768]{2,1,0:T(8,128)(2,1)} %param.17), calls=%async_computation.1 | async-start | bytes 3145728 | tf_op jit(solution)/shard_map/all_to_all | solution.py:488
  40.3 416.1 %reduce-scatter.7.cloned.1.call-start = ((), (), s32[]{:S(2)}) async-start(), calls=%async_computation.13 | async-start | bytes 1216512 | tf_op jit(solution)/shard_map/reduce_scatter | solution.py:514
  109.6 153.7 %copy-start.2 = (bf16[4,256,768]{2,1,0:T(8,128)(2,1)}, bf16[4,256,768]{2,1,0:T(8,128)(2,1)S(1)}, u32[]{:S(2)}) copy-start(bf16[4,256,768]{2,1,0:T(8,128)(2,1)S(1)} %all-to-all-done.1) | copy-start | bytes 4718596
  303.2 203.3 %reduce-scatter.5.cloned.1.call-start = ((), (), s32[]{:S(2)}) async-start(), calls=%async_computation.12 | async-start | bytes 3649536 | tf_op jit(solution)/shard_map/reduce_scatter | solution.py:514
  345.7 272.3 %reduce-scatter.11.cloned.1.call-start = ((), (), s32[]{:S(2)}) async-start(), calls=%async_computation.15 | async-start | bytes 4866048 | tf_op jit(solution)/shard_map/reduce_scatter | solution.py:514
  354.9 375.6 %reduce-scatter.9.cloned.1.call-start = ((), (), s32[]{:S(2)}) async-start(), calls=%async_computation.14 | async-start | bytes 4866048 | tf_op jit(solution)/shard_map/reduce_scatter | solution.py:514
  375.5 23.8 %all-to-all-start.3 = ((bf16[4,256,768]{2,1,0:T(8,128)(2,1)}), bf16[4,256,768]{2,1,0:T(8,128)(2,1)S(1)}, u32[]{:S(2)}, u32[]{:S(2)}) async-start(bf16[4,256,768]{2,1,0:T(8,128)(2,1)} %bitcast.43), calls=%async_computation.3 | async-start | bytes 3145728 | tf_op jit(solution)/shard_map/all_to_all | solution.py:488
  399.3 4.6 copy-start.3
  399.3 57.1 %all-to-all-start.2 = ((bf16[4,256,768]{2,1,0:T(8,128)(2,1)}), bf16[4,256,768]{2,1,0:T(8,128)(2,1)S(1)}, u32[]{:S(2)}, u32[]{:S(2)}) async-start(bf16[4,256,768]{2,1,0:T(8,128)(2,1)} %bitcast.41), calls=%async_computation.2 | async-start | bytes 3145728 | tf_op jit(solution)/shard_map/all_to_all | solution.py:488
  732.1 2.3 copy-start.1
Sparse Core Ops, SparseCore 0:
  10.9 66.2 all-gather.4
  80.1 52.5 all-gather.6
  135.6 62.4 all-gather.8
  200.9 62.3 all-gather.10
  303.4 96.1 reduce-scatter.6
  404.9 101.5 reduce-scatter.4
  512.0 105.9 reduce-scatter.10
  624.4 106.0 reduce-scatter.8

commit v2 on v1

v2 whole, which is shorter than its diff:
```python
import functools
import math

import jax
import jax.numpy as jnp
from jax import lax
from jax.experimental import pallas as pl
from jax.experimental.pallas import tpu as pltpu
from jax.sharding import PartitionSpec as P

D = 768
H = 12
HD = 64
FF = 3072
DEPTH = 48
DOCS = 8
BLK = 256
QUAD = 4

EPSILON = 1e-05
TANH_ROOT = 0.7978845608028654
TANH_CUBIC = 0.044715
BETA = 1.0 / math.sqrt(DEPTH)
SCALE = 1.0 / math.sqrt(HD)
F32 = jnp.float32
BF16 = jnp.bfloat16
VMEM_LIMIT = 56 * 2**20
EASE = 8

NT = (((1,), (1,)), ((), ()))
NN = (((1,), (0,)), ((), ()))
TN = (((0,), (0,)), ((), ()))


def mm(a, b, dims=NN):
    return lax.dot_general(a, b, dims, preferred_element_type=F32)


def params():
    return pltpu.CompilerParams(vmem_limit_bytes=VMEM_LIMIT)


def cost(flops, nbytes, trans=0):
    return pl.CostEstimate(
        flops=int(flops // EASE), bytes_accessed=int(nbytes // EASE), transcendentals=int(trans // EASE)
    )


def norm_parts(x):
    centre = x - jnp.mean(x, axis=-1, keepdims=True)
    inverse = lax.rsqrt(jnp.mean(centre * centre, axis=-1, keepdims=True) + EPSILON)
    return centre * inverse, inverse


def norm_back(grad, normed, inverse, gain):
    spread = grad * gain
    return inverse * (
        spread
        - jnp.mean(spread, axis=-1, keepdims=True)
        - normed * jnp.mean(spread * normed, axis=-1, keepdims=True)
    )


def whole(ref, sem):
    return pltpu.make_async_copy(ref, ref, sem)


def place_pieces(ids, pieces, quad_first, targets):
    count = len(pieces) // 2
    for side in range(2):
        for block in range(count):
            ref = pieces[side * count + block]
            for slot in range(ref.shape[0]):
                d, e = (slot, block) if quad_first else (block, slot)
                shard = (ids[1] ^ e) * QUAD + (ids[0] ^ d)
                rows = ref.shape[1]
                here = pl.ds(pl.multiple_of(shard * rows, 16), rows)
                for at, lanes, w, sem in targets:
                    there = pl.ds(pl.multiple_of((ids[2] ^ side) * lanes, 128), lanes)
                    src = ref.at[slot, :, pl.ds(at, lanes)]
                    pltpu.make_async_copy(src, w.at[here, there], sem).start()


def place_halves(halves, w, sem):
    cols = halves.shape[2]
    for h in range(2):
        pltpu.make_async_copy(halves.at[h], w.at[:, pl.ds(h * cols, cols)], sem).start()


def place(ids, parts, w, sem):
    if len(parts) == 1:
        place_halves(parts[0], w, sem)
    else:
        place_pieces(ids, parts, False, [(0, parts[0].shape[2], w, sem)])


def qkv_kernel(parts, ids, x_ref, g_ref, b_ref, qb_ref, *rest):
    w_hbm, (act_ref, qkv_ref, w_vmem, sem) = rest[:parts], rest[parts:]
    first = pl.program_id(0) == 0

    @pl.when(first)
    def _():
        place(ids, w_hbm, w_vmem, sem)

    normed, _ = norm_parts(x_ref[...].astype(F32))
    act = (normed * g_ref[...] + b_ref[...]).astype(BF16)
    act_ref[...] = act

    @pl.when(first)
    def _():
        whole(w_vmem, sem).wait()

    qkv_ref[...] = (mm(act, w_vmem[...]) + qb_ref[...]).astype(BF16)


def norm_qkv(ids, x, gain, bias, qkv_bias, w):
    n = x.shape[0]
    tile = BLK
    const = lambda i: (0, 0)
    return pl.pallas_call(
        functools.partial(qkv_kernel, len(w)),
        grid=(n // tile,),
        in_specs=[
            pl.BlockSpec(memory_space=pltpu.SMEM),
            pl.BlockSpec((tile, D), lambda i: (i, 0)),
            pl.BlockSpec((1, D), const),
            pl.BlockSpec((1, D), const),
            pl.BlockSpec((1, 3 * D), const),
        ]
        + [pl.BlockSpec(memory_space=pl.ANY)] * len(w),
        out_specs=[
            pl.BlockSpec((tile, D), lambda i: (i, 0)),
            pl.BlockSpec((tile, 3 * D), lambda i: (i, 0)),
        ],
        out_shape=[
            jax.ShapeDtypeStruct((n, D), BF16),
            jax.ShapeDtypeStruct((n, 3 * D), BF16),
        ],
        scratch_shapes=[pltpu.VMEM((D, 3 * D), BF16), pltpu.SemaphoreType.DMA],
        compiler_params=params(),
        cost_estimate=cost(2 * n * D * 3 * D, 2 * (n * 5 * D + 3 * D * D)),
        name="norm_qkv",
    )(ids, x, gain, bias, qkv_bias, *w)


def first_of_doc(lens_ref, positions):
    start = jnp.zeros_like(positions)
    end = 0
    for d in range(DOCS):
        end = end + lens_ref[0, d]
        start = jnp.where(positions >= end, end, start)
    return start


def lane_half(h):
    lane = lax.broadcasted_iota(jnp.int32, (1, 128), 1)
    return (lane >= h * HD) & (lane < (h + 1) * HD)


def attn_kernel(lens_ref, q_ref, k_ref, v_ref, o_ref, l_ref, start_ref):
    pair = pl.program_id(0)
    n = q_ref.shape[0]
    nb = n // BLK

    @pl.when(pair == 0)
    def _():
        start_ref[...] = first_of_doc(lens_ref, lax.broadcasted_iota(jnp.int32, (n, 1), 0))
        l_ref[...] = jnp.zeros_like(l_ref)

    lane = lax.broadcasted_iota(jnp.int32, (1, 128), 1)
    for i in range(nb):
        lo = max(0, i - 2)
        rows = pl.ds(i * BLK, BLK)
        keys = pl.ds(lo * BLK, (i + 1 - lo) * BLK)
        width = (i + 1 - lo) * BLK
        q = q_ref[rows, :] * jnp.asarray(SCALE, BF16)
        k = k_ref[keys, :]
        v = v_ref[keys, :]
        kpos = lax.broadcasted_iota(jnp.int32, (1, width), 1) + lo * BLK
        qpos = lax.broadcasted_iota(jnp.int32, (BLK, 1), 0) + i * BLK
        allowed = (kpos >= start_ref[rows, :]) & (kpos <= qpos)
        outs = []
        stats = l_ref[rows, :]
        for h in range(2):
            qh = jnp.where(lane_half(h), q, jnp.zeros_like(q))
            s = jnp.where(allowed, mm(qh, k, NT), -1e9)
            m = jnp.max(s, axis=-1, keepdims=True)
            p = jnp.exp(s - m)
            total = jnp.sum(p, axis=-1, keepdims=True)
            outs.append(mm(p.astype(BF16), v) / total)
            stats = jnp.where(lane == 2 * pair + h, m + jnp.log(total), stats)
        l_ref[rows, :] = stats
        o_ref[rows, :] = jnp.where(lane_half(0), outs[0], outs[1]).astype(BF16)


def attention(lens, qkv):
    n = qkv.shape[0]
    pairs = H // 2
    spec = lambda w: pl.BlockSpec((n, 128), lambda p: (0, w * pairs + p))
    return pl.pallas_call(
        attn_kernel,
        grid=(pairs,),
        in_specs=[pl.BlockSpec(memory_space=pltpu.SMEM), spec(0), spec(1), spec(2)],
        out_specs=[
            pl.BlockSpec((n, 128), lambda p: (0, p)),
            pl.BlockSpec((n, 128), lambda p: (0, 0)),
        ],
        out_shape=[jax.ShapeDtypeStruct((n, D), BF16), jax.ShapeDtypeStruct((n, 128), F32)],
        scratch_shapes=[pltpu.VMEM((n, 1), jnp.int32)],
        compiler_params=params(),
        cost_estimate=cost(2 * 2 * H * n * n * HD * 0.6, 2 * n * 4 * D, H * n * n * 0.6),
        name="attention",
    )(lens, qkv, qkv, qkv)


def attn_back_kernel(
    lens_ref, q_ref, k_ref, v_ref, o_ref, do_ref, l_ref, out_hbm,
    start_ref, lt_ref, dk_acc, dv_acc, bufs, sems,
):
    pair = pl.program_id(0)
    pairs = pl.num_programs(0)
    n = q_ref.shape[0]
    nb = n // BLK
    slot = pair % 2

    def copies(p, at):
        return [
            pltpu.make_async_copy(
                bufs.at[at, w],
                out_hbm.at[:, pl.ds(pl.multiple_of(w * D + p * 128, 128), 128)],
                sems.at[at, w],
            )
            for w in range(3)
        ]

    @pl.when(pair == 0)
    def _():
        start_ref[...] = first_of_doc(lens_ref, lax.broadcasted_iota(jnp.int32, (8, n), 1))
        lt_ref[...] = l_ref[...].T

    @pl.when(pair >= 2)
    def _():
        for c in copies(pair - 2, slot):
            c.wait()

    prod = (o_ref[...].astype(F32) * do_ref[...].astype(F32)).T
    for h in range(2):
        half = lane_half(h)
        delta = jnp.sum(prod[h * HD : (h + 1) * HD, :], axis=0, keepdims=True)
        logs = lt_ref[pl.ds(2 * pair + h, 1), :]
        for i in range(nb):
            rows = pl.ds(i * BLK, BLK)
            q = q_ref[rows, :] * jnp.asarray(SCALE, BF16)
            q = jnp.where(half, q, jnp.zeros_like(q))
            do = do_ref[rows, :]
            do = jnp.where(half, do, jnp.zeros_like(do))
            logs_i = logs[:, i * BLK : (i + 1) * BLK]
            delta_i = delta[:, i * BLK : (i + 1) * BLK]
            start_i = start_ref[0:1, i * BLK : (i + 1) * BLK]
            qpos = lax.broadcasted_iota(jnp.int32, (1, BLK), 1) + i * BLK
            dq = jnp.zeros((BLK, 128), F32)
            for j in range(max(0, i - 2), i + 1):
                keys = pl.ds(j * BLK, BLK)
                k = k_ref[keys, :]
                v = v_ref[keys, :]
                kpos = lax.broadcasted_iota(jnp.int32, (BLK, 1), 0) + j * BLK
                allowed = kpos >= start_i
                if i == j:
                    allowed = allowed & (kpos <= qpos)
                p = jnp.where(allowed, jnp.exp(mm(k, q, NT) - logs_i), 0.0)
                dp = mm(v, do, NT)
                ds = (p * (dp - delta_i)).astype(BF16)
                dv = mm(p.astype(BF16), do)
                dk = mm(ds, q)
                if h == 0 and i == j:
                    dv_acc[keys, :] = dv
                    dk_acc[keys, :] = dk
                else:
                    dv_acc[keys, :] += dv
                    dk_acc[keys, :] += dk
                kh = jnp.where(half, k, jnp.zeros_like(k))
                dq = dq + mm(ds, kh, TN)
            dq = (dq * SCALE).astype(BF16)
            if h == 0:
                bufs[slot, 0, rows, :] = dq
            else:
                bufs[slot, 0, rows, :] = jnp.where(half, dq, bufs[slot, 0, rows, :])
    bufs[slot, 1] = dk_acc[...].astype(BF16)
    bufs[slot, 2] = dv_acc[...].astype(BF16)
    for c in copies(pair, slot):
        c.start()

    @pl.when(pair == pairs - 1)
    def _():
        for c in copies(pair - 1, 1 - slot) + copies(pair, slot):
            c.wait()


def attention_back(lens, qkv, attended, dout, stats):
    n = qkv.shape[0]
    pairs = H // 2
    spec = lambda w: pl.BlockSpec((n, 128), lambda p: (0, w * pairs + p))
    one = pl.BlockSpec((n, 128), lambda p: (0, p))
    return pl.pallas_call(
        attn_back_kernel,
        grid=(pairs,),
        in_specs=[
            pl.BlockSpec(memory_space=pltpu.SMEM), spec(0), spec(1), spec(2), one, one,
            pl.BlockSpec((n, 128), lambda p: (0, 0)),
        ],
        out_specs=pl.BlockSpec(memory_space=pl.ANY),
        out_shape=jax.ShapeDtypeStruct((n, 3 * D), BF16),
        scratch_shapes=[
            pltpu.VMEM((8, n), jnp.int32),
            pltpu.VMEM((128, n), F32),
            pltpu.VMEM((n, 128), F32),
            pltpu.VMEM((n, 128), F32),
            pltpu.VMEM((2, 3, n, 128), BF16),
            pltpu.SemaphoreType.DMA((2, 3)),
        ],
        compiler_params=params(),
        cost_estimate=cost(5 * 2 * H * n * n * HD * 0.6, 2 * n * 8 * D, H * n * n * 0.6),
        name="attention_back",
    )(lens, qkv, qkv, qkv, attended, dout, stats)


def start_mlp_weights(ids, w_hbm, wp, wu, wd, sem):
    if len(w_hbm) == 3:
        place_halves(w_hbm[0], wp, sem.at[0])
        place_halves(w_hbm[1], wu, sem.at[1])
    else:
        up = (0, FF // 2, wu, sem.at[1])
        place_pieces(ids, w_hbm[:-1], False, [(FF // 2, D // 2, wp, sem.at[0]), up])
    place_halves(w_hbm[-1], wd, sem.at[2])


def mlp_kernel(
    parts, ids, x_ref, att_ref, pb_ref, g_ref, b_ref, ub_ref, db_ref, *rest
):
    w_hbm = rest[:parts]
    mid_ref, out_ref, hid_ref, slope_ref, act_ref, wp, wu, wd, sem = rest[parts:]
    step = pl.program_id(0)

    @pl.when(step == 0)
    def _():
        start_mlp_weights(ids, w_hbm, wp, wu, wd, sem)
        whole(wp, sem.at[0]).wait()

    middle = x_ref[...].astype(F32) + BETA * (mm(att_ref[...], wp[...]) + pb_ref[...])
    mid_ref[...] = middle
    normed, _ = norm_parts(middle)
    act = (normed * g_ref[...] + b_ref[...]).astype(BF16)
    act_ref[...] = act

    @pl.when(step == 0)
    def _():
        whole(wu, sem.at[1]).wait()
        whole(wd, sem.at[2]).wait()

    chunk = 768
    branch = jnp.zeros(middle.shape, F32)
    for f in range(FF // chunk):
        cols = pl.ds(f * chunk, chunk)
        u = mm(act, wu[:, cols]) + ub_ref[:, cols]
        u2 = u * u
        half_t = 0.5 * jnp.tanh(u * (TANH_ROOT + (TANH_ROOT * TANH_CUBIC) * u2))
        gate = 0.5 + half_t
        hidden = (u * gate).astype(BF16)
        hid_ref[:, cols] = hidden
        branch = branch + mm(hidden, wd[cols, :])
        slope = gate + u * (0.5 - 2.0 * half_t * half_t) * (
            TANH_ROOT + (3.0 * TANH_ROOT * TANH_CUBIC) * u2
        )
        slope_ref[:, cols] = slope.astype(BF16)
    out_ref[...] = (middle + BETA * (branch + db_ref[...])).astype(BF16)


MLP_SCRATCH = [
    pltpu.VMEM((D, D), BF16),
    pltpu.VMEM((D, FF), BF16),
    pltpu.VMEM((FF, D), BF16),
    pltpu.SemaphoreType.DMA((3,)),
]


def mlp(ids, x, att, pb, gain, bias, ub, db, w):
    n = x.shape[0]
    tile = BLK
    row = lambda w: pl.BlockSpec((tile, w), lambda i: (i, 0))
    vec = lambda w: pl.BlockSpec((1, w), lambda i: (0, 0))
    sds = jax.ShapeDtypeStruct
    return pl.pallas_call(
        functools.partial(mlp_kernel, len(w)),
        grid=(n // tile,),
        in_specs=[pl.BlockSpec(memory_space=pltpu.SMEM)]
        + [row(D), row(D), vec(D), vec(D), vec(D), vec(FF), vec(D)]
        + [pl.BlockSpec(memory_space=pl.ANY)] * len(w),
        out_specs=[row(D), row(D), row(FF), row(FF), row(D)],
        out_shape=[
            sds((n, D), F32), sds((n, D), BF16), sds((n, FF), BF16), sds((n, FF), BF16),
            sds((n, D), BF16),
        ],
        scratch_shapes=MLP_SCRATCH,
        compiler_params=params(),
        cost_estimate=cost(2 * n * (2 * D * FF + D * D), 2 * n * (7 * D + 2 * FF), n * FF),
        name="mlp",
    )(ids, x, att, pb, gain, bias, ub, db, *w)


def mlp_back_kernel(parts, ids, c_ref, mid_ref, slope_ref, g_ref, *rest):
    w_hbm = rest[:parts]
    du_ref, dm_ref, dy_ref, do_ref, vec_ref, uvec_ref, wp, wu, wd, sem = rest[parts:]
    step = pl.program_id(0)

    @pl.when(step == 0)
    def _():
        start_mlp_weights(ids, w_hbm, wp, wu, wd, sem)
        vec_ref[...] = jnp.zeros_like(vec_ref)
        uvec_ref[...] = jnp.zeros_like(uvec_ref)

    grad_out = c_ref[...].astype(F32)
    dz = (BETA * grad_out).astype(BF16)
    normed, inverse = norm_parts(mid_ref[...])

    @pl.when(step == 0)
    def _():
        whole(wd, sem.at[2]).wait()
        whole(wu, sem.at[1]).wait()
        whole(wp, sem.at[0]).wait()

    chunk = 768
    da = jnp.zeros(normed.shape, F32)
    for f in range(FF // chunk):
        cols = pl.ds(f * chunk, chunk)
        du = (mm(dz, wd[cols, :], NT) * slope_ref[:, cols].astype(F32)).astype(BF16)
        du_ref[:, cols] = du
        uvec_ref[0:1, cols] += jnp.sum(du.astype(F32), axis=0, keepdims=True)
        da = da + mm(du, wu[:, cols], NT)
    dm = grad_out + norm_back(da, normed, inverse, g_ref[...])
    dm_ref[...] = dm
    dy = (BETA * dm).astype(BF16)
    dy_ref[...] = dy
    do_ref[...] = mm(dy, wp[...], NT).astype(BF16)
    vec_ref[0:1, :] += jnp.sum(da * normed, axis=0, keepdims=True)
    vec_ref[1:2, :] += jnp.sum(da, axis=0, keepdims=True)
    vec_ref[2:3, :] += jnp.sum(dy.astype(F32), axis=0, keepdims=True)
    vec_ref[3:4, :] += jnp.sum(dz.astype(F32), axis=0, keepdims=True)


def mlp_back(ids, c, middle, slope, gain, w):
    n = c.shape[0]
    tile = BLK
    const = lambda i: (0, 0)
    row = lambda w: pl.BlockSpec((tile, w), lambda i: (i, 0))
    sds = jax.ShapeDtypeStruct
    return pl.pallas_call(
        functools.partial(mlp_back_kernel, len(w)),
        grid=(n // tile,),
        in_specs=[pl.BlockSpec(memory_space=pltpu.SMEM)]
        + [row(D), row(D), row(FF), pl.BlockSpec((1, D), const)]
        + [pl.BlockSpec(memory_space=pl.ANY)] * len(w),
        out_specs=[
            row(FF), row(D), row(D), row(D), pl.BlockSpec((8, D), const), pl.BlockSpec((8, FF), const),
        ],
        out_shape=[
            sds((n, FF), BF16), sds((n, D), F32), sds((n, D), BF16), sds((n, D), BF16),
            sds((8, D), F32), sds((8, FF), F32),
        ],
        scratch_shapes=MLP_SCRATCH,
        compiler_params=params(),
        cost_estimate=cost(2 * n * (2 * D * FF + D * D), 2 * n * (7 * D + 2 * FF), n * FF),
        name="mlp_back",
    )(ids, c, middle, slope, gain, *w)


def store_sides(row, r, mine, theirs):
    width = r.shape[1] // 2

    @pl.when(row == 0)
    def _():
        mine[...] = r[:, :width].astype(BF16)
        theirs[...] = r[:, width:].astype(BF16)

    @pl.when(row == 1)
    def _():
        theirs[...] = r[:, :width].astype(BF16)
        mine[...] = r[:, width:].astype(BF16)


def down_outer_kernel(a_ref, c_ref, o_ref, dz):
    @pl.when(pl.program_id(0) == 0)
    def _():
        dz[...] = (BETA * c_ref[...].astype(F32)).astype(BF16)

    r = mm(a_ref[...], dz[...], TN).astype(BF16)
    width = o_ref.shape[2]
    o_ref[0] = r[:, :width]
    o_ref[1] = r[:, width:]


def down_outer(hidden, c):
    n = hidden.shape[0]
    return pl.pallas_call(
        down_outer_kernel,
        grid=(FF // D,),
        in_specs=[
            pl.BlockSpec((n, D), lambda i: (0, i)),
            pl.BlockSpec((n, D), lambda i: (0, 0)),
        ],
        out_specs=pl.BlockSpec((2, D, D // 2), lambda i: (0, i, 0)),
        out_shape=jax.ShapeDtypeStruct((2, FF, D // 2), BF16),
        scratch_shapes=[pltpu.VMEM((n, D), BF16)],
        compiler_params=params(),
        cost_estimate=cost(2 * n * FF * D, 2 * (n * (FF + D) + FF * D)),
        name="down_outer",
    )(hidden, c)


def up_outer_kernel(ids, act_ref, du_ref, att_ref, dy_ref, mine, theirs):
    step = pl.program_id(0)
    r = mm(act_ref[...], du_ref[...], TN).astype(BF16)

    @pl.when(step < 2)
    def _():
        theirs[:, pl.ds(pl.multiple_of(step * D, 128), D)] = r

    @pl.when(step >= 2)
    def _():
        mine[:, pl.ds(pl.multiple_of((step - 2) * D, 128), D)] = r

    @pl.when(step == 3)
    def _():
        tail = slice(FF // 2, (FF + D) // 2)
        store_sides(ids[2], mm(att_ref[...], dy_ref[...], TN), mine.at[:, tail], theirs.at[:, tail])


def up_outer(ids, act, du, attended, dy):
    n = act.shape[0]
    width = (FF + D) // 2
    once = pl.BlockSpec((n, D), lambda i, s: (0, 0))
    out = pl.BlockSpec((D, width), lambda i, s: (0, 0))
    return pl.pallas_call(
        up_outer_kernel,
        grid_spec=pltpu.PrefetchScalarGridSpec(
            num_scalar_prefetch=1,
            grid=(FF // D,),
            in_specs=[
                once,
                pl.BlockSpec((n, D), lambda i, s: (0, (i + 2 * (1 - s[2])) % 4)),
                once,
                once,
            ],
            out_specs=[out, out],
        ),
        out_shape=[jax.ShapeDtypeStruct((D, width), BF16)] * 2,
        compiler_params=params(),
        cost_estimate=cost(2 * n * D * 2 * width, 2 * (n * (FF + 3 * D) + 2 * D * width)),
        name="up_outer",
    )(ids, act, du, attended, dy)


def qkv_outer_kernel(ids, act_ref, dqkv_ref, mine, theirs):
    step = pl.program_id(0)
    r = mm(act_ref[...], dqkv_ref[...], TN).astype(BF16)

    @pl.when(step == 0)
    def _():
        theirs[...] = r

    @pl.when(step == 1)
    def _():
        mine[...] = r


def qkv_outer(ids, act, dqkv):
    n = act.shape[0]
    width = 3 * D // 2
    out = pl.BlockSpec((D, width), lambda i, s: (0, 0))
    return pl.pallas_call(
        qkv_outer_kernel,
        grid_spec=pltpu.PrefetchScalarGridSpec(
            num_scalar_prefetch=1,
            grid=(2,),
            in_specs=[
                pl.BlockSpec((n, D), lambda i, s: (0, 0)),
                pl.BlockSpec((n, width), lambda i, s: (0, (i + 1 - s[2]) % 2)),
            ],
            out_specs=[out, out],
        ),
        out_shape=[jax.ShapeDtypeStruct((D, width), BF16)] * 2,
        compiler_params=params(),
        cost_estimate=cost(2 * n * D * 2 * width, 2 * (n * (D + 2 * width) + 2 * D * width)),
        name="qkv_outer",
    )(ids, act, dqkv)


def merge_kernel(quad_first, rows, ids, mine, theirs, *outs):
    for block, o in enumerate(outs):
        for slot in range(o.shape[0]):
            e, d = (block, slot) if quad_first else (slot, block)
            shard = (ids[1] ^ e) * QUAD + (ids[0] ^ d)
            here = pl.ds(pl.multiple_of(shard * rows, 16), rows)
            o[slot] = (mine[here, :].astype(F32) + theirs[here, :].astype(F32)).astype(BF16)


def merge(ids, mine, theirs, quad_first, name):
    left, width = mine.shape
    rows = left // (4 * QUAD)
    spec = pl.BlockSpec(memory_space=pltpu.VMEM)
    return pl.pallas_call(
        functools.partial(merge_kernel, quad_first, rows),
        in_specs=[pl.BlockSpec(memory_space=pltpu.SMEM), spec, spec],
        out_shape=[jax.ShapeDtypeStruct((4, rows, width), BF16)] * 4,
        compiler_params=params(),
        cost_estimate=cost(2 * mine.size, 6 * mine.size),
        name=name,
    )(ids, mine, theirs)


def add_quad_kernel(ids, a, b, c, d, *outs):
    for e in range(a.shape[0]):
        total = (a[e].astype(F32) + b[e].astype(F32)) + (c[e].astype(F32) + d[e].astype(F32))
        if len(outs) == 1:
            outs[0][ids[1] ^ e] = total.astype(BF16)
        else:
            outs[e][...] = total.astype(BF16)


def add_quad(ids, parts, apart, name):
    block = parts[0].shape
    sds = jax.ShapeDtypeStruct
    spec = pl.BlockSpec(memory_space=pltpu.VMEM)
    return pl.pallas_call(
        add_quad_kernel,
        in_specs=[pl.BlockSpec(memory_space=pltpu.SMEM)] + [spec] * 4,
        out_shape=[sds(block[1:], BF16)] * block[0] if apart else sds(block, BF16),
        compiler_params=params(),
        cost_estimate=cost(4 * parts[0].size, 10 * parts[0].size),
        name=name,
    )(ids, *parts)


def input_grad_kernel(parts, ids, x_ref, dm_ref, g_ref, dqkv_ref, *rest):
    w_hbm, (o_ref, vec_ref, w, sem) = rest[:parts], rest[parts:]
    first = pl.program_id(0) == 0

    @pl.when(first)
    def _():
        place(ids, w_hbm, w, sem)
        vec_ref[...] = jnp.zeros_like(vec_ref)
        whole(w, sem).wait()

    dqkv = dqkv_ref[...]
    da = mm(dqkv, w[...], NT)
    normed, inverse = norm_parts(x_ref[...].astype(F32))
    o_ref[...] = (dm_ref[...] + norm_back(da, normed, inverse, g_ref[...])).astype(BF16)
    vec_ref[0:1, 0:D] += jnp.sum(da * normed, axis=0, keepdims=True)
    vec_ref[1:2, 0:D] += jnp.sum(da, axis=0, keepdims=True)
    vec_ref[2:3, :] += jnp.sum(dqkv.astype(F32), axis=0, keepdims=True)


def input_grad(ids, x, dm, gain, dqkv, w):
    n = x.shape[0]
    tile = BLK
    const = lambda i: (0, 0)
    row = lambda wide: pl.BlockSpec((tile, wide), lambda i: (i, 0))
    return pl.pallas_call(
        functools.partial(input_grad_kernel, len(w)),
        grid=(n // tile,),
        in_specs=[pl.BlockSpec(memory_space=pltpu.SMEM), row(D), row(D), pl.BlockSpec((1, D), const), row(3 * D)]
        + [pl.BlockSpec(memory_space=pl.ANY)] * len(w),
        out_specs=[row(D), pl.BlockSpec((8, 3 * D), const)],
        out_shape=[jax.ShapeDtypeStruct((n, D), BF16), jax.ShapeDtypeStruct((8, 3 * D), F32)],
        scratch_shapes=[pltpu.VMEM((D, 3 * D), BF16), pltpu.SemaphoreType.DMA],
        compiler_params=params(),
        cost_estimate=cost(2 * n * D * 3 * D, 2 * (n * 7 * D + 3 * D * D)),
        name="input_grad",
    )(ids, x, dm, gain, dqkv, *w)


def swap(block, axis, distance):
    count = lax.axis_size(axis)
    return lax.ppermute(block, axis, [(i, i ^ distance) for i in range(count)])


def quad_swap(pieces):
    count = lax.axis_size("tok")
    groups = [list(range(g, g + QUAD)) for g in range(0, count, QUAD)]
    return lax.all_to_all(pieces, "tok", 0, 0, axis_index_groups=groups, tiled=True)


def by_halves(whole):
    over_row, height, cols = whole.shape
    if over_row == 2:
        return whole
    return (
        whole.reshape(2, over_row // 2, height, cols)
        .transpose(0, 2, 1, 3)
        .reshape(2, height, over_row // 2 * cols)
    )


def gather(shard):
    rows, cols = shard.shape
    whole = lax.all_gather(shard, ("row", "tok"), axis=0, tiled=True)
    return by_halves(whole.reshape(lax.axis_size("row"), rows * lax.axis_size("tok"), cols))


def gather_line(shard):
    return jnp.stack([shard] + [swap(shard, "tok", QUAD * e) for e in range(1, 4)])


def spread(block, steps):
    return [block] + [swap(block, "tok", step) for step in steps]


def with_partner(blocks):
    return blocks + [swap(t, "row", 1) for t in blocks]


QUAD_STEPS = (1, 2, 3)
LINE_STEPS = (QUAD, 2 * QUAD, 3 * QUAD)


def after(value, *others):
    return lax.optimization_barrier((value,) + others)[0]


def from_peers(blocks, steps):
    return [blocks[0]] + [swap(t, "tok", step) for t, step in zip(blocks[1:], steps)]


def line_swap(pieces):
    count = lax.axis_size("tok")
    groups = [list(range(q, count, QUAD)) for q in range(QUAD)]
    return lax.all_to_all(pieces, "tok", 0, 0, axis_index_groups=groups, tiled=True)


def total_of(terms):
    return sum([t.astype(F32) for t in terms[1:]], terms[0].astype(F32))


def scatter(halves):
    over_row = lax.axis_size("row")
    _, height, width = halves.shape
    cols = 2 * width // over_row
    if over_row != 2:
        halves = halves.reshape(2, height, over_row // 2, cols).transpose(0, 2, 1, 3)
    flat = halves.reshape(over_row * height, cols)
    return lax.psum_scatter(flat, ("row", "tok"), scatter_dimension=0, tiled=True).astype(F32)


def scatter_sides(sides, row_index):
    flat = jnp.stack(sides)
    return scatter(jnp.where(row_index % 2 == 0, flat, flat[::-1]))


def all_sum(block, steps):
    for step in steps:
        block = block + (swap(block, "tok", step) if step else swap(block, "row", 1))
    return block


def per_device(
    tokens,
    out_grad,
    doc_lengths,
    first_gain,
    first_bias,
    qkv_weight,
    query_bias,
    value_bias,
    proj_weight,
    proj_bias,
    second_gain,
    second_bias,
    up_weight,
    up_bias,
    down_weight,
    down_bias,
):
    row_count, piece_len, width = tokens.shape
    n = row_count * piece_len
    tok_index = lax.axis_index("tok")
    row_index = lax.axis_index("row")
    groups = lax.axis_size("tok") // QUAD
    by_permutes = lax.axis_size("row") == 2 and groups == 4
    ids = jnp.stack([tok_index % QUAD, tok_index // QUAD, row_index % 2]).astype(jnp.int32)
    lens = lax.dynamic_slice(
        doc_lengths,
        (tok_index % QUAD, tok_index // QUAD, 0),
        (1, 1, doc_lengths.shape[2]),
    )[0]

    down_full = gather(down_weight)
    x = quad_swap(tokens).reshape(n, width)
    if by_permutes:
        qkv_line = gather_line(qkv_weight)
        up_weights = jnp.concatenate([up_weight, proj_weight], axis=1)
        up_line = gather_line(after(up_weights, qkv_line))
        qkv_pieces = spread(after(qkv_line, x), QUAD_STEPS)
        qkv_full = with_partner(qkv_pieces)
        up_pieces = spread(after(up_line, *qkv_pieces), QUAD_STEPS)
        others = with_partner(up_pieces) + [down_full]
    else:
        qkv_full = [gather(qkv_weight)]
        others = [gather(proj_weight), gather(up_weight), down_full]
    qkv_bias = jnp.concatenate([query_bias, jnp.zeros_like(query_bias), value_bias])[None]
    act1, qkv = norm_qkv(ids, x, first_gain[None], first_bias[None], qkv_bias, qkv_full)
    attended, stats = attention(lens, qkv)
    c = quad_swap(after(out_grad, attended)).reshape(n, width)
    middle, out, hidden, slope, act2 = mlp(
        ids, x, attended, proj_bias[None], second_gain[None], second_bias[None],
        up_bias[None], down_bias[None], others,
    )
    output = quad_swap(out.reshape(row_count, piece_len, width))
    down_outer_grad = down_outer(hidden, c)
    down_grad = scatter(down_outer_grad)
    c = after(c, down_outer_grad)
    du, dm, dy, dout, vecs, uvec = mlp_back(ids, c, middle, slope, second_gain[None], others)
    up_sides = up_outer(ids, after(act2, output), du, attended, dy)
    if by_permutes:
        up_blocks = merge(ids, up_sides[0], swap(up_sides[1], "row", 1), False, "up_merge")
        dout = after(dout, *up_blocks)
    dqkv = attention_back(lens, qkv, attended, dout, stats)
    if by_permutes:
        up_got = from_peers(up_blocks, QUAD_STEPS)
        act1 = after(act1, *up_got[1:])
    qkv_sides = qkv_outer(ids, act1, dqkv)
    if by_permutes:
        up_got[0] = after(up_got[0], *qkv_sides)
        up_line = add_quad(ids, up_got, False, "up_add")
        qkv_mine = after(qkv_sides[0], up_line)
        up_line = line_swap(up_line)
        qkv_blocks = merge(ids, qkv_mine, swap(qkv_sides[1], "row", 1), False, "qkv_merge")
        dqkv = after(dqkv, down_grad, *qkv_blocks)
        qkv_got = from_peers(qkv_blocks, QUAD_STEPS)
        qkv_got[0] = after(qkv_got[0], up_line)
        qkv_shards = add_quad(ids, qkv_got, True, "qkv_add")
        qkv_grad = total_of(from_peers(qkv_shards, LINE_STEPS))
        up_proj = total_of([up_line[e] for e in range(groups)])
        up_grad, proj_grad = up_proj[:, : FF // 2], up_proj[:, FF // 2 :]
    else:
        up_grad = scatter_sides([t[:, : FF // 2] for t in up_sides], row_index)
        proj_grad = scatter_sides([t[:, FF // 2 :] for t in up_sides], row_index)
        qkv_grad = scatter_sides(qkv_sides, row_index)
    dx, vecs1 = input_grad(ids, x, dm, first_gain[None], dqkv, qkv_full)
    tokens_grad = quad_swap(dx.reshape(row_count, piece_len, width))
    packed = jnp.concatenate(
        [
            vecs1[0, :D], vecs1[1, :D], vecs1[2, :D], vecs1[2, 2 * D :], vecs[2], vecs[0], vecs[1],
            vecs[3], uvec[0],
        ]
    ).reshape(-1, 128)
    if by_permutes:
        packed = all_sum(after(packed, *qkv_got[1:]), (0, 1, 2))
        total = all_sum(after(packed, tokens_grad), LINE_STEPS[:2]).reshape(-1)
    else:
        total = lax.psum(packed, ("tok", "row")).reshape(-1)
    v = [total[i * D : (i + 1) * D] for i in range(8)]
    return (
        output, tokens_grad, qkv_grad, proj_grad, up_grad, down_grad,
        v[0], v[1], v[2], v[3], v[4], v[5], v[6], total[8 * D :], v[7],
    )


def solution(mesh):
    rows = P("row", "tok", None)
    weight = P("tok", "row")
    in_specs = (
        rows, rows, P("row", None, None), P(), P(), weight, P(), P(), weight, P(), P(), P(),
        weight, P(), weight, P(),
    )
    out_specs = (rows, rows, weight, weight, weight, weight) + (P(),) * 9
    return jax.shard_map(
        per_device, mesh=mesh, in_specs=in_specs, out_specs=out_specs, check_vma=False
    )
```

time: 742 us -> 355 us (0.48)
  waiting for transfers between devices: 477 us -> 83.8 us
  blocking collectives: 77.6 us -> 0 us
  starting transfers between devices: 11.3 us -> 65.4 us
  Pallas kernels: 144 us -> 171 us
    reduce_scatter x4 -> x1, waiting for transfers between devices: 269 us -> 12.8 us  [scatter(): lax.psum_scatter(flat, ('row', 'tok'), scatter_dimension=0, tiled=True)]
    all_gather x4 -> x1, waiting for transfers between devices: 186 us -> 0.01 us  [gather(): whole = lax.all_gather(shard, ('row', 'tok'), axis=0, tiled=True)]
    ppermute x0 -> x36, waiting for transfers between devices: none -> 63.1 us  [swap(): return lax.ppermute(block, axis, [(i, i ^ distance) for i in range(count)])]
    psum x1 -> x0, blocking collectives: 51.1 us -> none  [per_device(): total = lax.psum(packed, ('tok', 'row')).reshape(-1)]
    ppermute x0 -> x36, starting transfers between devices: none -> 39.5 us  [swap(): return lax.ppermute(block, axis, [(i, i ^ distance) for i in range(count)])]
    all_to_all x1 -> x0, blocking collectives: 26.5 us -> none  [quad_swap(): lax.all_to_all(pieces, 'tok', 0, 0, axis_index_groups=groups, tiled=True)]
    pallas_call x7 -> x11, Pallas kernels: 87.6 us -> 114 us  [the longest x1 24.4 us: mlp(): pl.pallas_call(functools.partial(mlp_kernel, len(w)), grid=(n // tile,),...]
    all_to_all x3 -> x4, waiting for transfers between devices: 18.5 us -> 7.19 us  [quad_swap(): lax.all_to_all(pieces, 'tok', 0, 0, axis_index_groups=groups, tiled=True)]
  transfers between devices with their start and end apart: 11 -> 43, of which waited for: 8 -> 18; matrix products, arithmetic and copies ran while one was open for 2% -> 3% of each run, Pallas kernels for 14% -> 48%
where the time goes in v2:
time: 355 us; the launch traced here: 354 us
  Pallas kernels  171 us (48%)
  waiting for transfers between devices  83.8 us (24%)
  starting transfers between devices  65.4 us (18%)
  local copies, waits for them, and re-layouts  16.1 us (5%)
  between operations  14.5 us (4%)
    ppermute x36, waiting for transfers between devices, swap(): return lax.ppermute(block, axis, [(i, i ^ distance) for i in range(count)])  63.1 us
    ppermute x36, starting transfers between devices, swap(): return lax.ppermute(block, axis, [(i, i ^ distance) for i in range(count)])  39.5 us
    pallas_call x1, Pallas kernels, attention_back(): pl.pallas_call(attn_back_kernel, grid=(pairs,), in_specs=[pl.BlockSpec(me...  34 us
    pallas_call x1, Pallas kernels, mlp(): pl.pallas_call(functools.partial(mlp_kernel, len(w)), grid=(n // tile,),...  24.4 us
    pallas_call x1, Pallas kernels, attention(): pl.pallas_call(attn_kernel, grid=(pairs,), in_specs=[pl.BlockSpec(memory_...  22.9 us
    pallas_call x1, Pallas kernels, mlp_back(): pl.pallas_call(functools.partial(mlp_back_kernel, len(w)), grid=(n // til...  22.6 us
    all_to_all x4, starting transfers between devices, quad_swap(): lax.all_to_all(pieces, 'tok', 0, 0, axis_index_groups=groups, tiled=True)  18.6 us
    pallas_call x1, Pallas kernels, up_outer(): pl.pallas_call(up_outer_kernel, grid_spec=pltpu.PrefetchScalarGridSpec(nu...  14.1 us
  transfers between devices with their start and end apart: 43, of which 18 were waited for; matrix products, arithmetic and copies ran while one was open for 3% of the time, Pallas kernels for 48%

profile of v2, /device:TPU:0, one launch (start us, length us, event | category | flops | bytes accessed | tf_op | source)
XLA Modules:
  0.0 354.2 jit_solution(15895585764835961665)
XLA Ops:
  7.3 0.7 all-gather.2.cloned.1.call-update
  8.0 5.3 %all-to-all-start = ((bf16[4,256,768]{2,1,0:T(8,128)(2,1)}), bf16[4,256,768]{2,1,0:T(8,128)(2,1)S(1)}, u32[]{:S(2)}, u32[]{:S(2)}) async-start(bf16[4,256,768]{2,1,0:T(8,128)(2,1)} %param.16), calls=%async_computation | async-start | bytes 3145728 | tf_op jit(solution)/shard_map/all_to_all | solution.py:689
  13.3 1.6 collective-permute-start
  14.9 2.6 collective-permute-start.1
  17.8 1.4 collective-permute-done
  19.2 7.1 %collective-permute-done.1 = bf16[48,1152]{1,0:T(8,128)(2,1)S(1)} collective-permute-done((bf16[48,1152]{1,0:T(8,128)(2,1)S(1)}, bf16[48,1152]{1,0:T(8,128)(2,1)S(1)}, u32[]{:S(2)}, u32[]{:S(2)}) %collective-permute-start.1) | collective-permute-done | bytes 110624 | tf_op jit(solution)/shard_map/ppermute | solution.py:683
  26.4 7.2 %all-to-all-done = bf16[4,256,768]{2,1,0:T(8,128)(2,1)S(1)} async-done(((bf16[4,256,768]{2,1,0:T(8,128)(2,1)}), bf16[4,256,768]{2,1,0:T(8,128)(2,1)S(1)}, u32[]{:S(2)}, u32[]{:S(2)}) %all-to-all-start) | async-done | bytes 1572896 | tf_op jit(solution)/shard_map/all_to_all | solution.py:689
  33.6 1.4 collective-permute-start.3
  35.3 1.7 collective-permute-start.5
  37.1 1.7 collective-permute-start.10
  38.8 2.6 collective-permute-start.11
  41.4 3.9 %collective-permute-done.10 = bf16[48,1920]{1,0:T(8,128)(2,1)S(1)} collective-permute-done((bf16[48,1920]{1,0:T(8,128)(2,1)S(1)}, bf16[48,1920]{1,0:T(8,128)(2,1)S(1)}, u32[]{:S(2)}, u32[]{:S(2)}) %collective-permute-start.10) | collective-permute-done | bytes 184352 | tf_op jit(solution)/shard_map/ppermute | solution.py:683
  45.3 1.4 collective-permute-done.3.rest_1_
  46.7 1.6 collective-permute-done.11
  48.3 2.5 collective-permute-start.12
  50.8 8.3 %collective-permute-done.5.rest_3_ = bf16[4,48,1152]{2,1,0:T(8,128)(2,1)} collective-permute-done((bf16[4,48,1152]{2,1,0:T(8,128)(2,1)S(1)}, bf16[4,48,1152]{2,1,0:T(8,128)(2,1)}, u32[]{:S(2)}, u32[]{:S(2)}) %collective-permute-start.5) | collective-permute-done | bytes 442400 | tf_op jit(solution)/shard_map/ppermute | solution.py:683
  59.8 1.6 collective-permute-start.14
  61.4 1.5 collective-permute-start.15
  65.8 9.6 %norm_qkv.1 = (bf16[1024,768]{1,0:T(8,128)(2,1)}, bf16[1024,2304]{1,0:T(8,128)(2,1)}) custom-call(s32[3]{0:T(128)} %pad_add_fusion.ids, bf16[1024,768]{1,0:T(8,128)(2,1)} %bitcast.42, f32[1,768]{1,0:T(1,128)} %broadcast_in_dim.29.g_ref, f32[1,768]{1,0:T(1,128)} %broadcast_in_dim.30.b_ref, f32[1,2304]{1,0:T(1,128)} %broadcast_in_dim.32.qb_ref, ...), custom_call_target="tpu_custom_call" | custom-call | flops 452984832 | bytes 1425408 | tf_op jit(solution)/shard_map/norm_qkv/pallas_call | solution.py:120
  75.4 22.9 %attention.1 = (bf16[1024,768]{1,0:T(8,128)(2,1)}, f32[1024,128]{1,0:T(8,128)}) custom-call(s32[1,8]{1,0:T(1,128)} %dynamic-slice_bitcast_fusion.lens_ref, bf16[1024,2304]{1,0:T(8,128)(2,1)} %get-tuple-element.63.q_ref.k_ref.v_ref, bf16[1024,2304]{1,0:T(8,128)(2,1)} %get-tuple-element.63.q_ref.k_ref.v_ref, bf16[1024,2304]{1,0:T(8,128)(2,1)} %get-tuple-element.63.q_ref.k_ref.v_ref), custom_call_target="tpu_custom_call" | custom-call | flops 241591904 | bytes 786432 | tf_op jit(solution)/shard_map/attention/pallas_call | solution.py:200
  98.3 3.7 %all-to-all-start.2 = ((bf16[4,256,768]{2,1,0:T(8,128)(2,1)}), bf16[4,256,768]{2,1,0:T(8,128)(2,1)S(1)}, u32[]{:S(2)}, u32[]{:S(2)}) async-start(bf16[4,256,768]{2,1,0:T(8,128)(2,1)} %param.17), calls=%async_computation.2 | async-start | bytes 3145728 | tf_op jit(solution)/shard_map/all_to_all | solution.py:689
  105.5 2.0 collective-permute-done.17.rest_5_
  107.7 0.7 copy-done.8
  108.4 0.9 copy-done.9
  109.2 24.4 %mlp.1 = (f32[1024,768]{1,0:T(8,128)}, bf16[1024,768]{1,0:T(8,128)(2,1)}, bf16[1024,3072]{1,0:T(8,128)(2,1)}, bf16[1024,3072]{1,0:T(8,128)(2,1)}, bf16[1024,768]{1,0:T(8,128)(2,1)}) custom-call(s32[3]{0:T(128)} %pad_add_fusion.ids, bf16[1024,768]{1,0:T(8,128)(2,1)} %bitcast.43, bf16[1024,768]{1,0:T(8,128)(2,1)} %get-tuple-element.64.att_ref.o_ref, ...), custom_call_target="tpu_custom_call" | custom-call | flops 1358954496 | bytes 2949120 | tf_op jit(solution)/shard_map/mlp/pallas_call | solution.py:392
  133.7 5.2 %all-to-all-start.1 = ((bf16[4,256,768]{2,1,0:T(8,128)(2,1)}), bf16[4,256,768]{2,1,0:T(8,128)(2,1)S(1)}, u32[]{:S(2)}, u32[]{:S(2)}) async-start(bf16[4,256,768]{2,1,0:T(8,128)(2,1)} %bitcast.51), calls=%async_computation.1 | async-start | bytes 3145728 | tf_op jit(solution)/shard_map/all_to_all | solution.py:689
  138.9 9.5 %down_outer.1 = bf16[2,3072,384]{2,1,0:T(8,128)(2,1)} custom-call(bf16[1024,3072]{1,0:T(8,128)(2,1)} %get-tuple-element.69.a_ref, bf16[1024,768]{1,0:T(8,128)(2,1)} %bitcast.48), custom_call_target="tpu_custom_call" | custom-call | flops 603979776 | bytes 1572864 | tf_op jit(solution)/shard_map/down_outer/pallas_call | solution.py:503
  148.4 22.6 %mlp_back.1 = (bf16[1024,3072]{1,0:T(8,128)(2,1)}, f32[1024,768]{1,0:T(8,128)}, bf16[1024,768]{1,0:T(8,128)(2,1)}, bf16[1024,768]{1,0:T(8,128)(2,1)}, f32[8,768]{1,0:T(8,128)}, /*index=5*/f32[8,3072]{1,0:T(8,128)}) custom-call(s32[3]{0:T(128)} %pad_add_fusion.ids, bf16[1024,768]{1,0:T(8,128)(2,1)} %bitcast.49, f32[1024,768]{1,0:T(8,128)} %get-tuple-element.71.mid_ref, ...), custom_call_target="tpu_custom_call" | custom-call | flops 1358954496 | bytes 2949120 | tf_op jit(solution)/shard_map/mlp_back/pallas_call | solution.py:456
  171.0 14.1 %up_outer.1 = (bf16[768,1920]{1,0:T(8,128)(2,1)}, bf16[768,1920]{1,0:T(8,128)(2,1)}) custom-call(s32[3]{0:T(128)} %pad_add_fusion.ids, bf16[1024,768]{1,0:T(8,128)(2,1)} %get-tuple-element.76.act_ref, bf16[1024,3072]{1,0:T(8,128)(2,1)} %get-tuple-element.77.du_ref, bf16[1024,768]{1,0:T(8,128)(2,1)} %get-tuple-element.64.att_ref.o_ref, ...), custom_call_target="tpu_custom_call" | custom-call | flops 754974720 | bytes 2113536 | tf_op jit(solution)/shard_map/up_outer/pallas_call | solution.py:542
  185.1 5.8 %collective-permute-done.20.theirs = bf16[768,1920]{1,0:T(8,128)(2,1)S(1)} collective-permute-done((bf16[768,1920]{1,0:T(8,128)(2,1)}, bf16[768,1920]{1,0:T(8,128)(2,1)S(1)}, u32[]{:S(2)}, u32[]{:S(2)}) %collective-permute-start.20) | collective-permute-done | bytes 2949152 | tf_op jit(solution)/shard_map/ppermute | solution.py:683
  190.9 1.6 copy-done.10
  192.5 4.8 %up_merge.1 = (bf16[4,48,1920]{2,1,0:T(8,128)(2,1)}, bf16[4,48,1920]{2,1,0:T(8,128)(2,1)}, bf16[4,48,1920]{2,1,0:T(8,128)(2,1)}, bf16[4,48,1920]{2,1,0:T(8,128)(2,1)}) custom-call(s32[3]{0:T(128)} %pad_add_fusion.ids, bf16[768,1920]{1,0:T(8,128)(2,1)} %get-tuple-element.79.mine, bf16[768,1920]{1,0:T(8,128)(2,1)} %copy-done.10), custom_call_target="tpu_custom_call" | custom-call | flops 368640 | bytes 1105920 | tf_op jit(solution)/shard_map/up_merge/pallas_call | solution.py:610
  197.2 1.9 collective-permute-start.21
  199.2 1.5 collective-permute-start.22
  200.7 34.0 %attention_back.1.dqkv_ref = bf16[1024,2304]{1,0:T(8,128)(2,1)} custom-call(s32[1,8]{1,0:T(1,128)} %dynamic-slice_bitcast_fusion.lens_ref, bf16[1024,2304]{1,0:T(8,128)(2,1)} %get-tuple-element.63.q_ref.k_ref.v_ref, bf16[1024,2304]{1,0:T(8,128)(2,1)} %get-tuple-element.63.q_ref.k_ref.v_ref, bf16[1024,2304]{1,0:T(8,128)(2,1)} %get-tuple-element.63.q_ref.k_ref.v_ref, ...), custom_call_target="tpu_custom_call" | custom-call | flops 603979776 | bytes 1572864 | tf_op jit(solution)/shard_map/attention_back/pallas_call | solution.py:304
  234.8 8.5 %collective-permute-done.22.c = bf16[4,48,1920]{2,1,0:T(8,128)(2,1)S(1)} collective-permute-done((bf16[4,48,1920]{2,1,0:T(8,128)(2,1)}, bf16[4,48,1920]{2,1,0:T(8,128)(2,1)S(1)}, u32[]{:S(2)}, u32[]{:S(2)}) %collective-permute-start.22) | collective-permute-done | bytes 737312 | tf_op jit(solution)/shard_map/ppermute | solution.py:683
  243.3 9.5 %qkv_outer.1 = (bf16[768,1152]{1,0:T(8,128)(2,1)}, bf16[768,1152]{1,0:T(8,128)(2,1)}) custom-call(s32[3]{0:T(128)} %pad_add_fusion.ids, bf16[1024,768]{1,0:T(8,128)(2,1)} %get-tuple-element.88.act_ref, bf16[1024,2304]{1,0:T(8,128)(2,1)} %attention_back.1.dqkv_ref), custom_call_target="tpu_custom_call" | custom-call | flops 452984832 | bytes 1228800 | tf_op jit(solution)/shard_map/qkv_outer/pallas_call | solution.py:579
  252.9 3.1 up_add.1
  256.0 7.4 %all-to-all-start.4 = ((bf16[4,48,1920]{2,1,0:T(8,128)(2,1)}), bf16[4,48,1920]{2,1,0:T(8,128)(2,1)S(1)}, u32[]{:S(2)}, u32[]{:S(2)}) async-start(bf16[4,48,1920]{2,1,0:T(8,128)(2,1)} %up_add.1), calls=%async_computation.5 | async-start | bytes 1474560 | tf_op jit(solution)/shard_map/all_to_all | solution.py:736
  263.3 0.9 slice.113
  264.3 12.8 %reduce-scatter.2.cloned.1.call-done = bf16[192,384]{1,0:T(8,128)(2,1)} async-done(((bf16[6144,384]{1,0:T(8,128)(2,1)}), bf16[192,384]{1,0:T(8,128)(2,1)}) %reduce-scatter.2.cloned.1.call-update) | async-done | bytes 147472 | tf_op jit(solution)/shard_map/reduce_scatter | solution.py:750
  277.1 1.6 convert_element_type.31
  278.8 3.5 qkv_merge.1
  282.3 1.4 collective-permute-start.25
  283.7 1.2 collective-permute-start.26
  284.9 0.8 collective-permute-start.27
  285.8 10.8 %input_grad.1 = (bf16[1024,768]{1,0:T(8,128)(2,1)}, f32[8,2304]{1,0:T(8,128)}) custom-call(s32[3]{0:T(128)} %pad_add_fusion.ids, bf16[1024,768]{1,0:T(8,128)(2,1)} %bitcast.44, f32[1024,768]{1,0:T(8,128)} %get-tuple-element.73.dm_ref, f32[1,768]{1,0:T(1,128)} %broadcast_in_dim.29.g_ref, bf16[1024,2304]{1,0:T(8,128)(2,1)} %attention_back.1.dqkv_ref, ...), custom_call_target="tpu_custom_call" | custom-call | flops 452984832 | bytes 1818624 | tf_op jit(solution)/shard_map/input_grad/pallas_call | solution.py:667
  296.6 4.4 %all-to-all-start.3 = ((bf16[4,256,768]{2,1,0:T(8,128)(2,1)}), bf16[4,256,768]{2,1,0:T(8,128)(2,1)}, u32[]{:S(2)}, u32[]{:S(2)}) async-start(bf16[4,256,768]{2,1,0:T(8,128)(2,1)} %bitcast.50), calls=%async_computation.4 | async-start | bytes 3145728 | tf_op jit(solution)/shard_map/all_to_all | solution.py:689
  301.0 0.9 slice_reduce_fusion.4
  302.0 10.6 %collective-permute-done.26.c = bf16[4,48,1152]{2,1,0:T(8,128)(2,1)} collective-permute-done((bf16[4,48,1152]{2,1,0:T(8,128)(2,1)}, bf16[4,48,1152]{2,1,0:T(8,128)(2,1)}, u32[]{:S(2)}, u32[]{:S(2)}) %collective-permute-start.26) | collective-permute-done | bytes 442400 | tf_op jit(solution)/shard_map/ppermute | solution.py:683
  312.7 1.2 collective-permute-done.31
  313.9 7.3 %collective-permute-done.32 = f32[72,128]{1,0:T(8,128)S(1)} collective-permute-done((f32[72,128]{1,0:T(8,128)S(1)}, f32[72,128]{1,0:T(8,128)S(1)}, u32[]{:S(2)}, u32[]{:S(2)}) %collective-permute-start.32) | collective-permute-done | bytes 36896 | tf_op jit(solution)/shard_map/ppermute | solution.py:683
  321.3 1.5 collective-permute-start.33
  322.8 2.3 qkv_add.1
  325.1 1.3 collective-permute-start.28
  326.3 6.1 %collective-permute-start.29 = (bf16[48,1152]{1,0:T(8,128)(2,1)}, bf16[48,1152]{1,0:T(8,128)(2,1)S(1)}, u32[]{:S(2)}, u32[]{:S(2)}) collective-permute-start(bf16[48,1152]{1,0:T(8,128)(2,1)} %get-tuple-element.102), channel_id=1, source_target_pairs={{0,16},{2,18},{4,20},{6,22},{8,24},{10,26},{12,28},{14,30},{16,0},... | collective-permute-start | bytes 331784 | tf_op jit(solution)/shard_map/ppermute | solution.py:683
  333.2 0.7 slice.137
  333.9 0.6 slice.136
  334.5 2.3 collective-permute-done.34
  336.9 3.5 collective-permute-start.35
  340.4 0.7 convert_add_fusion
  341.1 1.2 collective-permute-done.35
  343.6 1.1 copy.42
  344.7 2.7 copy.43
  (140 shorter events, 10.3 us)
Async XLA Ops:
  7.2 58.1 %copy-start = (s32[4,4,8]{2,1,0:T(4,128)S(1)}, s32[4,4,8]{2,1,0:T(4,128)}, u32[]{:S(2)}) copy-start(s32[4,4,8]{2,1,0:T(4,128)} %param.18) | copy-start | bytes 1540
  7.2 6.1 %copy-start.19 = (bf16[48,1152]{1,0:T(8,128)(2,1)S(1)}, bf16[48,1152]{1,0:T(8,128)(2,1)}, u32[]{:S(2)}) copy-start(bf16[48,1152]{1,0:T(8,128)(2,1)} %param.21) | copy-start | bytes 331780
  7.2 102.0 %all-gather.2.cloned.1.call-start = ((), (), s32[]{:S(2)}) async-start(), calls=%async_computation.6 | async-start | bytes 4866048 | tf_op jit(solution)/shard_map/all_gather | solution.py:705
  7.9 29.1 %copy-start.18 = (bf16[48,1536]{1,0:T(8,128)(2,1)S(1)}, bf16[48,1536]{1,0:T(8,128)(2,1)}, u32[]{:S(2)}) copy-start(bf16[48,1536]{1,0:T(8,128)(2,1)} %param.28) | copy-start | bytes 442372
  8.0 29.1 %copy-start.21 = (bf16[48,384]{1,0:T(8,128)(2,1)S(1)}, bf16[48,384]{1,0:T(8,128)(2,1)}, u32[]{:S(2)}) copy-start(bf16[48,384]{1,0:T(8,128)(2,1)} %param.24) | copy-start | bytes 110596
  8.0 25.6 %all-to-all-start = ((bf16[4,256,768]{2,1,0:T(8,128)(2,1)}), bf16[4,256,768]{2,1,0:T(8,128)(2,1)S(1)}, u32[]{:S(2)}, u32[]{:S(2)}) async-start(bf16[4,256,768]{2,1,0:T(8,128)(2,1)} %param.16), calls=%async_computation | async-start | bytes 3145728 | tf_op jit(solution)/shard_map/all_to_all | solution.py:689
  13.3 49.6 %copy-start.23 = (f32[768]{0:T(1024)S(1)}, f32[768]{0:T(1024)}, u32[]{:S(2)}) copy-start(f32[768]{0:T(1024)} %param.19) | copy-start | bytes 9220
  13.3 50.2 %copy-start.29 = (f32[768]{0:T(1024)S(1)}, f32[768]{0:T(1024)}, u32[]{:S(2)}) copy-start(f32[768]{0:T(1024)} %param.23) | copy-start | bytes 9220
  13.3 50.2 %copy-start.30 = (f32[768]{0:T(1024)S(1)}, f32[768]{0:T(1024)}, u32[]{:S(2)}) copy-start(f32[768]{0:T(1024)} %param.22) | copy-start | bytes 9220
  13.3 50.8 %copy-start.24 = (f32[768]{0:T(1024)S(1)}, f32[768]{0:T(1024)}, u32[]{:S(2)}) copy-start(f32[768]{0:T(1024)} %param.20) | copy-start | bytes 9220
  13.3 5.9 %collective-permute-start = (bf16[48,1152]{1,0:T(8,128)(2,1)S(1)}, bf16[48,1152]{1,0:T(8,128)(2,1)S(1)}, u32[]{:S(2)}, u32[]{:S(2)}) collective-permute-start(bf16[48,1152]{1,0:T(8,128)(2,1)S(1)} %copy-done.19), channel_id=1, source_target_pairs={{0,8},{2,10},{4,12},{6,14},{8,0},{10,2},{12,4},{14,6},{16,24},{18,... | collective-permute-start | bytes 331784 | tf_op jit(solution)/shard_map/ppermute | solution.py:683
  14.9 11.4 %collective-permute-start.1 = (bf16[48,1152]{1,0:T(8,128)(2,1)S(1)}, bf16[48,1152]{1,0:T(8,128)(2,1)S(1)}, u32[]{:S(2)}, u32[]{:S(2)}) collective-permute-start(bf16[48,1152]{1,0:T(8,128)(2,1)S(1)} %copy-done.19), channel_id=1, source_target_pairs={{0,16},{2,18},{4,20},{6,22},{8,24},{10,26},{12,28},{14,30},{16,0},... | collective-permute-start | bytes 331784 | tf_op jit(solution)/shard_map/ppermute | solution.py:683
  17.5 8.8 %collective-permute-start.2 = (bf16[48,1152]{1,0:T(8,128)(2,1)S(1)}, bf16[48,1152]{1,0:T(8,128)(2,1)S(1)}, u32[]{:S(2)}, u32[]{:S(2)}) collective-permute-start(bf16[48,1152]{1,0:T(8,128)(2,1)S(1)} %copy-done.19), channel_id=1, source_target_pairs={{0,24},{2,26},{4,28},{6,30},{8,16},{10,18},{12,20},{14,22},{16,8},... | collective-permute-start | bytes 331784 | tf_op jit(solution)/shard_map/ppermute | solution.py:683
  26.4 39.4 %copy-start.5 = (bf16[4,48,1152]{2,1,0:T(8,128)(2,1)}, bf16[4,48,1152]{2,1,0:T(8,128)(2,1)S(1)}, u32[]{:S(2)}) copy-start(bf16[4,48,1152]{2,1,0:T(8,128)(2,1)S(1)} %pad_maximum_fusion.1.rest_0_) | copy-start | bytes 1327108
  33.6 32.2 %copy-start.2 = (bf16[4,256,768]{2,1,0:T(8,128)(2,1)}, bf16[4,256,768]{2,1,0:T(8,128)(2,1)S(1)}, u32[]{:S(2)}) copy-start(bf16[4,256,768]{2,1,0:T(8,128)(2,1)S(1)} %all-to-all-done) | copy-start | bytes 4718596
  33.6 13.1 %collective-permute-start.3 = (bf16[4,48,1152]{2,1,0:T(8,128)(2,1)S(1)}, bf16[4,48,1152]{2,1,0:T(8,128)(2,1)S(1)}, u32[]{:S(2)}, u32[]{:S(2)}) collective-permute-start(bf16[4,48,1152]{2,1,0:T(8,128)(2,1)S(1)} %pad_maximum_fusion.1.rest_0_), channel_id=1, source_target_pairs={{0,2},{2,0},{4,6},{6,4},{8,10},{10,8},{12,14},{14,12},{16,18},{18,... | collective-permute-start | bytes 1327112 | tf_op jit(solution)/shard_map/ppermute | solution.py:683
  35.0 15.8 %collective-permute-start.4 = (bf16[4,48,1152]{2,1,0:T(8,128)(2,1)S(1)}, bf16[4,48,1152]{2,1,0:T(8,128)(2,1)}, u32[]{:S(2)}, u32[]{:S(2)}) collective-permute-start(bf16[4,48,1152]{2,1,0:T(8,128)(2,1)S(1)} %pad_maximum_fusion.1.rest_0_), channel_id=1, source_target_pairs={{0,4},{2,6},{4,0},{6,2},{8,12},{10,14},{12,8},{14,10},{16,20},{18,... | collective-permute-start | bytes 1327112 | tf_op jit(solution)/shard_map/ppermute | solution.py:683
  35.3 23.7 %collective-permute-start.5 = (bf16[4,48,1152]{2,1,0:T(8,128)(2,1)S(1)}, bf16[4,48,1152]{2,1,0:T(8,128)(2,1)}, u32[]{:S(2)}, u32[]{:S(2)}) collective-permute-start(bf16[4,48,1152]{2,1,0:T(8,128)(2,1)S(1)} %pad_maximum_fusion.1.rest_0_), channel_id=1, source_target_pairs={{0,6},{2,4},{4,2},{6,0},{8,14},{10,12},{12,10},{14,8},{16,22},{18,... | collective-permute-start | bytes 1327112 | tf_op jit(solution)/shard_map/ppermute | solution.py:683
  37.1 8.2 %collective-permute-start.10 = (bf16[48,1920]{1,0:T(8,128)(2,1)S(1)}, bf16[48,1920]{1,0:T(8,128)(2,1)S(1)}, u32[]{:S(2)}, u32[]{:S(2)}) collective-permute-start(bf16[48,1920]{1,0:T(8,128)(2,1)S(1)} %pad_maximum_fusion.2), channel_id=1, source_target_pairs={{0,8},{2,10},{4,12},{6,14},{8,0},{10,2},{12,4},{14,6},{16,24},{18,... | collective-permute-start | bytes 552968 | tf_op jit(solution)/shard_map/ppermute | solution.py:683
  38.8 9.4 %collective-permute-start.11 = (bf16[48,1920]{1,0:T(8,128)(2,1)S(1)}, bf16[48,1920]{1,0:T(8,128)(2,1)S(1)}, u32[]{:S(2)}, u32[]{:S(2)}) collective-permute-start(bf16[48,1920]{1,0:T(8,128)(2,1)S(1)} %pad_maximum_fusion.2), channel_id=1, source_target_pairs={{0,16},{2,18},{4,20},{6,22},{8,24},{10,26},{12,28},{14,30},{16,0},... | collective-permute-start | bytes 552968 | tf_op jit(solution)/shard_map/ppermute | solution.py:683
  45.3 14.5 %collective-permute-start.6 = (bf16[4,48,1152]{2,1,0:T(8,128)(2,1)S(1)}, bf16[4,48,1152]{2,1,0:T(8,128)(2,1)S(1)}, u32[]{:S(2)}, u32[]{:S(2)}) collective-permute-start(bf16[4,48,1152]{2,1,0:T(8,128)(2,1)S(1)} %pad_maximum_fusion.1.rest_0_), channel_id=1, source_target_pairs={{0,1},{1,0},{2,3},{3,2},{4,5},{5,4},{6,7},{7,6},{8,9},{9,8},{10,11... | collective-permute-start | bytes 1327112 | tf_op jit(solution)/shard_map/ppermute | solution.py:683
  46.7 14.7 %copy-start.11 = (bf16[4,48,1152]{2,1,0:T(8,128)(2,1)}, bf16[4,48,1152]{2,1,0:T(8,128)(2,1)S(1)}, u32[]{:S(2)}) copy-start(bf16[4,48,1152]{2,1,0:T(8,128)(2,1)S(1)} %collective-permute-done.3.rest_1_) | copy-start | bytes 1327108
  46.7 14.7 %collective-permute-start.7 = (bf16[4,48,1152]{2,1,0:T(8,128)(2,1)S(1)}, bf16[4,48,1152]{2,1,0:T(8,128)(2,1)S(1)}, u32[]{:S(2)}, u32[]{:S(2)}) collective-permute-start(bf16[4,48,1152]{2,1,0:T(8,128)(2,1)S(1)} %collective-permute-done.3.rest_1_), channel_id=1, source_target_pairs={{0,1},{1,0},{2,3},{3,2},{4,5},{5,4},{6,7},{7,6},{8,9},{9,8},{10,11... | collective-permute-start | bytes 1327112 | tf_op jit(solution)/shard_map/ppermute | solution.py:683
  48.3 10.8 %collective-permute-start.12 = (bf16[48,1920]{1,0:T(8,128)(2,1)S(1)}, bf16[48,1920]{1,0:T(8,128)(2,1)S(1)}, u32[]{:S(2)}, u32[]{:S(2)}) collective-permute-start(bf16[48,1920]{1,0:T(8,128)(2,1)S(1)} %pad_maximum_fusion.2), channel_id=1, source_target_pairs={{0,24},{2,26},{4,28},{6,30},{8,16},{10,18},{12,20},{14,22},{16,8},... | collective-permute-start | bytes 552968 | tf_op jit(solution)/shard_map/ppermute | solution.py:683
  50.8 15.0 %collective-permute-start.8 = (bf16[4,48,1152]{2,1,0:T(8,128)(2,1)}, bf16[4,48,1152]{2,1,0:T(8,128)(2,1)}, u32[]{:S(2)}, u32[]{:S(2)}) collective-permute-start(bf16[4,48,1152]{2,1,0:T(8,128)(2,1)} %collective-permute-done.4.rest_2_), channel_id=1, source_target_pairs={{0,1},{1,0},{2,3},{3,2},{4,5},{5,4},{6,7},{7,6},{8,9},{9,8},{10,11... | collective-permute-start | bytes 1327112 | tf_op jit(solution)/shard_map/ppermute | solution.py:683
  59.1 6.7 %collective-permute-start.9 = (bf16[4,48,1152]{2,1,0:T(8,128)(2,1)}, bf16[4,48,1152]{2,1,0:T(8,128)(2,1)}, u32[]{:S(2)}, u32[]{:S(2)}) collective-permute-start(bf16[4,48,1152]{2,1,0:T(8,128)(2,1)} %collective-permute-done.5.rest_3_), channel_id=1, source_target_pairs={{0,1},{1,0},{2,3},{3,2},{4,5},{5,4},{6,7},{7,6},{8,9},{9,8},{10,11... | collective-permute-start | bytes 1327112 | tf_op jit(solution)/shard_map/ppermute | solution.py:683
  59.2 42.8 %copy-start.4 = (bf16[4,48,1920]{2,1,0:T(8,128)(2,1)}, bf16[4,48,1920]{2,1,0:T(8,128)(2,1)S(1)}, u32[]{:S(2)}) copy-start(bf16[4,48,1920]{2,1,0:T(8,128)(2,1)S(1)} %pad_maximum_fusion.rest_0_) | copy-start | bytes 2211844
  59.2 42.9 %collective-permute-start.13 = (bf16[4,48,1920]{2,1,0:T(8,128)(2,1)S(1)}, bf16[4,48,1920]{2,1,0:T(8,128)(2,1)S(1)}, u32[]{:S(2)}, u32[]{:S(2)}) collective-permute-start(bf16[4,48,1920]{2,1,0:T(8,128)(2,1)S(1)} %pad_maximum_fusion.rest_0_), channel_id=1, source_target_pairs={{0,2},{2,0},{4,6},{6,4},{8,10},{10,8},{12,14},{14,12},{16,18},{18,... | collective-permute-start | bytes 2211848 | tf_op jit(solution)/shard_map/ppermute | solution.py:683
  59.8 42.8 %collective-permute-start.14 = (bf16[4,48,1920]{2,1,0:T(8,128)(2,1)S(1)}, bf16[4,48,1920]{2,1,0:T(8,128)(2,1)}, u32[]{:S(2)}, u32[]{:S(2)}) collective-permute-start(bf16[4,48,1920]{2,1,0:T(8,128)(2,1)S(1)} %pad_maximum_fusion.rest_0_), channel_id=1, source_target_pairs={{0,4},{2,6},{4,0},{6,2},{8,12},{10,14},{12,8},{14,10},{16,20},{18,... | collective-permute-start | bytes 2211848 | tf_op jit(solution)/shard_map/ppermute | solution.py:683
  61.4 41.4 %collective-permute-start.15 = (bf16[4,48,1920]{2,1,0:T(8,128)(2,1)S(1)}, bf16[4,48,1920]{2,1,0:T(8,128)(2,1)}, u32[]{:S(2)}, u32[]{:S(2)}) collective-permute-start(bf16[4,48,1920]{2,1,0:T(8,128)(2,1)S(1)} %pad_maximum_fusion.rest_0_), channel_id=1, source_target_pairs={{0,6},{2,4},{4,2},{6,0},{8,14},{10,12},{12,10},{14,8},{16,22},{18,... | collective-permute-start | bytes 2211848 | tf_op jit(solution)/shard_map/ppermute | solution.py:683
  98.3 6.0 %copy-start.27 = (f32[768]{0:T(1024)S(1)}, f32[768]{0:T(1024)}, u32[]{:S(2)}) copy-start(f32[768]{0:T(1024)} %param.27) | copy-start | bytes 9220
  98.3 6.6 %copy-start.28 = (f32[768]{0:T(1024)S(1)}, f32[768]{0:T(1024)}, u32[]{:S(2)}) copy-start(f32[768]{0:T(1024)} %param.31) | copy-start | bytes 9220
  98.3 35.3 %all-to-all-start.2 = ((bf16[4,256,768]{2,1,0:T(8,128)(2,1)}), bf16[4,256,768]{2,1,0:T(8,128)(2,1)S(1)}, u32[]{:S(2)}, u32[]{:S(2)}) async-start(bf16[4,256,768]{2,1,0:T(8,128)(2,1)} %param.17), calls=%async_computation.2 | async-start | bytes 3145728 | tf_op jit(solution)/shard_map/all_to_all | solution.py:689
  102.0 3.4 collective-permute-start.16
  102.1 7.1 %copy-start.6 = (bf16[4,48,1920]{2,1,0:T(8,128)(2,1)}, bf16[4,48,1920]{2,1,0:T(8,128)(2,1)S(1)}, u32[]{:S(2)}) copy-start(bf16[4,48,1920]{2,1,0:T(8,128)(2,1)S(1)} %collective-permute-done.13.rest_1_) | copy-start | bytes 2211844
  102.1 5.3 %collective-permute-start.17 = (bf16[4,48,1920]{2,1,0:T(8,128)(2,1)S(1)}, bf16[4,48,1920]{2,1,0:T(8,128)(2,1)S(1)}, u32[]{:S(2)}, u32[]{:S(2)}) collective-permute-start(bf16[4,48,1920]{2,1,0:T(8,128)(2,1)S(1)} %collective-permute-done.13.rest_1_), channel_id=1, source_target_pairs={{0,1},{1,0},{2,3},{3,2},{4,5},{5,4},{6,7},{7,6},{8,9},{9,8},{10,11... | collective-permute-start | bytes 2211848 | tf_op jit(solution)/shard_map/ppermute | solution.py:683
  102.6 5.1 %collective-permute-start.18 = (bf16[4,48,1920]{2,1,0:T(8,128)(2,1)}, bf16[4,48,1920]{2,1,0:T(8,128)(2,1)S(1)}, u32[]{:S(2)}, u32[]{:S(2)}) collective-permute-start(bf16[4,48,1920]{2,1,0:T(8,128)(2,1)} %collective-permute-done.14.rest_2_), channel_id=1, source_target_pairs={{0,1},{1,0},{2,3},{3,2},{4,5},{5,4},{6,7},{7,6},{8,9},{9,8},{10,11... | collective-permute-start | bytes 2211848 | tf_op jit(solution)/shard_map/ppermute | solution.py:683
  102.8 6.4 %collective-permute-start.19 = (bf16[4,48,1920]{2,1,0:T(8,128)(2,1)}, bf16[4,48,1920]{2,1,0:T(8,128)(2,1)}, u32[]{:S(2)}, u32[]{:S(2)}) collective-permute-start(bf16[4,48,1920]{2,1,0:T(8,128)(2,1)} %collective-permute-done.15.rest_3_), channel_id=1, source_target_pairs={{0,1},{1,0},{2,3},{3,2},{4,5},{5,4},{6,7},{7,6},{8,9},{9,8},{10,11... | collective-permute-start | bytes 2211848 | tf_op jit(solution)/shard_map/ppermute | solution.py:683
  133.7 37.3 %all-to-all-start.1 = ((bf16[4,256,768]{2,1,0:T(8,128)(2,1)}), bf16[4,256,768]{2,1,0:T(8,128)(2,1)S(1)}, u32[]{:S(2)}, u32[]{:S(2)}) async-start(bf16[4,256,768]{2,1,0:T(8,128)(2,1)} %bitcast.51), calls=%async_computation.1 | async-start | bytes 3145728 | tf_op jit(solution)/shard_map/all_to_all | solution.py:689
  138.9 138.2 %reduce-scatter.2.cloned.1.call-start = ((), (), s32[]{:S(2)}) async-start(), calls=%async_computation.7 | async-start | bytes 4866048 | tf_op jit(solution)/shard_map/reduce_scatter | solution.py:750
  185.1 5.9 %collective-permute-start.20 = (bf16[768,1920]{1,0:T(8,128)(2,1)}, bf16[768,1920]{1,0:T(8,128)(2,1)S(1)}, u32[]{:S(2)}, u32[]{:S(2)}) collective-permute-start(bf16[768,1920]{1,0:T(8,128)(2,1)} %get-tuple-element.80), channel_id=1, source_target_pairs={{0,1},{1,0},{2,3},{3,2},{4,5},{5,4},{6,7},{7,6},{8,9},{9,8},{10,11... | collective-permute-start | bytes 8847368 | tf_op jit(solution)/shard_map/ppermute | solution.py:683
  197.2 37.5 %collective-permute-start.21 = (bf16[4,48,1920]{2,1,0:T(8,128)(2,1)}, bf16[4,48,1920]{2,1,0:T(8,128)(2,1)S(1)}, u32[]{:S(2)}, u32[]{:S(2)}) collective-permute-start(bf16[4,48,1920]{2,1,0:T(8,128)(2,1)} %get-tuple-element.82), channel_id=1, source_target_pairs={{0,2},{2,0},{4,6},{6,4},{8,10},{10,8},{12,14},{14,12},{16,18},{18,... | collective-permute-start | bytes 2211848 | tf_op jit(solution)/shard_map/ppermute | solution.py:683
  199.2 44.1 %collective-permute-start.22 = (bf16[4,48,1920]{2,1,0:T(8,128)(2,1)}, bf16[4,48,1920]{2,1,0:T(8,128)(2,1)S(1)}, u32[]{:S(2)}, u32[]{:S(2)}) collective-permute-start(bf16[4,48,1920]{2,1,0:T(8,128)(2,1)} %get-tuple-element.83), channel_id=1, source_target_pairs={{0,4},{2,6},{4,0},{6,2},{8,12},{10,14},{12,8},{14,10},{16,20},{18,... | collective-permute-start | bytes 2211848 | tf_op jit(solution)/shard_map/ppermute | solution.py:683
  200.6 42.7 %collective-permute-start.23 = (bf16[4,48,1920]{2,1,0:T(8,128)(2,1)}, bf16[4,48,1920]{2,1,0:T(8,128)(2,1)S(1)}, u32[]{:S(2)}, u32[]{:S(2)}) collective-permute-start(bf16[4,48,1920]{2,1,0:T(8,128)(2,1)} %get-tuple-element.84), channel_id=1, source_target_pairs={{0,6},{2,4},{4,2},{6,0},{8,14},{10,12},{12,10},{14,8},{16,22},{18,... | collective-permute-start | bytes 2211848 | tf_op jit(solution)/shard_map/ppermute | solution.py:683
  234.8 18.0 %copy-start.14 = (bf16[4,48,1920]{2,1,0:T(8,128)(2,1)}, bf16[4,48,1920]{2,1,0:T(8,128)(2,1)S(1)}, u32[]{:S(2)}) copy-start(bf16[4,48,1920]{2,1,0:T(8,128)(2,1)S(1)} %collective-permute-done.21.b) | copy-start | bytes 2211844
  243.3 9.5 %copy-start.15 = (bf16[4,48,1920]{2,1,0:T(8,128)(2,1)}, bf16[4,48,1920]{2,1,0:T(8,128)(2,1)S(1)}, u32[]{:S(2)}) copy-start(bf16[4,48,1920]{2,1,0:T(8,128)(2,1)S(1)} %collective-permute-done.22.c) | copy-start | bytes 2211844
  243.3 9.5 %copy-start.16 = (bf16[4,48,1920]{2,1,0:T(8,128)(2,1)}, bf16[4,48,1920]{2,1,0:T(8,128)(2,1)S(1)}, u32[]{:S(2)}) copy-start(bf16[4,48,1920]{2,1,0:T(8,128)(2,1)S(1)} %collective-permute-done.23.d) | copy-start | bytes 2211844
  252.8 25.9 %collective-permute-start.24 = (bf16[768,1152]{1,0:T(8,128)(2,1)}, bf16[768,1152]{1,0:T(8,128)(2,1)}, u32[]{:S(2)}, u32[]{:S(2)}) collective-permute-start(bf16[768,1152]{1,0:T(8,128)(2,1)} %get-tuple-element.90), channel_id=1, source_target_pairs={{0,1},{1,0},{2,3},{3,2},{4,5},{5,4},{6,7},{7,6},{8,9},{9,8},{10,11... | collective-permute-start | bytes 5308424 | tf_op jit(solution)/shard_map/ppermute | solution.py:683
  252.9 11.3 %copy-start.22 = (f32[8,768]{1,0:T(8,128)S(1)}, f32[8,768]{1,0:T(8,128)}, u32[]{:S(2)}) copy-start(f32[8,768]{1,0:T(8,128)} %get-tuple-element.105) | copy-start | bytes 73732
  256.0 40.7 %all-to-all-start.4 = ((bf16[4,48,1920]{2,1,0:T(8,128)(2,1)}), bf16[4,48,1920]{2,1,0:T(8,128)(2,1)S(1)}, u32[]{:S(2)}, u32[]{:S(2)}) async-start(bf16[4,48,1920]{2,1,0:T(8,128)(2,1)} %up_add.1), calls=%async_computation.5 | async-start | bytes 1474560 | tf_op jit(solution)/shard_map/all_to_all | solution.py:736
  282.3 19.7 %collective-permute-start.25 = (bf16[4,48,1152]{2,1,0:T(8,128)(2,1)}, bf16[4,48,1152]{2,1,0:T(8,128)(2,1)S(1)}, u32[]{:S(2)}, u32[]{:S(2)}) collective-permute-start(bf16[4,48,1152]{2,1,0:T(8,128)(2,1)} %get-tuple-element.94), channel_id=1, source_target_pairs={{0,2},{2,0},{4,6},{6,4},{8,10},{10,8},{12,14},{14,12},{16,18},{18,... | collective-permute-start | bytes 1327112 | tf_op jit(solution)/shard_map/ppermute | solution.py:683
  283.7 28.9 %collective-permute-start.26 = (bf16[4,48,1152]{2,1,0:T(8,128)(2,1)}, bf16[4,48,1152]{2,1,0:T(8,128)(2,1)}, u32[]{:S(2)}, u32[]{:S(2)}) collective-permute-start(bf16[4,48,1152]{2,1,0:T(8,128)(2,1)} %get-tuple-element.95), channel_id=1, source_target_pairs={{0,4},{2,6},{4,0},{6,2},{8,12},{10,14},{12,8},{14,10},{16,20},{18,... | collective-permute-start | bytes 1327112 | tf_op jit(solution)/shard_map/ppermute | solution.py:683
  284.9 27.7 %collective-permute-start.27 = (bf16[4,48,1152]{2,1,0:T(8,128)(2,1)}, bf16[4,48,1152]{2,1,0:T(8,128)(2,1)}, u32[]{:S(2)}, u32[]{:S(2)}) collective-permute-start(bf16[4,48,1152]{2,1,0:T(8,128)(2,1)} %get-tuple-element.96), channel_id=1, source_target_pairs={{0,6},{2,4},{4,2},{6,0},{8,14},{10,12},{12,10},{14,8},{16,22},{18,... | collective-permute-start | bytes 1327112 | tf_op jit(solution)/shard_map/ppermute | solution.py:683
  296.6 35.8 %all-to-all-start.3 = ((bf16[4,256,768]{2,1,0:T(8,128)(2,1)}), bf16[4,256,768]{2,1,0:T(8,128)(2,1)}, u32[]{:S(2)}, u32[]{:S(2)}) async-start(bf16[4,256,768]{2,1,0:T(8,128)(2,1)} %bitcast.50), calls=%async_computation.4 | async-start | bytes 3145728 | tf_op jit(solution)/shard_map/all_to_all | solution.py:689
  302.0 20.8 %copy-start.17 = (bf16[4,48,1152]{2,1,0:T(8,128)(2,1)}, bf16[4,48,1152]{2,1,0:T(8,128)(2,1)S(1)}, u32[]{:S(2)}) copy-start(bf16[4,48,1152]{2,1,0:T(8,128)(2,1)S(1)} %collective-permute-done.25.b) | copy-start | bytes 1327108
  312.7 1.2 collective-permute-start.31
  313.9 7.4 %collective-permute-start.32 = (f32[72,128]{1,0:T(8,128)S(1)}, f32[72,128]{1,0:T(8,128)S(1)}, u32[]{:S(2)}, u32[]{:S(2)}) collective-permute-start(f32[72,128]{1,0:T(8,128)S(1)} %add.66), channel_id=1, source_target_pairs={{0,2},{2,0},{4,6},{6,4},{8,10},{10,8},{12,14},{14,12},{16,18},{18,... | collective-permute-start | bytes 110600 | tf_op jit(solution)/shard_map/ppermute | solution.py:683
  321.3 11.2 %collective-permute-start.33 = (f32[72,128]{1,0:T(8,128)S(1)}, f32[72,128]{1,0:T(8,128)S(1)}, u32[]{:S(2)}, u32[]{:S(2)}) collective-permute-start(f32[72,128]{1,0:T(8,128)S(1)} %add.67), channel_id=1, source_target_pairs={{0,4},{2,6},{4,0},{6,2},{8,12},{10,14},{12,8},{14,10},{16,20},{18,... | collective-permute-start | bytes 110600 | tf_op jit(solution)/shard_map/ppermute | solution.py:683
  325.1 15.3 %copy-start.20 = (bf16[48,1152]{1,0:T(8,128)(2,1)S(1)}, bf16[48,1152]{1,0:T(8,128)(2,1)}, u32[]{:S(2)}) copy-start(bf16[48,1152]{1,0:T(8,128)(2,1)} %get-tuple-element.100) | copy-start | bytes 331780
  325.1 15.3 %collective-permute-start.28 = (bf16[48,1152]{1,0:T(8,128)(2,1)}, bf16[48,1152]{1,0:T(8,128)(2,1)S(1)}, u32[]{:S(2)}, u32[]{:S(2)}) collective-permute-start(bf16[48,1152]{1,0:T(8,128)(2,1)} %get-tuple-element.101), channel_id=1, source_target_pairs={{0,8},{2,10},{4,12},{6,14},{8,0},{10,2},{12,4},{14,6},{16,24},{18,... | collective-permute-start | bytes 331784 | tf_op jit(solution)/shard_map/ppermute | solution.py:683
  326.3 14.0 %collective-permute-start.29 = (bf16[48,1152]{1,0:T(8,128)(2,1)}, bf16[48,1152]{1,0:T(8,128)(2,1)S(1)}, u32[]{:S(2)}, u32[]{:S(2)}) collective-permute-start(bf16[48,1152]{1,0:T(8,128)(2,1)} %get-tuple-element.102), channel_id=1, source_target_pairs={{0,16},{2,18},{4,20},{6,22},{8,24},{10,26},{12,28},{14,30},{16,0},... | collective-permute-start | bytes 331784 | tf_op jit(solution)/shard_map/ppermute | solution.py:683
  332.4 8.0 %collective-permute-start.30 = (bf16[48,1152]{1,0:T(8,128)(2,1)}, bf16[48,1152]{1,0:T(8,128)(2,1)S(1)}, u32[]{:S(2)}, u32[]{:S(2)}) collective-permute-start(bf16[48,1152]{1,0:T(8,128)(2,1)} %get-tuple-element.103), channel_id=1, source_target_pairs={{0,24},{2,26},{4,28},{6,30},{8,16},{10,18},{12,20},{14,22},{16,8},... | collective-permute-start | bytes 331784 | tf_op jit(solution)/shard_map/ppermute | solution.py:683
  332.4 4.4 %collective-permute-start.34 = (f32[72,128]{1,0:T(8,128)S(1)}, f32[72,128]{1,0:T(8,128)S(1)}, u32[]{:S(2)}, u32[]{:S(2)}) collective-permute-start(f32[72,128]{1,0:T(8,128)S(1)} %add.68), channel_id=1, source_target_pairs={{0,8},{2,10},{4,12},{6,14},{8,0},{10,2},{12,4},{14,6},{16,24},{18,... | collective-permute-start | bytes 110600 | tf_op jit(solution)/shard_map/ppermute | solution.py:683
  336.9 5.4 %collective-permute-start.35 = (f32[72,128]{1,0:T(8,128)S(1)}, f32[72,128]{1,0:T(8,128)S(1)}, u32[]{:S(2)}, u32[]{:S(2)}) collective-permute-start(f32[72,128]{1,0:T(8,128)S(1)} %add.69), channel_id=1, source_target_pairs={{0,16},{2,18},{4,20},{6,22},{8,24},{10,26},{12,28},{14,30},{16,0},... | collective-permute-start | bytes 110600 | tf_op jit(solution)/shard_map/ppermute | solution.py:683
  (10 other events, 27.7 us)
Sparse Core Ops, SparseCore 0:
  10.9 86.1 all-gather.1
  148.5 128.5 reduce-scatter.1

commit v3 on v2

--- a/solution.py
+++ b/solution.py
@@ -18,6 +18,7 @@
 QUAD = 4
 
 EPSILON = 1e-05
+MASKED = -1e9
 TANH_ROOT = 0.7978845608028654
 TANH_CUBIC = 0.044715
 BETA = 1.0 / math.sqrt(DEPTH)
@@ -157,40 +158,45 @@
     return (lane >= h * HD) & (lane < (h + 1) * HD)
 
 
-def attn_kernel(lens_ref, q_ref, k_ref, v_ref, o_ref, l_ref, start_ref):
+WINDOW = 2
+
+
+def mask(lens_ref, keys_at, keys, queries_at, queries):
+    qpos = lax.broadcasted_iota(jnp.int32, (1, queries), 1) + queries_at
+    kpos = lax.broadcasted_iota(jnp.int32, (keys, 1), 0) + keys_at
+    return jnp.where((kpos >= first_of_doc(lens_ref, qpos)) & (kpos <= qpos), 0.0, MASKED)
+
+
+def attn_kernel(lens_ref, q_ref, k_ref, v_ref, o_ref, l_ref, mask_ref):
     pair = pl.program_id(0)
-    n = q_ref.shape[0]
-    nb = n // BLK
+    blocks = []
+    for i in range(q_ref.shape[0] // BLK):
+        low = max(0, i - WINDOW)
+        blocks.append((low * BLK, (i + 1 - low) * BLK, i * BLK))
 
     @pl.when(pair == 0)
     def _():
-        start_ref[...] = first_of_doc(lens_ref, lax.broadcasted_iota(jnp.int32, (n, 1), 0))
         l_ref[...] = jnp.zeros_like(l_ref)
-
-    lane = lax.broadcasted_iota(jnp.int32, (1, 128), 1)
-    for i in range(nb):
-        lo = max(0, i - 2)
-        rows = pl.ds(i * BLK, BLK)
-        keys = pl.ds(lo * BLK, (i + 1 - lo) * BLK)
-        width = (i + 1 - lo) * BLK
+        for first, count, at in blocks:
+            mask_ref[0:count, at : at + BLK] = mask(lens_ref, first, count, at, BLK)
+
+    for first, count, at in blocks:
+        rows = slice(at, at + BLK)
         q = q_ref[rows, :] * jnp.asarray(SCALE, BF16)
-        k = k_ref[keys, :]
-        v = v_ref[keys, :]
-        kpos = lax.broadcasted_iota(jnp.int32, (1, width), 1) + lo * BLK
-        qpos = lax.broadcasted_iota(jnp.int32, (BLK, 1), 0) + i * BLK
-        allowed = (kpos >= start_ref[rows, :]) & (kpos <= qpos)
-        outs = []
-        stats = l_ref[rows, :]
+        k = k_ref[first : first + count, :]
+        v = v_ref[first : first + count, :]
+        out = None
         for h in range(2):
-            qh = jnp.where(lane_half(h), q, jnp.zeros_like(q))
-            s = jnp.where(allowed, mm(qh, k, NT), -1e9)
-            m = jnp.max(s, axis=-1, keepdims=True)
+            half = lane_half(h)
+            s = mm(k, jnp.where(half, q, jnp.zeros_like(q)), NT) + mask_ref[0:count, rows]
+            m = jnp.max(s, axis=0, keepdims=True)
             p = jnp.exp(s - m)
-            total = jnp.sum(p, axis=-1, keepdims=True)
-            outs.append(mm(p.astype(BF16), v) / total)
-            stats = jnp.where(lane == 2 * pair + h, m + jnp.log(total), stats)
-        l_ref[rows, :] = stats
-        o_ref[rows, :] = jnp.where(lane_half(0), outs[0], outs[1]).astype(BF16)
+            total = jnp.sum(p, axis=0, keepdims=True)
+            probs = (p * (1.0 / total)).astype(BF16)
+            o = mm(probs, jnp.where(half, v, jnp.zeros_like(v)), TN)
+            out = o if out is None else out + o
+            l_ref[pl.ds(2 * pair + h, 1), rows] = m + jnp.log(total)
+        o_ref[rows, :] = out.astype(BF16)
 
 
 def attention(lens, qkv):
@@ -203,10 +209,10 @@
         in_specs=[pl.BlockSpec(memory_space=pltpu.SMEM), spec(0), spec(1), spec(2)],
         out_specs=[
             pl.BlockSpec((n, 128), lambda p: (0, p)),
-            pl.BlockSpec((n, 128), lambda p: (0, 0)),
+            pl.BlockSpec((16, n), lambda p: (0, 0)),
         ],
-        out_shape=[jax.ShapeDtypeStruct((n, D), BF16), jax.ShapeDtypeStruct((n, 128), F32)],
-        scratch_shapes=[pltpu.VMEM((n, 1), jnp.int32)],
+        out_shape=[jax.ShapeDtypeStruct((n, D), BF16), jax.ShapeDtypeStruct((16, n), F32)],
+        scratch_shapes=[pltpu.VMEM(((WINDOW + 1) * BLK, n), F32)],
         compiler_params=params(),
         cost_estimate=cost(2 * 2 * H * n * n * HD * 0.6, 2 * n * 4 * D, H * n * n * 0.6),
         name="attention",
@@ -214,14 +220,13 @@
 
 
 def attn_back_kernel(
-    lens_ref, q_ref, k_ref, v_ref, o_ref, do_ref, l_ref, out_hbm,
-    start_ref, lt_ref, dk_acc, dv_acc, bufs, sems,
+    lens_ref, q_ref, k_ref, v_ref, o_ref, do_ref, l_ref, out_hbm, mask_ref, dq_acc, bufs, sems
 ):
     pair = pl.program_id(0)
     pairs = pl.num_programs(0)
     n = q_ref.shape[0]
-    nb = n // BLK
     slot = pair % 2
+    blocks = [(at, min((WINDOW + 1) * BLK, n - at)) for at in range(0, n, BLK)]
 
     def copies(p, at):
         return [
@@ -235,8 +240,8 @@
 
     @pl.when(pair == 0)
     def _():
-        start_ref[...] = first_of_doc(lens_ref, lax.broadcasted_iota(jnp.int32, (8, n), 1))
-        lt_ref[...] = l_ref[...].T
+        for at, count in blocks:
+            mask_ref[at : at + BLK, 0:count] = mask(lens_ref, at, BLK, at, count)
 
     @pl.when(pair >= 2)
     def _():
@@ -244,49 +249,31 @@
             c.wait()
 
     prod = (o_ref[...].astype(F32) * do_ref[...].astype(F32)).T
-    for h in range(2):
-        half = lane_half(h)
-        delta = jnp.sum(prod[h * HD : (h + 1) * HD, :], axis=0, keepdims=True)
-        logs = lt_ref[pl.ds(2 * pair + h, 1), :]
-        for i in range(nb):
-            rows = pl.ds(i * BLK, BLK)
-            q = q_ref[rows, :] * jnp.asarray(SCALE, BF16)
-            q = jnp.where(half, q, jnp.zeros_like(q))
-            do = do_ref[rows, :]
-            do = jnp.where(half, do, jnp.zeros_like(do))
-            logs_i = logs[:, i * BLK : (i + 1) * BLK]
-            delta_i = delta[:, i * BLK : (i + 1) * BLK]
-            start_i = start_ref[0:1, i * BLK : (i + 1) * BLK]
-            qpos = lax.broadcasted_iota(jnp.int32, (1, BLK), 1) + i * BLK
-            dq = jnp.zeros((BLK, 128), F32)
-            for j in range(max(0, i - 2), i + 1):
-                keys = pl.ds(j * BLK, BLK)
-                k = k_ref[keys, :]
-                v = v_ref[keys, :]
-                kpos = lax.broadcasted_iota(jnp.int32, (BLK, 1), 0) + j * BLK
-                allowed = kpos >= start_i
-                if i == j:
-                    allowed = allowed & (kpos <= qpos)
-                p = jnp.where(allowed, jnp.exp(mm(k, q, NT) - logs_i), 0.0)
-                dp = mm(v, do, NT)
-                ds = (p * (dp - delta_i)).astype(BF16)
-                dv = mm(p.astype(BF16), do)
-                dk = mm(ds, q)
-                if h == 0 and i == j:
-                    dv_acc[keys, :] = dv
-                    dk_acc[keys, :] = dk
-                else:
-                    dv_acc[keys, :] += dv
-                    dk_acc[keys, :] += dk
-                kh = jnp.where(half, k, jnp.zeros_like(k))
-                dq = dq + mm(ds, kh, TN)
-            dq = (dq * SCALE).astype(BF16)
-            if h == 0:
-                bufs[slot, 0, rows, :] = dq
-            else:
-                bufs[slot, 0, rows, :] = jnp.where(half, dq, bufs[slot, 0, rows, :])
-    bufs[slot, 1] = dk_acc[...].astype(BF16)
-    bufs[slot, 2] = dv_acc[...].astype(BF16)
+    dq_acc[...] = jnp.zeros_like(dq_acc)
+    for at, count in blocks:
+        keys = slice(at, at + BLK)
+        queries = slice(at, at + count)
+        k = k_ref[keys, :]
+        v = v_ref[keys, :]
+        q = q_ref[queries, :] * jnp.asarray(SCALE, BF16)
+        do = do_ref[queries, :]
+        dk = dv = None
+        for h in range(2):
+            half = lane_half(h)
+            inner = jnp.sum(prod[h * HD : (h + 1) * HD, queries], axis=0, keepdims=True)
+            logs = l_ref[pl.ds(2 * pair + h, 1), queries]
+            qh = jnp.where(half, q, jnp.zeros_like(q))
+            doh = jnp.where(half, do, jnp.zeros_like(do))
+            kh = jnp.where(half, k, jnp.zeros_like(k))
+            p = jnp.exp(mm(k, qh, NT) + (mask_ref[keys, 0:count] - logs))
+            ds = (p * (mm(v, doh, NT) - inner)).astype(BF16)
+            dvh = mm(p.astype(BF16), doh)
+            dkh = mm(ds, qh)
+            dv, dk = (dvh, dkh) if h == 0 else (dv + dvh, dk + dkh)
+            dq_acc[queries, :] += mm(ds, kh, TN)
+        bufs[slot, 1, keys, :] = dk.astype(BF16)
+        bufs[slot, 2, keys, :] = dv.astype(BF16)
+    bufs[slot, 0] = (dq_acc[...] * SCALE).astype(BF16)
     for c in copies(pair, slot):
         c.start()
 
@@ -306,14 +293,12 @@
         grid=(pairs,),
         in_specs=[
             pl.BlockSpec(memory_space=pltpu.SMEM), spec(0), spec(1), spec(2), one, one,
-            pl.BlockSpec((n, 128), lambda p: (0, 0)),
+            pl.BlockSpec((16, n), lambda p: (0, 0)),
         ],
         out_specs=pl.BlockSpec(memory_space=pl.ANY),
         out_shape=jax.ShapeDtypeStruct((n, 3 * D), BF16),
         scratch_shapes=[
-            pltpu.VMEM((8, n), jnp.int32),
-            pltpu.VMEM((128, n), F32),
-            pltpu.VMEM((n, 128), F32),
+            pltpu.VMEM((n, (WINDOW + 1) * BLK), F32),
             pltpu.VMEM((n, 128), F32),
             pltpu.VMEM((2, 3, n, 128), BF16),
             pltpu.SemaphoreType.DMA((2, 3)),
@@ -487,76 +472,57 @@
         mine[...] = r[:, width:].astype(BF16)
 
 
-def down_outer_kernel(a_ref, c_ref, o_ref, dz):
+def down_outer_kernel(ids, a_ref, c_ref, mine, theirs, dz):
     @pl.when(pl.program_id(0) == 0)
     def _():
         dz[...] = (BETA * c_ref[...].astype(F32)).astype(BF16)
 
-    r = mm(a_ref[...], dz[...], TN).astype(BF16)
-    width = o_ref.shape[2]
-    o_ref[0] = r[:, :width]
-    o_ref[1] = r[:, width:]
-
-
-def down_outer(hidden, c):
+    store_sides(ids[2], mm(a_ref[...], dz[...], TN), mine, theirs)
+
+
+def down_outer(ids, hidden, c):
     n = hidden.shape[0]
+    half = pl.BlockSpec((D, D // 2), lambda i, s: (i, 0))
     return pl.pallas_call(
         down_outer_kernel,
-        grid=(FF // D,),
-        in_specs=[
-            pl.BlockSpec((n, D), lambda i: (0, i)),
-            pl.BlockSpec((n, D), lambda i: (0, 0)),
-        ],
-        out_specs=pl.BlockSpec((2, D, D // 2), lambda i: (0, i, 0)),
-        out_shape=jax.ShapeDtypeStruct((2, FF, D // 2), BF16),
-        scratch_shapes=[pltpu.VMEM((n, D), BF16)],
-        compiler_params=params(),
-        cost_estimate=cost(2 * n * FF * D, 2 * (n * (FF + D) + FF * D)),
-        name="down_outer",
-    )(hidden, c)
-
-
-def up_outer_kernel(ids, act_ref, du_ref, att_ref, dy_ref, mine, theirs):
-    step = pl.program_id(0)
-    r = mm(act_ref[...], du_ref[...], TN).astype(BF16)
-
-    @pl.when(step < 2)
-    def _():
-        theirs[:, pl.ds(pl.multiple_of(step * D, 128), D)] = r
-
-    @pl.when(step >= 2)
-    def _():
-        mine[:, pl.ds(pl.multiple_of((step - 2) * D, 128), D)] = r
-
-    @pl.when(step == 3)
-    def _():
-        tail = slice(FF // 2, (FF + D) // 2)
-        store_sides(ids[2], mm(att_ref[...], dy_ref[...], TN), mine.at[:, tail], theirs.at[:, tail])
-
-
-def up_outer(ids, act, du, attended, dy):
-    n = act.shape[0]
-    width = (FF + D) // 2
-    once = pl.BlockSpec((n, D), lambda i, s: (0, 0))
-    out = pl.BlockSpec((D, width), lambda i, s: (0, 0))
-    return pl.pallas_call(
-        up_outer_kernel,
         grid_spec=pltpu.PrefetchScalarGridSpec(
             num_scalar_prefetch=1,
             grid=(FF // D,),
             in_specs=[
-                once,
-                pl.BlockSpec((n, D), lambda i, s: (0, (i + 2 * (1 - s[2])) % 4)),
-                once,
-                once,
+                pl.BlockSpec((n, D), lambda i, s: (0, i)),
+                pl.BlockSpec((n, D), lambda i, s: (0, 0)),
             ],
-            out_specs=[out, out],
+            out_specs=[half, half],
+            scratch_shapes=[pltpu.VMEM((n, D), BF16)],
         ),
-        out_shape=[jax.ShapeDtypeStruct((D, width), BF16)] * 2,
+        out_shape=[jax.ShapeDtypeStruct((FF, D // 2), BF16)] * 2,
+        compiler_params=params(),
+        cost_estimate=cost(2 * n * FF * D, 2 * (n * (FF + D) + FF * D)),
+        name="down_outer",
+    )(ids, hidden, c)
+
+
+def up_outer_kernel(act_ref, du_ref, att_ref, dy_ref, o_ref):
+    o_ref[0, :, : FF // 4] = mm(act_ref[...], du_ref[:, : FF // 4], TN).astype(BF16)
+    o_ref[0, :, FF // 4 : FF // 2] = mm(act_ref[...], du_ref[:, FF // 4 :], TN).astype(BF16)
+    o_ref[0, :, FF // 2 :] = mm(att_ref[...], dy_ref[...], TN).astype(BF16)
+
+
+def up_outer(act, du, attended, dy):
+    n = act.shape[0]
+    width = (FF + D) // 2
+    once = pl.BlockSpec((n, D), lambda i: (0, 0))
+    half = lambda w: pl.BlockSpec((n, w), lambda i: (0, i))
+    return pl.pallas_call(
+        up_outer_kernel,
+        grid=(2,),
+        in_specs=[once, half(FF // 2), once, half(D // 2)],
+        out_specs=pl.BlockSpec((1, D, width), lambda i: (i, 0, 0)),
+        out_shape=jax.ShapeDtypeStruct((2, D, width), BF16),
         compiler_params=params(),
         cost_estimate=cost(2 * n * D * 2 * width, 2 * (n * (FF + 3 * D) + 2 * D * width)),
         name="up_outer",
-    )(ids, act, du, attended, dy)
+    )(act, du, attended, dy)
 
 
 def qkv_outer_kernel(ids, act_ref, dqkv_ref, mine, theirs):
@@ -792,59 +758,67 @@
         (1, 1, doc_lengths.shape[2]),
     )[0]
 
+    qkv_bias = jnp.concatenate([query_bias, jnp.zeros_like(query_bias), value_bias])[None]
+    first_gain, first_bias = first_gain[None], first_bias[None]
     down_full = gather(down_weight)
     x = quad_swap(tokens).reshape(n, width)
     if by_permutes:
         qkv_line = gather_line(qkv_weight)
         up_weights = jnp.concatenate([up_weight, proj_weight], axis=1)
-        up_line = gather_line(after(up_weights, qkv_line))
-        qkv_pieces = spread(after(qkv_line, x), QUAD_STEPS)
+        up_weights = after(up_weights, qkv_line)
+        qkv_line, x, ids, lens, qkv_bias, first_gain, first_bias = lax.optimization_barrier(
+            (qkv_line, x, ids, lens, qkv_bias, first_gain, first_bias)
+        )
+        up_line = gather_line(up_weights)
+        qkv_pieces = spread(qkv_line, QUAD_STEPS)
         qkv_full = with_partner(qkv_pieces)
         up_pieces = spread(after(up_line, *qkv_pieces), QUAD_STEPS)
-        others = with_partner(up_pieces) + [down_full]
+        others = []
     else:
         qkv_full = [gather(qkv_weight)]
         others = [gather(proj_weight), gather(up_weight), down_full]
-    qkv_bias = jnp.concatenate([query_bias, jnp.zeros_like(query_bias), value_bias])[None]
-    act1, qkv = norm_qkv(ids, x, first_gain[None], first_bias[None], qkv_bias, qkv_full)
+    act1, qkv = norm_qkv(ids, x, first_gain, first_bias, qkv_bias, qkv_full)
     attended, stats = attention(lens, qkv)
-    c = quad_swap(after(out_grad, attended)).reshape(n, width)
+    if by_permutes:
+        up_pieces = list(lax.optimization_barrier((attended, *up_pieces))[1:])
+        others = with_partner(up_pieces) + [down_full]
+    c = quad_swap(after(out_grad, attended, *others)).reshape(n, width)
     middle, out, hidden, slope, act2 = mlp(
         ids, x, attended, proj_bias[None], second_gain[None], second_bias[None],
         up_bias[None], down_bias[None], others,
     )
-    output = quad_swap(out.reshape(row_count, piece_len, width))
-    down_outer_grad = down_outer(hidden, c)
-    down_grad = scatter(down_outer_grad)
-    c = after(c, down_outer_grad)
+    output = quad_swap(after(out, c).reshape(row_count, piece_len, width))
     du, dm, dy, dout, vecs, uvec = mlp_back(ids, c, middle, slope, second_gain[None], others)
-    up_sides = up_outer(ids, after(act2, output), du, attended, dy)
+    up_outer_grad = up_outer(after(act2, output), du, attended, dy)
+    down_sides = down_outer(ids, after(hidden, up_outer_grad), c)
     if by_permutes:
-        up_blocks = merge(ids, up_sides[0], swap(up_sides[1], "row", 1), False, "up_merge")
-        dout = after(dout, *up_blocks)
+        down_blocks = merge(ids, down_sides[0], swap(down_sides[1], "row", 1), False, "down_merge")
+        dout = after(dout, *down_blocks)
     dqkv = attention_back(lens, qkv, attended, dout, stats)
     if by_permutes:
-        up_got = from_peers(up_blocks, QUAD_STEPS)
-        act1 = after(act1, *up_got[1:])
+        up_proj = scatter(up_outer_grad)
+        up_grad, proj_grad = up_proj[:, : FF // 2], up_proj[:, FF // 2 :]
+        down_got = from_peers(down_blocks, QUAD_STEPS)
+        act1 = after(act1, *down_got[1:])
     qkv_sides = qkv_outer(ids, act1, dqkv)
     if by_permutes:
-        up_got[0] = after(up_got[0], *qkv_sides)
-        up_line = add_quad(ids, up_got, False, "up_add")
-        qkv_mine = after(qkv_sides[0], up_line)
-        up_line = line_swap(up_line)
+        down_got[0] = after(down_got[0], *qkv_sides)
+        down_line = add_quad(ids, down_got, False, "down_add")
+        qkv_mine = after(qkv_sides[0], down_line)
+        down_line = line_swap(down_line)
         qkv_blocks = merge(ids, qkv_mine, swap(qkv_sides[1], "row", 1), False, "qkv_merge")
-        dqkv = after(dqkv, down_grad, *qkv_blocks)
+        dqkv = after(dqkv, *qkv_blocks)
         qkv_got = from_peers(qkv_blocks, QUAD_STEPS)
-        qkv_got[0] = after(qkv_got[0], up_line)
+        qkv_got[0] = after(qkv_got[0], down_line)
         qkv_shards = add_quad(ids, qkv_got, True, "qkv_add")
         qkv_grad = total_of(from_peers(qkv_shards, LINE_STEPS))
-        up_proj = total_of([up_line[e] for e in range(groups)])
-        up_grad, proj_grad = up_proj[:, : FF // 2], up_proj[:, FF // 2 :]
+        down_grad = total_of([down_line[e] for e in range(groups)])
     else:
-        up_grad = scatter_sides([t[:, : FF // 2] for t in up_sides], row_index)
-        proj_grad = scatter_sides([t[:, FF // 2 :] for t in up_sides], row_index)
+        down_grad = scatter_sides(down_sides, row_index)
+        up_grad = scatter(up_outer_grad[:, :, : FF // 2])
+        proj_grad = scatter(up_outer_grad[:, :, FF // 2 :])
         qkv_grad = scatter_sides(qkv_sides, row_index)
-    dx, vecs1 = input_grad(ids, x, dm, first_gain[None], dqkv, qkv_full)
+    dx, vecs1 = input_grad(ids, x, dm, first_gain, dqkv, qkv_full)
     tokens_grad = quad_swap(dx.reshape(row_count, piece_len, width))
     packed = jnp.concatenate(
         [

time: 355 us -> 333 us (0.938)
  Pallas kernels: 171 us -> 158 us
  waiting for transfers between devices: 83.8 us -> 75.9 us
    reduce_scatter x1, waiting for transfers between devices: 12.8 us -> 3.59 us  [scatter(): lax.psum_scatter(flat, ('row', 'tok'), scatter_dimension=0, tiled=True)]
    pallas_call x1, Pallas kernels: 34 us -> 25.8 us  [attention_back(): pl.pallas_call(attn_back_kernel, grid=(pairs,), in_specs=[pl.BlockSpec(me...]
    unnamed x72 -> x84, local copies, waits for them, and re-layouts: 7.09 us -> 7.1 us
  transfers between devices with their start and end apart: 43 -> 43, of which waited for: 18 -> 22; matrix products, arithmetic and copies ran while one was open for 3% -> 3% of each run, Pallas kernels for 48% -> 44%
where the time goes in v3:
time: 333 us; the launch traced here: 332 us
  Pallas kernels  158 us (47%)
  waiting for transfers between devices  75.9 us (23%)
  starting transfers between devices  62.4 us (19%)
  local copies, waits for them, and re-layouts  17.8 us (5%)
  between operations  14.6 us (4%)
    ppermute x36, waiting for transfers between devices, swap(): return lax.ppermute(block, axis, [(i, i ^ distance) for i in range(count)])  61.5 us
    ppermute x36, starting transfers between devices, swap(): return lax.ppermute(block, axis, [(i, i ^ distance) for i in range(count)])  38.7 us
    pallas_call x1, Pallas kernels, attention_back(): pl.pallas_call(attn_back_kernel, grid=(pairs,), in_specs=[pl.BlockSpec(me...  25.8 us
    pallas_call x1, Pallas kernels, mlp(): pl.pallas_call(functools.partial(mlp_kernel, len(w)), grid=(n // tile,),...  24.3 us
    pallas_call x1, Pallas kernels, mlp_back(): pl.pallas_call(functools.partial(mlp_back_kernel, len(w)), grid=(n // til...  22.6 us
    pallas_call x1, Pallas kernels, attention(): pl.pallas_call(attn_kernel, grid=(pairs,), in_specs=[pl.BlockSpec(memory_...  19.6 us
    all_to_all x4, starting transfers between devices, quad_swap(): lax.all_to_all(pieces, 'tok', 0, 0, axis_index_groups=groups, tiled=True)  18.5 us
    pallas_call x1, Pallas kernels, up_outer(): pl.pallas_call(up_outer_kernel, grid=(2,), in_specs=[once, half(FF // 2),...  11.7 us
  transfers between devices with their start and end apart: 43, of which 22 were waited for; matrix products, arithmetic and copies ran while one was open for 3% of the time, Pallas kernels for 44%

profile of v3, /device:TPU:0, one launch (start us, length us, event | category | flops | bytes accessed | tf_op | source)
XLA Modules:
  0.0 332.0 jit_solution(16374681718533774780)
XLA Ops:
  8.0 5.3 %all-to-all-start = ((bf16[4,256,768]{2,1,0:T(8,128)(2,1)}), bf16[4,256,768]{2,1,0:T(8,128)(2,1)S(1)}, u32[]{:S(2)}, u32[]{:S(2)}) async-start(bf16[4,256,768]{2,1,0:T(8,128)(2,1)} %param.16), calls=%async_computation | async-start | bytes 3145728 | tf_op jit(solution)/shard_map/all_to_all | solution.py:655
  13.3 1.6 collective-permute-start
  14.9 2.6 collective-permute-start.1
  20.6 5.7 %collective-permute-done.1 = bf16[48,1152]{1,0:T(8,128)(2,1)S(1)} collective-permute-done((bf16[48,1152]{1,0:T(8,128)(2,1)S(1)}, bf16[48,1152]{1,0:T(8,128)(2,1)S(1)}, u32[]{:S(2)}, u32[]{:S(2)}) %collective-permute-start.1) | collective-permute-done | bytes 110624 | tf_op jit(solution)/shard_map/ppermute | solution.py:649
  26.4 7.3 %all-to-all-done = bf16[4,256,768]{2,1,0:T(8,128)(2,1)S(1)} async-done(((bf16[4,256,768]{2,1,0:T(8,128)(2,1)}), bf16[4,256,768]{2,1,0:T(8,128)(2,1)S(1)}, u32[]{:S(2)}, u32[]{:S(2)}) %all-to-all-start) | async-done | bytes 1572896 | tf_op jit(solution)/shard_map/all_to_all | solution.py:655
  33.6 1.4 collective-permute-start.3
  35.1 1.7 collective-permute-start.10
  37.2 1.7 collective-permute-start.5
  38.9 2.6 collective-permute-start.11
  41.5 4.3 %collective-permute-start.12 = (bf16[48,1920]{1,0:T(8,128)(2,1)S(1)}, bf16[48,1920]{1,0:T(8,128)(2,1)S(1)}, u32[]{:S(2)}, u32[]{:S(2)}) collective-permute-start(bf16[48,1920]{1,0:T(8,128)(2,1)S(1)} %pad_maximum_fusion.2), channel_id=1, source_target_pairs={{0,24},{2,26},{4,28},{6,30},{8,16},{10,18},{12,20},{14,22},{16,8},... | collective-permute-start | bytes 552968 | tf_op jit(solution)/shard_map/ppermute | solution.py:649
  45.7 10.0 %collective-permute-done.11 = bf16[48,1920]{1,0:T(8,128)(2,1)S(1)} collective-permute-done((bf16[48,1920]{1,0:T(8,128)(2,1)S(1)}, bf16[48,1920]{1,0:T(8,128)(2,1)S(1)}, u32[]{:S(2)}, u32[]{:S(2)}) %collective-permute-start.11) | collective-permute-done | bytes 184352 | tf_op jit(solution)/shard_map/ppermute | solution.py:649
  57.0 2.0 collective-permute-done.5.rest_3_
  59.7 1.3 collective-permute-start.14
  61.0 1.5 collective-permute-start.15
  63.0 1.3 collective-permute-done.8.rest_6_
  65.8 10.2 %norm_qkv.1 = (bf16[1024,768]{1,0:T(8,128)(2,1)}, bf16[1024,2304]{1,0:T(8,128)(2,1)}) custom-call(s32[3]{0:T(128)} %pad_add_fusion.ids, bf16[1024,768]{1,0:T(8,128)(2,1)} %bitcast.42, f32[1,768]{1,0:T(1,128)} %broadcast_in_dim.30.g_ref, f32[1,768]{1,0:T(1,128)} %broadcast_in_dim.31.b_ref, f32[1,2304]{1,0:T(1,128)} %broadcast_in_dim.29.qb_ref, ...), custom_call_target="tpu_custom_call" | custom-call | flops 452984832 | bytes 1425408 | tf_op jit(solution)/shard_map/norm_qkv/pallas_call | solution.py:121
  76.1 19.6 %attention.1 = (bf16[1024,768]{1,0:T(8,128)(2,1)}, f32[16,1024]{1,0:T(8,128)}) custom-call(s32[1,8]{1,0:T(1,128)} %dynamic-slice_bitcast_fusion.lens_ref, bf16[1024,2304]{1,0:T(8,128)(2,1)} %get-tuple-element.80.q_ref.k_ref.v_ref, bf16[1024,2304]{1,0:T(8,128)(2,1)} %get-tuple-element.80.q_ref.k_ref.v_ref, bf16[1024,2304]{1,0:T(8,128)(2,1)} %get-tuple-element.80.q_ref.k_ref.v_ref), custom_call_target="tpu_custom_call" | custom-call | flops 241591904 | bytes 786432 | tf_op jit(solution)/shard_map/attention/pallas_call | solution.py:206
  95.7 4.2 %collective-permute-done.14.rest_2_ = bf16[4,48,1920]{2,1,0:T(8,128)(2,1)S(1)} collective-permute-done((bf16[4,48,1920]{2,1,0:T(8,128)(2,1)S(1)}, bf16[4,48,1920]{2,1,0:T(8,128)(2,1)S(1)}, u32[]{:S(2)}, u32[]{:S(2)}) %collective-permute-start.14) | collective-permute-done | bytes 737312 | tf_op jit(solution)/shard_map/ppermute | solution.py:649
  99.9 1.1 collective-permute-done.15.rest_3_
  102.1 1.2 collective-permute-done.16.rest_4_
  103.3 2.1 collective-permute-done.17.rest_5_
  105.4 1.0 collective-permute-done.18.rest_6_
  107.3 4.6 %all-to-all-start.1 = ((bf16[4,256,768]{2,1,0:T(8,128)(2,1)}), bf16[4,256,768]{2,1,0:T(8,128)(2,1)S(1)}, u32[]{:S(2)}, u32[]{:S(2)}) async-start(bf16[4,256,768]{2,1,0:T(8,128)(2,1)} %param.17), calls=%async_computation.1 | async-start | bytes 3145728 | tf_op jit(solution)/shard_map/all_to_all | solution.py:655
  114.3 24.3 %mlp.1 = (f32[1024,768]{1,0:T(8,128)}, bf16[1024,768]{1,0:T(8,128)(2,1)}, bf16[1024,3072]{1,0:T(8,128)(2,1)}, bf16[1024,3072]{1,0:T(8,128)(2,1)}, bf16[1024,768]{1,0:T(8,128)(2,1)}) custom-call(s32[3]{0:T(128)} %pad_add_fusion.ids, bf16[1024,768]{1,0:T(8,128)(2,1)} %bitcast.43, bf16[1024,768]{1,0:T(8,128)(2,1)} %get-tuple-element.81.att_ref.o_ref, ...), custom_call_target="tpu_custom_call" | custom-call | flops 1358954496 | bytes 2949120 | tf_op jit(solution)/shard_map/mlp/pallas_call | solution.py:377
  138.7 4.2 %all-to-all-start.2 = ((bf16[4,256,768]{2,1,0:T(8,128)(2,1)}), bf16[4,256,768]{2,1,0:T(8,128)(2,1)S(1)}, u32[]{:S(2)}, u32[]{:S(2)}) async-start(bf16[4,256,768]{2,1,0:T(8,128)(2,1)} %bitcast.51), calls=%async_computation.2 | async-start | bytes 3145728 | tf_op jit(solution)/shard_map/all_to_all | solution.py:655
  142.9 22.6 %mlp_back.1 = (bf16[1024,3072]{1,0:T(8,128)(2,1)}, f32[1024,768]{1,0:T(8,128)}, bf16[1024,768]{1,0:T(8,128)(2,1)}, bf16[1024,768]{1,0:T(8,128)(2,1)}, f32[8,768]{1,0:T(8,128)}, /*index=5*/f32[8,3072]{1,0:T(8,128)}) custom-call(s32[3]{0:T(128)} %pad_add_fusion.ids, bf16[1024,768]{1,0:T(8,128)(2,1)} %bitcast.48, f32[1024,768]{1,0:T(8,128)} %get-tuple-element.91.mid_ref, ...), custom_call_target="tpu_custom_call" | custom-call | flops 1358954496 | bytes 2949120 | tf_op jit(solution)/shard_map/mlp_back/pallas_call | solution.py:441
  165.5 11.7 %up_outer.1 = bf16[2,768,1920]{2,1,0:T(8,128)(2,1)} custom-call(bf16[1024,768]{1,0:T(8,128)(2,1)} %get-tuple-element.97.act_ref, bf16[1024,3072]{1,0:T(8,128)(2,1)} %get-tuple-element.98.du_ref, bf16[1024,768]{1,0:T(8,128)(2,1)} %get-tuple-element.81.att_ref.o_ref, bf16[1024,768]{1,0:T(8,128)(2,1)} %get-tuple-element.99.dy_ref), custom_call_target="tpu_custom_call" | custom-call | flops 754974720 | bytes 2113536 | tf_op jit(solution)/shard_map/up_outer/pallas_call | solution.py:516
  177.2 10.5 %down_outer.1 = (bf16[3072,384]{1,0:T(8,128)(2,1)}, bf16[3072,384]{1,0:T(8,128)(2,1)}) custom-call(s32[3]{0:T(128)} %pad_add_fusion.ids, bf16[1024,3072]{1,0:T(8,128)(2,1)} %get-tuple-element.100.a_ref, bf16[1024,768]{1,0:T(8,128)(2,1)} %bitcast.49), custom_call_target="tpu_custom_call" | custom-call | flops 603979776 | bytes 1572864 | tf_op jit(solution)/shard_map/down_outer/pallas_call | solution.py:486
  187.7 4.8 %collective-permute-done.20.theirs = bf16[3072,384]{1,0:T(8,128)(2,1)S(1)} collective-permute-done((bf16[3072,384]{1,0:T(8,128)(2,1)}, bf16[3072,384]{1,0:T(8,128)(2,1)S(1)}, u32[]{:S(2)}, u32[]{:S(2)}) %collective-permute-start.20) | collective-permute-done | bytes 2359328 | tf_op jit(solution)/shard_map/ppermute | solution.py:649
  192.5 1.4 copy-done.12
  193.9 4.3 %down_merge.1 = (bf16[4,192,384]{2,1,0:T(8,128)(2,1)}, bf16[4,192,384]{2,1,0:T(8,128)(2,1)}, bf16[4,192,384]{2,1,0:T(8,128)(2,1)}, bf16[4,192,384]{2,1,0:T(8,128)(2,1)}) custom-call(s32[3]{0:T(128)} %pad_add_fusion.ids, bf16[3072,384]{1,0:T(8,128)(2,1)} %get-tuple-element.101.mine, bf16[3072,384]{1,0:T(8,128)(2,1)} %copy-done.12), custom_call_target="tpu_custom_call" | custom-call | flops 294912 | bytes 884736 | tf_op jit(solution)/shard_map/down_merge/pallas_call | solution.py:576
  198.2 1.9 collective-permute-start.21
  200.2 1.5 collective-permute-start.22
  201.7 25.8 %attention_back.1.dqkv_ref = bf16[1024,2304]{1,0:T(8,128)(2,1)} custom-call(s32[1,8]{1,0:T(1,128)} %dynamic-slice_bitcast_fusion.lens_ref, bf16[1024,2304]{1,0:T(8,128)(2,1)} %get-tuple-element.80.q_ref.k_ref.v_ref, bf16[1024,2304]{1,0:T(8,128)(2,1)} %get-tuple-element.80.q_ref.k_ref.v_ref, bf16[1024,2304]{1,0:T(8,128)(2,1)} %get-tuple-element.80.q_ref.k_ref.v_ref, ...), custom_call_target="tpu_custom_call" | custom-call | flops 603979776 | bytes 1572864 | tf_op jit(solution)/shard_map/attention_back/pallas_call | solution.py:291
  228.1 9.4 %qkv_outer.1 = (bf16[768,1152]{1,0:T(8,128)(2,1)}, bf16[768,1152]{1,0:T(8,128)(2,1)}) custom-call(s32[3]{0:T(128)} %pad_add_fusion.ids, bf16[1024,768]{1,0:T(8,128)(2,1)} %get-tuple-element.110.act_ref, bf16[1024,2304]{1,0:T(8,128)(2,1)} %attention_back.1.dqkv_ref), custom_call_target="tpu_custom_call" | custom-call | flops 452984832 | bytes 1228800 | tf_op jit(solution)/shard_map/qkv_outer/pallas_call | solution.py:545
  237.6 2.7 down_add.1
  240.3 5.2 %all-to-all-start.4 = ((bf16[4,192,384]{2,1,0:T(8,128)(2,1)}), bf16[4,192,384]{2,1,0:T(8,128)(2,1)S(1)}, u32[]{:S(2)}, u32[]{:S(2)}) async-start(bf16[4,192,384]{2,1,0:T(8,128)(2,1)} %down_add.1), calls=%async_computation.4 | async-start | bytes 1179648 | tf_op jit(solution)/shard_map/all_to_all | solution.py:702
  245.5 0.9 slice.113
  246.5 3.7 %qkv_merge.1 = (bf16[4,48,1152]{2,1,0:T(8,128)(2,1)}, bf16[4,48,1152]{2,1,0:T(8,128)(2,1)}, bf16[4,48,1152]{2,1,0:T(8,128)(2,1)}, bf16[4,48,1152]{2,1,0:T(8,128)(2,1)}) custom-call(s32[3]{0:T(128)} %pad_add_fusion.ids, bf16[768,1152]{1,0:T(8,128)(2,1)} %get-tuple-element.114.mine, bf16[768,1152]{1,0:T(8,128)(2,1)} %collective-permute-done.24.theirs), custom_call_target="tpu_custom_call" | custom-call | flops 221184 | bytes 663552 | tf_op jit(solution)/shard_map/qkv_merge/pallas_call | solution.py:576
  250.2 1.3 collective-permute-start.25
  251.5 1.4 collective-permute-start.26
  253.7 10.8 %input_grad.1 = (bf16[1024,768]{1,0:T(8,128)(2,1)}, f32[8,2304]{1,0:T(8,128)}) custom-call(s32[3]{0:T(128)} %pad_add_fusion.ids, bf16[1024,768]{1,0:T(8,128)(2,1)} %bitcast.44, f32[1024,768]{1,0:T(8,128)} %get-tuple-element.93.dm_ref, f32[1,768]{1,0:T(1,128)} %broadcast_in_dim.30.g_ref, bf16[1024,2304]{1,0:T(8,128)(2,1)} %attention_back.1.dqkv_ref, ...), custom_call_target="tpu_custom_call" | custom-call | flops 452984832 | bytes 1818624 | tf_op jit(solution)/shard_map/input_grad/pallas_call | solution.py:633
  264.5 2.8 all-to-all-done.4
  267.3 4.4 %all-to-all-start.3 = ((bf16[4,256,768]{2,1,0:T(8,128)(2,1)}), bf16[4,256,768]{2,1,0:T(8,128)(2,1)}, u32[]{:S(2)}, u32[]{:S(2)}) async-start(bf16[4,256,768]{2,1,0:T(8,128)(2,1)} %bitcast.50), calls=%async_computation.3 | async-start | bytes 3145728 | tf_op jit(solution)/shard_map/all_to_all | solution.py:655
  271.7 0.9 slice_reduce_fusion.4
  272.7 3.5 %collective-permute-done.27.d = bf16[4,48,1152]{2,1,0:T(8,128)(2,1)} collective-permute-done((bf16[4,48,1152]{2,1,0:T(8,128)(2,1)}, bf16[4,48,1152]{2,1,0:T(8,128)(2,1)}, u32[]{:S(2)}, u32[]{:S(2)}) %collective-permute-start.27) | collective-permute-done | bytes 442400 | tf_op jit(solution)/shard_map/ppermute | solution.py:649
  276.3 1.2 collective-permute-done.31
  277.5 1.5 collective-permute-start.32
  279.0 13.5 %collective-permute-done.32 = f32[72,128]{1,0:T(8,128)S(1)} collective-permute-done((f32[72,128]{1,0:T(8,128)S(1)}, f32[72,128]{1,0:T(8,128)S(1)}, u32[]{:S(2)}, u32[]{:S(2)}) %collective-permute-start.32) | collective-permute-done | bytes 36896 | tf_op jit(solution)/shard_map/ppermute | solution.py:649
  292.5 1.6 collective-permute-start.33
  294.0 2.3 qkv_add.1
  296.3 1.7 collective-permute-start.28
  298.0 2.5 collective-permute-start.29
  300.7 0.9 collective-permute-start.34
  302.4 5.0 %collective-permute-done.34 = f32[72,128]{1,0:T(8,128)S(1)} collective-permute-done((f32[72,128]{1,0:T(8,128)S(1)}, f32[72,128]{1,0:T(8,128)S(1)}, u32[]{:S(2)}, u32[]{:S(2)}) %collective-permute-start.34) | collective-permute-done | bytes 36896 | tf_op jit(solution)/shard_map/ppermute | solution.py:649
  307.4 1.4 collective-permute-start.35
  308.8 1.8 collective-permute-done.29
  310.5 1.6 convert_add_fusion
  312.2 1.3 collective-permute-done.35
  314.7 3.6 %reduce-scatter.2.cloned.1.call-done = bf16[48,1920]{1,0:T(8,128)(2,1)} async-done(((bf16[1536,1920]{1,0:T(8,128)(2,1)}), bf16[48,1920]{1,0:T(8,128)(2,1)}) %reduce-scatter.2.cloned.1.call-update) | async-done | bytes 184336 | tf_op jit(solution)/shard_map/reduce_scatter | solution.py:716
  318.3 1.6 slice.133
  319.9 1.4 slice.132
  321.3 1.1 copy.42
  322.5 2.7 copy.43
  (151 shorter events, 16.4 us)
Async XLA Ops:
  7.2 12.3 %copy-start = (s32[4,4,8]{2,1,0:T(4,128)S(1)}, s32[4,4,8]{2,1,0:T(4,128)}, u32[]{:S(2)}) copy-start(s32[4,4,8]{2,1,0:T(4,128)} %param.18) | copy-start | bytes 1540
  7.2 10.5 %copy-start.36 = (f32[768]{0:T(1024)S(1)}, f32[768]{0:T(1024)}, u32[]{:S(2)}) copy-start(f32[768]{0:T(1024)} %param.22) | copy-start | bytes 9220
  7.2 10.5 %copy-start.35 = (f32[768]{0:T(1024)S(1)}, f32[768]{0:T(1024)}, u32[]{:S(2)}) copy-start(f32[768]{0:T(1024)} %param.23) | copy-start | bytes 9220
  7.2 11.1 %copy-start.29 = (f32[768]{0:T(1024)S(1)}, f32[768]{0:T(1024)}, u32[]{:S(2)}) copy-start(f32[768]{0:T(1024)} %param.19) | copy-start | bytes 9220
  7.2 11.7 %copy-start.30 = (f32[768]{0:T(1024)S(1)}, f32[768]{0:T(1024)}, u32[]{:S(2)}) copy-start(f32[768]{0:T(1024)} %param.20) | copy-start | bytes 9220
  7.3 100.1 %all-gather.2.cloned.1.call-start = ((), (), s32[]{:S(2)}) async-start(), calls=%async_computation.6 | async-start | bytes 4866048 | tf_op jit(solution)/shard_map/all_gather | solution.py:671
  8.0 27.1 %copy-start.25 = (bf16[48,1536]{1,0:T(8,128)(2,1)S(1)}, bf16[48,1536]{1,0:T(8,128)(2,1)}, u32[]{:S(2)}) copy-start(bf16[48,1536]{1,0:T(8,128)(2,1)} %param.28) | copy-start | bytes 442372
  8.0 27.1 %copy-start.27 = (bf16[48,384]{1,0:T(8,128)(2,1)S(1)}, bf16[48,384]{1,0:T(8,128)(2,1)}, u32[]{:S(2)}) copy-start(bf16[48,384]{1,0:T(8,128)(2,1)} %param.24) | copy-start | bytes 110596
  8.0 25.6 %all-to-all-start = ((bf16[4,256,768]{2,1,0:T(8,128)(2,1)}), bf16[4,256,768]{2,1,0:T(8,128)(2,1)S(1)}, u32[]{:S(2)}, u32[]{:S(2)}) async-start(bf16[4,256,768]{2,1,0:T(8,128)(2,1)} %param.16), calls=%async_computation | async-start | bytes 3145728 | tf_op jit(solution)/shard_map/all_to_all | solution.py:655
  13.3 7.3 %collective-permute-start = (bf16[48,1152]{1,0:T(8,128)(2,1)S(1)}, bf16[48,1152]{1,0:T(8,128)(2,1)S(1)}, u32[]{:S(2)}, u32[]{:S(2)}) collective-permute-start(bf16[48,1152]{1,0:T(8,128)(2,1)S(1)} %copy-done.26), channel_id=1, source_target_pairs={{0,8},{2,10},{4,12},{6,14},{8,0},{10,2},{12,4},{14,6},{16,24},{18,... | collective-permute-start | bytes 331784 | tf_op jit(solution)/shard_map/ppermute | solution.py:649
  14.9 11.4 %collective-permute-start.1 = (bf16[48,1152]{1,0:T(8,128)(2,1)S(1)}, bf16[48,1152]{1,0:T(8,128)(2,1)S(1)}, u32[]{:S(2)}, u32[]{:S(2)}) collective-permute-start(bf16[48,1152]{1,0:T(8,128)(2,1)S(1)} %copy-done.26), channel_id=1, source_target_pairs={{0,16},{2,18},{4,20},{6,22},{8,24},{10,26},{12,28},{14,30},{16,0},... | collective-permute-start | bytes 331784 | tf_op jit(solution)/shard_map/ppermute | solution.py:649
  17.5 8.8 %collective-permute-start.2 = (bf16[48,1152]{1,0:T(8,128)(2,1)S(1)}, bf16[48,1152]{1,0:T(8,128)(2,1)S(1)}, u32[]{:S(2)}, u32[]{:S(2)}) collective-permute-start(bf16[48,1152]{1,0:T(8,128)(2,1)S(1)} %copy-done.26), channel_id=1, source_target_pairs={{0,24},{2,26},{4,28},{6,30},{8,16},{10,18},{12,20},{14,22},{16,8},... | collective-permute-start | bytes 331784 | tf_op jit(solution)/shard_map/ppermute | solution.py:649
  26.4 38.6 %copy-start.5 = (bf16[4,48,1152]{2,1,0:T(8,128)(2,1)}, bf16[4,48,1152]{2,1,0:T(8,128)(2,1)S(1)}, u32[]{:S(2)}) copy-start(bf16[4,48,1152]{2,1,0:T(8,128)(2,1)S(1)} %pad_maximum_fusion.1.rest_0_) | copy-start | bytes 1327108
  33.6 31.3 %copy-start.2 = (bf16[4,256,768]{2,1,0:T(8,128)(2,1)}, bf16[4,256,768]{2,1,0:T(8,128)(2,1)S(1)}, u32[]{:S(2)}) copy-start(bf16[4,256,768]{2,1,0:T(8,128)(2,1)S(1)} %all-to-all-done) | copy-start | bytes 4718596
  33.6 22.2 %collective-permute-start.3 = (bf16[4,48,1152]{2,1,0:T(8,128)(2,1)S(1)}, bf16[4,48,1152]{2,1,0:T(8,128)(2,1)S(1)}, u32[]{:S(2)}, u32[]{:S(2)}) collective-permute-start(bf16[4,48,1152]{2,1,0:T(8,128)(2,1)S(1)} %pad_maximum_fusion.1.rest_0_), channel_id=1, source_target_pairs={{0,2},{2,0},{4,6},{6,4},{8,10},{10,8},{12,14},{14,12},{16,18},{18,... | collective-permute-start | bytes 1327112 | tf_op jit(solution)/shard_map/ppermute | solution.py:649
  35.1 6.4 %collective-permute-start.10 = (bf16[48,1920]{1,0:T(8,128)(2,1)S(1)}, bf16[48,1920]{1,0:T(8,128)(2,1)S(1)}, u32[]{:S(2)}, u32[]{:S(2)}) collective-permute-start(bf16[48,1920]{1,0:T(8,128)(2,1)S(1)} %pad_maximum_fusion.2), channel_id=1, source_target_pairs={{0,8},{2,10},{4,12},{6,14},{8,0},{10,2},{12,4},{14,6},{16,24},{18,... | collective-permute-start | bytes 552968 | tf_op jit(solution)/shard_map/ppermute | solution.py:649
  36.8 20.2 %collective-permute-start.4 = (bf16[4,48,1152]{2,1,0:T(8,128)(2,1)S(1)}, bf16[4,48,1152]{2,1,0:T(8,128)(2,1)S(1)}, u32[]{:S(2)}, u32[]{:S(2)}) collective-permute-start(bf16[4,48,1152]{2,1,0:T(8,128)(2,1)S(1)} %pad_maximum_fusion.1.rest_0_), channel_id=1, source_target_pairs={{0,4},{2,6},{4,0},{6,2},{8,12},{10,14},{12,8},{14,10},{16,20},{18,... | collective-permute-start | bytes 1327112 | tf_op jit(solution)/shard_map/ppermute | solution.py:649
  37.2 21.9 %collective-permute-start.5 = (bf16[4,48,1152]{2,1,0:T(8,128)(2,1)S(1)}, bf16[4,48,1152]{2,1,0:T(8,128)(2,1)S(1)}, u32[]{:S(2)}, u32[]{:S(2)}) collective-permute-start(bf16[4,48,1152]{2,1,0:T(8,128)(2,1)S(1)} %pad_maximum_fusion.1.rest_0_), channel_id=1, source_target_pairs={{0,6},{2,4},{4,2},{6,0},{8,14},{10,12},{12,10},{14,8},{16,22},{18,... | collective-permute-start | bytes 1327112 | tf_op jit(solution)/shard_map/ppermute | solution.py:649
  38.9 16.9 %collective-permute-start.11 = (bf16[48,1920]{1,0:T(8,128)(2,1)S(1)}, bf16[48,1920]{1,0:T(8,128)(2,1)S(1)}, u32[]{:S(2)}, u32[]{:S(2)}) collective-permute-start(bf16[48,1920]{1,0:T(8,128)(2,1)S(1)} %pad_maximum_fusion.2), channel_id=1, source_target_pairs={{0,16},{2,18},{4,20},{6,22},{8,24},{10,26},{12,28},{14,30},{16,0},... | collective-permute-start | bytes 552968 | tf_op jit(solution)/shard_map/ppermute | solution.py:649
  41.5 14.8 %collective-permute-start.12 = (bf16[48,1920]{1,0:T(8,128)(2,1)S(1)}, bf16[48,1920]{1,0:T(8,128)(2,1)S(1)}, u32[]{:S(2)}, u32[]{:S(2)}) collective-permute-start(bf16[48,1920]{1,0:T(8,128)(2,1)S(1)} %pad_maximum_fusion.2), channel_id=1, source_target_pairs={{0,24},{2,26},{4,28},{6,30},{8,16},{10,18},{12,20},{14,22},{16,8},... | collective-permute-start | bytes 552968 | tf_op jit(solution)/shard_map/ppermute | solution.py:649
  55.8 6.7 %collective-permute-start.6 = (bf16[4,48,1152]{2,1,0:T(8,128)(2,1)S(1)}, bf16[4,48,1152]{2,1,0:T(8,128)(2,1)S(1)}, u32[]{:S(2)}, u32[]{:S(2)}) collective-permute-start(bf16[4,48,1152]{2,1,0:T(8,128)(2,1)S(1)} %pad_maximum_fusion.1.rest_0_), channel_id=1, source_target_pairs={{0,1},{1,0},{2,3},{3,2},{4,5},{5,4},{6,7},{7,6},{8,9},{9,8},{10,11... | collective-permute-start | bytes 1327112 | tf_op jit(solution)/shard_map/ppermute | solution.py:649
  55.8 9.2 %copy-start.13 = (bf16[4,48,1152]{2,1,0:T(8,128)(2,1)}, bf16[4,48,1152]{2,1,0:T(8,128)(2,1)S(1)}, u32[]{:S(2)}) copy-start(bf16[4,48,1152]{2,1,0:T(8,128)(2,1)S(1)} %collective-permute-done.3.rest_1_) | copy-start | bytes 1327108
  55.8 6.7 %collective-permute-start.7 = (bf16[4,48,1152]{2,1,0:T(8,128)(2,1)S(1)}, bf16[4,48,1152]{2,1,0:T(8,128)(2,1)S(1)}, u32[]{:S(2)}, u32[]{:S(2)}) collective-permute-start(bf16[4,48,1152]{2,1,0:T(8,128)(2,1)S(1)} %collective-permute-done.3.rest_1_), channel_id=1, source_target_pairs={{0,1},{1,0},{2,3},{3,2},{4,5},{5,4},{6,7},{7,6},{8,9},{9,8},{10,11... | collective-permute-start | bytes 1327112 | tf_op jit(solution)/shard_map/ppermute | solution.py:649
  56.4 44.6 %copy-start.4 = (bf16[4,48,1920]{2,1,0:T(8,128)(2,1)}, bf16[4,48,1920]{2,1,0:T(8,128)(2,1)S(1)}, u32[]{:S(2)}) copy-start(bf16[4,48,1920]{2,1,0:T(8,128)(2,1)S(1)} %pad_maximum_fusion.rest_0_) | copy-start | bytes 2211844
  59.0 36.7 %collective-permute-start.13 = (bf16[4,48,1920]{2,1,0:T(8,128)(2,1)S(1)}, bf16[4,48,1920]{2,1,0:T(8,128)(2,1)S(1)}, u32[]{:S(2)}, u32[]{:S(2)}) collective-permute-start(bf16[4,48,1920]{2,1,0:T(8,128)(2,1)S(1)} %pad_maximum_fusion.rest_0_), channel_id=1, source_target_pairs={{0,2},{2,0},{4,6},{6,4},{8,10},{10,8},{12,14},{14,12},{16,18},{18,... | collective-permute-start | bytes 2211848 | tf_op jit(solution)/shard_map/ppermute | solution.py:649
  59.7 40.2 %collective-permute-start.14 = (bf16[4,48,1920]{2,1,0:T(8,128)(2,1)S(1)}, bf16[4,48,1920]{2,1,0:T(8,128)(2,1)S(1)}, u32[]{:S(2)}, u32[]{:S(2)}) collective-permute-start(bf16[4,48,1920]{2,1,0:T(8,128)(2,1)S(1)} %pad_maximum_fusion.rest_0_), channel_id=1, source_target_pairs={{0,4},{2,6},{4,0},{6,2},{8,12},{10,14},{12,8},{14,10},{16,20},{18,... | collective-permute-start | bytes 2211848 | tf_op jit(solution)/shard_map/ppermute | solution.py:649
  61.0 40.1 %collective-permute-start.15 = (bf16[4,48,1920]{2,1,0:T(8,128)(2,1)S(1)}, bf16[4,48,1920]{2,1,0:T(8,128)(2,1)S(1)}, u32[]{:S(2)}, u32[]{:S(2)}) collective-permute-start(bf16[4,48,1920]{2,1,0:T(8,128)(2,1)S(1)} %pad_maximum_fusion.rest_0_), channel_id=1, source_target_pairs={{0,6},{2,4},{4,2},{6,0},{8,14},{10,12},{12,10},{14,8},{16,22},{18,... | collective-permute-start | bytes 2211848 | tf_op jit(solution)/shard_map/ppermute | solution.py:649
  62.5 1.8 collective-permute-start.8
  62.5 2.4 collective-permute-start.9
  95.7 16.3 %copy-start.31 = (f32[768]{0:T(1024)S(1)}, f32[768]{0:T(1024)}, u32[]{:S(2)}) copy-start(f32[768]{0:T(1024)} %param.26) | copy-start | bytes 9220
  95.7 16.9 %copy-start.32 = (f32[768]{0:T(1024)S(1)}, f32[768]{0:T(1024)}, u32[]{:S(2)}) copy-start(f32[768]{0:T(1024)} %param.25) | copy-start | bytes 9220
  95.7 17.4 %copy-start.33 = (f32[768]{0:T(1024)S(1)}, f32[768]{0:T(1024)}, u32[]{:S(2)}) copy-start(f32[768]{0:T(1024)} %param.27) | copy-start | bytes 9220
  95.7 18.0 %copy-start.34 = (f32[768]{0:T(1024)S(1)}, f32[768]{0:T(1024)}, u32[]{:S(2)}) copy-start(f32[768]{0:T(1024)} %param.31) | copy-start | bytes 9220
  95.7 18.6 %copy-start.6 = (bf16[4,48,1920]{2,1,0:T(8,128)(2,1)}, bf16[4,48,1920]{2,1,0:T(8,128)(2,1)S(1)}, u32[]{:S(2)}) copy-start(bf16[4,48,1920]{2,1,0:T(8,128)(2,1)S(1)} %collective-permute-done.13.rest_1_) | copy-start | bytes 2211844
  101.0 2.2 collective-permute-start.16
  101.1 4.3 %collective-permute-start.17 = (bf16[4,48,1920]{2,1,0:T(8,128)(2,1)S(1)}, bf16[4,48,1920]{2,1,0:T(8,128)(2,1)S(1)}, u32[]{:S(2)}, u32[]{:S(2)}) collective-permute-start(bf16[4,48,1920]{2,1,0:T(8,128)(2,1)S(1)} %collective-permute-done.13.rest_1_), channel_id=1, source_target_pairs={{0,1},{1,0},{2,3},{3,2},{4,5},{5,4},{6,7},{7,6},{8,9},{9,8},{10,11... | collective-permute-start | bytes 2211848 | tf_op jit(solution)/shard_map/ppermute | solution.py:649
  101.6 4.9 %collective-permute-start.18 = (bf16[4,48,1920]{2,1,0:T(8,128)(2,1)S(1)}, bf16[4,48,1920]{2,1,0:T(8,128)(2,1)S(1)}, u32[]{:S(2)}, u32[]{:S(2)}) collective-permute-start(bf16[4,48,1920]{2,1,0:T(8,128)(2,1)S(1)} %collective-permute-done.14.rest_2_), channel_id=1, source_target_pairs={{0,1},{1,0},{2,3},{3,2},{4,5},{5,4},{6,7},{7,6},{8,9},{9,8},{10,11... | collective-permute-start | bytes 2211848 | tf_op jit(solution)/shard_map/ppermute | solution.py:649
  101.6 5.7 %collective-permute-start.19 = (bf16[4,48,1920]{2,1,0:T(8,128)(2,1)S(1)}, bf16[4,48,1920]{2,1,0:T(8,128)(2,1)}, u32[]{:S(2)}, u32[]{:S(2)}) collective-permute-start(bf16[4,48,1920]{2,1,0:T(8,128)(2,1)S(1)} %collective-permute-done.15.rest_3_), channel_id=1, source_target_pairs={{0,1},{1,0},{2,3},{3,2},{4,5},{5,4},{6,7},{7,6},{8,9},{9,8},{10,11... | collective-permute-start | bytes 2211848 | tf_op jit(solution)/shard_map/ppermute | solution.py:649
  107.3 31.3 %all-to-all-start.1 = ((bf16[4,256,768]{2,1,0:T(8,128)(2,1)}), bf16[4,256,768]{2,1,0:T(8,128)(2,1)S(1)}, u32[]{:S(2)}, u32[]{:S(2)}) async-start(bf16[4,256,768]{2,1,0:T(8,128)(2,1)} %param.17), calls=%async_computation.1 | async-start | bytes 3145728 | tf_op jit(solution)/shard_map/all_to_all | solution.py:655
  138.7 26.8 %all-to-all-start.2 = ((bf16[4,256,768]{2,1,0:T(8,128)(2,1)}), bf16[4,256,768]{2,1,0:T(8,128)(2,1)S(1)}, u32[]{:S(2)}, u32[]{:S(2)}) async-start(bf16[4,256,768]{2,1,0:T(8,128)(2,1)} %bitcast.51), calls=%async_computation.2 | async-start | bytes 3145728 | tf_op jit(solution)/shard_map/all_to_all | solution.py:655
  142.9 175.4 %reduce-scatter.2.cloned.1.call-start = ((), (), s32[]{:S(2)}) async-start(), calls=%async_computation.7 | async-start | bytes 6082560 | tf_op jit(solution)/shard_map/reduce_scatter | solution.py:716
  187.7 4.8 %collective-permute-start.20 = (bf16[3072,384]{1,0:T(8,128)(2,1)}, bf16[3072,384]{1,0:T(8,128)(2,1)S(1)}, u32[]{:S(2)}, u32[]{:S(2)}) collective-permute-start(bf16[3072,384]{1,0:T(8,128)(2,1)} %get-tuple-element.102), channel_id=1, source_target_pairs={{0,1},{1,0},{2,3},{3,2},{4,5},{5,4},{6,7},{7,6},{8,9},{9,8},{10,11... | collective-permute-start | bytes 7077896 | tf_op jit(solution)/shard_map/ppermute | solution.py:649
  198.2 29.2 %collective-permute-start.21 = (bf16[4,192,384]{2,1,0:T(8,128)(2,1)}, bf16[4,192,384]{2,1,0:T(8,128)(2,1)S(1)}, u32[]{:S(2)}, u32[]{:S(2)}) collective-permute-start(bf16[4,192,384]{2,1,0:T(8,128)(2,1)} %get-tuple-element.104), channel_id=1, source_target_pairs={{0,2},{2,0},{4,6},{6,4},{8,10},{10,8},{12,14},{14,12},{16,18},{18,... | collective-permute-start | bytes 1769480 | tf_op jit(solution)/shard_map/ppermute | solution.py:649
  200.2 27.9 %collective-permute-start.22 = (bf16[4,192,384]{2,1,0:T(8,128)(2,1)}, bf16[4,192,384]{2,1,0:T(8,128)(2,1)S(1)}, u32[]{:S(2)}, u32[]{:S(2)}) collective-permute-start(bf16[4,192,384]{2,1,0:T(8,128)(2,1)} %get-tuple-element.105), channel_id=1, source_target_pairs={{0,4},{2,6},{4,0},{6,2},{8,12},{10,14},{12,8},{14,10},{16,20},{18,... | collective-permute-start | bytes 1769480 | tf_op jit(solution)/shard_map/ppermute | solution.py:649
  201.6 26.5 %collective-permute-start.23 = (bf16[4,192,384]{2,1,0:T(8,128)(2,1)}, bf16[4,192,384]{2,1,0:T(8,128)(2,1)S(1)}, u32[]{:S(2)}, u32[]{:S(2)}) collective-permute-start(bf16[4,192,384]{2,1,0:T(8,128)(2,1)} %get-tuple-element.106), channel_id=1, source_target_pairs={{0,6},{2,4},{4,2},{6,0},{8,14},{10,12},{12,10},{14,8},{16,22},{18,... | collective-permute-start | bytes 1769480 | tf_op jit(solution)/shard_map/ppermute | solution.py:649
  227.5 10.0 %copy-start.20 = (bf16[4,192,384]{2,1,0:T(8,128)(2,1)}, bf16[4,192,384]{2,1,0:T(8,128)(2,1)S(1)}, u32[]{:S(2)}) copy-start(bf16[4,192,384]{2,1,0:T(8,128)(2,1)S(1)} %collective-permute-done.21.b) | copy-start | bytes 1769476
  228.1 9.4 %copy-start.21 = (bf16[4,192,384]{2,1,0:T(8,128)(2,1)}, bf16[4,192,384]{2,1,0:T(8,128)(2,1)S(1)}, u32[]{:S(2)}) copy-start(bf16[4,192,384]{2,1,0:T(8,128)(2,1)S(1)} %collective-permute-done.22.c) | copy-start | bytes 1769476
  228.1 9.4 %copy-start.22 = (bf16[4,192,384]{2,1,0:T(8,128)(2,1)}, bf16[4,192,384]{2,1,0:T(8,128)(2,1)S(1)}, u32[]{:S(2)}) copy-start(bf16[4,192,384]{2,1,0:T(8,128)(2,1)S(1)} %collective-permute-done.23.d) | copy-start | bytes 1769476
  237.5 8.9 %collective-permute-start.24 = (bf16[768,1152]{1,0:T(8,128)(2,1)}, bf16[768,1152]{1,0:T(8,128)(2,1)}, u32[]{:S(2)}, u32[]{:S(2)}) collective-permute-start(bf16[768,1152]{1,0:T(8,128)(2,1)} %get-tuple-element.112), channel_id=1, source_target_pairs={{0,1},{1,0},{2,3},{3,2},{4,5},{5,4},{6,7},{7,6},{8,9},{9,8},{10,11... | collective-permute-start | bytes 5308424 | tf_op jit(solution)/shard_map/ppermute | solution.py:649
  240.3 27.0 %all-to-all-start.4 = ((bf16[4,192,384]{2,1,0:T(8,128)(2,1)}), bf16[4,192,384]{2,1,0:T(8,128)(2,1)S(1)}, u32[]{:S(2)}, u32[]{:S(2)}) async-start(bf16[4,192,384]{2,1,0:T(8,128)(2,1)} %down_add.1), calls=%async_computation.4 | async-start | bytes 1179648 | tf_op jit(solution)/shard_map/all_to_all | solution.py:702
  250.2 22.5 %collective-permute-start.25 = (bf16[4,48,1152]{2,1,0:T(8,128)(2,1)}, bf16[4,48,1152]{2,1,0:T(8,128)(2,1)S(1)}, u32[]{:S(2)}, u32[]{:S(2)}) collective-permute-start(bf16[4,48,1152]{2,1,0:T(8,128)(2,1)} %get-tuple-element.116), channel_id=1, source_target_pairs={{0,2},{2,0},{4,6},{6,4},{8,10},{10,8},{12,14},{14,12},{16,18},{18,... | collective-permute-start | bytes 1327112 | tf_op jit(solution)/shard_map/ppermute | solution.py:649
  251.5 21.2 %collective-permute-start.26 = (bf16[4,48,1152]{2,1,0:T(8,128)(2,1)}, bf16[4,48,1152]{2,1,0:T(8,128)(2,1)S(1)}, u32[]{:S(2)}, u32[]{:S(2)}) collective-permute-start(bf16[4,48,1152]{2,1,0:T(8,128)(2,1)} %get-tuple-element.117), channel_id=1, source_target_pairs={{0,4},{2,6},{4,0},{6,2},{8,12},{10,14},{12,8},{14,10},{16,20},{18,... | collective-permute-start | bytes 1327112 | tf_op jit(solution)/shard_map/ppermute | solution.py:649
  252.9 23.4 %collective-permute-start.27 = (bf16[4,48,1152]{2,1,0:T(8,128)(2,1)}, bf16[4,48,1152]{2,1,0:T(8,128)(2,1)}, u32[]{:S(2)}, u32[]{:S(2)}) collective-permute-start(bf16[4,48,1152]{2,1,0:T(8,128)(2,1)} %get-tuple-element.118), channel_id=1, source_target_pairs={{0,6},{2,4},{4,2},{6,0},{8,14},{10,12},{12,10},{14,8},{16,22},{18,... | collective-permute-start | bytes 1327112 | tf_op jit(solution)/shard_map/ppermute | solution.py:649
  267.3 33.4 %all-to-all-start.3 = ((bf16[4,256,768]{2,1,0:T(8,128)(2,1)}), bf16[4,256,768]{2,1,0:T(8,128)(2,1)}, u32[]{:S(2)}, u32[]{:S(2)}) async-start(bf16[4,256,768]{2,1,0:T(8,128)(2,1)} %bitcast.50), calls=%async_computation.3 | async-start | bytes 3145728 | tf_op jit(solution)/shard_map/all_to_all | solution.py:655
  272.7 21.3 %copy-start.23 = (bf16[4,48,1152]{2,1,0:T(8,128)(2,1)}, bf16[4,48,1152]{2,1,0:T(8,128)(2,1)S(1)}, u32[]{:S(2)}) copy-start(bf16[4,48,1152]{2,1,0:T(8,128)(2,1)S(1)} %collective-permute-done.25.b) | copy-start | bytes 1327108
  272.7 21.3 %copy-start.24 = (bf16[4,48,1152]{2,1,0:T(8,128)(2,1)}, bf16[4,48,1152]{2,1,0:T(8,128)(2,1)S(1)}, u32[]{:S(2)}) copy-start(bf16[4,48,1152]{2,1,0:T(8,128)(2,1)S(1)} %collective-permute-done.26.c) | copy-start | bytes 1327108
  276.3 1.2 collective-permute-start.31
  277.5 15.0 %collective-permute-start.32 = (f32[72,128]{1,0:T(8,128)S(1)}, f32[72,128]{1,0:T(8,128)S(1)}, u32[]{:S(2)}, u32[]{:S(2)}) collective-permute-start(f32[72,128]{1,0:T(8,128)S(1)} %add.66), channel_id=1, source_target_pairs={{0,2},{2,0},{4,6},{6,4},{8,10},{10,8},{12,14},{14,12},{16,18},{18,... | collective-permute-start | bytes 110600 | tf_op jit(solution)/shard_map/ppermute | solution.py:649
  292.5 8.2 %collective-permute-start.33 = (f32[72,128]{1,0:T(8,128)S(1)}, f32[72,128]{1,0:T(8,128)S(1)}, u32[]{:S(2)}, u32[]{:S(2)}) collective-permute-start(f32[72,128]{1,0:T(8,128)S(1)} %add.67), channel_id=1, source_target_pairs={{0,4},{2,6},{4,0},{6,2},{8,12},{10,14},{12,8},{14,10},{16,20},{18,... | collective-permute-start | bytes 110600 | tf_op jit(solution)/shard_map/ppermute | solution.py:649
  296.3 12.5 %collective-permute-start.28 = (bf16[48,1152]{1,0:T(8,128)(2,1)}, bf16[48,1152]{1,0:T(8,128)(2,1)S(1)}, u32[]{:S(2)}, u32[]{:S(2)}) collective-permute-start(bf16[48,1152]{1,0:T(8,128)(2,1)} %get-tuple-element.123), channel_id=1, source_target_pairs={{0,8},{2,10},{4,12},{6,14},{8,0},{10,2},{12,4},{14,6},{16,24},{18,... | collective-permute-start | bytes 331784 | tf_op jit(solution)/shard_map/ppermute | solution.py:649
  298.0 12.5 %collective-permute-start.29 = (bf16[48,1152]{1,0:T(8,128)(2,1)}, bf16[48,1152]{1,0:T(8,128)(2,1)S(1)}, u32[]{:S(2)}, u32[]{:S(2)}) collective-permute-start(bf16[48,1152]{1,0:T(8,128)(2,1)} %get-tuple-element.124), channel_id=1, source_target_pairs={{0,16},{2,18},{4,20},{6,22},{8,24},{10,26},{12,28},{14,30},{16,0},... | collective-permute-start | bytes 331784 | tf_op jit(solution)/shard_map/ppermute | solution.py:649
  300.5 10.0 %collective-permute-start.30 = (bf16[48,1152]{1,0:T(8,128)(2,1)}, bf16[48,1152]{1,0:T(8,128)(2,1)S(1)}, u32[]{:S(2)}, u32[]{:S(2)}) collective-permute-start(bf16[48,1152]{1,0:T(8,128)(2,1)} %get-tuple-element.125), channel_id=1, source_target_pairs={{0,24},{2,26},{4,28},{6,30},{8,16},{10,18},{12,20},{14,22},{16,8},... | collective-permute-start | bytes 331784 | tf_op jit(solution)/shard_map/ppermute | solution.py:649
  300.7 6.7 %collective-permute-start.34 = (f32[72,128]{1,0:T(8,128)S(1)}, f32[72,128]{1,0:T(8,128)S(1)}, u32[]{:S(2)}, u32[]{:S(2)}) collective-permute-start(f32[72,128]{1,0:T(8,128)S(1)} %add.68), channel_id=1, source_target_pairs={{0,8},{2,10},{4,12},{6,14},{8,0},{10,2},{12,4},{14,6},{16,24},{18,... | collective-permute-start | bytes 110600 | tf_op jit(solution)/shard_map/ppermute | solution.py:649
  307.4 6.0 %collective-permute-start.35 = (f32[72,128]{1,0:T(8,128)S(1)}, f32[72,128]{1,0:T(8,128)S(1)}, u32[]{:S(2)}, u32[]{:S(2)}) collective-permute-start(f32[72,128]{1,0:T(8,128)S(1)} %add.69), channel_id=1, source_target_pairs={{0,16},{2,18},{4,20},{6,22},{8,24},{10,26},{12,28},{14,30},{16,0},... | collective-permute-start | bytes 110600 | tf_op jit(solution)/shard_map/ppermute | solution.py:649
  (16 other events, 60.6 us)
Sparse Core Ops, SparseCore 0:
  11.0 88.3 all-gather.1
  177.3 140.9 reduce-scatter.1

commit v4 on v3

--- a/solution.py
+++ b/solution.py
@@ -311,12 +311,22 @@
 
 def start_mlp_weights(ids, w_hbm, wp, wu, wd, sem):
     if len(w_hbm) == 3:
-        place_halves(w_hbm[0], wp, sem.at[0])
-        place_halves(w_hbm[1], wu, sem.at[1])
-    else:
-        up = (0, FF // 2, wu, sem.at[1])
-        place_pieces(ids, w_hbm[:-1], False, [(FF // 2, D // 2, wp, sem.at[0]), up])
-    place_halves(w_hbm[-1], wd, sem.at[2])
+        for i, w in enumerate((wp, wu, wd)):
+            place_halves(w_hbm[i], w, sem.at[i])
+        return
+    packed = w_hbm[-1]
+    _, count, _, lanes = packed.shape
+
+    def body(t, carry):
+        for w, i, at, rows in ((wp, 0, FF // count, D // count), (wd, 2, 0, FF // count)):
+            here = pl.ds(pl.multiple_of(t * rows, 16), rows)
+            for h in range(2):
+                src = packed.at[h, t, pl.ds(at, rows), :]
+                pltpu.make_async_copy(src, w.at[here, pl.ds(h * lanes, lanes)], sem.at[i]).start()
+        return carry
+
+    lax.fori_loop(0, count, body, 0)
+    place_pieces(ids, w_hbm[:-1], False, [(0, FF // 2, wu, sem.at[1])])
 
 
 def mlp_kernel(
@@ -348,13 +358,13 @@
         cols = pl.ds(f * chunk, chunk)
         u = mm(act, wu[:, cols]) + ub_ref[:, cols]
         u2 = u * u
-        half_t = 0.5 * jnp.tanh(u * (TANH_ROOT + (TANH_ROOT * TANH_CUBIC) * u2))
-        gate = 0.5 + half_t
-        hidden = (u * gate).astype(BF16)
+        gate = 0.5 + 0.5 * jnp.tanh(u * (TANH_ROOT + (TANH_ROOT * TANH_CUBIC) * u2))
+        value = u * gate
+        hidden = value.astype(BF16)
         hid_ref[:, cols] = hidden
         branch = branch + mm(hidden, wd[cols, :])
-        slope = gate + u * (0.5 - 2.0 * half_t * half_t) * (
-            TANH_ROOT + (3.0 * TANH_ROOT * TANH_CUBIC) * u2
+        slope = gate + value * (1.0 - gate) * (
+            2.0 * TANH_ROOT + (6.0 * TANH_ROOT * TANH_CUBIC) * u2
         )
         slope_ref[:, cols] = slope.astype(BF16)
     out_ref[...] = (middle + BETA * (branch + db_ref[...])).astype(BF16)
@@ -607,10 +617,10 @@
 
 
 def input_grad_kernel(parts, ids, x_ref, dm_ref, g_ref, dqkv_ref, *rest):
-    w_hbm, (o_ref, vec_ref, w, sem) = rest[:parts], rest[parts:]
-    first = pl.program_id(0) == 0
-
-    @pl.when(first)
+    w_hbm, outs, (vec_ref, w, sem) = rest[:parts], rest[parts:-3], rest[-3:]
+    step = pl.program_id(0)
+
+    @pl.when(step == 0)
     def _():
         place(ids, w_hbm, w, sem)
         vec_ref[...] = jnp.zeros_like(vec_ref)
@@ -619,7 +629,13 @@
     dqkv = dqkv_ref[...]
     da = mm(dqkv, w[...], NT)
     normed, inverse = norm_parts(x_ref[...].astype(F32))
-    o_ref[...] = (dm_ref[...] + norm_back(da, normed, inverse, g_ref[...])).astype(BF16)
+    dx = (dm_ref[...] + norm_back(da, normed, inverse, g_ref[...])).astype(BF16)
+    for d, o in enumerate(outs):
+
+        @pl.when(step == d)
+        def _(o=o):
+            o[...] = dx
+
     vec_ref[0:1, 0:D] += jnp.sum(da * normed, axis=0, keepdims=True)
     vec_ref[1:2, 0:D] += jnp.sum(da, axis=0, keepdims=True)
     vec_ref[2:3, :] += jnp.sum(dqkv.astype(F32), axis=0, keepdims=True)
@@ -627,21 +643,52 @@
 
 def input_grad(ids, x, dm, gain, dqkv, w):
     n = x.shape[0]
-    tile = BLK
-    const = lambda i: (0, 0)
-    row = lambda wide: pl.BlockSpec((tile, wide), lambda i: (i, 0))
+    tile = n // QUAD
+    const = lambda i, s: (0, 0)
+    row = lambda wide: pl.BlockSpec((tile, wide), lambda i, s: (i ^ s[0], 0))
     return pl.pallas_call(
         functools.partial(input_grad_kernel, len(w)),
-        grid=(n // tile,),
-        in_specs=[pl.BlockSpec(memory_space=pltpu.SMEM), row(D), row(D), pl.BlockSpec((1, D), const), row(3 * D)]
-        + [pl.BlockSpec(memory_space=pl.ANY)] * len(w),
-        out_specs=[row(D), pl.BlockSpec((8, 3 * D), const)],
-        out_shape=[jax.ShapeDtypeStruct((n, D), BF16), jax.ShapeDtypeStruct((8, 3 * D), F32)],
-        scratch_shapes=[pltpu.VMEM((D, 3 * D), BF16), pltpu.SemaphoreType.DMA],
+        grid_spec=pltpu.PrefetchScalarGridSpec(
+            num_scalar_prefetch=1,
+            grid=(QUAD,),
+            in_specs=[row(D), row(D), pl.BlockSpec((1, D), const), row(3 * D)]
+            + [pl.BlockSpec(memory_space=pl.ANY)] * len(w),
+            out_specs=[pl.BlockSpec((tile, D), const)] * QUAD + [pl.BlockSpec((8, 3 * D), const)],
+            scratch_shapes=[pltpu.VMEM((D, 3 * D), BF16), pltpu.SemaphoreType.DMA],
+        ),
+        out_shape=[jax.ShapeDtypeStruct((tile, D), BF16)] * QUAD
+        + [jax.ShapeDtypeStruct((8, 3 * D), F32)],
         compiler_params=params(),
         cost_estimate=cost(2 * n * D * 3 * D, 2 * (n * 7 * D + 3 * D * D)),
         name="input_grad",
     )(ids, x, dm, gain, dqkv, *w)
+
+
+def join_kernel(ids, *refs):
+    out = refs[-1]
+    step = pl.program_id(0)
+    for d in range(QUAD):
+
+        @pl.when(step == d)
+        def _(d=d):
+            out[0] = refs[d][...]
+
+
+def join(ids, pieces):
+    tile, width = pieces[0].shape
+    return pl.pallas_call(
+        join_kernel,
+        grid_spec=pltpu.PrefetchScalarGridSpec(
+            num_scalar_prefetch=1,
+            grid=(QUAD,),
+            in_specs=[pl.BlockSpec((tile, width), lambda i, s: (0, 0))] * QUAD,
+            out_specs=pl.BlockSpec((1, tile, width), lambda i, s: (i ^ s[0], 0, 0)),
+        ),
+        out_shape=jax.ShapeDtypeStruct((QUAD, tile, width), BF16),
+        compiler_params=params(),
+        cost_estimate=cost(1000, 4 * QUAD * tile * width),
+        name="join",
+    )(ids, *pieces)
 
 
 def swap(block, axis, distance):
@@ -759,36 +806,40 @@
     )[0]
 
     qkv_bias = jnp.concatenate([query_bias, jnp.zeros_like(query_bias), value_bias])[None]
-    first_gain, first_bias = first_gain[None], first_bias[None]
-    down_full = gather(down_weight)
-    x = quad_swap(tokens).reshape(n, width)
+    vectors = [qkv_bias] + [
+        t[None]
+        for t in (first_gain, first_bias, proj_bias, second_gain, second_bias, up_bias, down_bias)
+    ]
     if by_permutes:
+        packed = jnp.concatenate([down_weight, proj_weight], axis=0)
+        rest = lax.all_gather(packed, ("row", "tok"), axis=0, tiled=True)
+        rest = rest.reshape((2, lax.axis_size("tok")) + packed.shape)
+        x = quad_swap(tokens).reshape(n, width)
         qkv_line = gather_line(qkv_weight)
-        up_weights = jnp.concatenate([up_weight, proj_weight], axis=1)
-        up_weights = after(up_weights, qkv_line)
-        qkv_line, x, ids, lens, qkv_bias, first_gain, first_bias = lax.optimization_barrier(
-            (qkv_line, x, ids, lens, qkv_bias, first_gain, first_bias)
+        up_shard = after(up_weight, qkv_line)
+        qkv_line, x, ids, lens, *vectors = lax.optimization_barrier(
+            (qkv_line, x, ids, lens, *vectors)
         )
-        up_line = gather_line(up_weights)
+        up_line = gather_line(up_shard)
         qkv_pieces = spread(qkv_line, QUAD_STEPS)
         qkv_full = with_partner(qkv_pieces)
         up_pieces = spread(after(up_line, *qkv_pieces), QUAD_STEPS)
-        others = []
     else:
+        x = quad_swap(tokens).reshape(n, width)
         qkv_full = [gather(qkv_weight)]
-        others = [gather(proj_weight), gather(up_weight), down_full]
+        others = [gather(proj_weight), gather(up_weight), gather(down_weight)]
+    qkv_bias, first_gain, first_bias, proj_bias, second_gain, second_bias, up_bias, down_bias = vectors
     act1, qkv = norm_qkv(ids, x, first_gain, first_bias, qkv_bias, qkv_full)
     attended, stats = attention(lens, qkv)
     if by_permutes:
         up_pieces = list(lax.optimization_barrier((attended, *up_pieces))[1:])
-        others = with_partner(up_pieces) + [down_full]
+        others = with_partner(up_pieces) + [rest]
     c = quad_swap(after(out_grad, attended, *others)).reshape(n, width)
     middle, out, hidden, slope, act2 = mlp(
-        ids, x, attended, proj_bias[None], second_gain[None], second_bias[None],
-        up_bias[None], down_bias[None], others,
+        ids, x, attended, proj_bias, second_gain, second_bias, up_bias, down_bias, others
     )
     output = quad_swap(after(out, c).reshape(row_count, piece_len, width))
-    du, dm, dy, dout, vecs, uvec = mlp_back(ids, c, middle, slope, second_gain[None], others)
+    du, dm, dy, dout, vecs, uvec = mlp_back(ids, c, middle, slope, second_gain, others)
     up_outer_grad = up_outer(after(act2, output), du, attended, dy)
     down_sides = down_outer(ids, after(hidden, up_outer_grad), c)
     if by_permutes:
@@ -809,7 +860,6 @@
         qkv_blocks = merge(ids, qkv_mine, swap(qkv_sides[1], "row", 1), False, "qkv_merge")
         dqkv = after(dqkv, *qkv_blocks)
         qkv_got = from_peers(qkv_blocks, QUAD_STEPS)
-        qkv_got[0] = after(qkv_got[0], down_line)
         qkv_shards = add_quad(ids, qkv_got, True, "qkv_add")
         qkv_grad = total_of(from_peers(qkv_shards, LINE_STEPS))
         down_grad = total_of([down_line[e] for e in range(groups)])
@@ -818,8 +868,11 @@
         up_grad = scatter(up_outer_grad[:, :, : FF // 2])
         proj_grad = scatter(up_outer_grad[:, :, FF // 2 :])
         qkv_grad = scatter_sides(qkv_sides, row_index)
-    dx, vecs1 = input_grad(ids, x, dm, first_gain, dqkv, qkv_full)
-    tokens_grad = quad_swap(dx.reshape(row_count, piece_len, width))
+    *dx, vecs1 = input_grad(ids, x, dm, first_gain, dqkv, qkv_full)
+    dx = from_peers(dx, QUAD_STEPS)
+    if by_permutes:
+        dx[0] = after(dx[0], down_line)
+    tokens_grad = join(ids, dx)
     packed = jnp.concatenate(
         [
             vecs1[0, :D], vecs1[1, :D], vecs1[2, :D], vecs1[2, 2 * D :], vecs[2], vecs[0], vecs[1],
@@ -827,8 +880,8 @@
         ]
     ).reshape(-1, 128)
     if by_permutes:
-        packed = all_sum(after(packed, *qkv_got[1:]), (0, 1, 2))
-        total = all_sum(after(packed, tokens_grad), LINE_STEPS[:2]).reshape(-1)
+        packed = all_sum(after(packed, *qkv_shards), (0,) + LINE_STEPS[:2])
+        total = all_sum(after(packed, *dx), QUAD_STEPS[:2]).reshape(-1)
     else:
         total = lax.psum(packed, ("tok", "row")).reshape(-1)
     v = [total[i * D : (i + 1) * D] for i in range(8)]

time: 333 us -> 318 us (0.955)
  waiting for transfers between devices: 75.9 us -> 54.9 us
  Pallas kernels: 158 us -> 163 us
    ppermute x36 -> x39, waiting for transfers between devices: 61.5 us -> 44.7 us  [swap(): return lax.ppermute(block, axis, [(i, i ^ distance) for i in range(count)])]
    ppermute x36 -> x39, starting transfers between devices: 38.7 us -> 46.4 us  [swap(): return lax.ppermute(block, axis, [(i, i ^ distance) for i in range(count)])]
    pallas_call x1 -> x2, Pallas kernels: 10.8 us -> 16.6 us  [the longest x1 12.7 us: input_grad(): pl.pallas_call(functools.partial(input_grad_kernel, len(w)), grid_spec=pl...]
    all_to_all x4 -> x3, starting transfers between devices: 18.5 us -> 13.3 us  [quad_swap(): lax.all_to_all(pieces, 'tok', 0, 0, axis_index_groups=groups, tiled=True)]
    unnamed x84 -> x87, local copies, waits for them, and re-layouts: 7.1 us -> 5.2 us
    all_to_all x4 -> x3, waiting for transfers between devices: 7.26 us -> 6.65 us  [quad_swap(): lax.all_to_all(pieces, 'tok', 0, 0, axis_index_groups=groups, tiled=True)]
  transfers between devices with their start and end apart: 43 -> 45, of which waited for: 22 -> 19; matrix products, arithmetic and copies ran while one was open for 3% -> 3% of each run, Pallas kernels for 44% -> 48%
where the time goes in v4:
time: 318 us; the launch traced here: 317 us
  Pallas kernels  163 us (51%)
  starting transfers between devices  64 us (20%)
  waiting for transfers between devices  54.9 us (17%)
  local copies, waits for them, and re-layouts  15.9 us (5%)
  between operations  14.5 us (5%)
  other arithmetic  4.04 us (1%)
    ppermute x39, starting transfers between devices, swap(): return lax.ppermute(block, axis, [(i, i ^ distance) for i in range(count)])  46.4 us
    ppermute x39, waiting for transfers between devices, swap(): return lax.ppermute(block, axis, [(i, i ^ distance) for i in range(count)])  44.7 us
    pallas_call x1, Pallas kernels, attention_back(): pl.pallas_call(attn_back_kernel, grid=(pairs,), in_specs=[pl.BlockSpec(me...  25.8 us
    pallas_call x1, Pallas kernels, mlp(): pl.pallas_call(functools.partial(mlp_kernel, len(w)), grid=(n // tile,),...  23.5 us
    pallas_call x1, Pallas kernels, mlp_back(): pl.pallas_call(functools.partial(mlp_back_kernel, len(w)), grid=(n // til...  22.4 us
    pallas_call x1, Pallas kernels, attention(): pl.pallas_call(attn_kernel, grid=(pairs,), in_specs=[pl.BlockSpec(memory_...  19.7 us
    all_to_all x3, starting transfers between devices, quad_swap(): lax.all_to_all(pieces, 'tok', 0, 0, axis_index_groups=groups, tiled=True)  13.3 us
    pallas_call x1, Pallas kernels, input_grad(): pl.pallas_call(functools.partial(input_grad_kernel, len(w)), grid_spec=pl...  12.7 us
  transfers between devices with their start and end apart: 45, of which 19 were waited for; matrix products, arithmetic and copies ran while one was open for 3% of the time, Pallas kernels for 48%

profile of v4, /device:TPU:0, one launch (start us, length us, event | category | flops | bytes accessed | tf_op | source)
XLA Modules:
  0.0 316.6 jit_solution(5237061867535035566)
XLA Ops:
  7.3 1.7 pad_maximum_fusion.2
  9.0 5.3 %all-to-all-start = ((bf16[4,256,768]{2,1,0:T(8,128)(2,1)}), bf16[4,256,768]{2,1,0:T(8,128)(2,1)S(1)}, u32[]{:S(2)}, u32[]{:S(2)}) async-start(bf16[4,256,768]{2,1,0:T(8,128)(2,1)} %param.16), calls=%async_computation | async-start | bytes 3145728 | tf_op jit(solution)/shard_map/all_to_all | solution.py:702
  14.3 1.6 collective-permute-start
  15.9 2.6 collective-permute-start.1
  24.0 4.1 %collective-permute-done.1 = bf16[48,1152]{1,0:T(8,128)(2,1)S(1)} collective-permute-done((bf16[48,1152]{1,0:T(8,128)(2,1)S(1)}, bf16[48,1152]{1,0:T(8,128)(2,1)S(1)}, u32[]{:S(2)}, u32[]{:S(2)}) %collective-permute-start.1) | collective-permute-done | bytes 110624 | tf_op jit(solution)/shard_map/ppermute | solution.py:696
  28.2 6.6 %all-to-all-done = bf16[4,256,768]{2,1,0:T(8,128)(2,1)S(1)} async-done(((bf16[4,256,768]{2,1,0:T(8,128)(2,1)}), bf16[4,256,768]{2,1,0:T(8,128)(2,1)S(1)}, u32[]{:S(2)}, u32[]{:S(2)}) %all-to-all-start) | async-done | bytes 1572896 | tf_op jit(solution)/shard_map/all_to_all | solution.py:702
  34.9 1.4 collective-permute-start.3
  36.3 1.7 collective-permute-start.10
  38.0 2.6 collective-permute-start.11
  40.9 1.7 collective-permute-start.5
  43.3 3.3 %collective-permute-start.12 = (bf16[48,1536]{1,0:T(8,128)(2,1)S(1)}, bf16[48,1536]{1,0:T(8,128)(2,1)S(1)}, u32[]{:S(2)}, u32[]{:S(2)}) collective-permute-start(bf16[48,1536]{1,0:T(8,128)(2,1)S(1)} %copy-done.27), channel_id=1, source_target_pairs={{0,24},{2,26},{4,28},{6,30},{8,16},{10,18},{12,20},{14,22},{16,8},... | collective-permute-start | bytes 442376 | tf_op jit(solution)/shard_map/ppermute | solution.py:696
  46.5 3.9 %collective-permute-done.11 = bf16[48,1536]{1,0:T(8,128)(2,1)S(1)} collective-permute-done((bf16[48,1536]{1,0:T(8,128)(2,1)S(1)}, bf16[48,1536]{1,0:T(8,128)(2,1)S(1)}, u32[]{:S(2)}, u32[]{:S(2)}) %collective-permute-start.11) | collective-permute-done | bytes 147488 | tf_op jit(solution)/shard_map/ppermute | solution.py:696
  51.8 12.2 %collective-permute-done.4.rest_2_ = bf16[4,48,1152]{2,1,0:T(8,128)(2,1)S(1)} collective-permute-done((bf16[4,48,1152]{2,1,0:T(8,128)(2,1)S(1)}, bf16[4,48,1152]{2,1,0:T(8,128)(2,1)S(1)}, u32[]{:S(2)}, u32[]{:S(2)}) %collective-permute-start.4) | collective-permute-done | bytes 442400 | tf_op jit(solution)/shard_map/ppermute | solution.py:696
  64.0 1.6 collective-permute-start.13
  66.3 1.3 collective-permute-start.15
  68.1 1.3 collective-permute-done.8.rest_6_
  70.9 9.7 %norm_qkv.1 = (bf16[1024,768]{1,0:T(8,128)(2,1)}, bf16[1024,2304]{1,0:T(8,128)(2,1)}) custom-call(s32[3]{0:T(128)} %pad_add_fusion.ids, bf16[1024,768]{1,0:T(8,128)(2,1)} %bitcast.41, f32[1,768]{1,0:T(1,128)} %broadcast_in_dim.29.g_ref, f32[1,768]{1,0:T(1,128)} %broadcast_in_dim.30.b_ref, f32[1,2304]{1,0:T(1,128)} %broadcast_in_dim.28.qb_ref, ...), custom_call_target="tpu_custom_call" | custom-call | flops 452984832 | bytes 1425408 | tf_op jit(solution)/shard_map/norm_qkv/pallas_call | solution.py:121
  80.7 19.7 %attention.1 = (bf16[1024,768]{1,0:T(8,128)(2,1)}, f32[16,1024]{1,0:T(8,128)}) custom-call(s32[1,8]{1,0:T(1,128)} %dynamic-slice_bitcast_fusion.lens_ref, bf16[1024,2304]{1,0:T(8,128)(2,1)} %get-tuple-element.88.q_ref.k_ref.v_ref, bf16[1024,2304]{1,0:T(8,128)(2,1)} %get-tuple-element.88.q_ref.k_ref.v_ref, bf16[1024,2304]{1,0:T(8,128)(2,1)} %get-tuple-element.88.q_ref.k_ref.v_ref), custom_call_target="tpu_custom_call" | custom-call | flops 241591904 | bytes 786432 | tf_op jit(solution)/shard_map/attention/pallas_call | solution.py:206
  101.5 1.7 collective-permute-done.16.rest_4_
  103.2 1.8 collective-permute-done.17.rest_5_
  105.0 1.1 collective-permute-done.18.rest_6_
  106.1 0.8 copy-done.11
  106.9 3.8 %all-to-all-start.1 = ((bf16[4,256,768]{2,1,0:T(8,128)(2,1)}), bf16[4,256,768]{2,1,0:T(8,128)(2,1)S(1)}, u32[]{:S(2)}, u32[]{:S(2)}) async-start(bf16[4,256,768]{2,1,0:T(8,128)(2,1)} %param.17), calls=%async_computation.1 | async-start | bytes 3145728 | tf_op jit(solution)/shard_map/all_to_all | solution.py:702
  110.6 23.5 %mlp.1 = (f32[1024,768]{1,0:T(8,128)}, bf16[1024,768]{1,0:T(8,128)(2,1)}, bf16[1024,3072]{1,0:T(8,128)(2,1)}, bf16[1024,3072]{1,0:T(8,128)(2,1)}, bf16[1024,768]{1,0:T(8,128)(2,1)}) custom-call(s32[3]{0:T(128)} %pad_add_fusion.ids, bf16[1024,768]{1,0:T(8,128)(2,1)} %bitcast.42, bf16[1024,768]{1,0:T(8,128)(2,1)} %get-tuple-element.89.att_ref.o_ref, ...), custom_call_target="tpu_custom_call" | custom-call | flops 1358954496 | bytes 2949120 | tf_op jit(solution)/shard_map/mlp/pallas_call | solution.py:387
  134.2 4.2 %all-to-all-start.2 = ((bf16[4,256,768]{2,1,0:T(8,128)(2,1)}), bf16[4,256,768]{2,1,0:T(8,128)(2,1)S(1)}, u32[]{:S(2)}, u32[]{:S(2)}) async-start(bf16[4,256,768]{2,1,0:T(8,128)(2,1)} %bitcast.49), calls=%async_computation.2 | async-start | bytes 3145728 | tf_op jit(solution)/shard_map/all_to_all | solution.py:702
  138.4 22.4 %mlp_back.1 = (bf16[1024,3072]{1,0:T(8,128)(2,1)}, f32[1024,768]{1,0:T(8,128)}, bf16[1024,768]{1,0:T(8,128)(2,1)}, bf16[1024,768]{1,0:T(8,128)(2,1)}, f32[8,768]{1,0:T(8,128)}, /*index=5*/f32[8,3072]{1,0:T(8,128)}) custom-call(s32[3]{0:T(128)} %pad_add_fusion.ids, bf16[1024,768]{1,0:T(8,128)(2,1)} %bitcast.47, f32[1024,768]{1,0:T(8,128)} %get-tuple-element.104.mid_ref, ...), custom_call_target="tpu_custom_call" | custom-call | flops 1358954496 | bytes 2949120 | tf_op jit(solution)/shard_map/mlp_back/pallas_call | solution.py:451
  160.8 11.7 %up_outer.1 = bf16[2,768,1920]{2,1,0:T(8,128)(2,1)} custom-call(bf16[1024,768]{1,0:T(8,128)(2,1)} %get-tuple-element.110.act_ref, bf16[1024,3072]{1,0:T(8,128)(2,1)} %get-tuple-element.111.du_ref, bf16[1024,768]{1,0:T(8,128)(2,1)} %get-tuple-element.89.att_ref.o_ref, bf16[1024,768]{1,0:T(8,128)(2,1)} %get-tuple-element.112.dy_ref), custom_call_target="tpu_custom_call" | custom-call | flops 754974720 | bytes 2113536 | tf_op jit(solution)/shard_map/up_outer/pallas_call | solution.py:526
  172.5 10.5 %down_outer.1 = (bf16[3072,384]{1,0:T(8,128)(2,1)}, bf16[3072,384]{1,0:T(8,128)(2,1)}) custom-call(s32[3]{0:T(128)} %pad_add_fusion.ids, bf16[1024,3072]{1,0:T(8,128)(2,1)} %get-tuple-element.113.a_ref, bf16[1024,768]{1,0:T(8,128)(2,1)} %bitcast.48), custom_call_target="tpu_custom_call" | custom-call | flops 603979776 | bytes 1572864 | tf_op jit(solution)/shard_map/down_outer/pallas_call | solution.py:496
  183.1 4.8 %collective-permute-done.20.theirs = bf16[3072,384]{1,0:T(8,128)(2,1)S(1)} collective-permute-done((bf16[3072,384]{1,0:T(8,128)(2,1)}, bf16[3072,384]{1,0:T(8,128)(2,1)S(1)}, u32[]{:S(2)}, u32[]{:S(2)}) %collective-permute-start.20) | collective-permute-done | bytes 2359328 | tf_op jit(solution)/shard_map/ppermute | solution.py:696
  187.9 1.4 copy-done.12
  189.3 4.3 %down_merge.1 = (bf16[4,192,384]{2,1,0:T(8,128)(2,1)}, bf16[4,192,384]{2,1,0:T(8,128)(2,1)}, bf16[4,192,384]{2,1,0:T(8,128)(2,1)}, bf16[4,192,384]{2,1,0:T(8,128)(2,1)}) custom-call(s32[3]{0:T(128)} %pad_add_fusion.ids, bf16[3072,384]{1,0:T(8,128)(2,1)} %get-tuple-element.114.mine, bf16[3072,384]{1,0:T(8,128)(2,1)} %copy-done.12), custom_call_target="tpu_custom_call" | custom-call | flops 294912 | bytes 884736 | tf_op jit(solution)/shard_map/down_merge/pallas_call | solution.py:586
  193.5 2.0 collective-permute-start.21
  195.5 1.5 collective-permute-start.22
  197.0 25.8 %attention_back.1.dqkv_ref = bf16[1024,2304]{1,0:T(8,128)(2,1)} custom-call(s32[1,8]{1,0:T(1,128)} %dynamic-slice_bitcast_fusion.lens_ref, bf16[1024,2304]{1,0:T(8,128)(2,1)} %get-tuple-element.88.q_ref.k_ref.v_ref, bf16[1024,2304]{1,0:T(8,128)(2,1)} %get-tuple-element.88.q_ref.k_ref.v_ref, bf16[1024,2304]{1,0:T(8,128)(2,1)} %get-tuple-element.88.q_ref.k_ref.v_ref, ...), custom_call_target="tpu_custom_call" | custom-call | flops 603979776 | bytes 1572864 | tf_op jit(solution)/shard_map/attention_back/pallas_call | solution.py:291
  223.4 10.2 %qkv_outer.1 = (bf16[768,1152]{1,0:T(8,128)(2,1)}, bf16[768,1152]{1,0:T(8,128)(2,1)}) custom-call(s32[3]{0:T(128)} %pad_add_fusion.ids, bf16[1024,768]{1,0:T(8,128)(2,1)} %get-tuple-element.123.act_ref, bf16[1024,2304]{1,0:T(8,128)(2,1)} %attention_back.1.dqkv_ref), custom_call_target="tpu_custom_call" | custom-call | flops 452984832 | bytes 1228800 | tf_op jit(solution)/shard_map/qkv_outer/pallas_call | solution.py:555
  233.8 0.9 slice.113
  234.7 2.7 down_add.1
  237.5 4.3 %all-to-all-start.3 = ((bf16[4,192,384]{2,1,0:T(8,128)(2,1)}), bf16[4,192,384]{2,1,0:T(8,128)(2,1)S(1)}, u32[]{:S(2)}, u32[]{:S(2)}) async-start(bf16[4,192,384]{2,1,0:T(8,128)(2,1)} %down_add.1), calls=%async_computation.3 | async-start | bytes 1179648 | tf_op jit(solution)/shard_map/all_to_all | solution.py:749
  241.8 3.7 %qkv_merge.1 = (bf16[4,48,1152]{2,1,0:T(8,128)(2,1)}, bf16[4,48,1152]{2,1,0:T(8,128)(2,1)}, bf16[4,48,1152]{2,1,0:T(8,128)(2,1)}, bf16[4,48,1152]{2,1,0:T(8,128)(2,1)}) custom-call(s32[3]{0:T(128)} %pad_add_fusion.ids, bf16[768,1152]{1,0:T(8,128)(2,1)} %get-tuple-element.127.mine, bf16[768,1152]{1,0:T(8,128)(2,1)} %collective-permute-done.24.theirs), custom_call_target="tpu_custom_call" | custom-call | flops 221184 | bytes 663552 | tf_op jit(solution)/shard_map/qkv_merge/pallas_call | solution.py:586
  245.5 1.2 collective-permute-start.28
  246.6 1.4 collective-permute-start.29
  248.0 0.9 collective-permute-start.30
  249.0 12.7 %input_grad.1 = (bf16[256,768]{1,0:T(8,128)(2,1)}, bf16[256,768]{1,0:T(8,128)(2,1)}, bf16[256,768]{1,0:T(8,128)(2,1)}, bf16[256,768]{1,0:T(8,128)(2,1)}, f32[8,2304]{1,0:T(8,128)}) custom-call(s32[3]{0:T(128)} %pad_add_fusion.ids, bf16[1024,768]{1,0:T(8,128)(2,1)} %bitcast.43, f32[1024,768]{1,0:T(8,128)} %get-tuple-element.106.dm_ref, ...), custom_call_target="tpu_custom_call" | custom-call | flops 452984832 | bytes 1818624 | tf_op jit(solution)/shard_map/input_grad/pallas_call | solution.py:649
  261.7 1.1 collective-permute-start.25
  262.8 1.4 collective-permute-start.26
  264.2 0.9 slice_reduce_fusion.4
  265.2 1.1 collective-permute-start.27
  266.3 5.3 %collective-permute-done.30.d = bf16[4,48,1152]{2,1,0:T(8,128)(2,1)S(1)} collective-permute-done((bf16[4,48,1152]{2,1,0:T(8,128)(2,1)}, bf16[4,48,1152]{2,1,0:T(8,128)(2,1)S(1)}, u32[]{:S(2)}, u32[]{:S(2)}) %collective-permute-start.30) | collective-permute-done | bytes 442400 | tf_op jit(solution)/shard_map/ppermute | solution.py:696
  272.5 2.3 qkv_add.1
  274.8 1.2 collective-permute-done.34
  276.0 2.0 collective-permute-start.35
  278.0 2.2 collective-permute-done.35
  280.2 2.9 collective-permute-start.36
  283.0 3.2 %collective-permute-start.31 = (bf16[48,1152]{1,0:T(8,128)(2,1)}, bf16[48,1152]{1,0:T(8,128)(2,1)S(1)}, u32[]{:S(2)}, u32[]{:S(2)}) collective-permute-start(bf16[48,1152]{1,0:T(8,128)(2,1)} %get-tuple-element.139), channel_id=1, source_target_pairs={{0,8},{2,10},{4,12},{6,14},{8,0},{10,2},{12,4},{14,6},{16,24},{18,... | collective-permute-start | bytes 331784 | tf_op jit(solution)/shard_map/ppermute | solution.py:696
  286.3 1.6 collective-permute-start.32
  287.9 2.8 collective-permute-start.33
  290.8 1.3 collective-permute-start.37
  292.8 3.9 %join.1 = bf16[4,256,768]{2,1,0:T(8,128)(2,1)} custom-call(s32[3]{0:T(128)} %pad_add_fusion.ids, bf16[256,768]{1,0:T(8,128)(2,1)} %get-tuple-element.134.refs_0_, bf16[256,768]{1,0:T(8,128)(2,1)} %copy-done.26, bf16[256,768]{1,0:T(8,128)(2,1)} %collective-permute-done.26.refs_2_, bf16[256,768]{1,0:T(8,128)(2,1)} %collective-permute-done.27.refs_3_), custom_call_target="tpu_custom_call" | custom-call | flops 125 | bytes 393216 | tf_op jit(solution)/shard_map/join/pallas_call | solution.py:679
  296.7 0.9 collective-permute-start.38
  298.9 1.8 collective-permute-done.38
  302.0 3.5 %reduce-scatter.2.cloned.1.call-done = bf16[48,1920]{1,0:T(8,128)(2,1)} async-done(((bf16[1536,1920]{1,0:T(8,128)(2,1)}), bf16[48,1920]{1,0:T(8,128)(2,1)}) %reduce-scatter.2.cloned.1.call-update) | async-done | bytes 184336 | tf_op jit(solution)/shard_map/reduce_scatter | solution.py:763
  305.5 1.7 slice.133
  307.2 1.4 slice.132
  308.6 1.1 copy.41
  (159 shorter events, 17.0 us)
Async XLA Ops:
  7.2 15.7 %copy-start = (s32[4,4,8]{2,1,0:T(4,128)S(1)}, s32[4,4,8]{2,1,0:T(4,128)}, u32[]{:S(2)}) copy-start(s32[4,4,8]{2,1,0:T(4,128)} %param.18) | copy-start | bytes 1540
  7.2 99.7 %all-gather.2.cloned.1.call-start = ((), (), s32[]{:S(2)}) async-start(), calls=%async_computation.5 | async-start | bytes 6082560 | tf_op jit(solution)/shard_map/all_gather | solution.py:815
  8.9 9.8 %copy-start.37 = (f32[768]{0:T(1024)S(1)}, f32[768]{0:T(1024)}, u32[]{:S(2)}) copy-start(f32[768]{0:T(1024)} %param.23) | copy-start | bytes 9220
  8.9 9.8 %copy-start.38 = (f32[768]{0:T(1024)S(1)}, f32[768]{0:T(1024)}, u32[]{:S(2)}) copy-start(f32[768]{0:T(1024)} %param.22) | copy-start | bytes 9220
  8.9 10.4 %copy-start.31 = (f32[768]{0:T(1024)S(1)}, f32[768]{0:T(1024)}, u32[]{:S(2)}) copy-start(f32[768]{0:T(1024)} %param.19) | copy-start | bytes 9220
  8.9 11.0 %copy-start.32 = (f32[768]{0:T(1024)S(1)}, f32[768]{0:T(1024)}, u32[]{:S(2)}) copy-start(f32[768]{0:T(1024)} %param.20) | copy-start | bytes 9220
  8.9 11.6 %copy-start.33 = (f32[768]{0:T(1024)S(1)}, f32[768]{0:T(1024)}, u32[]{:S(2)}) copy-start(f32[768]{0:T(1024)} %param.25) | copy-start | bytes 9220
  8.9 12.1 %copy-start.34 = (f32[768]{0:T(1024)S(1)}, f32[768]{0:T(1024)}, u32[]{:S(2)}) copy-start(f32[768]{0:T(1024)} %param.26) | copy-start | bytes 9220
  8.9 12.7 %copy-start.35 = (f32[768]{0:T(1024)S(1)}, f32[768]{0:T(1024)}, u32[]{:S(2)}) copy-start(f32[768]{0:T(1024)} %param.27) | copy-start | bytes 9220
  9.0 13.3 %copy-start.36 = (f32[768]{0:T(1024)S(1)}, f32[768]{0:T(1024)}, u32[]{:S(2)}) copy-start(f32[768]{0:T(1024)} %param.31) | copy-start | bytes 9220
  9.0 27.3 %copy-start.27 = (bf16[48,1536]{1,0:T(8,128)(2,1)S(1)}, bf16[48,1536]{1,0:T(8,128)(2,1)}, u32[]{:S(2)}) copy-start(bf16[48,1536]{1,0:T(8,128)(2,1)} %param.28) | copy-start | bytes 442372
  9.0 25.9 %all-to-all-start = ((bf16[4,256,768]{2,1,0:T(8,128)(2,1)}), bf16[4,256,768]{2,1,0:T(8,128)(2,1)S(1)}, u32[]{:S(2)}, u32[]{:S(2)}) async-start(bf16[4,256,768]{2,1,0:T(8,128)(2,1)} %param.16), calls=%async_computation | async-start | bytes 3145728 | tf_op jit(solution)/shard_map/all_to_all | solution.py:702
  14.3 9.7 %collective-permute-start = (bf16[48,1152]{1,0:T(8,128)(2,1)S(1)}, bf16[48,1152]{1,0:T(8,128)(2,1)S(1)}, u32[]{:S(2)}, u32[]{:S(2)}) collective-permute-start(bf16[48,1152]{1,0:T(8,128)(2,1)S(1)} %copy-done.28), channel_id=1, source_target_pairs={{0,8},{2,10},{4,12},{6,14},{8,0},{10,2},{12,4},{14,6},{16,24},{18,... | collective-permute-start | bytes 331784 | tf_op jit(solution)/shard_map/ppermute | solution.py:696
  15.9 12.3 %collective-permute-start.1 = (bf16[48,1152]{1,0:T(8,128)(2,1)S(1)}, bf16[48,1152]{1,0:T(8,128)(2,1)S(1)}, u32[]{:S(2)}, u32[]{:S(2)}) collective-permute-start(bf16[48,1152]{1,0:T(8,128)(2,1)S(1)} %copy-done.28), channel_id=1, source_target_pairs={{0,16},{2,18},{4,20},{6,22},{8,24},{10,26},{12,28},{14,30},{16,0},... | collective-permute-start | bytes 331784 | tf_op jit(solution)/shard_map/ppermute | solution.py:696
  18.5 9.7 %collective-permute-start.2 = (bf16[48,1152]{1,0:T(8,128)(2,1)S(1)}, bf16[48,1152]{1,0:T(8,128)(2,1)S(1)}, u32[]{:S(2)}, u32[]{:S(2)}) collective-permute-start(bf16[48,1152]{1,0:T(8,128)(2,1)S(1)} %copy-done.28), channel_id=1, source_target_pairs={{0,24},{2,26},{4,28},{6,30},{8,16},{10,18},{12,20},{14,22},{16,8},... | collective-permute-start | bytes 331784 | tf_op jit(solution)/shard_map/ppermute | solution.py:696
  28.2 41.8 %copy-start.5 = (bf16[4,48,1152]{2,1,0:T(8,128)(2,1)}, bf16[4,48,1152]{2,1,0:T(8,128)(2,1)S(1)}, u32[]{:S(2)}) copy-start(bf16[4,48,1152]{2,1,0:T(8,128)(2,1)S(1)} %pad_maximum_fusion.1.rest_0_) | copy-start | bytes 1327108
  34.9 35.1 %copy-start.2 = (bf16[4,256,768]{2,1,0:T(8,128)(2,1)}, bf16[4,256,768]{2,1,0:T(8,128)(2,1)S(1)}, u32[]{:S(2)}) copy-start(bf16[4,256,768]{2,1,0:T(8,128)(2,1)S(1)} %all-to-all-done) | copy-start | bytes 4718596
  34.9 15.5 %collective-permute-start.3 = (bf16[4,48,1152]{2,1,0:T(8,128)(2,1)S(1)}, bf16[4,48,1152]{2,1,0:T(8,128)(2,1)S(1)}, u32[]{:S(2)}, u32[]{:S(2)}) collective-permute-start(bf16[4,48,1152]{2,1,0:T(8,128)(2,1)S(1)} %pad_maximum_fusion.1.rest_0_), channel_id=1, source_target_pairs={{0,2},{2,0},{4,6},{6,4},{8,10},{10,8},{12,14},{14,12},{16,18},{18,... | collective-permute-start | bytes 1327112 | tf_op jit(solution)/shard_map/ppermute | solution.py:696
  36.3 6.9 %collective-permute-start.10 = (bf16[48,1536]{1,0:T(8,128)(2,1)S(1)}, bf16[48,1536]{1,0:T(8,128)(2,1)S(1)}, u32[]{:S(2)}, u32[]{:S(2)}) collective-permute-start(bf16[48,1536]{1,0:T(8,128)(2,1)S(1)} %copy-done.27), channel_id=1, source_target_pairs={{0,8},{2,10},{4,12},{6,14},{8,0},{10,2},{12,4},{14,6},{16,24},{18,... | collective-permute-start | bytes 442376 | tf_op jit(solution)/shard_map/ppermute | solution.py:696
  38.0 12.4 %collective-permute-start.11 = (bf16[48,1536]{1,0:T(8,128)(2,1)S(1)}, bf16[48,1536]{1,0:T(8,128)(2,1)S(1)}, u32[]{:S(2)}, u32[]{:S(2)}) collective-permute-start(bf16[48,1536]{1,0:T(8,128)(2,1)S(1)} %copy-done.27), channel_id=1, source_target_pairs={{0,16},{2,18},{4,20},{6,22},{8,24},{10,26},{12,28},{14,30},{16,0},... | collective-permute-start | bytes 442376 | tf_op jit(solution)/shard_map/ppermute | solution.py:696
  40.6 23.4 %collective-permute-start.4 = (bf16[4,48,1152]{2,1,0:T(8,128)(2,1)S(1)}, bf16[4,48,1152]{2,1,0:T(8,128)(2,1)S(1)}, u32[]{:S(2)}, u32[]{:S(2)}) collective-permute-start(bf16[4,48,1152]{2,1,0:T(8,128)(2,1)S(1)} %pad_maximum_fusion.1.rest_0_), channel_id=1, source_target_pairs={{0,4},{2,6},{4,0},{6,2},{8,12},{10,14},{12,8},{14,10},{16,20},{18,... | collective-permute-start | bytes 1327112 | tf_op jit(solution)/shard_map/ppermute | solution.py:696
  40.9 23.0 %collective-permute-start.5 = (bf16[4,48,1152]{2,1,0:T(8,128)(2,1)S(1)}, bf16[4,48,1152]{2,1,0:T(8,128)(2,1)S(1)}, u32[]{:S(2)}, u32[]{:S(2)}) collective-permute-start(bf16[4,48,1152]{2,1,0:T(8,128)(2,1)S(1)} %pad_maximum_fusion.1.rest_0_), channel_id=1, source_target_pairs={{0,6},{2,4},{4,2},{6,0},{8,14},{10,12},{12,10},{14,8},{16,22},{18,... | collective-permute-start | bytes 1327112 | tf_op jit(solution)/shard_map/ppermute | solution.py:696
  43.3 8.5 %collective-permute-start.12 = (bf16[48,1536]{1,0:T(8,128)(2,1)S(1)}, bf16[48,1536]{1,0:T(8,128)(2,1)S(1)}, u32[]{:S(2)}, u32[]{:S(2)}) collective-permute-start(bf16[48,1536]{1,0:T(8,128)(2,1)S(1)} %copy-done.27), channel_id=1, source_target_pairs={{0,24},{2,26},{4,28},{6,30},{8,16},{10,18},{12,20},{14,22},{16,8},... | collective-permute-start | bytes 442376 | tf_op jit(solution)/shard_map/ppermute | solution.py:696
  50.4 17.2 %collective-permute-start.6 = (bf16[4,48,1152]{2,1,0:T(8,128)(2,1)S(1)}, bf16[4,48,1152]{2,1,0:T(8,128)(2,1)S(1)}, u32[]{:S(2)}, u32[]{:S(2)}) collective-permute-start(bf16[4,48,1152]{2,1,0:T(8,128)(2,1)S(1)} %pad_maximum_fusion.1.rest_0_), channel_id=1, source_target_pairs={{0,1},{1,0},{2,3},{3,2},{4,5},{5,4},{6,7},{7,6},{8,9},{9,8},{10,11... | collective-permute-start | bytes 1327112 | tf_op jit(solution)/shard_map/ppermute | solution.py:696
  50.4 19.6 %copy-start.13 = (bf16[4,48,1152]{2,1,0:T(8,128)(2,1)}, bf16[4,48,1152]{2,1,0:T(8,128)(2,1)S(1)}, u32[]{:S(2)}) copy-start(bf16[4,48,1152]{2,1,0:T(8,128)(2,1)S(1)} %collective-permute-done.3.rest_1_) | copy-start | bytes 1327108
  50.4 17.2 %collective-permute-start.7 = (bf16[4,48,1152]{2,1,0:T(8,128)(2,1)S(1)}, bf16[4,48,1152]{2,1,0:T(8,128)(2,1)S(1)}, u32[]{:S(2)}, u32[]{:S(2)}) collective-permute-start(bf16[4,48,1152]{2,1,0:T(8,128)(2,1)S(1)} %collective-permute-done.3.rest_1_), channel_id=1, source_target_pairs={{0,1},{1,0},{2,3},{3,2},{4,5},{5,4},{6,7},{7,6},{8,9},{9,8},{10,11... | collective-permute-start | bytes 1327112 | tf_op jit(solution)/shard_map/ppermute | solution.py:696
  51.8 48.6 %copy-start.4 = (bf16[4,48,1536]{2,1,0:T(8,128)(2,1)}, bf16[4,48,1536]{2,1,0:T(8,128)(2,1)S(1)}, u32[]{:S(2)}) copy-start(bf16[4,48,1536]{2,1,0:T(8,128)(2,1)S(1)} %pad_maximum_fusion.rest_0_) | copy-start | bytes 1769476
  64.0 36.3 %collective-permute-start.13 = (bf16[4,48,1536]{2,1,0:T(8,128)(2,1)S(1)}, bf16[4,48,1536]{2,1,0:T(8,128)(2,1)S(1)}, u32[]{:S(2)}, u32[]{:S(2)}) collective-permute-start(bf16[4,48,1536]{2,1,0:T(8,128)(2,1)S(1)} %pad_maximum_fusion.rest_0_), channel_id=1, source_target_pairs={{0,2},{2,0},{4,6},{6,4},{8,10},{10,8},{12,14},{14,12},{16,18},{18,... | collective-permute-start | bytes 1769480 | tf_op jit(solution)/shard_map/ppermute | solution.py:696
  65.6 34.8 %collective-permute-start.14 = (bf16[4,48,1536]{2,1,0:T(8,128)(2,1)S(1)}, bf16[4,48,1536]{2,1,0:T(8,128)(2,1)S(1)}, u32[]{:S(2)}, u32[]{:S(2)}) collective-permute-start(bf16[4,48,1536]{2,1,0:T(8,128)(2,1)S(1)} %pad_maximum_fusion.rest_0_), channel_id=1, source_target_pairs={{0,4},{2,6},{4,0},{6,2},{8,12},{10,14},{12,8},{14,10},{16,20},{18,... | collective-permute-start | bytes 1769480 | tf_op jit(solution)/shard_map/ppermute | solution.py:696
  66.3 34.1 %collective-permute-start.15 = (bf16[4,48,1536]{2,1,0:T(8,128)(2,1)S(1)}, bf16[4,48,1536]{2,1,0:T(8,128)(2,1)S(1)}, u32[]{:S(2)}, u32[]{:S(2)}) collective-permute-start(bf16[4,48,1536]{2,1,0:T(8,128)(2,1)S(1)} %pad_maximum_fusion.rest_0_), channel_id=1, source_target_pairs={{0,6},{2,4},{4,2},{6,0},{8,14},{10,12},{12,10},{14,8},{16,22},{18,... | collective-permute-start | bytes 1769480 | tf_op jit(solution)/shard_map/ppermute | solution.py:696
  67.6 1.8 collective-permute-start.8
  67.6 2.4 collective-permute-start.9
  100.3 10.3 %copy-start.6 = (bf16[4,48,1536]{2,1,0:T(8,128)(2,1)}, bf16[4,48,1536]{2,1,0:T(8,128)(2,1)S(1)}, u32[]{:S(2)}) copy-start(bf16[4,48,1536]{2,1,0:T(8,128)(2,1)S(1)} %collective-permute-done.13.rest_1_) | copy-start | bytes 1769476
  100.4 2.8 collective-permute-start.16
  100.6 4.4 %collective-permute-start.17 = (bf16[4,48,1536]{2,1,0:T(8,128)(2,1)S(1)}, bf16[4,48,1536]{2,1,0:T(8,128)(2,1)S(1)}, u32[]{:S(2)}, u32[]{:S(2)}) collective-permute-start(bf16[4,48,1536]{2,1,0:T(8,128)(2,1)S(1)} %collective-permute-done.13.rest_1_), channel_id=1, source_target_pairs={{0,1},{1,0},{2,3},{3,2},{4,5},{5,4},{6,7},{7,6},{8,9},{9,8},{10,11... | collective-permute-start | bytes 1769480 | tf_op jit(solution)/shard_map/ppermute | solution.py:696
  101.0 5.1 %collective-permute-start.18 = (bf16[4,48,1536]{2,1,0:T(8,128)(2,1)S(1)}, bf16[4,48,1536]{2,1,0:T(8,128)(2,1)S(1)}, u32[]{:S(2)}, u32[]{:S(2)}) collective-permute-start(bf16[4,48,1536]{2,1,0:T(8,128)(2,1)S(1)} %collective-permute-done.14.rest_2_), channel_id=1, source_target_pairs={{0,1},{1,0},{2,3},{3,2},{4,5},{5,4},{6,7},{7,6},{8,9},{9,8},{10,11... | collective-permute-start | bytes 1769480 | tf_op jit(solution)/shard_map/ppermute | solution.py:696
  101.1 5.8 %collective-permute-start.19 = (bf16[4,48,1536]{2,1,0:T(8,128)(2,1)S(1)}, bf16[4,48,1536]{2,1,0:T(8,128)(2,1)}, u32[]{:S(2)}, u32[]{:S(2)}) collective-permute-start(bf16[4,48,1536]{2,1,0:T(8,128)(2,1)S(1)} %collective-permute-done.15.rest_3_), channel_id=1, source_target_pairs={{0,1},{1,0},{2,3},{3,2},{4,5},{5,4},{6,7},{7,6},{8,9},{9,8},{10,11... | collective-permute-start | bytes 1769480 | tf_op jit(solution)/shard_map/ppermute | solution.py:696
  106.9 27.3 %all-to-all-start.1 = ((bf16[4,256,768]{2,1,0:T(8,128)(2,1)}), bf16[4,256,768]{2,1,0:T(8,128)(2,1)S(1)}, u32[]{:S(2)}, u32[]{:S(2)}) async-start(bf16[4,256,768]{2,1,0:T(8,128)(2,1)} %param.17), calls=%async_computation.1 | async-start | bytes 3145728 | tf_op jit(solution)/shard_map/all_to_all | solution.py:702
  134.2 26.7 %all-to-all-start.2 = ((bf16[4,256,768]{2,1,0:T(8,128)(2,1)}), bf16[4,256,768]{2,1,0:T(8,128)(2,1)S(1)}, u32[]{:S(2)}, u32[]{:S(2)}) async-start(bf16[4,256,768]{2,1,0:T(8,128)(2,1)} %bitcast.49), calls=%async_computation.2 | async-start | bytes 3145728 | tf_op jit(solution)/shard_map/all_to_all | solution.py:702
  138.4 167.1 %reduce-scatter.2.cloned.1.call-start = ((), (), s32[]{:S(2)}) async-start(), calls=%async_computation.6 | async-start | bytes 6082560 | tf_op jit(solution)/shard_map/reduce_scatter | solution.py:763
  183.1 4.8 %collective-permute-start.20 = (bf16[3072,384]{1,0:T(8,128)(2,1)}, bf16[3072,384]{1,0:T(8,128)(2,1)S(1)}, u32[]{:S(2)}, u32[]{:S(2)}) collective-permute-start(bf16[3072,384]{1,0:T(8,128)(2,1)} %get-tuple-element.115), channel_id=1, source_target_pairs={{0,1},{1,0},{2,3},{3,2},{4,5},{5,4},{6,7},{7,6},{8,9},{9,8},{10,11... | collective-permute-start | bytes 7077896 | tf_op jit(solution)/shard_map/ppermute | solution.py:696
  193.5 29.3 %collective-permute-start.21 = (bf16[4,192,384]{2,1,0:T(8,128)(2,1)}, bf16[4,192,384]{2,1,0:T(8,128)(2,1)S(1)}, u32[]{:S(2)}, u32[]{:S(2)}) collective-permute-start(bf16[4,192,384]{2,1,0:T(8,128)(2,1)} %get-tuple-element.117), channel_id=1, source_target_pairs={{0,2},{2,0},{4,6},{6,4},{8,10},{10,8},{12,14},{14,12},{16,18},{18,... | collective-permute-start | bytes 1769480 | tf_op jit(solution)/shard_map/ppermute | solution.py:696
  195.5 27.9 %collective-permute-start.22 = (bf16[4,192,384]{2,1,0:T(8,128)(2,1)}, bf16[4,192,384]{2,1,0:T(8,128)(2,1)S(1)}, u32[]{:S(2)}, u32[]{:S(2)}) collective-permute-start(bf16[4,192,384]{2,1,0:T(8,128)(2,1)} %get-tuple-element.118), channel_id=1, source_target_pairs={{0,4},{2,6},{4,0},{6,2},{8,12},{10,14},{12,8},{14,10},{16,20},{18,... | collective-permute-start | bytes 1769480 | tf_op jit(solution)/shard_map/ppermute | solution.py:696
  197.0 26.5 %collective-permute-start.23 = (bf16[4,192,384]{2,1,0:T(8,128)(2,1)}, bf16[4,192,384]{2,1,0:T(8,128)(2,1)S(1)}, u32[]{:S(2)}, u32[]{:S(2)}) collective-permute-start(bf16[4,192,384]{2,1,0:T(8,128)(2,1)} %get-tuple-element.119), channel_id=1, source_target_pairs={{0,6},{2,4},{4,2},{6,0},{8,14},{10,12},{12,10},{14,8},{16,22},{18,... | collective-permute-start | bytes 1769480 | tf_op jit(solution)/shard_map/ppermute | solution.py:696
  222.8 10.9 %copy-start.20 = (bf16[4,192,384]{2,1,0:T(8,128)(2,1)}, bf16[4,192,384]{2,1,0:T(8,128)(2,1)S(1)}, u32[]{:S(2)}) copy-start(bf16[4,192,384]{2,1,0:T(8,128)(2,1)S(1)} %collective-permute-done.21.b) | copy-start | bytes 1769476
  223.4 10.3 %copy-start.21 = (bf16[4,192,384]{2,1,0:T(8,128)(2,1)}, bf16[4,192,384]{2,1,0:T(8,128)(2,1)S(1)}, u32[]{:S(2)}) copy-start(bf16[4,192,384]{2,1,0:T(8,128)(2,1)S(1)} %collective-permute-done.22.c) | copy-start | bytes 1769476
  223.4 10.3 %copy-start.22 = (bf16[4,192,384]{2,1,0:T(8,128)(2,1)}, bf16[4,192,384]{2,1,0:T(8,128)(2,1)S(1)}, u32[]{:S(2)}) copy-start(bf16[4,192,384]{2,1,0:T(8,128)(2,1)S(1)} %collective-permute-done.23.d) | copy-start | bytes 1769476
  223.4 11.2 %copy-start.30 = (f32[8,768]{1,0:T(8,128)S(1)}, f32[8,768]{1,0:T(8,128)}, u32[]{:S(2)}) copy-start(f32[8,768]{1,0:T(8,128)} %get-tuple-element.143) | copy-start | bytes 73732
  233.7 8.1 %collective-permute-start.24 = (bf16[768,1152]{1,0:T(8,128)(2,1)}, bf16[768,1152]{1,0:T(8,128)(2,1)}, u32[]{:S(2)}, u32[]{:S(2)}) collective-permute-start(bf16[768,1152]{1,0:T(8,128)(2,1)} %get-tuple-element.125), channel_id=1, source_target_pairs={{0,1},{1,0},{2,3},{3,2},{4,5},{5,4},{6,7},{7,6},{8,9},{9,8},{10,11... | collective-permute-start | bytes 5308424 | tf_op jit(solution)/shard_map/ppermute | solution.py:696
  237.5 45.6 %all-to-all-start.3 = ((bf16[4,192,384]{2,1,0:T(8,128)(2,1)}), bf16[4,192,384]{2,1,0:T(8,128)(2,1)S(1)}, u32[]{:S(2)}, u32[]{:S(2)}) async-start(bf16[4,192,384]{2,1,0:T(8,128)(2,1)} %down_add.1), calls=%async_computation.3 | async-start | bytes 1179648 | tf_op jit(solution)/shard_map/all_to_all | solution.py:749
  245.5 19.7 %collective-permute-start.28 = (bf16[4,48,1152]{2,1,0:T(8,128)(2,1)}, bf16[4,48,1152]{2,1,0:T(8,128)(2,1)S(1)}, u32[]{:S(2)}, u32[]{:S(2)}) collective-permute-start(bf16[4,48,1152]{2,1,0:T(8,128)(2,1)} %get-tuple-element.129), channel_id=1, source_target_pairs={{0,2},{2,0},{4,6},{6,4},{8,10},{10,8},{12,14},{14,12},{16,18},{18,... | collective-permute-start | bytes 1327112 | tf_op jit(solution)/shard_map/ppermute | solution.py:696
  246.6 19.7 %collective-permute-start.29 = (bf16[4,48,1152]{2,1,0:T(8,128)(2,1)}, bf16[4,48,1152]{2,1,0:T(8,128)(2,1)S(1)}, u32[]{:S(2)}, u32[]{:S(2)}) collective-permute-start(bf16[4,48,1152]{2,1,0:T(8,128)(2,1)} %get-tuple-element.130), channel_id=1, source_target_pairs={{0,4},{2,6},{4,0},{6,2},{8,12},{10,14},{12,8},{14,10},{16,20},{18,... | collective-permute-start | bytes 1327112 | tf_op jit(solution)/shard_map/ppermute | solution.py:696
  248.0 23.6 %collective-permute-start.30 = (bf16[4,48,1152]{2,1,0:T(8,128)(2,1)}, bf16[4,48,1152]{2,1,0:T(8,128)(2,1)S(1)}, u32[]{:S(2)}, u32[]{:S(2)}) collective-permute-start(bf16[4,48,1152]{2,1,0:T(8,128)(2,1)} %get-tuple-element.131), channel_id=1, source_target_pairs={{0,6},{2,4},{4,2},{6,0},{8,14},{10,12},{12,10},{14,8},{16,22},{18,... | collective-permute-start | bytes 1327112 | tf_op jit(solution)/shard_map/ppermute | solution.py:696
  261.7 26.2 %collective-permute-start.25 = (bf16[256,768]{1,0:T(8,128)(2,1)}, bf16[256,768]{1,0:T(8,128)(2,1)S(1)}, u32[]{:S(2)}, u32[]{:S(2)}) collective-permute-start(bf16[256,768]{1,0:T(8,128)(2,1)} %get-tuple-element.135), channel_id=1, source_target_pairs={{0,2},{2,0},{4,6},{6,4},{8,10},{10,8},{12,14},{14,12},{16,18},{18,... | collective-permute-start | bytes 1179656 | tf_op jit(solution)/shard_map/ppermute | solution.py:696
  262.8 27.9 %collective-permute-start.26 = (bf16[256,768]{1,0:T(8,128)(2,1)}, bf16[256,768]{1,0:T(8,128)(2,1)}, u32[]{:S(2)}, u32[]{:S(2)}) collective-permute-start(bf16[256,768]{1,0:T(8,128)(2,1)} %get-tuple-element.136), channel_id=1, source_target_pairs={{0,4},{2,6},{4,0},{6,2},{8,12},{10,14},{12,8},{14,10},{16,20},{18,... | collective-permute-start | bytes 1179656 | tf_op jit(solution)/shard_map/ppermute | solution.py:696
  265.2 25.6 %collective-permute-start.27 = (bf16[256,768]{1,0:T(8,128)(2,1)}, bf16[256,768]{1,0:T(8,128)(2,1)}, u32[]{:S(2)}, u32[]{:S(2)}) collective-permute-start(bf16[256,768]{1,0:T(8,128)(2,1)} %get-tuple-element.137), channel_id=1, source_target_pairs={{0,6},{2,4},{4,2},{6,0},{8,14},{10,12},{12,10},{14,8},{16,22},{18,... | collective-permute-start | bytes 1179656 | tf_op jit(solution)/shard_map/ppermute | solution.py:696
  274.8 1.2 collective-permute-start.34
  276.0 4.2 %collective-permute-start.35 = (f32[72,128]{1,0:T(8,128)S(1)}, f32[72,128]{1,0:T(8,128)S(1)}, u32[]{:S(2)}, u32[]{:S(2)}) collective-permute-start(f32[72,128]{1,0:T(8,128)S(1)} %add.66), channel_id=1, source_target_pairs={{0,8},{2,10},{4,12},{6,14},{8,0},{10,2},{12,4},{14,6},{16,24},{18,... | collective-permute-start | bytes 110600 | tf_op jit(solution)/shard_map/ppermute | solution.py:696
  280.2 6.1 %collective-permute-start.36 = (f32[72,128]{1,0:T(8,128)S(1)}, f32[72,128]{1,0:T(8,128)S(1)}, u32[]{:S(2)}, u32[]{:S(2)}) collective-permute-start(f32[72,128]{1,0:T(8,128)S(1)} %add.67), channel_id=1, source_target_pairs={{0,16},{2,18},{4,20},{6,22},{8,24},{10,26},{12,28},{14,30},{16,0},... | collective-permute-start | bytes 110600 | tf_op jit(solution)/shard_map/ppermute | solution.py:696
  283.0 14.5 %collective-permute-start.31 = (bf16[48,1152]{1,0:T(8,128)(2,1)}, bf16[48,1152]{1,0:T(8,128)(2,1)S(1)}, u32[]{:S(2)}, u32[]{:S(2)}) collective-permute-start(bf16[48,1152]{1,0:T(8,128)(2,1)} %get-tuple-element.139), channel_id=1, source_target_pairs={{0,8},{2,10},{4,12},{6,14},{8,0},{10,2},{12,4},{14,6},{16,24},{18,... | collective-permute-start | bytes 331784 | tf_op jit(solution)/shard_map/ppermute | solution.py:696
  286.3 11.9 %collective-permute-start.32 = (bf16[48,1152]{1,0:T(8,128)(2,1)}, bf16[48,1152]{1,0:T(8,128)(2,1)S(1)}, u32[]{:S(2)}, u32[]{:S(2)}) collective-permute-start(bf16[48,1152]{1,0:T(8,128)(2,1)} %get-tuple-element.140), channel_id=1, source_target_pairs={{0,16},{2,18},{4,20},{6,22},{8,24},{10,26},{12,28},{14,30},{16,0},... | collective-permute-start | bytes 331784 | tf_op jit(solution)/shard_map/ppermute | solution.py:696
  287.9 10.3 %collective-permute-start.33 = (bf16[48,1152]{1,0:T(8,128)(2,1)}, bf16[48,1152]{1,0:T(8,128)(2,1)S(1)}, u32[]{:S(2)}, u32[]{:S(2)}) collective-permute-start(bf16[48,1152]{1,0:T(8,128)(2,1)} %get-tuple-element.141), channel_id=1, source_target_pairs={{0,24},{2,26},{4,28},{6,30},{8,16},{10,18},{12,20},{14,22},{16,8},... | collective-permute-start | bytes 331784 | tf_op jit(solution)/shard_map/ppermute | solution.py:696
  290.8 5.9 %collective-permute-start.37 = (f32[72,128]{1,0:T(8,128)S(1)}, f32[72,128]{1,0:T(8,128)S(1)}, u32[]{:S(2)}, u32[]{:S(2)}) collective-permute-start(f32[72,128]{1,0:T(8,128)S(1)} %add.68), channel_id=1, source_target_pairs={{0,2},{2,0},{4,6},{6,4},{8,10},{10,8},{12,14},{14,12},{16,18},{18,... | collective-permute-start | bytes 110600 | tf_op jit(solution)/shard_map/ppermute | solution.py:696
  296.7 4.0 %collective-permute-start.38 = (f32[72,128]{1,0:T(8,128)S(1)}, f32[72,128]{1,0:T(8,128)S(1)}, u32[]{:S(2)}, u32[]{:S(2)}) collective-permute-start(f32[72,128]{1,0:T(8,128)S(1)} %add.69), channel_id=1, source_target_pairs={{0,4},{2,6},{4,0},{6,2},{8,12},{10,14},{12,8},{14,10},{16,20},{18,... | collective-permute-start | bytes 110600 | tf_op jit(solution)/shard_map/ppermute | solution.py:696
  (20 other events, 73.4 us)
Sparse Core Ops, SparseCore 0:
  11.5 94.3 all-gather.1
  172.7 132.7 reduce-scatter.1

commit v5 on v4

--- a/solution.py
+++ b/solution.py
@@ -95,53 +95,57 @@
         place_pieces(ids, parts, False, [(0, parts[0].shape[2], w, sem)])
 
 
-def qkv_kernel(parts, ids, x_ref, g_ref, b_ref, qb_ref, *rest):
-    w_hbm, (act_ref, qkv_ref, w_vmem, sem) = rest[:parts], rest[parts:]
-    first = pl.program_id(0) == 0
-
-    @pl.when(first)
+def norm_kernel(x_ref, g_ref, b_ref, act_ref):
+    normed, _ = norm_parts(x_ref[...].astype(F32))
+    act_ref[...] = (normed * g_ref[...] + b_ref[...]).astype(BF16)
+
+
+def first_norm(x, gain, bias):
+    n = x.shape[0]
+    row = pl.BlockSpec((BLK, D), lambda i: (i, 0))
+    vec = pl.BlockSpec((1, D), lambda i: (0, 0))
+    return pl.pallas_call(
+        norm_kernel,
+        grid=(n // BLK,),
+        in_specs=[row, vec, vec],
+        out_specs=row,
+        out_shape=jax.ShapeDtypeStruct((n, D), BF16),
+        compiler_params=params(),
+        cost_estimate=cost(8 * n * D, 4 * n * D),
+        name="first_norm",
+    )(x, gain, bias)
+
+
+def qkv_kernel(parts, ids, act_ref, qb_ref, *rest):
+    w_hbm, (qkv_ref, w_vmem, sem) = rest[:parts], rest[parts:]
+
+    @pl.when(pl.program_id(0) == 0)
     def _():
         place(ids, w_hbm, w_vmem, sem)
-
-    normed, _ = norm_parts(x_ref[...].astype(F32))
-    act = (normed * g_ref[...] + b_ref[...]).astype(BF16)
-    act_ref[...] = act
-
-    @pl.when(first)
-    def _():
         whole(w_vmem, sem).wait()
 
-    qkv_ref[...] = (mm(act, w_vmem[...]) + qb_ref[...]).astype(BF16)
-
-
-def norm_qkv(ids, x, gain, bias, qkv_bias, w):
-    n = x.shape[0]
+    qkv_ref[...] = (mm(act_ref[...], w_vmem[...]) + qb_ref[...]).astype(BF16)
+
+
+def project_qkv(ids, act, qkv_bias, w):
+    n = act.shape[0]
     tile = BLK
-    const = lambda i: (0, 0)
     return pl.pallas_call(
         functools.partial(qkv_kernel, len(w)),
         grid=(n // tile,),
         in_specs=[
             pl.BlockSpec(memory_space=pltpu.SMEM),
             pl.BlockSpec((tile, D), lambda i: (i, 0)),
-            pl.BlockSpec((1, D), const),
-            pl.BlockSpec((1, D), const),
-            pl.BlockSpec((1, 3 * D), const),
+            pl.BlockSpec((1, 3 * D), lambda i: (0, 0)),
         ]
         + [pl.BlockSpec(memory_space=pl.ANY)] * len(w),
-        out_specs=[
-            pl.BlockSpec((tile, D), lambda i: (i, 0)),
-            pl.BlockSpec((tile, 3 * D), lambda i: (i, 0)),
-        ],
-        out_shape=[
-            jax.ShapeDtypeStruct((n, D), BF16),
-            jax.ShapeDtypeStruct((n, 3 * D), BF16),
-        ],
+        out_specs=pl.BlockSpec((tile, 3 * D), lambda i: (i, 0)),
+        out_shape=jax.ShapeDtypeStruct((n, 3 * D), BF16),
         scratch_shapes=[pltpu.VMEM((D, 3 * D), BF16), pltpu.SemaphoreType.DMA],
         compiler_params=params(),
-        cost_estimate=cost(2 * n * D * 3 * D, 2 * (n * 5 * D + 3 * D * D)),
-        name="norm_qkv",
-    )(ids, x, gain, bias, qkv_bias, *w)
+        cost_estimate=cost(2 * n * D * 3 * D, 2 * (n * 4 * D + 3 * D * D)),
+        name="project_qkv",
+    )(ids, act, qkv_bias, *w)
 
 
 def first_of_doc(lens_ref, positions):
@@ -616,6 +620,24 @@
     )(ids, *parts)
 
 
+def split_kernel(a_ref, left, right):
+    width = left.shape[1]
+    left[...] = a_ref[:, :width].astype(F32)
+    right[...] = a_ref[:, width:].astype(F32)
+
+
+def split(a, width):
+    rows, cols = a.shape
+    sds = jax.ShapeDtypeStruct
+    return pl.pallas_call(
+        split_kernel,
+        out_shape=[sds((rows, width), F32), sds((rows, cols - width), F32)],
+        compiler_params=params(),
+        cost_estimate=cost(a.size, 6 * a.size),
+        name="split",
+    )(a)
+
+
 def input_grad_kernel(parts, ids, x_ref, dm_ref, g_ref, dqkv_ref, *rest):
     w_hbm, outs, (vec_ref, w, sem) = rest[:parts], rest[parts:-3], rest[-3:]
     step = pl.program_id(0)
@@ -754,13 +776,17 @@
 
 
 def scatter(halves):
+    return scatter_narrow(halves).astype(F32)
+
+
+def scatter_narrow(halves):
     over_row = lax.axis_size("row")
     _, height, width = halves.shape
     cols = 2 * width // over_row
     if over_row != 2:
         halves = halves.reshape(2, height, over_row // 2, cols).transpose(0, 2, 1, 3)
     flat = halves.reshape(over_row * height, cols)
-    return lax.psum_scatter(flat, ("row", "tok"), scatter_dimension=0, tiled=True).astype(F32)
+    return lax.psum_scatter(flat, ("row", "tok"), scatter_dimension=0, tiled=True)
 
 
 def scatter_sides(sides, row_index):
@@ -822,19 +848,23 @@
         )
         up_line = gather_line(up_shard)
         qkv_pieces = spread(qkv_line, QUAD_STEPS)
-        qkv_full = with_partner(qkv_pieces)
         up_pieces = spread(after(up_line, *qkv_pieces), QUAD_STEPS)
     else:
         x = quad_swap(tokens).reshape(n, width)
         qkv_full = [gather(qkv_weight)]
         others = [gather(proj_weight), gather(up_weight), gather(down_weight)]
     qkv_bias, first_gain, first_bias, proj_bias, second_gain, second_bias, up_bias, down_bias = vectors
-    act1, qkv = norm_qkv(ids, x, first_gain, first_bias, qkv_bias, qkv_full)
+    act1 = first_norm(x, first_gain, first_bias)
+    if by_permutes:
+        act1, qkv_pieces[-1] = lax.optimization_barrier((act1, qkv_pieces[-1]))
+        qkv_full = with_partner(qkv_pieces)
+    qkv = project_qkv(ids, act1, qkv_bias, qkv_full)
     attended, stats = attention(lens, qkv)
     if by_permutes:
-        up_pieces = list(lax.optimization_barrier((attended, *up_pieces))[1:])
+        up_pieces[1:] = lax.optimization_barrier((attended, *up_pieces[1:]))[1:]
         others = with_partner(up_pieces) + [rest]
-    c = quad_swap(after(out_grad, attended, *others)).reshape(n, width)
+    held = others[:-1] if by_permutes else [attended]
+    c = quad_swap(after(out_grad, *held)).reshape(n, width)
     middle, out, hidden, slope, act2 = mlp(
         ids, x, attended, proj_bias, second_gain, second_bias, up_bias, down_bias, others
     )
@@ -847,8 +877,7 @@
         dout = after(dout, *down_blocks)
     dqkv = attention_back(lens, qkv, attended, dout, stats)
     if by_permutes:
-        up_proj = scatter(up_outer_grad)
-        up_grad, proj_grad = up_proj[:, : FF // 2], up_proj[:, FF // 2 :]
+        up_grad, proj_grad = split(scatter_narrow(up_outer_grad), FF // 2)
         down_got = from_peers(down_blocks, QUAD_STEPS)
         act1 = after(act1, *down_got[1:])
     qkv_sides = qkv_outer(ids, act1, dqkv)

time: 318 us -> 314 us (0.987)
  Pallas kernels: 163 us -> 169 us
  waiting for transfers between devices: 54.9 us -> 50.8 us
    ppermute x39, waiting for transfers between devices: 44.7 us -> 37.5 us  [swap(): return lax.ppermute(block, axis, [(i, i ^ distance) for i in range(count)])]
    pallas_call x1 -> x3, Pallas kernels: 9.74 us -> 14.7 us  [the longest x1 8.83 us: project_qkv(): pl.pallas_call(functools.partial(qkv_kernel, len(w)), grid=(n // tile,),...]
  transfers between devices with their start and end apart: 45 -> 45, of which waited for: 19 -> 19; matrix products, arithmetic and copies ran while one was open for 3% -> 3% of each run, Pallas kernels for 48% -> 50%
where the time goes in v5:
time: 314 us; the launch traced here: 313 us
  Pallas kernels  169 us (54%)
  starting transfers between devices  62.3 us (20%)
  waiting for transfers between devices  50.8 us (16%)
  between operations  14.6 us (5%)
  local copies, waits for them, and re-layouts  12.9 us (4%)
  other arithmetic  3.94 us (1%)
    ppermute x39, starting transfers between devices, swap(): return lax.ppermute(block, axis, [(i, i ^ distance) for i in range(count)])  46.1 us
    ppermute x39, waiting for transfers between devices, swap(): return lax.ppermute(block, axis, [(i, i ^ distance) for i in range(count)])  37.5 us
    pallas_call x1, Pallas kernels, attention_back(): pl.pallas_call(attn_back_kernel, grid=(pairs,), in_specs=[pl.BlockSpec(me...  25.8 us
    pallas_call x1, Pallas kernels, mlp(): pl.pallas_call(functools.partial(mlp_kernel, len(w)), grid=(n // tile,),...  23.6 us
    pallas_call x1, Pallas kernels, mlp_back(): pl.pallas_call(functools.partial(mlp_back_kernel, len(w)), grid=(n // til...  22.7 us
    pallas_call x1, Pallas kernels, attention(): pl.pallas_call(attn_kernel, grid=(pairs,), in_specs=[pl.BlockSpec(memory_...  19.7 us
    pallas_call x1, Pallas kernels, input_grad(): pl.pallas_call(functools.partial(input_grad_kernel, len(w)), grid_spec=pl...  12.9 us
    all_to_all x3, starting transfers between devices, quad_swap(): lax.all_to_all(pieces, 'tok', 0, 0, axis_index_groups=groups, tiled=True)  12.4 us
  transfers between devices with their start and end apart: 45, of which 19 were waited for; matrix products, arithmetic and copies ran while one was open for 3% of the time, Pallas kernels for 50%

profile of v5, /device:TPU:0, one launch (start us, length us, event | category | flops | bytes accessed | tf_op | source)
XLA Modules:
  0.0 313.2 jit_solution(16997099130876919196)
XLA Ops:
  7.3 1.7 pad_maximum_fusion.2
  9.0 5.3 %all-to-all-start = ((bf16[4,256,768]{2,1,0:T(8,128)(2,1)}), bf16[4,256,768]{2,1,0:T(8,128)(2,1)S(1)}, u32[]{:S(2)}, u32[]{:S(2)}) async-start(bf16[4,256,768]{2,1,0:T(8,128)(2,1)} %param.16), calls=%async_computation | async-start | bytes 3145728 | tf_op jit(solution)/shard_map/all_to_all | solution.py:724
  14.3 1.6 collective-permute-start
  15.9 2.6 collective-permute-start.1
  23.9 4.2 %collective-permute-done.1 = bf16[48,1152]{1,0:T(8,128)(2,1)S(1)} collective-permute-done((bf16[48,1152]{1,0:T(8,128)(2,1)S(1)}, bf16[48,1152]{1,0:T(8,128)(2,1)S(1)}, u32[]{:S(2)}, u32[]{:S(2)}) %collective-permute-start.1) | collective-permute-done | bytes 110624 | tf_op jit(solution)/shard_map/ppermute | solution.py:718
  28.2 6.6 %all-to-all-done = bf16[4,256,768]{2,1,0:T(8,128)(2,1)S(1)} async-done(((bf16[4,256,768]{2,1,0:T(8,128)(2,1)}), bf16[4,256,768]{2,1,0:T(8,128)(2,1)S(1)}, u32[]{:S(2)}, u32[]{:S(2)}) %all-to-all-start) | async-done | bytes 1572896 | tf_op jit(solution)/shard_map/all_to_all | solution.py:724
  34.9 1.2 collective-permute-start.3
  36.1 1.7 collective-permute-start.10
  37.8 2.6 collective-permute-start.11
  40.4 1.7 collective-permute-start.4
  42.6 6.3 %collective-permute-done.3.rest_3_ = bf16[4,48,1152]{2,1,0:T(8,128)(2,1)S(1)} collective-permute-done((bf16[4,48,1152]{2,1,0:T(8,128)(2,1)S(1)}, bf16[4,48,1152]{2,1,0:T(8,128)(2,1)S(1)}, u32[]{:S(2)}, u32[]{:S(2)}) %collective-permute-start.3) | collective-permute-done | bytes 442400 | tf_op jit(solution)/shard_map/ppermute | solution.py:718
  48.9 3.7 %collective-permute-start.12 = (bf16[48,1536]{1,0:T(8,128)(2,1)S(1)}, bf16[48,1536]{1,0:T(8,128)(2,1)S(1)}, u32[]{:S(2)}, u32[]{:S(2)}) collective-permute-start(bf16[48,1536]{1,0:T(8,128)(2,1)S(1)} %copy-done.29), channel_id=1, source_target_pairs={{0,24},{2,26},{4,28},{6,30},{8,16},{10,18},{12,20},{14,22},{16,8},... | collective-permute-start | bytes 442376 | tf_op jit(solution)/shard_map/ppermute | solution.py:718
  52.6 4.2 %first_norm.1.act_ref = bf16[1024,768]{1,0:T(8,128)(2,1)} custom-call(bf16[1024,768]{1,0:T(8,128)(2,1)} %bitcast.41, f32[1,768]{1,0:T(1,128)} %broadcast_in_dim.29.g_ref, f32[1,768]{1,0:T(1,128)} %broadcast_in_dim.30.b_ref), custom_call_target="tpu_custom_call" | custom-call | flops 786432 | bytes 393216 | tf_op jit(solution)/shard_map/first_norm/pallas_call | solution.py:107
  57.4 3.9 %collective-permute-done.4.rest_1_ = bf16[4,48,1152]{2,1,0:T(8,128)(2,1)S(1)} collective-permute-done((bf16[4,48,1152]{2,1,0:T(8,128)(2,1)S(1)}, bf16[4,48,1152]{2,1,0:T(8,128)(2,1)S(1)}, u32[]{:S(2)}, u32[]{:S(2)}) %collective-permute-start.4) | collective-permute-done | bytes 442400 | tf_op jit(solution)/shard_map/ppermute | solution.py:718
  61.9 1.7 collective-permute-start.14
  63.6 1.3 collective-permute-start.15
  65.4 1.3 collective-permute-done.7.rest_5_
  68.3 8.8 %project_qkv.1.q_ref.k_ref.v_ref = bf16[1024,2304]{1,0:T(8,128)(2,1)} custom-call(s32[3]{0:T(128)} %pad_add_fusion.ids, bf16[1024,768]{1,0:T(8,128)(2,1)} %first_norm.1.act_ref, f32[1,2304]{1,0:T(1,128)} %broadcast_in_dim.28.qb_ref, bf16[4,48,1152]{2,1,0:T(8,128)(2,1)} %copy-done.5, bf16[4,48,1152]{2,1,0:T(8,128)(2,1)} %copy-done.14, ...), custom_call_target="tpu_custom_call" | custom-call | flops 452984832 | bytes 1228800 | tf_op jit(solution)/shard_map/project_qkv/pallas_call | solution.py:133
  77.1 19.7 %attention.1 = (bf16[1024,768]{1,0:T(8,128)(2,1)}, f32[16,1024]{1,0:T(8,128)}) custom-call(s32[1,8]{1,0:T(1,128)} %dynamic-slice_bitcast_fusion.lens_ref, bf16[1024,2304]{1,0:T(8,128)(2,1)} %project_qkv.1.q_ref.k_ref.v_ref, bf16[1024,2304]{1,0:T(8,128)(2,1)} %project_qkv.1.q_ref.k_ref.v_ref, bf16[1024,2304]{1,0:T(8,128)(2,1)} %project_qkv.1.q_ref.k_ref.v_ref), custom_call_target="tpu_custom_call" | custom-call | flops 241591904 | bytes 786432 | tf_op jit(solution)/shard_map/attention/pallas_call | solution.py:210
  96.8 1.2 collective-permute-done.15.rest_3_
  98.5 1.5 collective-permute-done.17.rest_5_
  100.0 2.0 collective-permute-done.18.rest_6_
  102.0 0.8 copy-done.11
  102.8 3.6 %all-to-all-start.1 = ((bf16[4,256,768]{2,1,0:T(8,128)(2,1)}), bf16[4,256,768]{2,1,0:T(8,128)(2,1)S(1)}, u32[]{:S(2)}, u32[]{:S(2)}) async-start(bf16[4,256,768]{2,1,0:T(8,128)(2,1)} %param.17), calls=%async_computation.1 | async-start | bytes 3145728 | tf_op jit(solution)/shard_map/all_to_all | solution.py:724
  106.4 2.6 all-gather.2.cloned.1.call-done
  109.0 23.6 %mlp.1 = (f32[1024,768]{1,0:T(8,128)}, bf16[1024,768]{1,0:T(8,128)(2,1)}, bf16[1024,3072]{1,0:T(8,128)(2,1)}, bf16[1024,3072]{1,0:T(8,128)(2,1)}, bf16[1024,768]{1,0:T(8,128)(2,1)}) custom-call(s32[3]{0:T(128)} %pad_add_fusion.ids, bf16[1024,768]{1,0:T(8,128)(2,1)} %bitcast.42, bf16[1024,768]{1,0:T(8,128)(2,1)} %get-tuple-element.91.att_ref.o_ref, ...), custom_call_target="tpu_custom_call" | custom-call | flops 1358954496 | bytes 2949120 | tf_op jit(solution)/shard_map/mlp/pallas_call | solution.py:391
  132.6 3.6 %all-to-all-start.2 = ((bf16[4,256,768]{2,1,0:T(8,128)(2,1)}), bf16[4,256,768]{2,1,0:T(8,128)(2,1)S(1)}, u32[]{:S(2)}, u32[]{:S(2)}) async-start(bf16[4,256,768]{2,1,0:T(8,128)(2,1)} %bitcast.49), calls=%async_computation.2 | async-start | bytes 3145728 | tf_op jit(solution)/shard_map/all_to_all | solution.py:724
  136.4 22.7 %mlp_back.1 = (bf16[1024,3072]{1,0:T(8,128)(2,1)}, f32[1024,768]{1,0:T(8,128)}, bf16[1024,768]{1,0:T(8,128)(2,1)}, bf16[1024,768]{1,0:T(8,128)(2,1)}, f32[8,768]{1,0:T(8,128)}, /*index=5*/f32[8,3072]{1,0:T(8,128)}) custom-call(s32[3]{0:T(128)} %pad_add_fusion.ids, bf16[1024,768]{1,0:T(8,128)(2,1)} %bitcast.47, f32[1024,768]{1,0:T(8,128)} %get-tuple-element.105.mid_ref, ...), custom_call_target="tpu_custom_call" | custom-call | flops 1358954496 | bytes 2949120 | tf_op jit(solution)/shard_map/mlp_back/pallas_call | solution.py:455
  159.1 11.7 %up_outer.1 = bf16[2,768,1920]{2,1,0:T(8,128)(2,1)} custom-call(bf16[1024,768]{1,0:T(8,128)(2,1)} %get-tuple-element.111.act_ref, bf16[1024,3072]{1,0:T(8,128)(2,1)} %get-tuple-element.112.du_ref, bf16[1024,768]{1,0:T(8,128)(2,1)} %get-tuple-element.91.att_ref.o_ref, bf16[1024,768]{1,0:T(8,128)(2,1)} %get-tuple-element.113.dy_ref), custom_call_target="tpu_custom_call" | custom-call | flops 754974720 | bytes 2113536 | tf_op jit(solution)/shard_map/up_outer/pallas_call | solution.py:530
  170.9 10.5 %down_outer.1 = (bf16[3072,384]{1,0:T(8,128)(2,1)}, bf16[3072,384]{1,0:T(8,128)(2,1)}) custom-call(s32[3]{0:T(128)} %pad_add_fusion.ids, bf16[1024,3072]{1,0:T(8,128)(2,1)} %get-tuple-element.114.a_ref, bf16[1024,768]{1,0:T(8,128)(2,1)} %bitcast.48), custom_call_target="tpu_custom_call" | custom-call | flops 603979776 | bytes 1572864 | tf_op jit(solution)/shard_map/down_outer/pallas_call | solution.py:500
  181.7 4.5 %collective-permute-done.20.theirs = bf16[3072,384]{1,0:T(8,128)(2,1)S(1)} collective-permute-done((bf16[3072,384]{1,0:T(8,128)(2,1)}, bf16[3072,384]{1,0:T(8,128)(2,1)S(1)}, u32[]{:S(2)}, u32[]{:S(2)}) %collective-permute-start.20) | collective-permute-done | bytes 2359328 | tf_op jit(solution)/shard_map/ppermute | solution.py:718
  186.2 1.4 copy-done.12
  187.6 4.3 %down_merge.1 = (bf16[4,192,384]{2,1,0:T(8,128)(2,1)}, bf16[4,192,384]{2,1,0:T(8,128)(2,1)}, bf16[4,192,384]{2,1,0:T(8,128)(2,1)}, bf16[4,192,384]{2,1,0:T(8,128)(2,1)}) custom-call(s32[3]{0:T(128)} %pad_add_fusion.ids, bf16[3072,384]{1,0:T(8,128)(2,1)} %get-tuple-element.115.mine, bf16[3072,384]{1,0:T(8,128)(2,1)} %copy-done.12), custom_call_target="tpu_custom_call" | custom-call | flops 294912 | bytes 884736 | tf_op jit(solution)/shard_map/down_merge/pallas_call | solution.py:590
  191.9 1.7 collective-permute-start.21
  193.6 1.5 collective-permute-start.22
  195.3 25.8 %attention_back.1.dqkv_ref = bf16[1024,2304]{1,0:T(8,128)(2,1)} custom-call(s32[1,8]{1,0:T(1,128)} %dynamic-slice_bitcast_fusion.lens_ref, bf16[1024,2304]{1,0:T(8,128)(2,1)} %project_qkv.1.q_ref.k_ref.v_ref, bf16[1024,2304]{1,0:T(8,128)(2,1)} %project_qkv.1.q_ref.k_ref.v_ref, bf16[1024,2304]{1,0:T(8,128)(2,1)} %project_qkv.1.q_ref.k_ref.v_ref, ...), custom_call_target="tpu_custom_call" | custom-call | flops 603979776 | bytes 1572864 | tf_op jit(solution)/shard_map/attention_back/pallas_call | solution.py:295
  221.5 10.2 %qkv_outer.1 = (bf16[768,1152]{1,0:T(8,128)(2,1)}, bf16[768,1152]{1,0:T(8,128)(2,1)}) custom-call(s32[3]{0:T(128)} %pad_add_fusion.ids, bf16[1024,768]{1,0:T(8,128)(2,1)} %first_norm.1.act_ref, bf16[1024,2304]{1,0:T(8,128)(2,1)} %attention_back.1.dqkv_ref), custom_call_target="tpu_custom_call" | custom-call | flops 452984832 | bytes 1228800 | tf_op jit(solution)/shard_map/qkv_outer/pallas_call | solution.py:559
  231.9 0.9 slice.105
  232.8 2.7 down_add.1
  235.5 3.5 %all-to-all-start.3 = ((bf16[4,192,384]{2,1,0:T(8,128)(2,1)}), bf16[4,192,384]{2,1,0:T(8,128)(2,1)S(1)}, u32[]{:S(2)}, u32[]{:S(2)}) async-start(bf16[4,192,384]{2,1,0:T(8,128)(2,1)} %down_add.1), calls=%async_computation.3 | async-start | bytes 1179648 | tf_op jit(solution)/shard_map/all_to_all | solution.py:771
  239.1 3.7 %qkv_merge.1 = (bf16[4,48,1152]{2,1,0:T(8,128)(2,1)}, bf16[4,48,1152]{2,1,0:T(8,128)(2,1)}, bf16[4,48,1152]{2,1,0:T(8,128)(2,1)}, bf16[4,48,1152]{2,1,0:T(8,128)(2,1)}) custom-call(s32[3]{0:T(128)} %pad_add_fusion.ids, bf16[768,1152]{1,0:T(8,128)(2,1)} %get-tuple-element.127.mine, bf16[768,1152]{1,0:T(8,128)(2,1)} %collective-permute-done.24.theirs), custom_call_target="tpu_custom_call" | custom-call | flops 221184 | bytes 663552 | tf_op jit(solution)/shard_map/qkv_merge/pallas_call | solution.py:590
  242.8 1.2 collective-permute-start.28
  244.0 1.5 collective-permute-start.29
  245.4 0.8 collective-permute-start.30
  246.3 12.9 %input_grad.1 = (bf16[256,768]{1,0:T(8,128)(2,1)}, bf16[256,768]{1,0:T(8,128)(2,1)}, bf16[256,768]{1,0:T(8,128)(2,1)}, bf16[256,768]{1,0:T(8,128)(2,1)}, f32[8,2304]{1,0:T(8,128)}) custom-call(s32[3]{0:T(128)} %pad_add_fusion.ids, bf16[1024,768]{1,0:T(8,128)(2,1)} %bitcast.43, f32[1024,768]{1,0:T(8,128)} %get-tuple-element.107.dm_ref, ...), custom_call_target="tpu_custom_call" | custom-call | flops 452984832 | bytes 1818624 | tf_op jit(solution)/shard_map/input_grad/pallas_call | solution.py:671
  259.2 1.2 collective-permute-start.25
  260.4 1.4 collective-permute-start.26
  261.8 0.9 slice_reduce_fusion.4
  262.8 1.0 collective-permute-start.27
  263.9 5.2 %collective-permute-done.30.d = bf16[4,48,1152]{2,1,0:T(8,128)(2,1)S(1)} collective-permute-done((bf16[4,48,1152]{2,1,0:T(8,128)(2,1)}, bf16[4,48,1152]{2,1,0:T(8,128)(2,1)S(1)}, u32[]{:S(2)}, u32[]{:S(2)}) %collective-permute-start.30) | collective-permute-done | bytes 442400 | tf_op jit(solution)/shard_map/ppermute | solution.py:718
  269.8 2.3 qkv_add.1
  272.1 1.2 collective-permute-done.34
  273.4 1.9 collective-permute-start.35
  275.3 2.1 collective-permute-done.35
  277.4 3.2 %collective-permute-start.36 = (f32[72,128]{1,0:T(8,128)S(1)}, f32[72,128]{1,0:T(8,128)S(1)}, u32[]{:S(2)}, u32[]{:S(2)}) collective-permute-start(f32[72,128]{1,0:T(8,128)S(1)} %add.67), channel_id=1, source_target_pairs={{0,16},{2,18},{4,20},{6,22},{8,24},{10,26},{12,28},{14,30},{16,0},... | collective-permute-start | bytes 110600 | tf_op jit(solution)/shard_map/ppermute | solution.py:718
  280.6 2.3 collective-permute-start.31
  283.4 2.4 collective-permute-start.32
  285.8 2.0 collective-permute-start.33
  287.8 1.7 collective-permute-start.37
  290.3 3.9 %join.1 = bf16[4,256,768]{2,1,0:T(8,128)(2,1)} custom-call(s32[3]{0:T(128)} %pad_add_fusion.ids, bf16[256,768]{1,0:T(8,128)(2,1)} %get-tuple-element.134.refs_0_, bf16[256,768]{1,0:T(8,128)(2,1)} %copy-done.26, bf16[256,768]{1,0:T(8,128)(2,1)} %copy-done.27, bf16[256,768]{1,0:T(8,128)(2,1)} %copy-done.28), custom_call_target="tpu_custom_call" | custom-call | flops 125 | bytes 393216 | tf_op jit(solution)/shard_map/join/pallas_call | solution.py:701
  296.2 2.0 collective-permute-done.38
  299.5 4.0 %reduce-scatter.2.cloned.1.call-done.a_ref = bf16[48,1920]{1,0:T(8,128)(2,1)} async-done(((bf16[1536,1920]{1,0:T(8,128)(2,1)}), bf16[48,1920]{1,0:T(8,128)(2,1)}) %reduce-scatter.2.cloned.1.call-update) | async-done | bytes 184336 | tf_op jit(solution)/shard_map/reduce_scatter | solution.py:789
  303.5 1.7 split.1
  305.2 1.1 copy.41
  (163 shorter events, 16.6 us)
Async XLA Ops:
  7.2 15.7 %copy-start = (s32[4,4,8]{2,1,0:T(4,128)S(1)}, s32[4,4,8]{2,1,0:T(4,128)}, u32[]{:S(2)}) copy-start(s32[4,4,8]{2,1,0:T(4,128)} %param.18) | copy-start | bytes 1540
  7.2 101.8 %all-gather.2.cloned.1.call-start = ((), (), s32[]{:S(2)}) async-start(), calls=%async_computation.5 | async-start | bytes 6082560 | tf_op jit(solution)/shard_map/all_gather | solution.py:841
  8.9 9.8 %copy-start.39 = (f32[768]{0:T(1024)S(1)}, f32[768]{0:T(1024)}, u32[]{:S(2)}) copy-start(f32[768]{0:T(1024)} %param.23) | copy-start | bytes 9220
  8.9 9.8 %copy-start.40 = (f32[768]{0:T(1024)S(1)}, f32[768]{0:T(1024)}, u32[]{:S(2)}) copy-start(f32[768]{0:T(1024)} %param.22) | copy-start | bytes 9220
  8.9 10.4 %copy-start.33 = (f32[768]{0:T(1024)S(1)}, f32[768]{0:T(1024)}, u32[]{:S(2)}) copy-start(f32[768]{0:T(1024)} %param.19) | copy-start | bytes 9220
  8.9 11.0 %copy-start.34 = (f32[768]{0:T(1024)S(1)}, f32[768]{0:T(1024)}, u32[]{:S(2)}) copy-start(f32[768]{0:T(1024)} %param.20) | copy-start | bytes 9220
  8.9 11.6 %copy-start.35 = (f32[768]{0:T(1024)S(1)}, f32[768]{0:T(1024)}, u32[]{:S(2)}) copy-start(f32[768]{0:T(1024)} %param.25) | copy-start | bytes 9220
  8.9 12.1 %copy-start.36 = (f32[768]{0:T(1024)S(1)}, f32[768]{0:T(1024)}, u32[]{:S(2)}) copy-start(f32[768]{0:T(1024)} %param.26) | copy-start | bytes 9220
  8.9 12.7 %copy-start.37 = (f32[768]{0:T(1024)S(1)}, f32[768]{0:T(1024)}, u32[]{:S(2)}) copy-start(f32[768]{0:T(1024)} %param.27) | copy-start | bytes 9220
  9.0 13.3 %copy-start.38 = (f32[768]{0:T(1024)S(1)}, f32[768]{0:T(1024)}, u32[]{:S(2)}) copy-start(f32[768]{0:T(1024)} %param.31) | copy-start | bytes 9220
  9.0 27.1 %copy-start.29 = (bf16[48,1536]{1,0:T(8,128)(2,1)S(1)}, bf16[48,1536]{1,0:T(8,128)(2,1)}, u32[]{:S(2)}) copy-start(bf16[48,1536]{1,0:T(8,128)(2,1)} %param.28) | copy-start | bytes 442372
  9.0 25.9 %all-to-all-start = ((bf16[4,256,768]{2,1,0:T(8,128)(2,1)}), bf16[4,256,768]{2,1,0:T(8,128)(2,1)S(1)}, u32[]{:S(2)}, u32[]{:S(2)}) async-start(bf16[4,256,768]{2,1,0:T(8,128)(2,1)} %param.16), calls=%async_computation | async-start | bytes 3145728 | tf_op jit(solution)/shard_map/all_to_all | solution.py:724
  14.3 9.6 %collective-permute-start = (bf16[48,1152]{1,0:T(8,128)(2,1)S(1)}, bf16[48,1152]{1,0:T(8,128)(2,1)S(1)}, u32[]{:S(2)}, u32[]{:S(2)}) collective-permute-start(bf16[48,1152]{1,0:T(8,128)(2,1)S(1)} %copy-done.30), channel_id=1, source_target_pairs={{0,8},{2,10},{4,12},{6,14},{8,0},{10,2},{12,4},{14,6},{16,24},{18,... | collective-permute-start | bytes 331784 | tf_op jit(solution)/shard_map/ppermute | solution.py:718
  15.9 12.3 %collective-permute-start.1 = (bf16[48,1152]{1,0:T(8,128)(2,1)S(1)}, bf16[48,1152]{1,0:T(8,128)(2,1)S(1)}, u32[]{:S(2)}, u32[]{:S(2)}) collective-permute-start(bf16[48,1152]{1,0:T(8,128)(2,1)S(1)} %copy-done.30), channel_id=1, source_target_pairs={{0,16},{2,18},{4,20},{6,22},{8,24},{10,26},{12,28},{14,30},{16,0},... | collective-permute-start | bytes 331784 | tf_op jit(solution)/shard_map/ppermute | solution.py:718
  18.5 9.7 %collective-permute-start.2 = (bf16[48,1152]{1,0:T(8,128)(2,1)S(1)}, bf16[48,1152]{1,0:T(8,128)(2,1)S(1)}, u32[]{:S(2)}, u32[]{:S(2)}) collective-permute-start(bf16[48,1152]{1,0:T(8,128)(2,1)S(1)} %copy-done.30), channel_id=1, source_target_pairs={{0,24},{2,26},{4,28},{6,30},{8,16},{10,18},{12,20},{14,22},{16,8},... | collective-permute-start | bytes 331784 | tf_op jit(solution)/shard_map/ppermute | solution.py:718
  28.2 39.1 %copy-start.5 = (bf16[4,48,1152]{2,1,0:T(8,128)(2,1)}, bf16[4,48,1152]{2,1,0:T(8,128)(2,1)S(1)}, u32[]{:S(2)}) copy-start(bf16[4,48,1152]{2,1,0:T(8,128)(2,1)S(1)} %pad_maximum_fusion.1.rest_0_) | copy-start | bytes 1327108
  34.9 17.8 %copy-start.2 = (bf16[4,256,768]{2,1,0:T(8,128)(2,1)}, bf16[4,256,768]{2,1,0:T(8,128)(2,1)S(1)}, u32[]{:S(2)}) copy-start(bf16[4,256,768]{2,1,0:T(8,128)(2,1)S(1)} %all-to-all-done) | copy-start | bytes 4718596
  34.9 14.0 %collective-permute-start.3 = (bf16[4,48,1152]{2,1,0:T(8,128)(2,1)S(1)}, bf16[4,48,1152]{2,1,0:T(8,128)(2,1)S(1)}, u32[]{:S(2)}, u32[]{:S(2)}) collective-permute-start(bf16[4,48,1152]{2,1,0:T(8,128)(2,1)S(1)} %pad_maximum_fusion.1.rest_0_), channel_id=1, source_target_pairs={{0,6},{2,4},{4,2},{6,0},{8,14},{10,12},{12,10},{14,8},{16,22},{18,... | collective-permute-start | bytes 1327112 | tf_op jit(solution)/shard_map/ppermute | solution.py:718
  36.1 20.7 %collective-permute-start.10 = (bf16[48,1536]{1,0:T(8,128)(2,1)S(1)}, bf16[48,1536]{1,0:T(8,128)(2,1)S(1)}, u32[]{:S(2)}, u32[]{:S(2)}) collective-permute-start(bf16[48,1536]{1,0:T(8,128)(2,1)S(1)} %copy-done.29), channel_id=1, source_target_pairs={{0,8},{2,10},{4,12},{6,14},{8,0},{10,2},{12,4},{14,6},{16,24},{18,... | collective-permute-start | bytes 442376 | tf_op jit(solution)/shard_map/ppermute | solution.py:718
  37.8 19.0 %collective-permute-start.11 = (bf16[48,1536]{1,0:T(8,128)(2,1)S(1)}, bf16[48,1536]{1,0:T(8,128)(2,1)S(1)}, u32[]{:S(2)}, u32[]{:S(2)}) collective-permute-start(bf16[48,1536]{1,0:T(8,128)(2,1)S(1)} %copy-done.29), channel_id=1, source_target_pairs={{0,16},{2,18},{4,20},{6,22},{8,24},{10,26},{12,28},{14,30},{16,0},... | collective-permute-start | bytes 442376 | tf_op jit(solution)/shard_map/ppermute | solution.py:718
  40.4 21.0 %collective-permute-start.4 = (bf16[4,48,1152]{2,1,0:T(8,128)(2,1)S(1)}, bf16[4,48,1152]{2,1,0:T(8,128)(2,1)S(1)}, u32[]{:S(2)}, u32[]{:S(2)}) collective-permute-start(bf16[4,48,1152]{2,1,0:T(8,128)(2,1)S(1)} %pad_maximum_fusion.1.rest_0_), channel_id=1, source_target_pairs={{0,2},{2,0},{4,6},{6,4},{8,10},{10,8},{12,14},{14,12},{16,18},{18,... | collective-permute-start | bytes 1327112 | tf_op jit(solution)/shard_map/ppermute | solution.py:718
  42.1 19.3 %collective-permute-start.5 = (bf16[4,48,1152]{2,1,0:T(8,128)(2,1)S(1)}, bf16[4,48,1152]{2,1,0:T(8,128)(2,1)S(1)}, u32[]{:S(2)}, u32[]{:S(2)}) collective-permute-start(bf16[4,48,1152]{2,1,0:T(8,128)(2,1)S(1)} %pad_maximum_fusion.1.rest_0_), channel_id=1, source_target_pairs={{0,4},{2,6},{4,0},{6,2},{8,12},{10,14},{12,8},{14,10},{16,20},{18,... | collective-permute-start | bytes 1327112 | tf_op jit(solution)/shard_map/ppermute | solution.py:718
  48.9 8.4 %collective-permute-start.12 = (bf16[48,1536]{1,0:T(8,128)(2,1)S(1)}, bf16[48,1536]{1,0:T(8,128)(2,1)S(1)}, u32[]{:S(2)}, u32[]{:S(2)}) collective-permute-start(bf16[48,1536]{1,0:T(8,128)(2,1)S(1)} %copy-done.29), channel_id=1, source_target_pairs={{0,24},{2,26},{4,28},{6,30},{8,16},{10,18},{12,20},{14,22},{16,8},... | collective-permute-start | bytes 442376 | tf_op jit(solution)/shard_map/ppermute | solution.py:718
  56.8 8.1 %collective-permute-start.6 = (bf16[4,48,1152]{2,1,0:T(8,128)(2,1)S(1)}, bf16[4,48,1152]{2,1,0:T(8,128)(2,1)S(1)}, u32[]{:S(2)}, u32[]{:S(2)}) collective-permute-start(bf16[4,48,1152]{2,1,0:T(8,128)(2,1)S(1)} %pad_maximum_fusion.1.rest_0_), channel_id=1, source_target_pairs={{0,1},{1,0},{2,3},{3,2},{4,5},{5,4},{6,7},{7,6},{8,9},{9,8},{10,11... | collective-permute-start | bytes 1327112 | tf_op jit(solution)/shard_map/ppermute | solution.py:718
  56.8 8.1 %collective-permute-start.9 = (bf16[4,48,1152]{2,1,0:T(8,128)(2,1)S(1)}, bf16[4,48,1152]{2,1,0:T(8,128)(2,1)S(1)}, u32[]{:S(2)}, u32[]{:S(2)}) collective-permute-start(bf16[4,48,1152]{2,1,0:T(8,128)(2,1)S(1)} %collective-permute-done.3.rest_3_), channel_id=1, source_target_pairs={{0,1},{1,0},{2,3},{3,2},{4,5},{5,4},{6,7},{7,6},{8,9},{9,8},{10,11... | collective-permute-start | bytes 1327112 | tf_op jit(solution)/shard_map/ppermute | solution.py:718
  57.4 19.7 %copy-start.4 = (bf16[4,48,1536]{2,1,0:T(8,128)(2,1)}, bf16[4,48,1536]{2,1,0:T(8,128)(2,1)S(1)}, u32[]{:S(2)}) copy-start(bf16[4,48,1536]{2,1,0:T(8,128)(2,1)S(1)} %pad_maximum_fusion.rest_0_) | copy-start | bytes 1769476
  61.3 35.4 %collective-permute-start.13 = (bf16[4,48,1536]{2,1,0:T(8,128)(2,1)S(1)}, bf16[4,48,1536]{2,1,0:T(8,128)(2,1)S(1)}, u32[]{:S(2)}, u32[]{:S(2)}) collective-permute-start(bf16[4,48,1536]{2,1,0:T(8,128)(2,1)S(1)} %pad_maximum_fusion.rest_0_), channel_id=1, source_target_pairs={{0,2},{2,0},{4,6},{6,4},{8,10},{10,8},{12,14},{14,12},{16,18},{18,... | collective-permute-start | bytes 1769480 | tf_op jit(solution)/shard_map/ppermute | solution.py:718
  61.9 34.9 %collective-permute-start.14 = (bf16[4,48,1536]{2,1,0:T(8,128)(2,1)S(1)}, bf16[4,48,1536]{2,1,0:T(8,128)(2,1)S(1)}, u32[]{:S(2)}, u32[]{:S(2)}) collective-permute-start(bf16[4,48,1536]{2,1,0:T(8,128)(2,1)S(1)} %pad_maximum_fusion.rest_0_), channel_id=1, source_target_pairs={{0,4},{2,6},{4,0},{6,2},{8,12},{10,14},{12,8},{14,10},{16,20},{18,... | collective-permute-start | bytes 1769480 | tf_op jit(solution)/shard_map/ppermute | solution.py:718
  63.6 34.3 %collective-permute-start.15 = (bf16[4,48,1536]{2,1,0:T(8,128)(2,1)S(1)}, bf16[4,48,1536]{2,1,0:T(8,128)(2,1)S(1)}, u32[]{:S(2)}, u32[]{:S(2)}) collective-permute-start(bf16[4,48,1536]{2,1,0:T(8,128)(2,1)S(1)} %pad_maximum_fusion.rest_0_), channel_id=1, source_target_pairs={{0,6},{2,4},{4,2},{6,0},{8,14},{10,12},{12,10},{14,8},{16,22},{18,... | collective-permute-start | bytes 1769480 | tf_op jit(solution)/shard_map/ppermute | solution.py:718
  64.9 1.8 collective-permute-start.7
  64.9 2.4 collective-permute-start.8
  66.7 31.8 %collective-permute-start.16 = (bf16[4,48,1536]{2,1,0:T(8,128)(2,1)S(1)}, bf16[4,48,1536]{2,1,0:T(8,128)(2,1)S(1)}, u32[]{:S(2)}, u32[]{:S(2)}) collective-permute-start(bf16[4,48,1536]{2,1,0:T(8,128)(2,1)S(1)} %pad_maximum_fusion.rest_0_), channel_id=1, source_target_pairs={{0,1},{1,0},{2,3},{3,2},{4,5},{5,4},{6,7},{7,6},{8,9},{9,8},{10,11... | collective-permute-start | bytes 1769480 | tf_op jit(solution)/shard_map/ppermute | solution.py:718
  96.8 12.2 %copy-start.6 = (bf16[4,48,1536]{2,1,0:T(8,128)(2,1)}, bf16[4,48,1536]{2,1,0:T(8,128)(2,1)S(1)}, u32[]{:S(2)}) copy-start(bf16[4,48,1536]{2,1,0:T(8,128)(2,1)S(1)} %collective-permute-done.13.rest_1_) | copy-start | bytes 1769476
  98.0 2.0 collective-permute-start.17
  98.0 4.0 %collective-permute-start.18 = (bf16[4,48,1536]{2,1,0:T(8,128)(2,1)S(1)}, bf16[4,48,1536]{2,1,0:T(8,128)(2,1)S(1)}, u32[]{:S(2)}, u32[]{:S(2)}) collective-permute-start(bf16[4,48,1536]{2,1,0:T(8,128)(2,1)S(1)} %collective-permute-done.14.rest_2_), channel_id=1, source_target_pairs={{0,1},{1,0},{2,3},{3,2},{4,5},{5,4},{6,7},{7,6},{8,9},{9,8},{10,11... | collective-permute-start | bytes 1769480 | tf_op jit(solution)/shard_map/ppermute | solution.py:718
  98.5 4.4 %collective-permute-start.19 = (bf16[4,48,1536]{2,1,0:T(8,128)(2,1)S(1)}, bf16[4,48,1536]{2,1,0:T(8,128)(2,1)}, u32[]{:S(2)}, u32[]{:S(2)}) collective-permute-start(bf16[4,48,1536]{2,1,0:T(8,128)(2,1)S(1)} %collective-permute-done.15.rest_3_), channel_id=1, source_target_pairs={{0,1},{1,0},{2,3},{3,2},{4,5},{5,4},{6,7},{7,6},{8,9},{9,8},{10,11... | collective-permute-start | bytes 1769480 | tf_op jit(solution)/shard_map/ppermute | solution.py:718
  102.8 29.8 %all-to-all-start.1 = ((bf16[4,256,768]{2,1,0:T(8,128)(2,1)}), bf16[4,256,768]{2,1,0:T(8,128)(2,1)S(1)}, u32[]{:S(2)}, u32[]{:S(2)}) async-start(bf16[4,256,768]{2,1,0:T(8,128)(2,1)} %param.17), calls=%async_computation.1 | async-start | bytes 3145728 | tf_op jit(solution)/shard_map/all_to_all | solution.py:724
  132.6 26.5 %all-to-all-start.2 = ((bf16[4,256,768]{2,1,0:T(8,128)(2,1)}), bf16[4,256,768]{2,1,0:T(8,128)(2,1)S(1)}, u32[]{:S(2)}, u32[]{:S(2)}) async-start(bf16[4,256,768]{2,1,0:T(8,128)(2,1)} %bitcast.49), calls=%async_computation.2 | async-start | bytes 3145728 | tf_op jit(solution)/shard_map/all_to_all | solution.py:724
  136.2 167.3 %reduce-scatter.2.cloned.1.call-start = ((), (), s32[]{:S(2)}) async-start(), calls=%async_computation.6 | async-start | bytes 6082560 | tf_op jit(solution)/shard_map/reduce_scatter | solution.py:789
  181.4 4.7 %collective-permute-start.20 = (bf16[3072,384]{1,0:T(8,128)(2,1)}, bf16[3072,384]{1,0:T(8,128)(2,1)S(1)}, u32[]{:S(2)}, u32[]{:S(2)}) collective-permute-start(bf16[3072,384]{1,0:T(8,128)(2,1)} %get-tuple-element.116), channel_id=1, source_target_pairs={{0,1},{1,0},{2,3},{3,2},{4,5},{5,4},{6,7},{7,6},{8,9},{9,8},{10,11... | collective-permute-start | bytes 7077896 | tf_op jit(solution)/shard_map/ppermute | solution.py:718
  191.9 29.3 %collective-permute-start.21 = (bf16[4,192,384]{2,1,0:T(8,128)(2,1)}, bf16[4,192,384]{2,1,0:T(8,128)(2,1)S(1)}, u32[]{:S(2)}, u32[]{:S(2)}) collective-permute-start(bf16[4,192,384]{2,1,0:T(8,128)(2,1)} %get-tuple-element.118), channel_id=1, source_target_pairs={{0,2},{2,0},{4,6},{6,4},{8,10},{10,8},{12,14},{14,12},{16,18},{18,... | collective-permute-start | bytes 1769480 | tf_op jit(solution)/shard_map/ppermute | solution.py:718
  193.6 27.9 %collective-permute-start.22 = (bf16[4,192,384]{2,1,0:T(8,128)(2,1)}, bf16[4,192,384]{2,1,0:T(8,128)(2,1)S(1)}, u32[]{:S(2)}, u32[]{:S(2)}) collective-permute-start(bf16[4,192,384]{2,1,0:T(8,128)(2,1)} %get-tuple-element.119), channel_id=1, source_target_pairs={{0,4},{2,6},{4,0},{6,2},{8,12},{10,14},{12,8},{14,10},{16,20},{18,... | collective-permute-start | bytes 1769480 | tf_op jit(solution)/shard_map/ppermute | solution.py:718
  195.1 26.5 %collective-permute-start.23 = (bf16[4,192,384]{2,1,0:T(8,128)(2,1)}, bf16[4,192,384]{2,1,0:T(8,128)(2,1)S(1)}, u32[]{:S(2)}, u32[]{:S(2)}) collective-permute-start(bf16[4,192,384]{2,1,0:T(8,128)(2,1)} %get-tuple-element.120), channel_id=1, source_target_pairs={{0,6},{2,4},{4,2},{6,0},{8,14},{10,12},{12,10},{14,8},{16,22},{18,... | collective-permute-start | bytes 1769480 | tf_op jit(solution)/shard_map/ppermute | solution.py:718
  221.1 11.6 %copy-start.32 = (f32[8,768]{1,0:T(8,128)S(1)}, f32[8,768]{1,0:T(8,128)}, u32[]{:S(2)}) copy-start(f32[8,768]{1,0:T(8,128)} %get-tuple-element.145) | copy-start | bytes 73732
  221.2 10.6 %copy-start.20 = (bf16[4,192,384]{2,1,0:T(8,128)(2,1)}, bf16[4,192,384]{2,1,0:T(8,128)(2,1)S(1)}, u32[]{:S(2)}) copy-start(bf16[4,192,384]{2,1,0:T(8,128)(2,1)S(1)} %collective-permute-done.21.b) | copy-start | bytes 1769476
  221.5 10.3 %copy-start.21 = (bf16[4,192,384]{2,1,0:T(8,128)(2,1)}, bf16[4,192,384]{2,1,0:T(8,128)(2,1)S(1)}, u32[]{:S(2)}) copy-start(bf16[4,192,384]{2,1,0:T(8,128)(2,1)S(1)} %collective-permute-done.22.c) | copy-start | bytes 1769476
  221.5 10.2 %copy-start.22 = (bf16[4,192,384]{2,1,0:T(8,128)(2,1)}, bf16[4,192,384]{2,1,0:T(8,128)(2,1)S(1)}, u32[]{:S(2)}) copy-start(bf16[4,192,384]{2,1,0:T(8,128)(2,1)S(1)} %collective-permute-done.23.d) | copy-start | bytes 1769476
  231.8 7.3 %collective-permute-start.24 = (bf16[768,1152]{1,0:T(8,128)(2,1)}, bf16[768,1152]{1,0:T(8,128)(2,1)}, u32[]{:S(2)}, u32[]{:S(2)}) collective-permute-start(bf16[768,1152]{1,0:T(8,128)(2,1)} %get-tuple-element.125), channel_id=1, source_target_pairs={{0,1},{1,0},{2,3},{3,2},{4,5},{5,4},{6,7},{7,6},{8,9},{9,8},{10,11... | collective-permute-start | bytes 5308424 | tf_op jit(solution)/shard_map/ppermute | solution.py:718
  235.5 45.1 %all-to-all-start.3 = ((bf16[4,192,384]{2,1,0:T(8,128)(2,1)}), bf16[4,192,384]{2,1,0:T(8,128)(2,1)S(1)}, u32[]{:S(2)}, u32[]{:S(2)}) async-start(bf16[4,192,384]{2,1,0:T(8,128)(2,1)} %down_add.1), calls=%async_computation.3 | async-start | bytes 1179648 | tf_op jit(solution)/shard_map/all_to_all | solution.py:771
  242.8 20.0 %collective-permute-start.28 = (bf16[4,48,1152]{2,1,0:T(8,128)(2,1)}, bf16[4,48,1152]{2,1,0:T(8,128)(2,1)S(1)}, u32[]{:S(2)}, u32[]{:S(2)}) collective-permute-start(bf16[4,48,1152]{2,1,0:T(8,128)(2,1)} %get-tuple-element.129), channel_id=1, source_target_pairs={{0,2},{2,0},{4,6},{6,4},{8,10},{10,8},{12,14},{14,12},{16,18},{18,... | collective-permute-start | bytes 1327112 | tf_op jit(solution)/shard_map/ppermute | solution.py:718
  244.0 19.9 %collective-permute-start.29 = (bf16[4,48,1152]{2,1,0:T(8,128)(2,1)}, bf16[4,48,1152]{2,1,0:T(8,128)(2,1)S(1)}, u32[]{:S(2)}, u32[]{:S(2)}) collective-permute-start(bf16[4,48,1152]{2,1,0:T(8,128)(2,1)} %get-tuple-element.130), channel_id=1, source_target_pairs={{0,4},{2,6},{4,0},{6,2},{8,12},{10,14},{12,8},{14,10},{16,20},{18,... | collective-permute-start | bytes 1327112 | tf_op jit(solution)/shard_map/ppermute | solution.py:718
  245.4 23.6 %collective-permute-start.30 = (bf16[4,48,1152]{2,1,0:T(8,128)(2,1)}, bf16[4,48,1152]{2,1,0:T(8,128)(2,1)S(1)}, u32[]{:S(2)}, u32[]{:S(2)}) collective-permute-start(bf16[4,48,1152]{2,1,0:T(8,128)(2,1)} %get-tuple-element.131), channel_id=1, source_target_pairs={{0,6},{2,4},{4,2},{6,0},{8,14},{10,12},{12,10},{14,8},{16,22},{18,... | collective-permute-start | bytes 1327112 | tf_op jit(solution)/shard_map/ppermute | solution.py:718
  259.2 26.6 %collective-permute-start.25 = (bf16[256,768]{1,0:T(8,128)(2,1)}, bf16[256,768]{1,0:T(8,128)(2,1)S(1)}, u32[]{:S(2)}, u32[]{:S(2)}) collective-permute-start(bf16[256,768]{1,0:T(8,128)(2,1)} %get-tuple-element.135), channel_id=1, source_target_pairs={{0,2},{2,0},{4,6},{6,4},{8,10},{10,8},{12,14},{14,12},{16,18},{18,... | collective-permute-start | bytes 1179656 | tf_op jit(solution)/shard_map/ppermute | solution.py:718
  260.4 27.4 %collective-permute-start.26 = (bf16[256,768]{1,0:T(8,128)(2,1)}, bf16[256,768]{1,0:T(8,128)(2,1)S(1)}, u32[]{:S(2)}, u32[]{:S(2)}) collective-permute-start(bf16[256,768]{1,0:T(8,128)(2,1)} %get-tuple-element.136), channel_id=1, source_target_pairs={{0,4},{2,6},{4,0},{6,2},{8,12},{10,14},{12,8},{14,10},{16,20},{18,... | collective-permute-start | bytes 1179656 | tf_op jit(solution)/shard_map/ppermute | solution.py:718
  262.8 25.0 %collective-permute-start.27 = (bf16[256,768]{1,0:T(8,128)(2,1)}, bf16[256,768]{1,0:T(8,128)(2,1)S(1)}, u32[]{:S(2)}, u32[]{:S(2)}) collective-permute-start(bf16[256,768]{1,0:T(8,128)(2,1)} %get-tuple-element.137), channel_id=1, source_target_pairs={{0,6},{2,4},{4,2},{6,0},{8,14},{10,12},{12,10},{14,8},{16,22},{18,... | collective-permute-start | bytes 1179656 | tf_op jit(solution)/shard_map/ppermute | solution.py:718
  272.1 1.2 collective-permute-start.34
  273.4 4.0 %collective-permute-start.35 = (f32[72,128]{1,0:T(8,128)S(1)}, f32[72,128]{1,0:T(8,128)S(1)}, u32[]{:S(2)}, u32[]{:S(2)}) collective-permute-start(f32[72,128]{1,0:T(8,128)S(1)} %add.66), channel_id=1, source_target_pairs={{0,8},{2,10},{4,12},{6,14},{8,0},{10,2},{12,4},{14,6},{16,24},{18,... | collective-permute-start | bytes 110600 | tf_op jit(solution)/shard_map/ppermute | solution.py:718
  277.4 6.0 %collective-permute-start.36 = (f32[72,128]{1,0:T(8,128)S(1)}, f32[72,128]{1,0:T(8,128)S(1)}, u32[]{:S(2)}, u32[]{:S(2)}) collective-permute-start(f32[72,128]{1,0:T(8,128)S(1)} %add.67), channel_id=1, source_target_pairs={{0,16},{2,18},{4,20},{6,22},{8,24},{10,26},{12,28},{14,30},{16,0},... | collective-permute-start | bytes 110600 | tf_op jit(solution)/shard_map/ppermute | solution.py:718
  280.6 14.2 %collective-permute-start.31 = (bf16[48,1152]{1,0:T(8,128)(2,1)}, bf16[48,1152]{1,0:T(8,128)(2,1)S(1)}, u32[]{:S(2)}, u32[]{:S(2)}) collective-permute-start(bf16[48,1152]{1,0:T(8,128)(2,1)} %get-tuple-element.139), channel_id=1, source_target_pairs={{0,8},{2,10},{4,12},{6,14},{8,0},{10,2},{12,4},{14,6},{16,24},{18,... | collective-permute-start | bytes 331784 | tf_op jit(solution)/shard_map/ppermute | solution.py:718
  283.4 12.0 %collective-permute-start.32 = (bf16[48,1152]{1,0:T(8,128)(2,1)}, bf16[48,1152]{1,0:T(8,128)(2,1)S(1)}, u32[]{:S(2)}, u32[]{:S(2)}) collective-permute-start(bf16[48,1152]{1,0:T(8,128)(2,1)} %get-tuple-element.140), channel_id=1, source_target_pairs={{0,16},{2,18},{4,20},{6,22},{8,24},{10,26},{12,28},{14,30},{16,0},... | collective-permute-start | bytes 331784 | tf_op jit(solution)/shard_map/ppermute | solution.py:718
  285.8 9.6 %collective-permute-start.33 = (bf16[48,1152]{1,0:T(8,128)(2,1)}, bf16[48,1152]{1,0:T(8,128)(2,1)S(1)}, u32[]{:S(2)}, u32[]{:S(2)}) collective-permute-start(bf16[48,1152]{1,0:T(8,128)(2,1)} %get-tuple-element.141), channel_id=1, source_target_pairs={{0,24},{2,26},{4,28},{6,30},{8,16},{10,18},{12,20},{14,22},{16,8},... | collective-permute-start | bytes 331784 | tf_op jit(solution)/shard_map/ppermute | solution.py:718
  287.8 6.4 %collective-permute-start.37 = (f32[72,128]{1,0:T(8,128)S(1)}, f32[72,128]{1,0:T(8,128)S(1)}, u32[]{:S(2)}, u32[]{:S(2)}) collective-permute-start(f32[72,128]{1,0:T(8,128)S(1)} %add.68), channel_id=1, source_target_pairs={{0,2},{2,0},{4,6},{6,4},{8,10},{10,8},{12,14},{14,12},{16,18},{18,... | collective-permute-start | bytes 110600 | tf_op jit(solution)/shard_map/ppermute | solution.py:718
  294.2 4.0 %collective-permute-start.38 = (f32[72,128]{1,0:T(8,128)S(1)}, f32[72,128]{1,0:T(8,128)S(1)}, u32[]{:S(2)}, u32[]{:S(2)}) collective-permute-start(f32[72,128]{1,0:T(8,128)S(1)} %add.69), channel_id=1, source_target_pairs={{0,4},{2,6},{4,0},{6,2},{8,12},{10,14},{12,8},{14,10},{16,20},{18,... | collective-permute-start | bytes 110600 | tf_op jit(solution)/shard_map/ppermute | solution.py:718
  295.4 10.9 %copy-start.1 = (s32[4,4,8]{2,1,0:T(4,128)S(1)}, s32[4,4,8]{2,1,0:T(4,128)}, u32[]{:S(2)}) copy-start(s32[4,4,8]{2,1,0:T(4,128)} %param.18) | copy-start | bytes 1540
  (22 other events, 79.7 us)
Sparse Core Ops, SparseCore 0:
  11.5 97.4 all-gather.1
  171.0 132.4 reduce-scatter.1

commit v6 on v5

--- a/solution.py
+++ b/solution.py
@@ -879,7 +879,8 @@
     if by_permutes:
         up_grad, proj_grad = split(scatter_narrow(up_outer_grad), FF // 2)
         down_got = from_peers(down_blocks, QUAD_STEPS)
-        act1 = after(act1, *down_got[1:])
+        output = lax.reduce_precision(output, 8, 7)
+        act1 = after(act1, output, *down_got[1:])
     qkv_sides = qkv_outer(ids, act1, dqkv)
     if by_permutes:
         down_got[0] = after(down_got[0], *qkv_sides)

time: 314 us -> 316 us (level)
  waiting for transfers between devices: 50.8 us -> 54.8 us
  starting transfers between devices: 62.3 us -> 58.5 us
    ppermute x39, waiting for transfers between devices: 37.5 us -> 41.9 us  [swap(): return lax.ppermute(block, axis, [(i, i ^ distance) for i in range(count)])]
    ppermute x39, starting transfers between devices: 46.1 us -> 41.8 us  [swap(): return lax.ppermute(block, axis, [(i, i ^ distance) for i in range(count)])]
  transfers between devices with their start and end apart: 45 -> 45, of which waited for: 19 -> 17; matrix products, arithmetic and copies ran while one was open for 3% -> 4% of each run, Pallas kernels for 50% -> 49%
where the time goes in v6:
time: 316 us; the launch traced here: 315 us
  Pallas kernels  168 us (53%)
  starting transfers between devices  58.5 us (19%)
  waiting for transfers between devices  54.8 us (17%)
  between operations  14.6 us (5%)
  local copies, waits for them, and re-layouts  13.7 us (4%)
  other arithmetic  5.29 us (2%)
    ppermute x39, waiting for transfers between devices, swap(): return lax.ppermute(block, axis, [(i, i ^ distance) for i in range(count)])  41.9 us
    ppermute x39, starting transfers between devices, swap(): return lax.ppermute(block, axis, [(i, i ^ distance) for i in range(count)])  41.8 us
    pallas_call x1, Pallas kernels, attention_back(): pl.pallas_call(attn_back_kernel, grid=(pairs,), in_specs=[pl.BlockSpec(me...  25.7 us
    pallas_call x1, Pallas kernels, mlp(): pl.pallas_call(functools.partial(mlp_kernel, len(w)), grid=(n // tile,),...  23.5 us
    pallas_call x1, Pallas kernels, mlp_back(): pl.pallas_call(functools.partial(mlp_back_kernel, len(w)), grid=(n // til...  22.7 us
    pallas_call x1, Pallas kernels, attention(): pl.pallas_call(attn_kernel, grid=(pairs,), in_specs=[pl.BlockSpec(memory_...  19.6 us
    pallas_call x1, Pallas kernels, input_grad(): pl.pallas_call(functools.partial(input_grad_kernel, len(w)), grid_spec=pl...  12.9 us
    all_to_all x3, starting transfers between devices, quad_swap(): lax.all_to_all(pieces, 'tok', 0, 0, axis_index_groups=groups, tiled=True)  12.4 us
  transfers between devices with their start and end apart: 45, of which 17 were waited for; matrix products, arithmetic and copies ran while one was open for 4% of the time, Pallas kernels for 49%

profile of v6, /device:TPU:0, one launch (start us, length us, event | category | flops | bytes accessed | tf_op | source)
XLA Modules:
  0.0 315.1 jit_solution(6110916383779516590)
XLA Ops:
  7.3 1.7 pad_maximum_fusion.2
  9.0 5.3 %all-to-all-start = ((bf16[4,256,768]{2,1,0:T(8,128)(2,1)}), bf16[4,256,768]{2,1,0:T(8,128)(2,1)S(1)}, u32[]{:S(2)}, u32[]{:S(2)}) async-start(bf16[4,256,768]{2,1,0:T(8,128)(2,1)} %param.16), calls=%async_computation | async-start | bytes 3145728 | tf_op jit(solution)/shard_map/all_to_all | solution.py:724
  14.3 1.6 collective-permute-start
  15.9 2.6 collective-permute-start.1
  23.9 4.2 %collective-permute-done.1 = bf16[48,1152]{1,0:T(8,128)(2,1)S(1)} collective-permute-done((bf16[48,1152]{1,0:T(8,128)(2,1)S(1)}, bf16[48,1152]{1,0:T(8,128)(2,1)S(1)}, u32[]{:S(2)}, u32[]{:S(2)}) %collective-permute-start.1) | collective-permute-done | bytes 110624 | tf_op jit(solution)/shard_map/ppermute | solution.py:718
  28.2 6.6 %all-to-all-done = bf16[4,256,768]{2,1,0:T(8,128)(2,1)S(1)} async-done(((bf16[4,256,768]{2,1,0:T(8,128)(2,1)}), bf16[4,256,768]{2,1,0:T(8,128)(2,1)S(1)}, u32[]{:S(2)}, u32[]{:S(2)}) %all-to-all-start) | async-done | bytes 1572896 | tf_op jit(solution)/shard_map/all_to_all | solution.py:724
  34.9 1.2 collective-permute-start.3
  36.1 1.7 collective-permute-start.10
  37.8 2.6 collective-permute-start.11
  40.4 1.7 collective-permute-start.4
  42.6 6.3 %collective-permute-done.3.rest_3_ = bf16[4,48,1152]{2,1,0:T(8,128)(2,1)S(1)} collective-permute-done((bf16[4,48,1152]{2,1,0:T(8,128)(2,1)S(1)}, bf16[4,48,1152]{2,1,0:T(8,128)(2,1)S(1)}, u32[]{:S(2)}, u32[]{:S(2)}) %collective-permute-start.3) | collective-permute-done | bytes 442400 | tf_op jit(solution)/shard_map/ppermute | solution.py:718
  48.9 3.7 %collective-permute-start.12 = (bf16[48,1536]{1,0:T(8,128)(2,1)S(1)}, bf16[48,1536]{1,0:T(8,128)(2,1)S(1)}, u32[]{:S(2)}, u32[]{:S(2)}) collective-permute-start(bf16[48,1536]{1,0:T(8,128)(2,1)S(1)} %copy-done.30), channel_id=1, source_target_pairs={{0,24},{2,26},{4,28},{6,30},{8,16},{10,18},{12,20},{14,22},{16,8},... | collective-permute-start | bytes 442376 | tf_op jit(solution)/shard_map/ppermute | solution.py:718
  52.6 4.2 %first_norm.1.act_ref = bf16[1024,768]{1,0:T(8,128)(2,1)} custom-call(bf16[1024,768]{1,0:T(8,128)(2,1)} %bitcast.41, f32[1,768]{1,0:T(1,128)} %broadcast_in_dim.29.g_ref, f32[1,768]{1,0:T(1,128)} %broadcast_in_dim.30.b_ref), custom_call_target="tpu_custom_call" | custom-call | flops 786432 | bytes 393216 | tf_op jit(solution)/shard_map/first_norm/pallas_call | solution.py:107
  57.4 3.9 %collective-permute-done.4.rest_1_ = bf16[4,48,1152]{2,1,0:T(8,128)(2,1)S(1)} collective-permute-done((bf16[4,48,1152]{2,1,0:T(8,128)(2,1)S(1)}, bf16[4,48,1152]{2,1,0:T(8,128)(2,1)S(1)}, u32[]{:S(2)}, u32[]{:S(2)}) %collective-permute-start.4) | collective-permute-done | bytes 442400 | tf_op jit(solution)/shard_map/ppermute | solution.py:718
  61.9 1.7 collective-permute-start.14
  63.6 1.3 collective-permute-start.15
  65.4 1.3 collective-permute-done.7.rest_5_
  68.2 8.8 %project_qkv.1.q_ref.k_ref.v_ref = bf16[1024,2304]{1,0:T(8,128)(2,1)} custom-call(s32[3]{0:T(128)} %pad_add_fusion.ids, bf16[1024,768]{1,0:T(8,128)(2,1)} %first_norm.1.act_ref, f32[1,2304]{1,0:T(1,128)} %broadcast_in_dim.28.qb_ref, bf16[4,48,1152]{2,1,0:T(8,128)(2,1)} %copy-done.5, bf16[4,48,1152]{2,1,0:T(8,128)(2,1)} %copy-done.15, ...), custom_call_target="tpu_custom_call" | custom-call | flops 452984832 | bytes 1228800 | tf_op jit(solution)/shard_map/project_qkv/pallas_call | solution.py:133
  77.1 19.6 %attention.1 = (bf16[1024,768]{1,0:T(8,128)(2,1)}, f32[16,1024]{1,0:T(8,128)}) custom-call(s32[1,8]{1,0:T(1,128)} %dynamic-slice_bitcast_fusion.lens_ref, bf16[1024,2304]{1,0:T(8,128)(2,1)} %project_qkv.1.q_ref.k_ref.v_ref, bf16[1024,2304]{1,0:T(8,128)(2,1)} %project_qkv.1.q_ref.k_ref.v_ref, bf16[1024,2304]{1,0:T(8,128)(2,1)} %project_qkv.1.q_ref.k_ref.v_ref), custom_call_target="tpu_custom_call" | custom-call | flops 241591904 | bytes 786432 | tf_op jit(solution)/shard_map/attention/pallas_call | solution.py:210
  96.8 1.2 collective-permute-done.15.rest_3_
  98.5 1.5 collective-permute-done.17.rest_5_
  100.0 2.0 collective-permute-done.18.rest_6_
  102.0 0.8 copy-done.11
  102.8 3.6 %all-to-all-start.1 = ((bf16[4,256,768]{2,1,0:T(8,128)(2,1)}), bf16[4,256,768]{2,1,0:T(8,128)(2,1)S(1)}, u32[]{:S(2)}, u32[]{:S(2)}) async-start(bf16[4,256,768]{2,1,0:T(8,128)(2,1)} %param.17), calls=%async_computation.1 | async-start | bytes 3145728 | tf_op jit(solution)/shard_map/all_to_all | solution.py:724
  106.4 2.6 all-gather.2.cloned.1.call-done
  109.0 23.5 %mlp.1 = (f32[1024,768]{1,0:T(8,128)}, bf16[1024,768]{1,0:T(8,128)(2,1)}, bf16[1024,3072]{1,0:T(8,128)(2,1)}, bf16[1024,3072]{1,0:T(8,128)(2,1)}, bf16[1024,768]{1,0:T(8,128)(2,1)}) custom-call(s32[3]{0:T(128)} %pad_add_fusion.ids, bf16[1024,768]{1,0:T(8,128)(2,1)} %bitcast.42, bf16[1024,768]{1,0:T(8,128)(2,1)} %get-tuple-element.91.att_ref.o_ref, ...), custom_call_target="tpu_custom_call" | custom-call | flops 1358954496 | bytes 2949120 | tf_op jit(solution)/shard_map/mlp/pallas_call | solution.py:391
  132.6 3.6 %all-to-all-start.2 = ((bf16[4,256,768]{2,1,0:T(8,128)(2,1)}), bf16[4,256,768]{2,1,0:T(8,128)(2,1)S(1)}, u32[]{:S(2)}, u32[]{:S(2)}) async-start(bf16[4,256,768]{2,1,0:T(8,128)(2,1)} %bitcast.49), calls=%async_computation.2 | async-start | bytes 3145728 | tf_op jit(solution)/shard_map/all_to_all | solution.py:724
  136.4 22.7 %mlp_back.1 = (bf16[1024,3072]{1,0:T(8,128)(2,1)}, f32[1024,768]{1,0:T(8,128)}, bf16[1024,768]{1,0:T(8,128)(2,1)}, bf16[1024,768]{1,0:T(8,128)(2,1)}, f32[8,768]{1,0:T(8,128)}, /*index=5*/f32[8,3072]{1,0:T(8,128)}) custom-call(s32[3]{0:T(128)} %pad_add_fusion.ids, bf16[1024,768]{1,0:T(8,128)(2,1)} %bitcast.47, f32[1024,768]{1,0:T(8,128)} %get-tuple-element.105.mid_ref, ...), custom_call_target="tpu_custom_call" | custom-call | flops 1358954496 | bytes 2949120 | tf_op jit(solution)/shard_map/mlp_back/pallas_call | solution.py:455
  159.1 11.7 %up_outer.1 = bf16[2,768,1920]{2,1,0:T(8,128)(2,1)} custom-call(bf16[1024,768]{1,0:T(8,128)(2,1)} %get-tuple-element.111.act_ref, bf16[1024,3072]{1,0:T(8,128)(2,1)} %get-tuple-element.112.du_ref, bf16[1024,768]{1,0:T(8,128)(2,1)} %get-tuple-element.91.att_ref.o_ref, bf16[1024,768]{1,0:T(8,128)(2,1)} %get-tuple-element.113.dy_ref), custom_call_target="tpu_custom_call" | custom-call | flops 754974720 | bytes 2113536 | tf_op jit(solution)/shard_map/up_outer/pallas_call | solution.py:530
  170.8 10.5 %down_outer.1 = (bf16[3072,384]{1,0:T(8,128)(2,1)}, bf16[3072,384]{1,0:T(8,128)(2,1)}) custom-call(s32[3]{0:T(128)} %pad_add_fusion.ids, bf16[1024,3072]{1,0:T(8,128)(2,1)} %get-tuple-element.114.a_ref, bf16[1024,768]{1,0:T(8,128)(2,1)} %bitcast.48), custom_call_target="tpu_custom_call" | custom-call | flops 603979776 | bytes 1572864 | tf_op jit(solution)/shard_map/down_outer/pallas_call | solution.py:500
  181.6 4.5 %collective-permute-done.20.theirs = bf16[3072,384]{1,0:T(8,128)(2,1)S(1)} collective-permute-done((bf16[3072,384]{1,0:T(8,128)(2,1)}, bf16[3072,384]{1,0:T(8,128)(2,1)S(1)}, u32[]{:S(2)}, u32[]{:S(2)}) %collective-permute-start.20) | collective-permute-done | bytes 2359328 | tf_op jit(solution)/shard_map/ppermute | solution.py:718
  186.1 1.4 copy-done.12
  187.4 4.3 %down_merge.1 = (bf16[4,192,384]{2,1,0:T(8,128)(2,1)}, bf16[4,192,384]{2,1,0:T(8,128)(2,1)}, bf16[4,192,384]{2,1,0:T(8,128)(2,1)}, bf16[4,192,384]{2,1,0:T(8,128)(2,1)}) custom-call(s32[3]{0:T(128)} %pad_add_fusion.ids, bf16[3072,384]{1,0:T(8,128)(2,1)} %get-tuple-element.115.mine, bf16[3072,384]{1,0:T(8,128)(2,1)} %copy-done.12), custom_call_target="tpu_custom_call" | custom-call | flops 294912 | bytes 884736 | tf_op jit(solution)/shard_map/down_merge/pallas_call | solution.py:590
  191.7 1.8 collective-permute-start.21
  193.5 1.5 collective-permute-start.22
  195.2 1.2 reduce_precision.3
  196.5 25.7 %attention_back.1.dqkv_ref = bf16[1024,2304]{1,0:T(8,128)(2,1)} custom-call(s32[1,8]{1,0:T(1,128)} %dynamic-slice_bitcast_fusion.lens_ref, bf16[1024,2304]{1,0:T(8,128)(2,1)} %project_qkv.1.q_ref.k_ref.v_ref, bf16[1024,2304]{1,0:T(8,128)(2,1)} %project_qkv.1.q_ref.k_ref.v_ref, bf16[1024,2304]{1,0:T(8,128)(2,1)} %project_qkv.1.q_ref.k_ref.v_ref, ...), custom_call_target="tpu_custom_call" | custom-call | flops 603979776 | bytes 1572864 | tf_op jit(solution)/shard_map/attention_back/pallas_call | solution.py:295
  222.3 9.9 %qkv_outer.1 = (bf16[768,1152]{1,0:T(8,128)(2,1)}, bf16[768,1152]{1,0:T(8,128)(2,1)}) custom-call(s32[3]{0:T(128)} %pad_add_fusion.ids, bf16[1024,768]{1,0:T(8,128)(2,1)} %first_norm.1.act_ref, bf16[1024,2304]{1,0:T(8,128)(2,1)} %attention_back.1.dqkv_ref), custom_call_target="tpu_custom_call" | custom-call | flops 452984832 | bytes 1228800 | tf_op jit(solution)/shard_map/qkv_outer/pallas_call | solution.py:559
  232.3 0.9 slice.105
  233.2 2.7 down_add.1
  236.0 3.9 %all-to-all-start.3 = ((bf16[4,192,384]{2,1,0:T(8,128)(2,1)}), bf16[4,192,384]{2,1,0:T(8,128)(2,1)S(1)}, u32[]{:S(2)}, u32[]{:S(2)}) async-start(bf16[4,192,384]{2,1,0:T(8,128)(2,1)} %down_add.1), calls=%async_computation.3 | async-start | bytes 1179648 | tf_op jit(solution)/shard_map/all_to_all | solution.py:771
  239.9 1.2 copy-done.13
  241.1 3.7 %qkv_merge.1 = (bf16[4,48,1152]{2,1,0:T(8,128)(2,1)}, bf16[4,48,1152]{2,1,0:T(8,128)(2,1)}, bf16[4,48,1152]{2,1,0:T(8,128)(2,1)}, bf16[4,48,1152]{2,1,0:T(8,128)(2,1)}) custom-call(s32[3]{0:T(128)} %pad_add_fusion.ids, bf16[768,1152]{1,0:T(8,128)(2,1)} %get-tuple-element.127.mine, bf16[768,1152]{1,0:T(8,128)(2,1)} %copy-done.13), custom_call_target="tpu_custom_call" | custom-call | flops 221184 | bytes 663552 | tf_op jit(solution)/shard_map/qkv_merge/pallas_call | solution.py:590
  244.8 1.6 collective-permute-start.28
  246.4 1.4 collective-permute-start.29
  248.3 12.9 %input_grad.1 = (bf16[256,768]{1,0:T(8,128)(2,1)}, bf16[256,768]{1,0:T(8,128)(2,1)}, bf16[256,768]{1,0:T(8,128)(2,1)}, bf16[256,768]{1,0:T(8,128)(2,1)}, f32[8,2304]{1,0:T(8,128)}) custom-call(s32[3]{0:T(128)} %pad_add_fusion.ids, bf16[1024,768]{1,0:T(8,128)(2,1)} %bitcast.43, f32[1024,768]{1,0:T(8,128)} %get-tuple-element.107.dm_ref, ...), custom_call_target="tpu_custom_call" | custom-call | flops 452984832 | bytes 1818624 | tf_op jit(solution)/shard_map/input_grad/pallas_call | solution.py:671
  261.2 1.6 collective-permute-start.25
  262.8 1.4 collective-permute-start.26
  264.2 0.9 slice_reduce_fusion.4
  265.9 6.2 %collective-permute-done.29.c = bf16[4,48,1152]{2,1,0:T(8,128)(2,1)S(1)} collective-permute-done((bf16[4,48,1152]{2,1,0:T(8,128)(2,1)}, bf16[4,48,1152]{2,1,0:T(8,128)(2,1)S(1)}, u32[]{:S(2)}, u32[]{:S(2)}) %collective-permute-start.29) | collective-permute-done | bytes 442400 | tf_op jit(solution)/shard_map/ppermute | solution.py:718
  272.0 0.8 copy-done.25
  273.6 2.3 qkv_add.1
  275.9 1.2 collective-permute-done.34
  277.1 2.2 collective-permute-start.35
  279.2 3.8 %collective-permute-done.35 = f32[72,128]{1,0:T(8,128)S(1)} collective-permute-done((f32[72,128]{1,0:T(8,128)S(1)}, f32[72,128]{1,0:T(8,128)S(1)}, u32[]{:S(2)}, u32[]{:S(2)}) %collective-permute-start.35) | collective-permute-done | bytes 36896 | tf_op jit(solution)/shard_map/ppermute | solution.py:718
  283.1 1.9 collective-permute-start.36
  285.7 2.6 collective-permute-done.36
  288.3 1.9 collective-permute-start.32
  291.0 0.9 add_bitcast_fusion
  291.9 3.9 %join.1 = bf16[4,256,768]{2,1,0:T(8,128)(2,1)} custom-call(s32[3]{0:T(128)} %pad_add_fusion.ids, bf16[256,768]{1,0:T(8,128)(2,1)} %get-tuple-element.134.refs_0_, bf16[256,768]{1,0:T(8,128)(2,1)} %copy-done.27, bf16[256,768]{1,0:T(8,128)(2,1)} %copy-done.28, bf16[256,768]{1,0:T(8,128)(2,1)} %copy-done.29), custom_call_target="tpu_custom_call" | custom-call | flops 125 | bytes 393216 | tf_op jit(solution)/shard_map/join/pallas_call | solution.py:701
  295.8 2.4 collective-permute-start.38
  298.2 2.7 collective-permute-done.32
  302.9 3.7 %reduce-scatter.2.cloned.1.call-done.a_ref = bf16[48,1920]{1,0:T(8,128)(2,1)} async-done(((bf16[1536,1920]{1,0:T(8,128)(2,1)}), bf16[48,1920]{1,0:T(8,128)(2,1)}) %reduce-scatter.2.cloned.1.call-update) | async-done | bytes 184336 | tf_op jit(solution)/shard_map/reduce_scatter | solution.py:789
  306.5 1.7 split.1
  (165 shorter events, 16.3 us)
Async XLA Ops:
  7.2 15.7 %copy-start = (s32[4,4,8]{2,1,0:T(4,128)S(1)}, s32[4,4,8]{2,1,0:T(4,128)}, u32[]{:S(2)}) copy-start(s32[4,4,8]{2,1,0:T(4,128)} %param.18) | copy-start | bytes 1540
  7.2 101.8 %all-gather.2.cloned.1.call-start = ((), (), s32[]{:S(2)}) async-start(), calls=%async_computation.5 | async-start | bytes 6082560 | tf_op jit(solution)/shard_map/all_gather | solution.py:841
  8.9 9.8 %copy-start.40 = (f32[768]{0:T(1024)S(1)}, f32[768]{0:T(1024)}, u32[]{:S(2)}) copy-start(f32[768]{0:T(1024)} %param.23) | copy-start | bytes 9220
  8.9 9.8 %copy-start.41 = (f32[768]{0:T(1024)S(1)}, f32[768]{0:T(1024)}, u32[]{:S(2)}) copy-start(f32[768]{0:T(1024)} %param.22) | copy-start | bytes 9220
  8.9 10.4 %copy-start.34 = (f32[768]{0:T(1024)S(1)}, f32[768]{0:T(1024)}, u32[]{:S(2)}) copy-start(f32[768]{0:T(1024)} %param.19) | copy-start | bytes 9220
  8.9 11.0 %copy-start.35 = (f32[768]{0:T(1024)S(1)}, f32[768]{0:T(1024)}, u32[]{:S(2)}) copy-start(f32[768]{0:T(1024)} %param.20) | copy-start | bytes 9220
  8.9 11.6 %copy-start.36 = (f32[768]{0:T(1024)S(1)}, f32[768]{0:T(1024)}, u32[]{:S(2)}) copy-start(f32[768]{0:T(1024)} %param.25) | copy-start | bytes 9220
  8.9 12.1 %copy-start.37 = (f32[768]{0:T(1024)S(1)}, f32[768]{0:T(1024)}, u32[]{:S(2)}) copy-start(f32[768]{0:T(1024)} %param.26) | copy-start | bytes 9220
  8.9 12.7 %copy-start.38 = (f32[768]{0:T(1024)S(1)}, f32[768]{0:T(1024)}, u32[]{:S(2)}) copy-start(f32[768]{0:T(1024)} %param.27) | copy-start | bytes 9220
  9.0 13.3 %copy-start.39 = (f32[768]{0:T(1024)S(1)}, f32[768]{0:T(1024)}, u32[]{:S(2)}) copy-start(f32[768]{0:T(1024)} %param.31) | copy-start | bytes 9220
  9.0 27.1 %copy-start.30 = (bf16[48,1536]{1,0:T(8,128)(2,1)S(1)}, bf16[48,1536]{1,0:T(8,128)(2,1)}, u32[]{:S(2)}) copy-start(bf16[48,1536]{1,0:T(8,128)(2,1)} %param.28) | copy-start | bytes 442372
  9.0 25.9 %all-to-all-start = ((bf16[4,256,768]{2,1,0:T(8,128)(2,1)}), bf16[4,256,768]{2,1,0:T(8,128)(2,1)S(1)}, u32[]{:S(2)}, u32[]{:S(2)}) async-start(bf16[4,256,768]{2,1,0:T(8,128)(2,1)} %param.16), calls=%async_computation | async-start | bytes 3145728 | tf_op jit(solution)/shard_map/all_to_all | solution.py:724
  14.3 9.6 %collective-permute-start = (bf16[48,1152]{1,0:T(8,128)(2,1)S(1)}, bf16[48,1152]{1,0:T(8,128)(2,1)S(1)}, u32[]{:S(2)}, u32[]{:S(2)}) collective-permute-start(bf16[48,1152]{1,0:T(8,128)(2,1)S(1)} %copy-done.31), channel_id=1, source_target_pairs={{0,8},{2,10},{4,12},{6,14},{8,0},{10,2},{12,4},{14,6},{16,24},{18,... | collective-permute-start | bytes 331784 | tf_op jit(solution)/shard_map/ppermute | solution.py:718
  15.9 12.3 %collective-permute-start.1 = (bf16[48,1152]{1,0:T(8,128)(2,1)S(1)}, bf16[48,1152]{1,0:T(8,128)(2,1)S(1)}, u32[]{:S(2)}, u32[]{:S(2)}) collective-permute-start(bf16[48,1152]{1,0:T(8,128)(2,1)S(1)} %copy-done.31), channel_id=1, source_target_pairs={{0,16},{2,18},{4,20},{6,22},{8,24},{10,26},{12,28},{14,30},{16,0},... | collective-permute-start | bytes 331784 | tf_op jit(solution)/shard_map/ppermute | solution.py:718
  18.5 9.7 %collective-permute-start.2 = (bf16[48,1152]{1,0:T(8,128)(2,1)S(1)}, bf16[48,1152]{1,0:T(8,128)(2,1)S(1)}, u32[]{:S(2)}, u32[]{:S(2)}) collective-permute-start(bf16[48,1152]{1,0:T(8,128)(2,1)S(1)} %copy-done.31), channel_id=1, source_target_pairs={{0,24},{2,26},{4,28},{6,30},{8,16},{10,18},{12,20},{14,22},{16,8},... | collective-permute-start | bytes 331784 | tf_op jit(solution)/shard_map/ppermute | solution.py:718
  28.2 39.1 %copy-start.5 = (bf16[4,48,1152]{2,1,0:T(8,128)(2,1)}, bf16[4,48,1152]{2,1,0:T(8,128)(2,1)S(1)}, u32[]{:S(2)}) copy-start(bf16[4,48,1152]{2,1,0:T(8,128)(2,1)S(1)} %pad_maximum_fusion.1.rest_0_) | copy-start | bytes 1327108
  34.9 17.8 %copy-start.2 = (bf16[4,256,768]{2,1,0:T(8,128)(2,1)}, bf16[4,256,768]{2,1,0:T(8,128)(2,1)S(1)}, u32[]{:S(2)}) copy-start(bf16[4,256,768]{2,1,0:T(8,128)(2,1)S(1)} %all-to-all-done) | copy-start | bytes 4718596
  34.9 14.0 %collective-permute-start.3 = (bf16[4,48,1152]{2,1,0:T(8,128)(2,1)S(1)}, bf16[4,48,1152]{2,1,0:T(8,128)(2,1)S(1)}, u32[]{:S(2)}, u32[]{:S(2)}) collective-permute-start(bf16[4,48,1152]{2,1,0:T(8,128)(2,1)S(1)} %pad_maximum_fusion.1.rest_0_), channel_id=1, source_target_pairs={{0,6},{2,4},{4,2},{6,0},{8,14},{10,12},{12,10},{14,8},{16,22},{18,... | collective-permute-start | bytes 1327112 | tf_op jit(solution)/shard_map/ppermute | solution.py:718
  36.1 20.7 %collective-permute-start.10 = (bf16[48,1536]{1,0:T(8,128)(2,1)S(1)}, bf16[48,1536]{1,0:T(8,128)(2,1)S(1)}, u32[]{:S(2)}, u32[]{:S(2)}) collective-permute-start(bf16[48,1536]{1,0:T(8,128)(2,1)S(1)} %copy-done.30), channel_id=1, source_target_pairs={{0,8},{2,10},{4,12},{6,14},{8,0},{10,2},{12,4},{14,6},{16,24},{18,... | collective-permute-start | bytes 442376 | tf_op jit(solution)/shard_map/ppermute | solution.py:718
  37.8 19.1 %collective-permute-start.11 = (bf16[48,1536]{1,0:T(8,128)(2,1)S(1)}, bf16[48,1536]{1,0:T(8,128)(2,1)S(1)}, u32[]{:S(2)}, u32[]{:S(2)}) collective-permute-start(bf16[48,1536]{1,0:T(8,128)(2,1)S(1)} %copy-done.30), channel_id=1, source_target_pairs={{0,16},{2,18},{4,20},{6,22},{8,24},{10,26},{12,28},{14,30},{16,0},... | collective-permute-start | bytes 442376 | tf_op jit(solution)/shard_map/ppermute | solution.py:718
  40.4 21.0 %collective-permute-start.4 = (bf16[4,48,1152]{2,1,0:T(8,128)(2,1)S(1)}, bf16[4,48,1152]{2,1,0:T(8,128)(2,1)S(1)}, u32[]{:S(2)}, u32[]{:S(2)}) collective-permute-start(bf16[4,48,1152]{2,1,0:T(8,128)(2,1)S(1)} %pad_maximum_fusion.1.rest_0_), channel_id=1, source_target_pairs={{0,2},{2,0},{4,6},{6,4},{8,10},{10,8},{12,14},{14,12},{16,18},{18,... | collective-permute-start | bytes 1327112 | tf_op jit(solution)/shard_map/ppermute | solution.py:718
  42.1 19.3 %collective-permute-start.5 = (bf16[4,48,1152]{2,1,0:T(8,128)(2,1)S(1)}, bf16[4,48,1152]{2,1,0:T(8,128)(2,1)S(1)}, u32[]{:S(2)}, u32[]{:S(2)}) collective-permute-start(bf16[4,48,1152]{2,1,0:T(8,128)(2,1)S(1)} %pad_maximum_fusion.1.rest_0_), channel_id=1, source_target_pairs={{0,4},{2,6},{4,0},{6,2},{8,12},{10,14},{12,8},{14,10},{16,20},{18,... | collective-permute-start | bytes 1327112 | tf_op jit(solution)/shard_map/ppermute | solution.py:718
  48.9 8.4 %collective-permute-start.12 = (bf16[48,1536]{1,0:T(8,128)(2,1)S(1)}, bf16[48,1536]{1,0:T(8,128)(2,1)S(1)}, u32[]{:S(2)}, u32[]{:S(2)}) collective-permute-start(bf16[48,1536]{1,0:T(8,128)(2,1)S(1)} %copy-done.30), channel_id=1, source_target_pairs={{0,24},{2,26},{4,28},{6,30},{8,16},{10,18},{12,20},{14,22},{16,8},... | collective-permute-start | bytes 442376 | tf_op jit(solution)/shard_map/ppermute | solution.py:718
  56.8 8.1 %collective-permute-start.6 = (bf16[4,48,1152]{2,1,0:T(8,128)(2,1)S(1)}, bf16[4,48,1152]{2,1,0:T(8,128)(2,1)S(1)}, u32[]{:S(2)}, u32[]{:S(2)}) collective-permute-start(bf16[4,48,1152]{2,1,0:T(8,128)(2,1)S(1)} %pad_maximum_fusion.1.rest_0_), channel_id=1, source_target_pairs={{0,1},{1,0},{2,3},{3,2},{4,5},{5,4},{6,7},{7,6},{8,9},{9,8},{10,11... | collective-permute-start | bytes 1327112 | tf_op jit(solution)/shard_map/ppermute | solution.py:718
  56.8 8.1 %collective-permute-start.9 = (bf16[4,48,1152]{2,1,0:T(8,128)(2,1)S(1)}, bf16[4,48,1152]{2,1,0:T(8,128)(2,1)S(1)}, u32[]{:S(2)}, u32[]{:S(2)}) collective-permute-start(bf16[4,48,1152]{2,1,0:T(8,128)(2,1)S(1)} %collective-permute-done.3.rest_3_), channel_id=1, source_target_pairs={{0,1},{1,0},{2,3},{3,2},{4,5},{5,4},{6,7},{7,6},{8,9},{9,8},{10,11... | collective-permute-start | bytes 1327112 | tf_op jit(solution)/shard_map/ppermute | solution.py:718
  57.4 19.7 %copy-start.4 = (bf16[4,48,1536]{2,1,0:T(8,128)(2,1)}, bf16[4,48,1536]{2,1,0:T(8,128)(2,1)S(1)}, u32[]{:S(2)}) copy-start(bf16[4,48,1536]{2,1,0:T(8,128)(2,1)S(1)} %pad_maximum_fusion.rest_0_) | copy-start | bytes 1769476
  61.3 35.4 %collective-permute-start.13 = (bf16[4,48,1536]{2,1,0:T(8,128)(2,1)S(1)}, bf16[4,48,1536]{2,1,0:T(8,128)(2,1)S(1)}, u32[]{:S(2)}, u32[]{:S(2)}) collective-permute-start(bf16[4,48,1536]{2,1,0:T(8,128)(2,1)S(1)} %pad_maximum_fusion.rest_0_), channel_id=1, source_target_pairs={{0,2},{2,0},{4,6},{6,4},{8,10},{10,8},{12,14},{14,12},{16,18},{18,... | collective-permute-start | bytes 1769480 | tf_op jit(solution)/shard_map/ppermute | solution.py:718
  61.9 34.8 %collective-permute-start.14 = (bf16[4,48,1536]{2,1,0:T(8,128)(2,1)S(1)}, bf16[4,48,1536]{2,1,0:T(8,128)(2,1)S(1)}, u32[]{:S(2)}, u32[]{:S(2)}) collective-permute-start(bf16[4,48,1536]{2,1,0:T(8,128)(2,1)S(1)} %pad_maximum_fusion.rest_0_), channel_id=1, source_target_pairs={{0,4},{2,6},{4,0},{6,2},{8,12},{10,14},{12,8},{14,10},{16,20},{18,... | collective-permute-start | bytes 1769480 | tf_op jit(solution)/shard_map/ppermute | solution.py:718
  63.6 34.3 %collective-permute-start.15 = (bf16[4,48,1536]{2,1,0:T(8,128)(2,1)S(1)}, bf16[4,48,1536]{2,1,0:T(8,128)(2,1)S(1)}, u32[]{:S(2)}, u32[]{:S(2)}) collective-permute-start(bf16[4,48,1536]{2,1,0:T(8,128)(2,1)S(1)} %pad_maximum_fusion.rest_0_), channel_id=1, source_target_pairs={{0,6},{2,4},{4,2},{6,0},{8,14},{10,12},{12,10},{14,8},{16,22},{18,... | collective-permute-start | bytes 1769480 | tf_op jit(solution)/shard_map/ppermute | solution.py:718
  64.9 1.8 collective-permute-start.7
  64.9 2.4 collective-permute-start.8
  66.7 31.8 %collective-permute-start.16 = (bf16[4,48,1536]{2,1,0:T(8,128)(2,1)S(1)}, bf16[4,48,1536]{2,1,0:T(8,128)(2,1)S(1)}, u32[]{:S(2)}, u32[]{:S(2)}) collective-permute-start(bf16[4,48,1536]{2,1,0:T(8,128)(2,1)S(1)} %pad_maximum_fusion.rest_0_), channel_id=1, source_target_pairs={{0,1},{1,0},{2,3},{3,2},{4,5},{5,4},{6,7},{7,6},{8,9},{9,8},{10,11... | collective-permute-start | bytes 1769480 | tf_op jit(solution)/shard_map/ppermute | solution.py:718
  96.7 12.3 %copy-start.6 = (bf16[4,48,1536]{2,1,0:T(8,128)(2,1)}, bf16[4,48,1536]{2,1,0:T(8,128)(2,1)S(1)}, u32[]{:S(2)}) copy-start(bf16[4,48,1536]{2,1,0:T(8,128)(2,1)S(1)} %collective-permute-done.13.rest_1_) | copy-start | bytes 1769476
  98.0 2.0 collective-permute-start.17
  98.0 4.0 %collective-permute-start.18 = (bf16[4,48,1536]{2,1,0:T(8,128)(2,1)S(1)}, bf16[4,48,1536]{2,1,0:T(8,128)(2,1)S(1)}, u32[]{:S(2)}, u32[]{:S(2)}) collective-permute-start(bf16[4,48,1536]{2,1,0:T(8,128)(2,1)S(1)} %collective-permute-done.14.rest_2_), channel_id=1, source_target_pairs={{0,1},{1,0},{2,3},{3,2},{4,5},{5,4},{6,7},{7,6},{8,9},{9,8},{10,11... | collective-permute-start | bytes 1769480 | tf_op jit(solution)/shard_map/ppermute | solution.py:718
  98.5 4.4 %collective-permute-start.19 = (bf16[4,48,1536]{2,1,0:T(8,128)(2,1)S(1)}, bf16[4,48,1536]{2,1,0:T(8,128)(2,1)}, u32[]{:S(2)}, u32[]{:S(2)}) collective-permute-start(bf16[4,48,1536]{2,1,0:T(8,128)(2,1)S(1)} %collective-permute-done.15.rest_3_), channel_id=1, source_target_pairs={{0,1},{1,0},{2,3},{3,2},{4,5},{5,4},{6,7},{7,6},{8,9},{9,8},{10,11... | collective-permute-start | bytes 1769480 | tf_op jit(solution)/shard_map/ppermute | solution.py:718
  102.8 29.7 %all-to-all-start.1 = ((bf16[4,256,768]{2,1,0:T(8,128)(2,1)}), bf16[4,256,768]{2,1,0:T(8,128)(2,1)S(1)}, u32[]{:S(2)}, u32[]{:S(2)}) async-start(bf16[4,256,768]{2,1,0:T(8,128)(2,1)} %param.17), calls=%async_computation.1 | async-start | bytes 3145728 | tf_op jit(solution)/shard_map/all_to_all | solution.py:724
  132.6 26.5 %all-to-all-start.2 = ((bf16[4,256,768]{2,1,0:T(8,128)(2,1)}), bf16[4,256,768]{2,1,0:T(8,128)(2,1)S(1)}, u32[]{:S(2)}, u32[]{:S(2)}) async-start(bf16[4,256,768]{2,1,0:T(8,128)(2,1)} %bitcast.49), calls=%async_computation.2 | async-start | bytes 3145728 | tf_op jit(solution)/shard_map/all_to_all | solution.py:724
  136.1 170.4 %reduce-scatter.2.cloned.1.call-start = ((), (), s32[]{:S(2)}) async-start(), calls=%async_computation.6 | async-start | bytes 6082560 | tf_op jit(solution)/shard_map/reduce_scatter | solution.py:789
  181.3 4.7 %collective-permute-start.20 = (bf16[3072,384]{1,0:T(8,128)(2,1)}, bf16[3072,384]{1,0:T(8,128)(2,1)S(1)}, u32[]{:S(2)}, u32[]{:S(2)}) collective-permute-start(bf16[3072,384]{1,0:T(8,128)(2,1)} %get-tuple-element.116), channel_id=1, source_target_pairs={{0,1},{1,0},{2,3},{3,2},{4,5},{5,4},{6,7},{7,6},{8,9},{9,8},{10,11... | collective-permute-start | bytes 7077896 | tf_op jit(solution)/shard_map/ppermute | solution.py:718
  191.7 30.5 %collective-permute-start.21 = (bf16[4,192,384]{2,1,0:T(8,128)(2,1)}, bf16[4,192,384]{2,1,0:T(8,128)(2,1)S(1)}, u32[]{:S(2)}, u32[]{:S(2)}) collective-permute-start(bf16[4,192,384]{2,1,0:T(8,128)(2,1)} %get-tuple-element.118), channel_id=1, source_target_pairs={{0,2},{2,0},{4,6},{6,4},{8,10},{10,8},{12,14},{14,12},{16,18},{18,... | collective-permute-start | bytes 1769480 | tf_op jit(solution)/shard_map/ppermute | solution.py:718
  193.5 28.8 %collective-permute-start.22 = (bf16[4,192,384]{2,1,0:T(8,128)(2,1)}, bf16[4,192,384]{2,1,0:T(8,128)(2,1)S(1)}, u32[]{:S(2)}, u32[]{:S(2)}) collective-permute-start(bf16[4,192,384]{2,1,0:T(8,128)(2,1)} %get-tuple-element.119), channel_id=1, source_target_pairs={{0,4},{2,6},{4,0},{6,2},{8,12},{10,14},{12,8},{14,10},{16,20},{18,... | collective-permute-start | bytes 1769480 | tf_op jit(solution)/shard_map/ppermute | solution.py:718
  195.0 27.3 %collective-permute-start.23 = (bf16[4,192,384]{2,1,0:T(8,128)(2,1)}, bf16[4,192,384]{2,1,0:T(8,128)(2,1)S(1)}, u32[]{:S(2)}, u32[]{:S(2)}) collective-permute-start(bf16[4,192,384]{2,1,0:T(8,128)(2,1)} %get-tuple-element.120), channel_id=1, source_target_pairs={{0,6},{2,4},{4,2},{6,0},{8,14},{10,12},{12,10},{14,8},{16,22},{18,... | collective-permute-start | bytes 1769480 | tf_op jit(solution)/shard_map/ppermute | solution.py:718
  222.2 11.0 %copy-start.33 = (f32[8,768]{1,0:T(8,128)S(1)}, f32[8,768]{1,0:T(8,128)}, u32[]{:S(2)}) copy-start(f32[8,768]{1,0:T(8,128)} %get-tuple-element.145) | copy-start | bytes 73732
  222.2 9.9 %copy-start.21 = (bf16[4,192,384]{2,1,0:T(8,128)(2,1)}, bf16[4,192,384]{2,1,0:T(8,128)(2,1)S(1)}, u32[]{:S(2)}) copy-start(bf16[4,192,384]{2,1,0:T(8,128)(2,1)S(1)} %collective-permute-done.21.b) | copy-start | bytes 1769476
  222.3 9.9 %copy-start.22 = (bf16[4,192,384]{2,1,0:T(8,128)(2,1)}, bf16[4,192,384]{2,1,0:T(8,128)(2,1)S(1)}, u32[]{:S(2)}) copy-start(bf16[4,192,384]{2,1,0:T(8,128)(2,1)S(1)} %collective-permute-done.22.c) | copy-start | bytes 1769476
  222.3 9.9 %copy-start.23 = (bf16[4,192,384]{2,1,0:T(8,128)(2,1)}, bf16[4,192,384]{2,1,0:T(8,128)(2,1)S(1)}, u32[]{:S(2)}) copy-start(bf16[4,192,384]{2,1,0:T(8,128)(2,1)S(1)} %collective-permute-done.23.d) | copy-start | bytes 1769476
  232.2 7.7 %collective-permute-start.24 = (bf16[768,1152]{1,0:T(8,128)(2,1)}, bf16[768,1152]{1,0:T(8,128)(2,1)S(1)}, u32[]{:S(2)}, u32[]{:S(2)}) collective-permute-start(bf16[768,1152]{1,0:T(8,128)(2,1)} %get-tuple-element.125), channel_id=1, source_target_pairs={{0,1},{1,0},{2,3},{3,2},{4,5},{5,4},{6,7},{7,6},{8,9},{9,8},{10,11... | collective-permute-start | bytes 5308424 | tf_op jit(solution)/shard_map/ppermute | solution.py:718
  236.0 49.0 %all-to-all-start.3 = ((bf16[4,192,384]{2,1,0:T(8,128)(2,1)}), bf16[4,192,384]{2,1,0:T(8,128)(2,1)S(1)}, u32[]{:S(2)}, u32[]{:S(2)}) async-start(bf16[4,192,384]{2,1,0:T(8,128)(2,1)} %down_add.1), calls=%async_computation.3 | async-start | bytes 1179648 | tf_op jit(solution)/shard_map/all_to_all | solution.py:771
  244.8 20.4 %collective-permute-start.28 = (bf16[4,48,1152]{2,1,0:T(8,128)(2,1)}, bf16[4,48,1152]{2,1,0:T(8,128)(2,1)S(1)}, u32[]{:S(2)}, u32[]{:S(2)}) collective-permute-start(bf16[4,48,1152]{2,1,0:T(8,128)(2,1)} %get-tuple-element.129), channel_id=1, source_target_pairs={{0,2},{2,0},{4,6},{6,4},{8,10},{10,8},{12,14},{14,12},{16,18},{18,... | collective-permute-start | bytes 1327112 | tf_op jit(solution)/shard_map/ppermute | solution.py:718
  246.4 25.7 %collective-permute-start.29 = (bf16[4,48,1152]{2,1,0:T(8,128)(2,1)}, bf16[4,48,1152]{2,1,0:T(8,128)(2,1)S(1)}, u32[]{:S(2)}, u32[]{:S(2)}) collective-permute-start(bf16[4,48,1152]{2,1,0:T(8,128)(2,1)} %get-tuple-element.130), channel_id=1, source_target_pairs={{0,4},{2,6},{4,0},{6,2},{8,12},{10,14},{12,8},{14,10},{16,20},{18,... | collective-permute-start | bytes 1327112 | tf_op jit(solution)/shard_map/ppermute | solution.py:718
  247.8 24.2 %collective-permute-start.30 = (bf16[4,48,1152]{2,1,0:T(8,128)(2,1)}, bf16[4,48,1152]{2,1,0:T(8,128)(2,1)S(1)}, u32[]{:S(2)}, u32[]{:S(2)}) collective-permute-start(bf16[4,48,1152]{2,1,0:T(8,128)(2,1)} %get-tuple-element.131), channel_id=1, source_target_pairs={{0,6},{2,4},{4,2},{6,0},{8,14},{10,12},{12,10},{14,8},{16,22},{18,... | collective-permute-start | bytes 1327112 | tf_op jit(solution)/shard_map/ppermute | solution.py:718
  261.2 29.0 %collective-permute-start.25 = (bf16[256,768]{1,0:T(8,128)(2,1)}, bf16[256,768]{1,0:T(8,128)(2,1)S(1)}, u32[]{:S(2)}, u32[]{:S(2)}) collective-permute-start(bf16[256,768]{1,0:T(8,128)(2,1)} %get-tuple-element.135), channel_id=1, source_target_pairs={{0,2},{2,0},{4,6},{6,4},{8,10},{10,8},{12,14},{14,12},{16,18},{18,... | collective-permute-start | bytes 1179656 | tf_op jit(solution)/shard_map/ppermute | solution.py:718
  262.8 28.1 %collective-permute-start.26 = (bf16[256,768]{1,0:T(8,128)(2,1)}, bf16[256,768]{1,0:T(8,128)(2,1)S(1)}, u32[]{:S(2)}, u32[]{:S(2)}) collective-permute-start(bf16[256,768]{1,0:T(8,128)(2,1)} %get-tuple-element.136), channel_id=1, source_target_pairs={{0,4},{2,6},{4,0},{6,2},{8,12},{10,14},{12,8},{14,10},{16,20},{18,... | collective-permute-start | bytes 1179656 | tf_op jit(solution)/shard_map/ppermute | solution.py:718
  265.2 25.7 %collective-permute-start.27 = (bf16[256,768]{1,0:T(8,128)(2,1)}, bf16[256,768]{1,0:T(8,128)(2,1)S(1)}, u32[]{:S(2)}, u32[]{:S(2)}) collective-permute-start(bf16[256,768]{1,0:T(8,128)(2,1)} %get-tuple-element.137), channel_id=1, source_target_pairs={{0,6},{2,4},{4,2},{6,0},{8,14},{10,12},{12,10},{14,8},{16,22},{18,... | collective-permute-start | bytes 1179656 | tf_op jit(solution)/shard_map/ppermute | solution.py:718
  275.9 1.2 collective-permute-start.34
  277.1 6.0 %collective-permute-start.35 = (f32[72,128]{1,0:T(8,128)S(1)}, f32[72,128]{1,0:T(8,128)S(1)}, u32[]{:S(2)}, u32[]{:S(2)}) collective-permute-start(f32[72,128]{1,0:T(8,128)S(1)} %add.66), channel_id=1, source_target_pairs={{0,8},{2,10},{4,12},{6,14},{8,0},{10,2},{12,4},{14,6},{16,24},{18,... | collective-permute-start | bytes 110600 | tf_op jit(solution)/shard_map/ppermute | solution.py:718
  283.1 5.2 %collective-permute-start.36 = (f32[72,128]{1,0:T(8,128)S(1)}, f32[72,128]{1,0:T(8,128)S(1)}, u32[]{:S(2)}, u32[]{:S(2)}) collective-permute-start(f32[72,128]{1,0:T(8,128)S(1)} %add.67), channel_id=1, source_target_pairs={{0,16},{2,18},{4,20},{6,22},{8,24},{10,26},{12,28},{14,30},{16,0},... | collective-permute-start | bytes 110600 | tf_op jit(solution)/shard_map/ppermute | solution.py:718
  285.0 13.2 %collective-permute-start.31 = (bf16[48,1152]{1,0:T(8,128)(2,1)}, bf16[48,1152]{1,0:T(8,128)(2,1)S(1)}, u32[]{:S(2)}, u32[]{:S(2)}) collective-permute-start(bf16[48,1152]{1,0:T(8,128)(2,1)} %get-tuple-element.139), channel_id=1, source_target_pairs={{0,8},{2,10},{4,12},{6,14},{8,0},{10,2},{12,4},{14,6},{16,24},{18,... | collective-permute-start | bytes 331784 | tf_op jit(solution)/shard_map/ppermute | solution.py:718
  288.3 12.6 %collective-permute-start.32 = (bf16[48,1152]{1,0:T(8,128)(2,1)}, bf16[48,1152]{1,0:T(8,128)(2,1)S(1)}, u32[]{:S(2)}, u32[]{:S(2)}) collective-permute-start(bf16[48,1152]{1,0:T(8,128)(2,1)} %get-tuple-element.140), channel_id=1, source_target_pairs={{0,16},{2,18},{4,20},{6,22},{8,24},{10,26},{12,28},{14,30},{16,0},... | collective-permute-start | bytes 331784 | tf_op jit(solution)/shard_map/ppermute | solution.py:718
  290.2 10.6 %collective-permute-start.33 = (bf16[48,1152]{1,0:T(8,128)(2,1)}, bf16[48,1152]{1,0:T(8,128)(2,1)S(1)}, u32[]{:S(2)}, u32[]{:S(2)}) collective-permute-start(bf16[48,1152]{1,0:T(8,128)(2,1)} %get-tuple-element.141), channel_id=1, source_target_pairs={{0,24},{2,26},{4,28},{6,30},{8,16},{10,18},{12,20},{14,22},{16,8},... | collective-permute-start | bytes 331784 | tf_op jit(solution)/shard_map/ppermute | solution.py:718
  290.9 4.8 %collective-permute-start.37 = (f32[72,128]{1,0:T(8,128)S(1)}, f32[72,128]{1,0:T(8,128)S(1)}, u32[]{:S(2)}, u32[]{:S(2)}) collective-permute-start(f32[72,128]{1,0:T(8,128)S(1)} %add.68), channel_id=1, source_target_pairs={{0,2},{2,0},{4,6},{6,4},{8,10},{10,8},{12,14},{14,12},{16,18},{18,... | collective-permute-start | bytes 110600 | tf_op jit(solution)/shard_map/ppermute | solution.py:718
  291.0 17.2 %copy-start.1 = (s32[4,4,8]{2,1,0:T(4,128)S(1)}, s32[4,4,8]{2,1,0:T(4,128)}, u32[]{:S(2)}) copy-start(s32[4,4,8]{2,1,0:T(4,128)} %param.18) | copy-start | bytes 1540
  295.8 5.8 %collective-permute-start.38 = (f32[72,128]{1,0:T(8,128)S(1)}, f32[72,128]{1,0:T(8,128)S(1)}, u32[]{:S(2)}, u32[]{:S(2)}) collective-permute-start(f32[72,128]{1,0:T(8,128)S(1)} %add.69), channel_id=1, source_target_pairs={{0,4},{2,6},{4,0},{6,2},{8,12},{10,14},{12,8},{14,10},{16,20},{18,... | collective-permute-start | bytes 110600 | tf_op jit(solution)/shard_map/ppermute | solution.py:718
  (23 other events, 75.0 us)
Sparse Core Ops, SparseCore 0:
  11.5 97.4 all-gather.1
  170.9 135.5 reduce-scatter.1
